TPU v7x, 256 devices: a whole 4x4x8 slice. The times are simulated.
256 devices in a mesh: group: 16 (over y, x_hi, core), tile: 16 (over x_lo, z).
Axes of the slice: x: 4 (x_hi: 2, x_lo: 2; x = x_hi * 2 + x_lo), y: 4, z: 8, core: 2. Of those that a mesh axis runs over, the one named last changes fastest.
Arguments:
- coupling: float32 [64, 1024, 768], P('group', None, 'tile'), may hold values from -6 to 6
- interior_solve: float32 [64, 768, 1024], P('group', 'tile'), may hold values from -0.21875 to 0.21875
- boundary_stiffness: float32 [64, 1024, 1024], P('group', 'tile'), may hold values from -6 to 6
- migration: int32 [64], replicated, may hold values from -1 to 31, as said below
Outputs:
- condensed: float32 [32, 1024, 1024], P('group', 'tile')
Inputs may be any that keep to these rules, and one draw needn't show every extreme that they name: `migration`: every condensed slot is named by exactly one RVE slot; RVE slots of group g are g * 4 to g * 4 + 3; the condensed slots of group g are named only by RVE slots of group g or of its partner, the group whose index differs from g in the lowest bit; some group holds 4 plastic RVEs.
All inputs are finite; a program needn't handle non-finite values.
Results may differ from a plain program's by a relative error of at most 0.000071.
Values sent between devices are 32-bit elements; how exact they have to be, the bound alone decides.
No kernel may reach another device: no remote copies, remote signals or barrier semaphores. Data moves between devices by JAX's collectives and lax.ppermute only.
A program may use at most 64 MiB of HBM per device.

v0:
```python
import jax
import jax.numpy as jnp
from jax import lax
from jax.sharding import Mesh
from jax.sharding import PartitionSpec as P

OWN = 2
TILE = ("tile_0", "tile_1")


def joined_along(tiles, dim):
    dims = list(tiles.shape[1:])
    dims[dim] *= tiles.shape[0]
    return jnp.moveaxis(tiles, 0, dim).reshape(dims)


def all_blocks(array, axes, order):
    tiles = array
    for k in order:
        tiles = lax.all_gather(tiles, axes[k])
    done = order[::-1]
    back = [done.index(k) for k in range(len(axes))]
    tiles = tiles.transpose(*back, *range(len(axes), tiles.ndim))
    return tiles.reshape(-1, *array.shape)


def whole_of(array, axes, order, dim):
    return joined_along(all_blocks(array, axes, order), dim)


def swapped(array, axis, distance):
    return lax.ppermute(array, axis, [(i, i ^ 1 << distance) for i in range(lax.axis_size(axis))])


def condense(coupling_cols, solve_rows, stiff_rows):
    coupling_block = lax.all_to_all(coupling_cols, TILE, split_axis=0, concat_axis=1, tiled=True)
    product = jnp.dot(
        coupling_block,
        whole_of(solve_rows, TILE, (0, 1), 0),
        precision=lax.Precision.HIGHEST,
        preferred_element_type=jnp.float32,
    )
    return stiff_rows - product


def select_slots(stacked, positions, present):
    chosen = jnp.take(stacked, positions, axis=0)
    shaped = present.reshape((-1,) + (1,) * (stacked.ndim - 1))
    return jnp.where(shaped, chosen, jnp.zeros_like(chosen))


def body(coupling, interior_solve, boundary_stiffness, migration):
    home_count = coupling.shape[0]
    mygroup = lax.axis_index("group")
    partner = jnp.bitwise_xor(mygroup, 1)
    own_plan = lax.dynamic_slice_in_dim(migration, mygroup * home_count, home_count)
    slot_ids = jnp.arange(OWN, dtype=jnp.int32)
    local_ids = jnp.arange(home_count, dtype=jnp.int32)

    def locate(wanted):
        matches = own_plan[None, :] == wanted[:, None]
        positions = jnp.sum(jnp.where(matches, local_ids[None, :], 0), axis=1)
        return (positions, jnp.any(matches, axis=1))

    mine_index, mine_here = locate(mygroup * OWN + slot_ids)
    their_index, their_here = locate(partner * OWN + slot_ids)
    keep_mask = mine_here[:, None, None]
    outgoing = (
        select_slots(coupling, their_index, their_here),
        select_slots(interior_solve, their_index, their_here),
        select_slots(boundary_stiffness, their_index, their_here),
    )
    arrived = swapped((outgoing[0], outgoing[1], outgoing[2]), "group", 0)
    kept_coupling = jnp.where(keep_mask, jnp.take(coupling, mine_index, axis=0), arrived[0])
    kept_solve = jnp.where(keep_mask, jnp.take(interior_solve, mine_index, axis=0), arrived[1])
    kept_stiff = jnp.where(keep_mask, jnp.take(boundary_stiffness, mine_index, axis=0), arrived[2])
    result = jnp.stack(
        [condense(kept_coupling[slot], kept_solve[slot], kept_stiff[slot]) for slot in range(OWN)]
    )
    return result


def solution(mesh):
    finer = Mesh(mesh.devices.reshape(mesh.shape["group"], 2, 8), ("group", "tile_0", "tile_1"))
    in_specs = (P("group", None, TILE), P("group", TILE, None), P("group", TILE, None), P())
    out_specs = P("group", TILE, None)
    return jax.shard_map(body, mesh=finer, in_specs=in_specs, out_specs=out_specs, check_vma=False)
```

profile of v0, /device:TPU:24, one launch (start us, length us, event | category | flops | bytes accessed | tf_op | source)
XLA Modules:
  0.0 136.2 jit_solution(11742060493607924064)
XLA Ops:
  6.5 0.0 copy-start
  6.5 0.0 all-gather.5.cloned.1.call-start
  6.5 0.8 dynamic_slice.3
  7.4 0.2 fusion.4
  7.6 0.2 compare_reduce_fusion.1
  7.8 0.0 copy-start.2
  7.8 1.8 %gather_fusion.5 = f32[2,48,1024]{2,1,0:T(8,128)S(1)} fusion(f32[4,48,1024]{2,1,0:T(8,128)} %param.11, s32[1024]{0:T(1024)S(1)} %pad_clamp_fusion), kind=kCustom, calls=%fused_computation.5.clone | custom fusion | bytes 786440 | tf_op jit(solution)/shard_map/jit(_take)/gather | solution.py:47
  9.6 0.1 select_select_fusion.2
  9.7 0.1 collective-permute-start.2
  9.9 1.7 %gather_fusion.4 = f32[2,48,1024]{2,1,0:T(8,128)S(1)} fusion(f32[4,48,1024]{2,1,0:T(8,128)} %param.11, s32[1024]{0:T(1024)S(1)} %pad_clamp_fusion.1), kind=kCustom, calls=%fused_computation.2.clone | custom fusion | bytes 786440 | tf_op jit(solution)/shard_map/jit(_take)/gather | solution.py:75
  11.6 0.0 collective-permute-done.2
  11.6 0.1 select_select_fusion.3
  11.8 8.1 %all_gather.18 = f32[2,48,1024]{2,1,0:T(8,128)} all-gather(f32[1,48,1024]{2,1,0:T(8,128)S(1)} %get-tuple-element.14), channel_id=1, replica_groups=mesh['group'=16,'tile_0'=2,'tile_1'=8] {'tile_0'}, dimensions={0}, use_global_device_ids=true | all-gather | bytes 589824 | tf_op jit(solution)/shard_map/all_gather | solution.py:20
  19.8 0.0 all-gather.5.cloned.1.call-update
  19.9 0.0 all-gather.7.cloned.1.call-start
  19.9 7.3 %all_gather.21 = f32[2,48,1024]{2,1,0:T(8,128)} all-gather(f32[1,48,1024]{2,1,0:T(8,128)S(1)} %get-tuple-element.15), channel_id=1, replica_groups=mesh['group'=16,'tile_0'=2,'tile_1'=8] {'tile_0'}, dimensions={0}, use_global_device_ids=true | all-gather | bytes 589824 | tf_op jit(solution)/shard_map/all_gather | solution.py:20
  27.2 0.0 all-gather.7.cloned.1.call-update
  27.2 0.0 copy-done.2
  27.2 0.6 gather_fusion.3
  27.8 0.1 select_select_fusion.4
  27.9 0.1 collective-permute-start.1
  28.0 0.0 copy-done
  28.0 0.6 gather_fusion.1
  28.6 0.1 select_select_fusion
  28.8 0.6 collective-permute-start
  29.3 0.6 gather_fusion.2
  29.9 0.0 collective-permute-done.1
  29.9 1.1 select_select_fusion.5
  31.1 0.1 all_to_all.28
  31.2 0.1 copy.32
  31.3 0.9 reshape.107
  32.2 9.5 %all-to-all-start = ((f32[16,1,3072]{2,1,0:T(1,128)}), f32[16,1,3072]{2,1,0:T(1,128)S(1)}, u32[]{:S(2)}, u32[]{:S(2)}) async-start(f32[16,1,3072]{2,1,0:T(1,128)} %reshape.107), calls=%async_computation | async-start | bytes 393216 | tf_op jit(solution)/shard_map/all_to_all | solution.py:36
  41.8 0.1 all_to_all.32
  41.9 0.1 copy.31
  42.0 0.9 reshape.105
  42.9 10.9 %all-to-all-done = f32[16,1,3072]{2,1,0:T(1,128)S(1)} async-done(((f32[16,1,3072]{2,1,0:T(1,128)}), f32[16,1,3072]{2,1,0:T(1,128)S(1)}, u32[]{:S(2)}, u32[]{:S(2)}) %all-to-all-start) | async-done | bytes 196640 | tf_op jit(solution)/shard_map/all_to_all | solution.py:36
  53.8 4.1 %all-to-all-start.1 = ((f32[16,1,3072]{2,1,0:T(1,128)}), f32[16,1,3072]{2,1,0:T(1,128)S(1)}, u32[]{:S(2)}, u32[]{:S(2)}) async-start(f32[16,1,3072]{2,1,0:T(1,128)} %reshape.105), calls=%async_computation.1 | async-start | bytes 393216 | tf_op jit(solution)/shard_map/all_to_all | solution.py:36
  57.9 0.6 gather_fusion
  58.5 0.0 collective-permute-done
  58.5 1.2 select_select_fusion.1
  59.7 0.5 broadcast.109
  60.2 1.1 reduce
  61.3 0.1 reshape.108
  61.5 8.1 %all-to-all-done.1 = f32[16,1,3072]{2,1,0:T(1,128)S(1)} async-done(((f32[16,1,3072]{2,1,0:T(1,128)}), f32[16,1,3072]{2,1,0:T(1,128)S(1)}, u32[]{:S(2)}, u32[]{:S(2)}) %all-to-all-start.1) | async-done | bytes 196640 | tf_op jit(solution)/shard_map/all_to_all | solution.py:36
  69.6 1.1 reduce.1
  70.7 0.1 reshape.106
  70.8 5.3 %all-gather.5.cloned.1.call-done = f32[16,48,1024]{2,1,0:T(8,128)} async-done(((f32[2,48,1024]{2,1,0:T(8,128)}), f32[16,48,1024]{2,1,0:T(8,128)}) %all-gather.5.cloned.1.call-update) | async-done | bytes 3145744 | tf_op jit(solution)/shard_map/all_gather | solution.py:20
  76.1 4.0 %copy.23 = f32[2,8,48,1024]{3,2,1,0:T(8,128)} copy(f32[2,8,48,1024]{3,2,0,1:T(8,128)} %bitcast.48) | data formatting | bytes 6291456 | tf_op jit(solution)/shard_map/transpose | solution.py:23
  80.1 41.4 %all-gather.7.cloned.1.call-done = f32[16,48,1024]{2,1,0:T(8,128)} async-done(((f32[2,48,1024]{2,1,0:T(8,128)}), f32[16,48,1024]{2,1,0:T(8,128)}) %all-gather.7.cloned.1.call-update) | async-done | bytes 3145744 | tf_op jit(solution)/shard_map/all_gather | solution.py:20
  121.6 0.0 copy-start.1
  121.6 2.3 %copy.26 = f32[2,8,48,1024]{3,2,1,0:T(8,128)S(1)} copy(f32[2,8,48,1024]{3,2,0,1:T(8,128)} %bitcast.49) | data formatting | bytes 6291456 | tf_op jit(solution)/shard_map/transpose | solution.py:23
  123.8 0.0 copy-start.3
  123.8 0.6 copy-done.1
  124.4 2.1 %fusion.8 = f32[64,1024]{1,0:T(8,128)S(1)} fusion(f32[64,768]{0,1:T(8,128)S(1)} %bitcast.50, f32[768,1024]{1,0:T(8,128)S(1)} %bitcast.47), kind=kOutput, calls=%fused_computation.37 | convolution fusion | flops 603979776 | bytes 3604480 | tf_op jit(solution)/shard_map/dot_general | solution.py:37
  126.5 0.0 copy-done.3
  126.5 2.1 %fusion.3 = (f32[2,64,1024]{2,1,0:T(8,128)S(1)}, f32[2,64,1024]{2,1,0:T(8,128)S(1)}) fusion(f32[64,1024]{1,0:T(8,128)S(1)} %fusion.8, f32[2,64,1024]{2,1,0:T(8,128)S(1)} %select_select_fusion.1, f32[64,768]{0,1:T(8,128)S(1)} %bitcast.51, f32[768,1024]{1,0:T(8,128)S(1)} %bitcast.46, ...), kind=kOutput, output_to_operand_aliasing={{0}: (4, {}), {1}: (4, {})}, calls=%fused_computation.18 | convolution fusion | flops 604110848 | bytes 4849664 | tf_op jit(solution)/shard_map/dot_general | solution.py:37
  128.5 0.0 copy-start.4
  128.5 0.8 copy-done.4
  (10 shorter events, 0.1 us)
Async XLA Ops:
  6.5 21.5 %copy-start = (f32[4,64,1024]{2,1,0:T(8,128)S(1)}, f32[4,64,1024]{2,1,0:T(8,128)}, u32[]{:S(2)}) copy-start(f32[4,64,1024]{2,1,0:T(8,128)} %param.12) | copy-start | bytes 3145732
  6.5 69.6 %all-gather.5.cloned.1.call-start = ((), (), s32[]{:S(2)}) async-start(), calls=%async_computation.2 | async-start | bytes 3538944 | tf_op jit(solution)/shard_map/all_gather | solution.py:20
  7.8 19.4 %copy-start.2 = (f32[4,1024,48]{1,2,0:T(8,128)S(1)}, f32[4,1024,48]{1,2,0:T(8,128)}, u32[]{:S(2)}) copy-start(f32[4,1024,48]{1,2,0:T(8,128)} %param.10) | copy-start | bytes 2359300
  9.7 1.9 %collective-permute-start.2 = (f32[2,48,1024]{2,1,0:T(8,128)S(1)}, f32[2,48,1024]{2,1,0:T(8,128)S(1)}, u32[]{:S(2)}, u32[]{:S(2)}) collective-permute-start(f32[2,48,1024]{2,1,0:T(8,128)S(1)} %select_select_fusion.2), channel_id=1, source_target_pairs={{0,16},{16,0},{32,48},{48,32},{64,80},{80,64},{96,112},{112,96},{1... | collective-permute-start | bytes 1179656 | tf_op jit(solution)/shard_map/ppermute | solution.py:32
  19.9 101.7 %all-gather.7.cloned.1.call-start = ((), (), s32[]{:S(2)}) async-start(), calls=%async_computation.3 | async-start | bytes 3538944 | tf_op jit(solution)/shard_map/all_gather | solution.py:20
  27.9 2.0 %collective-permute-start.1 = (f32[2,1024,48]{1,2,0:T(8,128)S(1)}, f32[2,1024,48]{1,2,0:T(8,128)}, u32[]{:S(2)}, u32[]{:S(2)}) collective-permute-start(f32[2,1024,48]{1,2,0:T(8,128)S(1)} %select_select_fusion.4), channel_id=1, source_target_pairs={{0,16},{16,0},{32,48},{48,32},{64,80},{80,64},{96,112},{112,96},{1... | collective-permute-start | bytes 1179656 | tf_op jit(solution)/shard_map/ppermute | solution.py:32
  28.8 29.7 %collective-permute-start = (f32[2,64,1024]{2,1,0:T(8,128)S(1)}, f32[2,64,1024]{2,1,0:T(8,128)}, u32[]{:S(2)}, u32[]{:S(2)}) collective-permute-start(f32[2,64,1024]{2,1,0:T(8,128)S(1)} %select_select_fusion), channel_id=1, source_target_pairs={{0,16},{16,0},{32,48},{48,32},{64,80},{80,64},{96,112},{112,96},{1... | collective-permute-start | bytes 1572872 | tf_op jit(solution)/shard_map/ppermute | solution.py:32
  32.2 21.5 %all-to-all-start = ((f32[16,1,3072]{2,1,0:T(1,128)}), f32[16,1,3072]{2,1,0:T(1,128)S(1)}, u32[]{:S(2)}, u32[]{:S(2)}) async-start(f32[16,1,3072]{2,1,0:T(1,128)} %reshape.107), calls=%async_computation | async-start | bytes 393216 | tf_op jit(solution)/shard_map/all_to_all | solution.py:36
  53.8 15.8 %all-to-all-start.1 = ((f32[16,1,3072]{2,1,0:T(1,128)}), f32[16,1,3072]{2,1,0:T(1,128)S(1)}, u32[]{:S(2)}, u32[]{:S(2)}) async-start(f32[16,1,3072]{2,1,0:T(1,128)} %reshape.105), calls=%async_computation.1 | async-start | bytes 393216 | tf_op jit(solution)/shard_map/all_to_all | solution.py:36
  121.6 2.8 %copy-start.1 = (f32[2,8,48,1024]{3,2,1,0:T(8,128)S(1)}, f32[2,8,48,1024]{3,2,1,0:T(8,128)}, u32[]{:S(2)}) copy-start(f32[2,8,48,1024]{3,2,1,0:T(8,128)} %copy.23) | copy-start | bytes 9437188
  123.8 2.6 %copy-start.3 = (f32[2,64,1024]{2,1,0:T(8,128)S(1)}, f32[2,64,1024]{2,1,0:T(8,128)}, u32[]{:S(2)}) copy-start(f32[2,64,1024]{2,1,0:T(8,128)} %custom-call.12) | copy-start | bytes 1572868
  128.5 0.8 copy-start.4
Sparse Core Ops, SparseCore 0:
  20.0 56.1 all-gather.4
  77.9 43.6 all-gather.6
where the time goes:
time: 138 us; the launch traced here: 136 us
  waiting for transfers between devices  65.8 us (48%)
  local copies, waits for them, and re-layouts  17.4 us (13%)
  blocking collectives  15.4 us (11%)
  starting transfers between devices  14.4 us (10%)
  between operations  13.7 us (10%)
  other arithmetic  5.39 us (4%)
  matrix products  4.12 us (3%)
    all_gather x2, waiting for transfers between devices, all_blocks(): tiles = lax.all_gather(tiles, axes[k])  46.7 us
    all_to_all x2, waiting for transfers between devices, condense(): lax.all_to_all(coupling_cols, TILE, split_axis=0, concat_axis=1, tiled=True)  19 us
    all_gather x2, blocking collectives, all_blocks(): tiles = lax.all_gather(tiles, axes[k])  15.4 us
    all_to_all x2, starting transfers between devices, condense(): lax.all_to_all(coupling_cols, TILE, split_axis=0, concat_axis=1, tiled=True)  13.6 us
    transpose x2, local copies, waits for them, and re-layouts, all_blocks(): tiles = tiles.transpose(*back, *range(len(axes), tiles.ndim))  6.27 us
    dot_general x2, matrix products, condense(): jnp.dot(coupling_block, whole_of(solve_rows, TILE, (0, 1), 0), precision=...  4.12 us
    unnamed x14, local copies, waits for them, and re-layouts  3.43 us
    gather x3, local copies, waits for them, and re-layouts, select_slots(): chosen = jnp.take(stacked, positions, axis=0)  2.93 us
  transfers between devices with their start and end apart: 7, of which 4 were waited for; matrix products, arithmetic and copies ran while one was open for 11% of the time, Pallas kernels for 0%

commit v1 on v0

v1 whole, which is shorter than its diff:
```python
import jax
import jax.numpy as jnp
from jax import lax
from jax.experimental import pallas as pl
from jax.experimental.pallas import tpu as pltpu
from jax.sharding import Mesh
from jax.sharding import PartitionSpec as P

OWN = 2
TILE = ("tile_0", "tile_1")
LANES = 128
PARAMS = pltpu.CompilerParams(vmem_limit_bytes=32 * 1024 * 1024)
SMEM = pl.BlockSpec(memory_space=pltpu.SMEM)
VMEM = pl.BlockSpec(memory_space=pltpu.VMEM)
HBM = pl.BlockSpec(memory_space=pltpu.HBM)


def hops(slot):
    return (4, 3) if slot == 0 else (3, 4)


def locate(plan, group, wanted, home):
    position, here = jnp.int32(0), jnp.bool_(False)
    for k in range(home):
        match = plan[group * home + k] == wanted
        position = jnp.where(match, jnp.int32(k), position)
        here = jnp.logical_or(here, match)
    return position, here


def pack(plan, coupling, solve, for_partner):
    home, depth, width = solve.shape
    blocks = width // LANES

    def kernel(plan_ref, c_hbm, x_hbm, out0, out1, c_buf, x_sem, c_sem):
        group = lax.axis_index("group")
        place = lax.axis_index("tile_1")
        owner = jnp.bitwise_xor(group, 1) if for_partner else group
        outs = (out0, out1)
        copies = []
        for slot in range(OWN):
            position, _ = locate(plan_ref, group, owner * OWN + slot, home)
            c_copy = pltpu.make_async_copy(c_hbm.at[position], c_buf.at[slot], c_sem.at[slot])
            c_copy.start()
            x_copies = []
            up = hops(slot)[0]
            for n in range(blocks):
                x_copy = pltpu.make_async_copy(
                    x_hbm.at[position, :, pl.ds(n * LANES, LANES)], outs[slot].at[up + n], x_sem.at[slot, n]
                )
                x_copy.start()
                x_copies.append(x_copy)
            copies.append((c_copy, x_copies))
        low = lax.broadcasted_iota(jnp.int32, (depth, LANES), 1) < LANES // 2
        for slot in range(OWN):
            c_copy, x_copies = copies[slot]
            up = hops(slot)[0]
            c_copy.wait()
            for m in range(blocks // 2):
                first = c_buf[slot, :, pl.ds(m * LANES, LANES)]
                second = c_buf[slot, :, pl.ds((m + blocks // 2) * LANES, LANES)]
                even = jnp.where(low, first, pltpu.roll(second, LANES // 2, 1))
                odd = jnp.where(low, pltpu.roll(first, LANES // 2, 1), second)
                for to, piece in ((2 * m, even), (2 * m + 1, odd)):
                    ahead = jnp.bitwise_and(to - place, blocks - 1)
                    spot = jnp.where(ahead == 0, 15, jnp.where(ahead <= up, ahead - 1, ahead + 7))
                    outs[slot][spot] = piece
            for x_copy in x_copies:
                x_copy.wait()

    packet = jax.ShapeDtypeStruct((2 * blocks, depth, LANES), jnp.float32)
    return pl.pallas_call(
        kernel,
        out_shape=(packet, packet),
        in_specs=[SMEM, HBM, HBM],
        out_specs=(VMEM, VMEM),
        scratch_shapes=[
            pltpu.VMEM((OWN, depth, width), jnp.float32),
            pltpu.SemaphoreType.DMA((OWN, blocks)),
            pltpu.SemaphoreType.DMA((OWN,)),
        ],
        compiler_params=PARAMS,
        name="pack_partner" if for_partner else "pack_own",
    )(plan, coupling, solve)


def merge(plan, arrived, local, slot, home):
    total, depth, _ = arrived.shape
    up, down = hops(slot)
    blocks = total // 2

    def kernel(plan_ref, arrived_ref, local_ref, up_ref, down_ref, own_ref):
        group = lax.axis_index("group")
        _, here = locate(plan_ref, group, group * OWN + slot, home)

        def put(source):
            up_ref[...] = source[0 : up + blocks]
            down_ref[...] = source[up : total - 1]
            own_ref[...] = source[total - 1]

        @pl.when(here)
        def _():
            put(local_ref)

        @pl.when(jnp.logical_not(here))
        def _():
            put(arrived_ref)

    return pl.pallas_call(
        kernel,
        out_shape=(
            jax.ShapeDtypeStruct((up + blocks, depth, LANES), jnp.float32),
            jax.ShapeDtypeStruct((down + blocks, depth, LANES), jnp.float32),
            jax.ShapeDtypeStruct((depth, LANES), jnp.float32),
        ),
        in_specs=[SMEM, VMEM, VMEM],
        out_specs=(VMEM, VMEM, VMEM),
        compiler_params=PARAMS,
        name=f"merge_{slot}",
    )(plan, arrived, local)


def stiff_out(plan, stiff):
    home, rows, width = stiff.shape

    def kernel(plan_ref, b_hbm, out_ref, sem):
        group = lax.axis_index("group")
        copies = []
        for slot in range(OWN):
            position, _ = locate(plan_ref, group, jnp.bitwise_xor(group, 1) * OWN + slot, home)
            copy = pltpu.make_async_copy(b_hbm.at[position], out_ref.at[slot], sem.at[slot])
            copy.start()
            copies.append(copy)
        for copy in copies:
            copy.wait()

    return pl.pallas_call(
        kernel,
        out_shape=jax.ShapeDtypeStruct((OWN, rows, width), jnp.float32),
        in_specs=[SMEM, HBM],
        out_specs=VMEM,
        scratch_shapes=[pltpu.SemaphoreType.DMA((OWN,))],
        compiler_params=PARAMS,
        name="stiff_out",
    )(plan, stiff)


def stiff_merge(plan, stiff, arrived):
    home, rows, width = stiff.shape

    def kernel(plan_ref, b_hbm, arrived_ref, out_ref, sem):
        group = lax.axis_index("group")
        for slot in range(OWN):
            position, here = locate(plan_ref, group, group * OWN + slot, home)

            @pl.when(here)
            def _():
                copy = pltpu.make_async_copy(b_hbm.at[position], out_ref.at[slot], sem.at[slot])
                copy.start()
                copy.wait()

            @pl.when(jnp.logical_not(here))
            def _():
                out_ref[slot] = arrived_ref[slot]

    return pl.pallas_call(
        kernel,
        out_shape=jax.ShapeDtypeStruct((OWN, rows, width), jnp.float32),
        in_specs=[SMEM, HBM, VMEM],
        out_specs=VMEM,
        scratch_shapes=[pltpu.SemaphoreType.DMA((OWN,))],
        compiler_params=PARAMS,
        name="stiff_merge",
    )(plan, stiff, arrived)


def split(value):
    high = value.astype(jnp.bfloat16)
    return high, (value - high.astype(jnp.float32)).astype(jnp.bfloat16)


def add_chunks(total_ref, chunks, start):
    width = total_ref.shape[1]
    pairs = width // (2 * LANES)
    for packet, first, piece in chunks:
        c_high, c_low = split(piece)
        left = jnp.concatenate([c_high, c_high, c_low], axis=0)
        for n in range(pairs):
            x = jnp.concatenate([packet[first + 2 * n], packet[first + 2 * n + 1]], axis=1)
            x_high, x_low = split(x)
            right = jnp.concatenate([x_high, x_low, x_high], axis=0)
            product = lax.dot_general(left, right, (((0,), (0,)), ((), ())), preferred_element_type=jnp.float32)
            where = (slice(None), pl.ds(2 * n * LANES, 2 * LANES))
            total_ref[where] = product if start else total_ref[where] + product
        start = False


def accumulate(total, sources, width, name):
    packets = []
    layout = []
    for packet, first, piece in sources:
        packets.append(packet)
        if isinstance(piece, int):
            layout.append((len(packets) - 1, first, None, piece))
        else:
            packets.append(piece)
            layout.append((len(packets) - 2, first, len(packets) - 1, None))
    given = [] if total is None else [total]
    n_given = len(given)

    def kernel(*refs):
        total_ref = refs[-1]
        ins = refs[n_given:-1]
        if n_given:
            total_ref[...] = refs[0][...]
        chunks = [
            (ins[k], first, ins[own][...] if own is not None else ins[k][index]) for k, first, own, index in layout
        ]
        add_chunks(total_ref, chunks, not n_given)

    return pl.pallas_call(
        kernel,
        out_shape=jax.ShapeDtypeStruct((LANES, width), jnp.float32),
        in_specs=[VMEM] * (n_given + len(packets)),
        out_specs=VMEM,
        input_output_aliases={0: 0} if n_given else {},
        compiler_params=PARAMS,
        cost_estimate=pl.CostEstimate(flops=2 * 144 * 128 * 1024, bytes_accessed=1 << 20, transcendentals=0),
        name=name,
    )(*given, *packets)


def last_chunk(total, packet, first, index, stiff, slot, name):
    rows, width = LANES // 2, total.shape[1]

    def kernel(total_ref, packet_ref, stiff_ref, send_ref, keep_ref, sum_ref):
        sum_ref[...] = total_ref[...]
        add_chunks(sum_ref, [(packet_ref, first, packet_ref[index])], False)
        mine = lax.axis_index("tile_0")
        send_ref[...] = sum_ref[pl.ds(pl.multiple_of((1 - mine) * rows, rows), rows), :]
        keep_ref[...] = stiff_ref[slot] - sum_ref[pl.ds(pl.multiple_of(mine * rows, rows), rows), :]

    half = jax.ShapeDtypeStruct((rows, width), jnp.float32)
    return pl.pallas_call(
        kernel,
        out_shape=(half, half),
        in_specs=[VMEM] * 3,
        out_specs=(VMEM, VMEM),
        scratch_shapes=[pltpu.VMEM((LANES, width), jnp.float32)],
        compiler_params=PARAMS,
        name=name,
    )(total, packet, stiff)


def finish(keeps, others):
    rows, width = keeps[0].shape

    def kernel(k0, k1, o0, o1, out_ref):
        out_ref[0] = k0[...] - o0[...]
        out_ref[1] = k1[...] - o1[...]

    return pl.pallas_call(
        kernel,
        out_shape=jax.ShapeDtypeStruct((OWN, rows, width), jnp.float32),
        in_specs=[VMEM] * 4,
        out_specs=VMEM,
        compiler_params=PARAMS,
        name="finish",
    )(*keeps, *others)


def shifted(array, axis, distance):
    size = lax.axis_size(axis)
    return lax.ppermute(array, axis, [(i, (i + distance) % size) for i in range(size)])


def swapped(array, axis):
    return lax.ppermute(array, axis, [(i, i ^ 1) for i in range(lax.axis_size(axis))])


def body(coupling, interior_solve, boundary_stiffness, migration):
    home, depth, width = interior_solve.shape
    blocks = width // LANES
    pieces = jnp.swapaxes(coupling, 1, 2)
    outgoing = pack(migration, pieces, interior_solve, True)
    arrived = [swapped(outgoing[0], "group"), swapped(outgoing[1], "group")]
    local = pack(migration, pieces, interior_solve, False)
    ups, downs, totals = [], [], [None, None]
    owns = []
    for slot in range(OWN):
        up, down, own = merge(migration, arrived[slot], local[slot], slot, home)
        ups.append(up)
        downs.append(down)
        owns.append(own)
    stiff_arrived = swapped(stiff_out(migration, boundary_stiffness), "group")
    stiff = stiff_merge(migration, boundary_stiffness, stiff_arrived)
    pending = [[(ups[slot], hops(slot)[0], owns[slot])] for slot in range(OWN)]
    for step in range(1, 4):
        for slot in range(OWN):
            sent_up = ups[slot] if step == 1 else ups[slot][1:]
            sent_down = downs[slot] if step == 1 else downs[slot][:-1]
            ups[slot] = shifted(sent_up, "tile_1", 1)
            downs[slot] = shifted(sent_down, "tile_1", -1)
        for slot in range(OWN):
            totals[slot] = accumulate(totals[slot], pending[slot], width, f"chunks_{slot}")
            left_up, left_down = hops(slot)[0] - step, hops(slot)[1] - step
            pending[slot] = [(ups[slot], left_up + 1, 0), (downs[slot], 0, blocks + left_down)]
    far = [shifted(ups[0][1:], "tile_1", 1), shifted(downs[1][:-1], "tile_1", -1)]
    keeps, others = [], []
    for slot in range(OWN):
        totals[slot] = accumulate(totals[slot], pending[slot], width, f"chunks_{slot}")
        first, index = (1, 0) if slot == 0 else (0, blocks)
        send, keep = last_chunk(totals[slot], far[slot], first, index, stiff, slot, f"last_{slot}")
        keeps.append(keep)
        others.append(swapped(send, "tile_0"))
    return finish(keeps, others)


def solution(mesh):
    finer = Mesh(mesh.devices.reshape(mesh.shape["group"], 2, 8), ("group", "tile_0", "tile_1"))
    in_specs = (P("group", None, TILE), P("group", TILE, None), P("group", TILE, None), P())
    out_specs = P("group", TILE, None)
    return jax.shard_map(body, mesh=finer, in_specs=in_specs, out_specs=out_specs, check_vma=False)
```

time: 138 us -> 66 us (0.48); the launches traced: 136 us -> 65.8 us
  waiting for transfers between devices: 65.8 us -> 22.6 us
  starting transfers between devices: 14.4 us -> 30 us
  blocking collectives: 15.4 us -> 0 us
  local copies, waits for them, and re-layouts: 17.4 us -> 3.09 us
  between operations: 13.7 us -> 0.27 us
  Pallas kernels: 0 us -> 9.82 us
  other arithmetic: 5.39 us -> 0 us
  matrix products: 4.12 us -> 0 us
    all_gather x2 -> x0, waiting for transfers between devices: 46.7 us -> none  [all_blocks(): tiles = lax.all_gather(tiles, axes[k])]
    ppermute x3 -> x19, starting transfers between devices: 0.76 us -> 30 us  [the longest x14 27.1 us: shifted(): lax.ppermute(array, axis, [(i, (i + distance) % size) for i in range(size)])]
    ppermute x3 -> x19, waiting for transfers between devices: 0.01 us -> 22.6 us  [the longest x14 14 us: shifted(): lax.ppermute(array, axis, [(i, (i + distance) % size) for i in range(size)])]
    all_to_all x2 -> x0, waiting for transfers between devices: 19 us -> none  [condense(): lax.all_to_all(coupling_cols, TILE, split_axis=0, concat_axis=1, tiled=True)]
    all_gather x2 -> x0, blocking collectives: 15.4 us -> none  [all_blocks(): tiles = lax.all_gather(tiles, axes[k])]
    all_to_all x2 -> x0, starting transfers between devices: 13.6 us -> none  [condense(): lax.all_to_all(coupling_cols, TILE, split_axis=0, concat_axis=1, tiled=True)]
    pallas_call x0 -> x17, Pallas kernels: none -> 9.82 us  [the longest x2 3.16 us: pack(): pl.pallas_call(kernel, out_shape=(packet, packet), in_specs=[SMEM, HBM, H...]
    transpose x2 -> x0, local copies, waits for them, and re-layouts: 6.27 us -> none  [all_blocks(): tiles = tiles.transpose(*back, *range(len(axes), tiles.ndim))]
  transfers between devices with their start and end apart: 7 -> 19, of which waited for: 4 -> 11; matrix products, arithmetic and copies ran while one was open for 11% -> 0% of each run, Pallas kernels for 0% -> 11%
where the time goes in v1:
time: 66 us; the launch traced here: 65.8 us
  starting transfers between devices  30 us (45%)
  waiting for transfers between devices  22.6 us (34%)
  Pallas kernels  9.82 us (15%)
  local copies, waits for them, and re-layouts  3.09 us (5%)
    ppermute x14, starting transfers between devices, shifted(): lax.ppermute(array, axis, [(i, (i + distance) % size) for i in range(size)])  27.1 us
    ppermute x14, waiting for transfers between devices, shifted(): lax.ppermute(array, axis, [(i, (i + distance) % size) for i in range(size)])  14 us
    ppermute x5, waiting for transfers between devices, swapped(): lax.ppermute(array, axis, [(i, i ^ 1) for i in range(lax.axis_size(axis))])  8.6 us
    pallas_call x2, Pallas kernels, pack(): pl.pallas_call(kernel, out_shape=(packet, packet), in_specs=[SMEM, HBM, H...  3.16 us
    unnamed x8, local copies, waits for them, and re-layouts  2.93 us
    ppermute x5, starting transfers between devices, swapped(): lax.ppermute(array, axis, [(i, i ^ 1) for i in range(lax.axis_size(axis))])  2.88 us
    pallas_call x8, Pallas kernels, accumulate(): pl.pallas_call(kernel, out_shape=jax.ShapeDtypeStruct((LANES, width), jnp...  2.69 us
  transfers between devices with their start and end apart: 19, of which 11 were waited for; matrix products, arithmetic and copies ran while one was open for 0% of the time, Pallas kernels for 11%

profile of v1, /device:TPU:24, one launch (start us, length us, event | category | flops | bytes accessed | tf_op | source)
XLA Modules:
  0.0 65.8 jit_solution(3780735864389525498)
XLA Ops:
  0.0 0.0 copy-start.3
  0.0 0.7 copy-done.3
  0.7 0.0 copy-start.1
  0.7 1.1 %copy-done.1 = f32[4,1024,48]{1,2,0:T(8,128)S(1)} copy-done((f32[4,1024,48]{1,2,0:T(8,128)S(1)}, f32[4,1024,48]{1,2,0:T(8,128)}, u32[]{:S(2)}) %copy-start.1) | copy-done | bytes 786456
  1.8 0.0 copy-start.2
  1.8 1.1 %copy-done.2 = f32[4,48,1024]{2,1,0:T(8,128)S(1)} copy-done((f32[4,48,1024]{2,1,0:T(8,128)S(1)}, f32[4,48,1024]{2,1,0:T(8,128)}, u32[]{:S(2)}) %copy-start.2) | copy-done | bytes 786456
  2.9 1.6 %pack_partner.1 = (f32[16,48,128]{2,1,0:T(8,128)S(1)}, f32[16,48,128]{2,1,0:T(8,128)S(1)}) custom-call(s32[64]{0:T(128)S(1)} %copy-done.3, f32[4,48,1024]{2,1,0:T(8,128)S(1)} %bitcast.1, f32[4,48,1024]{2,1,0:T(8,128)S(1)} %copy-done.2), custom_call_target="tpu_custom_call" | custom-call | tf_op jit(solution)/shard_map/pack_partner/pallas_call | solution.py:72
  4.5 0.1 collective-permute-start
  4.6 0.5 collective-permute-start.9
  5.1 1.6 %pack_own.1 = (f32[16,48,128]{2,1,0:T(8,128)S(1)}, f32[16,48,128]{2,1,0:T(8,128)S(1)}) custom-call(s32[64]{0:T(128)S(1)} %copy-done.3, f32[4,48,1024]{2,1,0:T(8,128)S(1)} %bitcast.2, f32[4,48,1024]{2,1,0:T(8,128)S(1)} %copy-done.2), custom_call_target="tpu_custom_call" | custom-call | tf_op jit(solution)/shard_map/pack_own/pallas_call | solution.py:72
  6.7 0.0 collective-permute-done.arrived_ref
  6.7 0.6 merge_0.1
  7.3 0.0 copy-start
  7.3 2.0 %collective-permute-start.1 = (f32[12,48,128]{2,1,0:T(8,128)S(1)}, f32[12,48,128]{2,1,0:T(8,128)S(1)}, u32[]{:S(2)}, u32[]{:S(2)}) collective-permute-start(f32[12,48,128]{2,1,0:T(8,128)S(1)} %get-tuple-element.21.refs_0_), channel_id=1, source_target_pairs={{0,1},{1,2},{2,3},{3,4},{4,5},{5,6},{6,7},{7,0},{8,9},{9,10},{10,1... | collective-permute-start | bytes 884744 | tf_op jit(solution)/shard_map/ppermute | solution.py:274
  9.3 0.0 collective-permute-done.9.arrived_ref
  9.3 0.6 merge_1.1
  9.9 4.0 %collective-permute-start.11 = (f32[12,48,128]{2,1,0:T(8,128)S(1)}, f32[12,48,128]{2,1,0:T(8,128)S(1)}, u32[]{:S(2)}, u32[]{:S(2)}) collective-permute-start(f32[12,48,128]{2,1,0:T(8,128)S(1)} %get-tuple-element.29), channel_id=1, source_target_pairs={{0,7},{1,0},{2,1},{3,2},{4,3},{5,4},{6,5},{7,6},{8,15},{9,8},{10,9... | collective-permute-start | bytes 884744 | tf_op jit(solution)/shard_map/ppermute | solution.py:274
  14.0 2.0 %collective-permute-start.2 = (f32[11,48,128]{2,1,0:T(8,128)S(1)}, f32[11,48,128]{2,1,0:T(8,128)S(1)}, u32[]{:S(2)}, u32[]{:S(2)}) collective-permute-start(f32[11,48,128]{2,1,0:T(8,128)S(1)} %get-tuple-element.23), channel_id=1, source_target_pairs={{0,7},{1,0},{2,1},{3,2},{4,3},{5,4},{6,5},{7,6},{8,15},{9,8},{10,9... | collective-permute-start | bytes 811016 | tf_op jit(solution)/shard_map/ppermute | solution.py:274
  16.0 0.0 collective-permute-start.10
  16.0 5.1 %collective-permute-done.1.refs_1_ = f32[12,48,128]{2,1,0:T(8,128)S(1)} collective-permute-done((f32[12,48,128]{2,1,0:T(8,128)S(1)}, f32[12,48,128]{2,1,0:T(8,128)S(1)}, u32[]{:S(2)}, u32[]{:S(2)}) %collective-permute-start.1) | collective-permute-done | bytes 294944 | tf_op jit(solution)/shard_map/ppermute | solution.py:274
  21.1 0.1 collective-permute-start.3
  21.2 0.2 collective-permute-done.11.refs_2_
  21.4 3.8 %collective-permute-start.13 = (f32[11,48,128]{2,1,0:T(8,128)S(1)}, f32[11,48,128]{2,1,0:T(8,128)S(1)}, u32[]{:S(2)}, u32[]{:S(2)}) collective-permute-start(f32[11,48,128]{2,1,0:T(8,128)S(1)} %slice.46), channel_id=1, source_target_pairs={{0,7},{1,0},{2,1},{3,2},{4,3},{5,4},{6,5},{7,6},{8,15},{9,8},{10,9... | collective-permute-start | bytes 811016 | tf_op jit(solution)/shard_map/ppermute | solution.py:274
  25.1 0.0 copy-done
  25.1 0.6 stiff_out.1
  25.8 0.1 collective-permute-start.8
  25.9 1.3 %collective-permute-done.2.refs_2_ = f32[11,48,128]{2,1,0:T(8,128)S(1)} collective-permute-done((f32[11,48,128]{2,1,0:T(8,128)S(1)}, f32[11,48,128]{2,1,0:T(8,128)S(1)}, u32[]{:S(2)}, u32[]{:S(2)}) %collective-permute-start.2) | collective-permute-done | bytes 270368 | tf_op jit(solution)/shard_map/ppermute | solution.py:274
  27.2 3.8 %collective-permute-start.4 = (f32[10,48,128]{2,1,0:T(8,128)S(1)}, f32[10,48,128]{2,1,0:T(8,128)S(1)}, u32[]{:S(2)}, u32[]{:S(2)}) collective-permute-start(f32[10,48,128]{2,1,0:T(8,128)S(1)} %slice.41), channel_id=1, source_target_pairs={{0,7},{1,0},{2,1},{3,2},{4,3},{5,4},{6,5},{7,6},{8,15},{9,8},{10,9... | collective-permute-start | bytes 737288 | tf_op jit(solution)/shard_map/ppermute | solution.py:274
  30.9 0.0 collective-permute-done.10.refs_1_
  31.0 0.1 collective-permute-start.12
  31.0 1.1 %collective-permute-done.3.refs_1_ = f32[11,48,128]{2,1,0:T(8,128)S(1)} collective-permute-done((f32[11,48,128]{2,1,0:T(8,128)S(1)}, f32[11,48,128]{2,1,0:T(8,128)S(1)}, u32[]{:S(2)}, u32[]{:S(2)}) %collective-permute-start.3) | collective-permute-done | bytes 270368 | tf_op jit(solution)/shard_map/ppermute | solution.py:274
  32.1 0.1 collective-permute-start.5
  32.2 0.7 %collective-permute-done.13.refs_2_ = f32[11,48,128]{2,1,0:T(8,128)S(1)} collective-permute-done((f32[11,48,128]{2,1,0:T(8,128)S(1)}, f32[11,48,128]{2,1,0:T(8,128)S(1)}, u32[]{:S(2)}, u32[]{:S(2)}) %collective-permute-start.13) | collective-permute-done | bytes 270368 | tf_op jit(solution)/shard_map/ppermute | solution.py:274
  33.0 3.8 %collective-permute-start.15 = (f32[10,48,128]{2,1,0:T(8,128)S(1)}, f32[10,48,128]{2,1,0:T(8,128)S(1)}, u32[]{:S(2)}, u32[]{:S(2)}) collective-permute-start(f32[10,48,128]{2,1,0:T(8,128)S(1)} %slice.48), channel_id=1, source_target_pairs={{0,7},{1,0},{2,1},{3,2},{4,3},{5,4},{6,5},{7,6},{8,15},{9,8},{10,9... | collective-permute-start | bytes 737288 | tf_op jit(solution)/shard_map/ppermute | solution.py:274
  36.7 1.5 %collective-permute-done.4.refs_2_ = f32[10,48,128]{2,1,0:T(8,128)S(1)} collective-permute-done((f32[10,48,128]{2,1,0:T(8,128)S(1)}, f32[10,48,128]{2,1,0:T(8,128)S(1)}, u32[]{:S(2)}, u32[]{:S(2)}) %collective-permute-start.4) | collective-permute-done | bytes 245792 | tf_op jit(solution)/shard_map/ppermute | solution.py:274
  38.2 3.8 %collective-permute-start.6 = (f32[9,48,128]{2,1,0:T(8,128)S(1)}, f32[9,48,128]{2,1,0:T(8,128)S(1)}, u32[]{:S(2)}, u32[]{:S(2)}) collective-permute-start(f32[9,48,128]{2,1,0:T(8,128)S(1)} %slice.43), channel_id=1, source_target_pairs={{0,7},{1,0},{2,1},{3,2},{4,3},{5,4},{6,5},{7,6},{8,15},{9,8},{10,9... | collective-permute-start | bytes 663560 | tf_op jit(solution)/shard_map/ppermute | solution.py:274
  42.0 0.0 collective-permute-done.12.refs_1_
  42.0 0.1 collective-permute-start.14
  42.1 1.4 %collective-permute-done.5.refs_1_ = f32[10,48,128]{2,1,0:T(8,128)S(1)} collective-permute-done((f32[10,48,128]{2,1,0:T(8,128)S(1)}, f32[10,48,128]{2,1,0:T(8,128)S(1)}, u32[]{:S(2)}, u32[]{:S(2)}) %collective-permute-start.5) | collective-permute-done | bytes 245792 | tf_op jit(solution)/shard_map/ppermute | solution.py:274
  43.5 0.3 collective-permute-start.7
  43.8 0.0 collective-permute-done.15.refs_2_
  43.8 3.4 %collective-permute-start.16 = (f32[9,48,128]{2,1,0:T(8,128)S(1)}, f32[9,48,128]{2,1,0:T(8,128)S(1)}, u32[]{:S(2)}, u32[]{:S(2)}) collective-permute-start(f32[9,48,128]{2,1,0:T(8,128)S(1)} %slice.49), channel_id=1, source_target_pairs={{0,7},{1,0},{2,1},{3,2},{4,3},{5,4},{6,5},{7,6},{8,15},{9,8},{10,9... | collective-permute-start | bytes 663560 | tf_op jit(solution)/shard_map/ppermute | solution.py:274
  47.3 0.3 chunks_0.4.refs_0_
  47.5 0.3 chunks_1.4.refs_0_
  47.8 0.0 collective-permute-done.8.arrived_ref
  47.8 0.6 stiff_merge.1.stiff_ref
  48.4 0.4 chunks_0.5.refs_0_
  48.8 0.4 chunks_1.5.refs_0_
  49.2 0.4 chunks_0.6.refs_0_
  49.5 0.4 chunks_1.6.refs_0_
  49.9 0.0 collective-permute-done.6.refs_2_
  49.9 0.4 chunks_0.7.total_ref
  50.3 0.8 %collective-permute-done.14.refs_1_ = f32[9,48,128]{2,1,0:T(8,128)S(1)} collective-permute-done((f32[9,48,128]{2,1,0:T(8,128)S(1)}, f32[9,48,128]{2,1,0:T(8,128)S(1)}, u32[]{:S(2)}, u32[]{:S(2)}) %collective-permute-start.14) | collective-permute-done | bytes 221216 | tf_op jit(solution)/shard_map/ppermute | solution.py:274
  51.1 0.4 chunks_1.7.total_ref
  51.5 2.0 %collective-permute-done.7.packet_ref = f32[9,48,128]{2,1,0:T(8,128)S(1)} collective-permute-done((f32[9,48,128]{2,1,0:T(8,128)S(1)}, f32[9,48,128]{2,1,0:T(8,128)S(1)}, u32[]{:S(2)}, u32[]{:S(2)}) %collective-permute-start.7) | collective-permute-done | bytes 221216 | tf_op jit(solution)/shard_map/ppermute | solution.py:274
  53.5 0.3 last_0.1
  53.8 1.6 %collective-permute-start.17 = (f32[64,1024]{1,0:T(8,128)S(1)}, f32[64,1024]{1,0:T(8,128)S(1)}, u32[]{:S(2)}, u32[]{:S(2)}) collective-permute-start(f32[64,1024]{1,0:T(8,128)S(1)} %get-tuple-element.31), channel_id=1, source_target_pairs={{0,8},{8,0},{1,9},{9,1},{2,10},{10,2},{3,11},{11,3},{4,12},{12,4},... | collective-permute-start | bytes 786440 | tf_op jit(solution)/shard_map/ppermute | solution.py:278
  55.4 0.0 collective-permute-done.16.packet_ref
  55.4 0.3 last_1.1
  55.8 0.6 collective-permute-start.18
  56.4 5.8 %collective-permute-done.17.o0 = f32[64,1024]{1,0:T(8,128)S(1)} collective-permute-done((f32[64,1024]{1,0:T(8,128)S(1)}, f32[64,1024]{1,0:T(8,128)S(1)}, u32[]{:S(2)}, u32[]{:S(2)}) %collective-permute-start.17) | collective-permute-done | bytes 262176 | tf_op jit(solution)/shard_map/ppermute | solution.py:278
  62.2 2.8 %collective-permute-done.18.o1 = f32[64,1024]{1,0:T(8,128)S(1)} collective-permute-done((f32[64,1024]{1,0:T(8,128)S(1)}, f32[64,1024]{1,0:T(8,128)S(1)}, u32[]{:S(2)}, u32[]{:S(2)}) %collective-permute-start.18) | collective-permute-done | bytes 262176 | tf_op jit(solution)/shard_map/ppermute | solution.py:278
  65.0 0.9 %finish.1 = f32[2,64,1024]{2,1,0:T(8,128)} custom-call(f32[64,1024]{1,0:T(8,128)S(1)} %get-tuple-element.24.k0, f32[64,1024]{1,0:T(8,128)S(1)} %get-tuple-element.30.k1, f32[64,1024]{1,0:T(8,128)S(1)} %collective-permute-done.17.o0, f32[64,1024]{1,0:T(8,128)S(1)} %collective-permute-done.18.o1), custom_call_target="tpu_custom_call" | custom-call | tf_op jit(solution)/shard_map/finish/pallas_call | solution.py:262
  (10 shorter events, 0.2 us)
Async XLA Ops:
  0.0 0.7 copy-start.3
  0.7 1.1 %copy-start.1 = (f32[4,1024,48]{1,2,0:T(8,128)S(1)}, f32[4,1024,48]{1,2,0:T(8,128)}, u32[]{:S(2)}) copy-start(f32[4,1024,48]{1,2,0:T(8,128)} %param.4) | copy-start | bytes 2359300
  1.8 1.1 %copy-start.2 = (f32[4,48,1024]{2,1,0:T(8,128)S(1)}, f32[4,48,1024]{2,1,0:T(8,128)}, u32[]{:S(2)}) copy-start(f32[4,48,1024]{2,1,0:T(8,128)} %x_hbm.3) | copy-start | bytes 2359300
  4.5 2.2 %collective-permute-start = (f32[16,48,128]{2,1,0:T(8,128)S(1)}, f32[16,48,128]{2,1,0:T(8,128)S(1)}, u32[]{:S(2)}, u32[]{:S(2)}) collective-permute-start(f32[16,48,128]{2,1,0:T(8,128)S(1)} %get-tuple-element.19), channel_id=1, source_target_pairs={{0,16},{16,0},{32,48},{48,32},{64,80},{80,64},{96,112},{112,96},{1... | collective-permute-start | bytes 1179656 | tf_op jit(solution)/shard_map/ppermute | solution.py:278
  4.6 4.7 %collective-permute-start.9 = (f32[16,48,128]{2,1,0:T(8,128)S(1)}, f32[16,48,128]{2,1,0:T(8,128)S(1)}, u32[]{:S(2)}, u32[]{:S(2)}) collective-permute-start(f32[16,48,128]{2,1,0:T(8,128)S(1)} %get-tuple-element.25), channel_id=1, source_target_pairs={{0,16},{16,0},{32,48},{48,32},{64,80},{80,64},{96,112},{112,96},{1... | collective-permute-start | bytes 1179656 | tf_op jit(solution)/shard_map/ppermute | solution.py:278
  7.3 17.8 %copy-start = (f32[4,64,1024]{2,1,0:T(8,128)S(1)}, f32[4,64,1024]{2,1,0:T(8,128)}, u32[]{:S(2)}) copy-start(f32[4,64,1024]{2,1,0:T(8,128)} %b_hbm.3) | copy-start | bytes 3145732
  7.3 13.7 %collective-permute-start.1 = (f32[12,48,128]{2,1,0:T(8,128)S(1)}, f32[12,48,128]{2,1,0:T(8,128)S(1)}, u32[]{:S(2)}, u32[]{:S(2)}) collective-permute-start(f32[12,48,128]{2,1,0:T(8,128)S(1)} %get-tuple-element.21.refs_0_), channel_id=1, source_target_pairs={{0,1},{1,2},{2,3},{3,4},{4,5},{5,6},{6,7},{7,0},{8,9},{9,10},{10,1... | collective-permute-start | bytes 884744 | tf_op jit(solution)/shard_map/ppermute | solution.py:274
  9.9 11.4 %collective-permute-start.11 = (f32[12,48,128]{2,1,0:T(8,128)S(1)}, f32[12,48,128]{2,1,0:T(8,128)S(1)}, u32[]{:S(2)}, u32[]{:S(2)}) collective-permute-start(f32[12,48,128]{2,1,0:T(8,128)S(1)} %get-tuple-element.29), channel_id=1, source_target_pairs={{0,7},{1,0},{2,1},{3,2},{4,3},{5,4},{6,5},{7,6},{8,15},{9,8},{10,9... | collective-permute-start | bytes 884744 | tf_op jit(solution)/shard_map/ppermute | solution.py:274
  14.0 13.2 %collective-permute-start.2 = (f32[11,48,128]{2,1,0:T(8,128)S(1)}, f32[11,48,128]{2,1,0:T(8,128)S(1)}, u32[]{:S(2)}, u32[]{:S(2)}) collective-permute-start(f32[11,48,128]{2,1,0:T(8,128)S(1)} %get-tuple-element.23), channel_id=1, source_target_pairs={{0,7},{1,0},{2,1},{3,2},{4,3},{5,4},{6,5},{7,6},{8,15},{9,8},{10,9... | collective-permute-start | bytes 811016 | tf_op jit(solution)/shard_map/ppermute | solution.py:274
  16.0 15.0 %collective-permute-start.10 = (f32[11,48,128]{2,1,0:T(8,128)S(1)}, f32[11,48,128]{2,1,0:T(8,128)S(1)}, u32[]{:S(2)}, u32[]{:S(2)}) collective-permute-start(f32[11,48,128]{2,1,0:T(8,128)S(1)} %get-tuple-element.27.refs_0_), channel_id=1, source_target_pairs={{0,1},{1,2},{2,3},{3,4},{4,5},{5,6},{6,7},{7,0},{8,9},{9,10},{10,1... | collective-permute-start | bytes 811016 | tf_op jit(solution)/shard_map/ppermute | solution.py:274
  21.1 11.0 %collective-permute-start.3 = (f32[11,48,128]{2,1,0:T(8,128)S(1)}, f32[11,48,128]{2,1,0:T(8,128)S(1)}, u32[]{:S(2)}, u32[]{:S(2)}) collective-permute-start(f32[11,48,128]{2,1,0:T(8,128)S(1)} %slice.40), channel_id=1, source_target_pairs={{0,1},{1,2},{2,3},{3,4},{4,5},{5,6},{6,7},{7,0},{8,9},{9,10},{10,1... | collective-permute-start | bytes 811016 | tf_op jit(solution)/shard_map/ppermute | solution.py:274
  21.4 11.6 %collective-permute-start.13 = (f32[11,48,128]{2,1,0:T(8,128)S(1)}, f32[11,48,128]{2,1,0:T(8,128)S(1)}, u32[]{:S(2)}, u32[]{:S(2)}) collective-permute-start(f32[11,48,128]{2,1,0:T(8,128)S(1)} %slice.46), channel_id=1, source_target_pairs={{0,7},{1,0},{2,1},{3,2},{4,3},{5,4},{6,5},{7,6},{8,15},{9,8},{10,9... | collective-permute-start | bytes 811016 | tf_op jit(solution)/shard_map/ppermute | solution.py:274
  25.8 22.0 %collective-permute-start.8 = (f32[2,64,1024]{2,1,0:T(8,128)S(1)}, f32[2,64,1024]{2,1,0:T(8,128)S(1)}, u32[]{:S(2)}, u32[]{:S(2)}) collective-permute-start(f32[2,64,1024]{2,1,0:T(8,128)S(1)} %stiff_out.1), channel_id=1, source_target_pairs={{0,16},{16,0},{32,48},{48,32},{64,80},{80,64},{96,112},{112,96},{1... | collective-permute-start | bytes 1572872 | tf_op jit(solution)/shard_map/ppermute | solution.py:278
  27.2 11.0 %collective-permute-start.4 = (f32[10,48,128]{2,1,0:T(8,128)S(1)}, f32[10,48,128]{2,1,0:T(8,128)S(1)}, u32[]{:S(2)}, u32[]{:S(2)}) collective-permute-start(f32[10,48,128]{2,1,0:T(8,128)S(1)} %slice.41), channel_id=1, source_target_pairs={{0,7},{1,0},{2,1},{3,2},{4,3},{5,4},{6,5},{7,6},{8,15},{9,8},{10,9... | collective-permute-start | bytes 737288 | tf_op jit(solution)/shard_map/ppermute | solution.py:274
  31.0 11.0 %collective-permute-start.12 = (f32[10,48,128]{2,1,0:T(8,128)S(1)}, f32[10,48,128]{2,1,0:T(8,128)S(1)}, u32[]{:S(2)}, u32[]{:S(2)}) collective-permute-start(f32[10,48,128]{2,1,0:T(8,128)S(1)} %slice.45), channel_id=1, source_target_pairs={{0,1},{1,2},{2,3},{3,4},{4,5},{5,6},{6,7},{7,0},{8,9},{9,10},{10,1... | collective-permute-start | bytes 737288 | tf_op jit(solution)/shard_map/ppermute | solution.py:274
  32.1 11.4 %collective-permute-start.5 = (f32[10,48,128]{2,1,0:T(8,128)S(1)}, f32[10,48,128]{2,1,0:T(8,128)S(1)}, u32[]{:S(2)}, u32[]{:S(2)}) collective-permute-start(f32[10,48,128]{2,1,0:T(8,128)S(1)} %slice.42), channel_id=1, source_target_pairs={{0,1},{1,2},{2,3},{3,4},{4,5},{5,6},{6,7},{7,0},{8,9},{9,10},{10,1... | collective-permute-start | bytes 737288 | tf_op jit(solution)/shard_map/ppermute | solution.py:274
  33.0 10.8 %collective-permute-start.15 = (f32[10,48,128]{2,1,0:T(8,128)S(1)}, f32[10,48,128]{2,1,0:T(8,128)S(1)}, u32[]{:S(2)}, u32[]{:S(2)}) collective-permute-start(f32[10,48,128]{2,1,0:T(8,128)S(1)} %slice.48), channel_id=1, source_target_pairs={{0,7},{1,0},{2,1},{3,2},{4,3},{5,4},{6,5},{7,6},{8,15},{9,8},{10,9... | collective-permute-start | bytes 737288 | tf_op jit(solution)/shard_map/ppermute | solution.py:274
  38.2 11.7 %collective-permute-start.6 = (f32[9,48,128]{2,1,0:T(8,128)S(1)}, f32[9,48,128]{2,1,0:T(8,128)S(1)}, u32[]{:S(2)}, u32[]{:S(2)}) collective-permute-start(f32[9,48,128]{2,1,0:T(8,128)S(1)} %slice.43), channel_id=1, source_target_pairs={{0,7},{1,0},{2,1},{3,2},{4,3},{5,4},{6,5},{7,6},{8,15},{9,8},{10,9... | collective-permute-start | bytes 663560 | tf_op jit(solution)/shard_map/ppermute | solution.py:274
  42.0 9.1 %collective-permute-start.14 = (f32[9,48,128]{2,1,0:T(8,128)S(1)}, f32[9,48,128]{2,1,0:T(8,128)S(1)}, u32[]{:S(2)}, u32[]{:S(2)}) collective-permute-start(f32[9,48,128]{2,1,0:T(8,128)S(1)} %slice.47), channel_id=1, source_target_pairs={{0,1},{1,2},{2,3},{3,4},{4,5},{5,6},{6,7},{7,0},{8,9},{9,10},{10,1... | collective-permute-start | bytes 663560 | tf_op jit(solution)/shard_map/ppermute | solution.py:274
  43.5 10.0 %collective-permute-start.7 = (f32[9,48,128]{2,1,0:T(8,128)S(1)}, f32[9,48,128]{2,1,0:T(8,128)S(1)}, u32[]{:S(2)}, u32[]{:S(2)}) collective-permute-start(f32[9,48,128]{2,1,0:T(8,128)S(1)} %slice.44), channel_id=1, source_target_pairs={{0,1},{1,2},{2,3},{3,4},{4,5},{5,6},{6,7},{7,0},{8,9},{9,10},{10,1... | collective-permute-start | bytes 663560 | tf_op jit(solution)/shard_map/ppermute | solution.py:274
  43.8 11.6 %collective-permute-start.16 = (f32[9,48,128]{2,1,0:T(8,128)S(1)}, f32[9,48,128]{2,1,0:T(8,128)S(1)}, u32[]{:S(2)}, u32[]{:S(2)}) collective-permute-start(f32[9,48,128]{2,1,0:T(8,128)S(1)} %slice.49), channel_id=1, source_target_pairs={{0,7},{1,0},{2,1},{3,2},{4,3},{5,4},{6,5},{7,6},{8,15},{9,8},{10,9... | collective-permute-start | bytes 663560 | tf_op jit(solution)/shard_map/ppermute | solution.py:274
  53.8 8.3 %collective-permute-start.17 = (f32[64,1024]{1,0:T(8,128)S(1)}, f32[64,1024]{1,0:T(8,128)S(1)}, u32[]{:S(2)}, u32[]{:S(2)}) collective-permute-start(f32[64,1024]{1,0:T(8,128)S(1)} %get-tuple-element.31), channel_id=1, source_target_pairs={{0,8},{8,0},{1,9},{9,1},{2,10},{10,2},{3,11},{11,3},{4,12},{12,4},... | collective-permute-start | bytes 786440 | tf_op jit(solution)/shard_map/ppermute | solution.py:278
  55.8 9.2 %collective-permute-start.18 = (f32[64,1024]{1,0:T(8,128)S(1)}, f32[64,1024]{1,0:T(8,128)S(1)}, u32[]{:S(2)}, u32[]{:S(2)}) collective-permute-start(f32[64,1024]{1,0:T(8,128)S(1)} %get-tuple-element.32), channel_id=1, source_target_pairs={{0,8},{8,0},{1,9},{9,1},{2,10},{10,2},{3,11},{11,3},{4,12},{12,4},... | collective-permute-start | bytes 786440 | tf_op jit(solution)/shard_map/ppermute | solution.py:278

commit v2 on v1

v2 whole, which is shorter than its diff:
```python
import jax
import jax.numpy as jnp
from jax import lax
from jax.experimental import pallas as pl
from jax.experimental.pallas import tpu as pltpu
from jax.sharding import Mesh
from jax.sharding import PartitionSpec as P

OWN = 2
TILE = ("tile_0", "tile_1")
LANES = 128
PARAMS = pltpu.CompilerParams(vmem_limit_bytes=32 * 1024 * 1024)
SMEM = pl.BlockSpec(memory_space=pltpu.SMEM)
VMEM = pl.BlockSpec(memory_space=pltpu.VMEM)
HBM = pl.BlockSpec(memory_space=pltpu.HBM)


def hops(slot):
    return (3, 4) if slot == 0 else (4, 3)


def locate(plan, group, wanted, home):
    position, here = jnp.int32(0), jnp.bool_(False)
    for k in range(home):
        match = plan[group * home + k] == wanted
        position = jnp.where(match, jnp.int32(k), position)
        here = jnp.logical_or(here, match)
    return position, here


def pack(plan, coupling, solve, for_partner):
    home, depth, width = solve.shape
    blocks = width // LANES

    def kernel(plan_hbm, c_hbm, x_hbm, out0, out1, plan_ref, c_buf, x_buf, plan_sem, c_sem, x_sem):
        group = lax.axis_index("group")
        place = lax.axis_index("tile_1")
        owner = jnp.bitwise_xor(group, 1) if for_partner else group
        outs = (out0, out1)
        copies = [
            pltpu.make_async_copy(plan_hbm, plan_ref, plan_sem),
            pltpu.make_async_copy(c_hbm, c_buf, c_sem),
            pltpu.make_async_copy(x_hbm, x_buf, x_sem),
        ]
        for copy in copies:
            copy.start()
        low = lax.broadcasted_iota(jnp.int32, (depth, LANES), 1) < LANES // 2
        copies[0].wait()
        positions = [locate(plan_ref, group, owner * OWN + slot, home)[0] for slot in range(OWN)]
        copies[1].wait()
        for slot in range(OWN):
            up = hops(slot)[0]
            for m in range(blocks // 2):
                first = c_buf[positions[slot], :, pl.ds(m * LANES, LANES)]
                second = c_buf[positions[slot], :, pl.ds((m + blocks // 2) * LANES, LANES)]
                even = jnp.where(low, first, pltpu.roll(second, LANES // 2, 1))
                odd = jnp.where(low, pltpu.roll(first, LANES // 2, 1), second)
                for to, piece in ((2 * m, even), (2 * m + 1, odd)):
                    ahead = jnp.bitwise_and(to - place, blocks - 1)
                    spot = jnp.where(ahead == 0, 15, jnp.where(ahead <= up, ahead - 1, ahead + 7))
                    outs[slot][spot] = piece
        copies[2].wait()
        for slot in range(OWN):
            up = hops(slot)[0]
            for n in range(blocks):
                outs[slot][up + n] = x_buf[positions[slot], :, pl.ds(n * LANES, LANES)]

    packet = jax.ShapeDtypeStruct((2 * blocks, depth, LANES), jnp.float32)
    return pl.pallas_call(
        kernel,
        out_shape=(packet, packet),
        in_specs=[HBM] * 3,
        out_specs=(VMEM, VMEM),
        scratch_shapes=[
            pltpu.SMEM(plan.shape, jnp.int32),
            pltpu.VMEM((home, depth, width), jnp.float32),
            pltpu.VMEM((home, depth, width), jnp.float32),
            pltpu.SemaphoreType.DMA,
            pltpu.SemaphoreType.DMA,
            pltpu.SemaphoreType.DMA,
        ],
        compiler_params=PARAMS,
        name="pack_partner" if for_partner else "pack_own",
    )(plan, coupling, solve)


def merge(plan, arrived, local, slot, home):
    total, depth, _ = arrived.shape
    up, down = hops(slot)
    blocks = total // 2
    half = blocks // 2

    def kernel(plan_ref, arrived_ref, local_ref, up_ref, down_ref, own_ref):
        group = lax.axis_index("group")
        _, here = locate(plan_ref, group, group * OWN + slot, home)

        def put(source):
            up_ref[...] = source[0 : up + blocks]
            if slot == 0:
                down_ref[...] = source[up : total - 1]
            else:
                down_ref[0:half] = source[up + half : up + blocks]
                down_ref[half:blocks] = source[up : up + half]
                down_ref[blocks:] = source[up + blocks : total - 1]
            own_ref[...] = source[total - 1]

        @pl.when(here)
        def _():
            put(local_ref)

        @pl.when(jnp.logical_not(here))
        def _():
            put(arrived_ref)

    return pl.pallas_call(
        kernel,
        out_shape=(
            jax.ShapeDtypeStruct((up + blocks, depth, LANES), jnp.float32),
            jax.ShapeDtypeStruct((down + blocks, depth, LANES), jnp.float32),
            jax.ShapeDtypeStruct((depth, LANES), jnp.float32),
        ),
        in_specs=[SMEM, VMEM, VMEM],
        out_specs=(VMEM, VMEM, VMEM),
        compiler_params=PARAMS,
        name=f"merge_{slot}",
    )(plan, arrived, local)


def stiff_out(plan, stiff):
    home, rows, width = stiff.shape

    def kernel(plan_ref, b_hbm, out_ref, sem):
        group = lax.axis_index("group")
        copies = []
        for slot in range(OWN):
            position, _ = locate(plan_ref, group, jnp.bitwise_xor(group, 1) * OWN + slot, home)
            copy = pltpu.make_async_copy(b_hbm.at[position], out_ref.at[slot], sem.at[slot])
            copy.start()
            copies.append(copy)
        for copy in copies:
            copy.wait()

    return pl.pallas_call(
        kernel,
        out_shape=jax.ShapeDtypeStruct((OWN, rows, width), jnp.float32),
        in_specs=[SMEM, HBM],
        out_specs=VMEM,
        scratch_shapes=[pltpu.SemaphoreType.DMA((OWN,))],
        compiler_params=PARAMS,
        name="stiff_out",
    )(plan, stiff)


def stiff_merge(plan, stiff, arrived):
    home, rows, width = stiff.shape

    def kernel(plan_ref, b_hbm, arrived_ref, out_ref, sem):
        group = lax.axis_index("group")
        for slot in range(OWN):
            position, here = locate(plan_ref, group, group * OWN + slot, home)

            @pl.when(here)
            def _():
                copy = pltpu.make_async_copy(b_hbm.at[position], out_ref.at[slot], sem.at[slot])
                copy.start()
                copy.wait()

            @pl.when(jnp.logical_not(here))
            def _():
                out_ref[slot] = arrived_ref[slot]

    return pl.pallas_call(
        kernel,
        out_shape=jax.ShapeDtypeStruct((OWN, rows, width), jnp.float32),
        in_specs=[SMEM, HBM, VMEM],
        out_specs=VMEM,
        scratch_shapes=[pltpu.SemaphoreType.DMA((OWN,))],
        compiler_params=PARAMS,
        name="stiff_merge",
    )(plan, stiff, arrived)


def split(value):
    high = value.astype(jnp.bfloat16)
    return high, (value - high.astype(jnp.float32)).astype(jnp.bfloat16)


def add_chunks(total_ref, chunks, start):
    for packet, places, piece in chunks:
        c_high, c_low = split(piece)
        left = jnp.concatenate([c_high, c_high, c_low], axis=0)
        for n in range(0, len(places), 2):
            x = jnp.concatenate([packet[places[n]], packet[places[n + 1]]], axis=1)
            x_high, x_low = split(x)
            right = jnp.concatenate([x_high, x_low, x_high], axis=0)
            product = lax.dot_general(left, right, (((0,), (0,)), ((), ())), preferred_element_type=jnp.float32)
            where = (slice(None), pl.ds(n * LANES, 2 * LANES))
            total_ref[where] = product if start else total_ref[where] + product
        start = False


def gathered(sources):
    arrays, layout = [], []

    def place(array):
        for k, known in enumerate(arrays):
            if known is array:
                return k
        arrays.append(array)
        return len(arrays) - 1

    for packet, places, holder, index in sources:
        layout.append((place(packet), places, place(holder), index))
    return arrays, layout


def chunks_of(refs, layout):
    return [
        (refs[k], places, refs[holder][...] if index is None else refs[holder][index])
        for k, places, holder, index in layout
    ]


def accumulate(total, sources, width, name):
    arrays, layout = gathered(sources)
    given = [] if total is None else [total]
    n_given = len(given)

    def kernel(*refs):
        total_ref = refs[-1]
        if n_given:
            total_ref[...] = refs[0][...]
        add_chunks(total_ref, chunks_of(refs[n_given:-1], layout), not n_given)

    return pl.pallas_call(
        kernel,
        out_shape=jax.ShapeDtypeStruct((LANES, width), jnp.float32),
        in_specs=[VMEM] * (n_given + len(arrays)),
        out_specs=VMEM,
        input_output_aliases={0: 0} if n_given else {},
        compiler_params=PARAMS,
        cost_estimate=pl.CostEstimate(flops=2 * 144 * 128 * 1024, bytes_accessed=1 << 20, transcendentals=0),
        name=name,
    )(*given, *arrays)


def last_chunks(total, sources, stiff, slot, first, width, name):
    rows = LANES // 2
    arrays, layout = gathered(sources)
    columns = pl.ds(first, width)

    def kernel(total_ref, stiff_ref, *refs):
        send_ref, keep_ref, sum_ref = refs[-3:]
        sum_ref[...] = total_ref[:, columns]
        add_chunks(sum_ref, chunks_of(refs[:-3], layout), False)
        mine = lax.axis_index("tile_0")
        send_ref[...] = sum_ref[pl.ds(pl.multiple_of((1 - mine) * rows, rows), rows), :]
        keep_ref[...] = stiff_ref[slot, :, columns] - sum_ref[pl.ds(pl.multiple_of(mine * rows, rows), rows), :]

    half = jax.ShapeDtypeStruct((rows, width), jnp.float32)
    return pl.pallas_call(
        kernel,
        out_shape=(half, half),
        in_specs=[VMEM] * (2 + len(arrays)),
        out_specs=(VMEM, VMEM),
        scratch_shapes=[pltpu.VMEM((LANES, width), jnp.float32)],
        compiler_params=PARAMS,
        name=name,
    )(total, stiff, *arrays)


def finish(result, parts, slot, rows, width):
    flat = [array for pair in parts for array in pair]
    given = [] if result is None else [result]

    def kernel(*refs):
        ins = refs[len(given) : -3]
        out_hbm, buf, sem = refs[-3:]
        first = 0
        for k in range(0, len(ins), 2):
            columns = pl.ds(first, ins[k].shape[1])
            buf[:, columns] = ins[k][...] - ins[k + 1][...]
            first += ins[k].shape[1]
        copy = pltpu.make_async_copy(buf, out_hbm.at[slot], sem)
        copy.start()
        copy.wait()

    return pl.pallas_call(
        kernel,
        out_shape=jax.ShapeDtypeStruct((OWN, rows, width), jnp.float32),
        in_specs=[HBM] * len(given) + [VMEM] * len(flat),
        out_specs=HBM,
        scratch_shapes=[pltpu.VMEM((rows, width), jnp.float32), pltpu.SemaphoreType.DMA],
        input_output_aliases={0: 0} if given else {},
        compiler_params=PARAMS,
        name=f"finish_{slot}",
    )(*given, *flat)


def shifted(array, axis, distance):
    size = lax.axis_size(axis)
    return lax.ppermute(array, axis, [(i, (i + distance) % size) for i in range(size)])


def swapped(array, axis):
    return lax.ppermute(array, axis, [(i, i ^ 1) for i in range(lax.axis_size(axis))])


def up(array):
    return shifted(array, "tile_1", 1)


def down(array):
    return shifted(array, "tile_1", -1)


def body(coupling, interior_solve, boundary_stiffness, migration):
    home, depth, width = interior_solve.shape
    rows = boundary_stiffness.shape[1]
    blocks = width // LANES
    half = blocks // 2
    pieces = jnp.swapaxes(coupling, 1, 2)
    in_hbm = [pltpu.with_memory_space_constraint(a, pltpu.HBM) for a in (migration, pieces, interior_solve)]
    outgoing = pack(*in_hbm, True)
    arrived = [swapped(outgoing[0], "group"), swapped(outgoing[1], "group")]
    local = pack(*in_hbm, False)
    up0, down0, own0 = merge(migration, arrived[0], local[0], 0, home)
    up1, down1, own1 = merge(migration, arrived[1], local[1], 1, home)
    stiff_arrived = swapped(stiff_out(migration, boundary_stiffness), "group")
    stiff = stiff_merge(migration, boundary_stiffness, stiff_arrived)

    def run(first):
        return list(range(first, first + blocks))

    turned = list(range(half, blocks)) + list(range(half))
    u0, d0, u1, d1 = up(up0), down(down0), up(up1), down(down1)
    total0 = accumulate(None, [(up0, run(3), own0, None)], width, "chunks_0")
    total1 = accumulate(None, [(up1, run(4), own1, None)], width, "chunks_1")
    uu0, dd0 = up(u0[1:]), down(d0[:-1])
    total0 = accumulate(total0, [(u0, run(3), u0, 0), (d0, run(0), d0, blocks + 3)], width, "chunks_0")
    uu1, dd1 = up(u1[1:]), down(d1[:-1])
    total1 = accumulate(total1, [(u1, run(4), u1, 0), (d1, turned, d1, blocks + 2)], width, "chunks_1")
    uuu0, ddd0 = up(uu0[1:]), down(dd0[:-1])
    total0 = accumulate(total0, [(uu0, run(2), uu0, 0), (dd0, run(0), dd0, blocks + 2)], width, "chunks_0")
    uuu1a, ddd1a = up(uu1[1 : half + 3]), down(dd1[half : blocks + 1])
    total1 = accumulate(total1, [(uu1, run(3), uu1, 0), (dd1, turned, dd1, blocks + 1)], width, "chunks_1")
    far0a, far0b = up(uuu0[1 : half + 1]), down(ddd0[half : blocks + 1])
    total0 = accumulate(total0, [(uuu0, run(1), uuu0, 0), (ddd0, run(0), ddd0, blocks + 1)], width, "chunks_0")
    uuu1b, ddd1b = up(uu1[half + 3 :]), down(dd1[:half])
    far1a, far1b = up(uuu1a[1:]), down(ddd1b)
    left, right = list(range(half)), list(range(half, blocks))
    wide = width // 2
    send0a, keep0a = last_chunks(
        total0, [(far0a, left, far0b, half)], stiff, 0, 0, wide, "last_0a"
    )
    send0b, keep0b = last_chunks(
        total0, [(far0b, left, far0b, half)], stiff, 0, wide, wide, "last_0b"
    )
    del right
    other0a, other0b = swapped(send0a, "tile_0"), swapped(send0b, "tile_0")
    send1a, keep1a = last_chunks(
        total1,
        [(uuu1a, run(2)[:half], uuu1a, 0), (ddd1a, left, ddd1a, half), (far1a, run(1)[:half], far1a, 0)],
        stiff, 1, 0, wide, "last_1a",
    )
    other1a = swapped(send1a, "tile_0")
    send1b, keep1b = last_chunks(
        total1,
        [(uuu1b, left, uuu1a, 0), (ddd1b, left, ddd1a, half), (far1b, left, far1a, 0)],
        stiff, 1, wide, wide, "last_1b",
    )
    other1b = swapped(send1b, "tile_0")
    result = finish(None, [(keep0a, other0a), (keep0b, other0b)], 0, rows, width)
    return finish(result, [(keep1a, other1a), (keep1b, other1b)], 1, rows, width)


def solution(mesh):
    finer = Mesh(mesh.devices.reshape(mesh.shape["group"], 2, 8), ("group", "tile_0", "tile_1"))
    in_specs = (P("group", None, TILE), P("group", TILE, None), P("group", TILE, None), P())
    out_specs = P("group", TILE, None)
    return jax.shard_map(body, mesh=finer, in_specs=in_specs, out_specs=out_specs, check_vma=False)
```

time: 66 us -> 73.4 us (1.11)
  starting transfers between devices: 30 us -> 34.6 us
  waiting for transfers between devices: 22.6 us -> 27 us
  local copies, waits for them, and re-layouts: 3.09 us -> 0.81 us
    ppermute x14 -> x18, waiting for transfers between devices: 14 us -> 22.7 us  [shifted(): lax.ppermute(array, axis, [(i, (i + distance) % size) for i in range(size)])]
    ppermute x5 -> x7, waiting for transfers between devices: 8.6 us -> 4.31 us  [swapped(): lax.ppermute(array, axis, [(i, i ^ 1) for i in range(lax.axis_size(axis))])]
    ppermute x14 -> x18, starting transfers between devices: 27.1 us -> 29.5 us  [shifted(): lax.ppermute(array, axis, [(i, (i + distance) % size) for i in range(size)])]
    unnamed x8 -> x4, local copies, waits for them, and re-layouts: 2.93 us -> 0.64 us
    ppermute x5 -> x7, starting transfers between devices: 2.88 us -> 5.08 us  [swapped(): lax.ppermute(array, axis, [(i, i ^ 1) for i in range(lax.axis_size(axis))])]
    pallas_call x1 -> x2, Pallas kernels: 0.86 us -> 1.49 us  [finish(): pl.pallas_call(kernel, out_shape=jax.ShapeDtypeStruct((OWN, rows, width),...]
    pallas_call x8 -> x7, Pallas kernels: 2.69 us -> 2.33 us  [accumulate(): pl.pallas_call(kernel, out_shape=jax.ShapeDtypeStruct((LANES, width), jnp...]
    pallas_call x4 -> x6, Pallas kernels: 3.82 us -> 4.05 us  [the longest x2 2.85 us: pack(): pl.pallas_call(kernel, out_shape=(packet, packet), in_specs=[HBM] * 3, ou...]
  transfers between devices with their start and end apart: 19 -> 25, of which waited for: 11 -> 8; matrix products, arithmetic and copies ran while one was open for 0% -> 0% of each run, Pallas kernels for 11% -> 11%
where the time goes in v2:
time: 73.4 us; the launch traced here: 73.2 us
  starting transfers between devices  34.6 us (47%)
  waiting for transfers between devices  27 us (37%)
  Pallas kernels  10.3 us (14%)
  local copies, waits for them, and re-layouts  0.81 us (1%)
    ppermute x18, starting transfers between devices, shifted(): lax.ppermute(array, axis, [(i, (i + distance) % size) for i in range(size)])  29.5 us
    ppermute x18, waiting for transfers between devices, shifted(): lax.ppermute(array, axis, [(i, (i + distance) % size) for i in range(size)])  22.7 us
    ppermute x7, starting transfers between devices, swapped(): lax.ppermute(array, axis, [(i, i ^ 1) for i in range(lax.axis_size(axis))])  5.08 us
    ppermute x7, waiting for transfers between devices, swapped(): lax.ppermute(array, axis, [(i, i ^ 1) for i in range(lax.axis_size(axis))])  4.31 us
    pallas_call x2, Pallas kernels, pack(): pl.pallas_call(kernel, out_shape=(packet, packet), in_specs=[HBM] * 3, ou...  2.85 us
    pallas_call x7, Pallas kernels, accumulate(): pl.pallas_call(kernel, out_shape=jax.ShapeDtypeStruct((LANES, width), jnp...  2.33 us
    pallas_call x2, Pallas kernels, finish(): pl.pallas_call(kernel, out_shape=jax.ShapeDtypeStruct((OWN, rows, width),...  1.49 us
  transfers between devices with their start and end apart: 25, of which 8 were waited for; matrix products, arithmetic and copies ran while one was open for 0% of the time, Pallas kernels for 11%

profile of v2, /device:TPU:24, one launch (start us, length us, event | category | flops | bytes accessed | tf_op | source)
XLA Modules:
  0.0 73.2 jit_solution(277162034345948289)
XLA Ops:
  0.0 1.4 %pack_partner.1 = (f32[16,48,128]{2,1,0:T(8,128)S(1)}, f32[16,48,128]{2,1,0:T(8,128)S(1)}) custom-call(s32[64]{0:T(128)} %plan_ref.7, f32[4,48,1024]{2,1,0:T(8,128)} %bitcast.1, f32[4,48,1024]{2,1,0:T(8,128)} %x_hbm.3), custom_call_target="tpu_custom_call" | custom-call | tf_op jit(solution)/shard_map/pack_partner/pallas_call | solution.py:69
  1.4 0.1 collective-permute-start
  1.5 0.5 collective-permute-start.12
  2.0 1.4 %pack_own.1 = (f32[16,48,128]{2,1,0:T(8,128)S(1)}, f32[16,48,128]{2,1,0:T(8,128)S(1)}) custom-call(s32[64]{0:T(128)} %plan_ref.7, f32[4,48,1024]{2,1,0:T(8,128)} %bitcast.2, f32[4,48,1024]{2,1,0:T(8,128)} %x_hbm.3), custom_call_target="tpu_custom_call" | custom-call | tf_op jit(solution)/shard_map/pack_own/pallas_call | solution.py:69
  3.5 0.0 copy-start.1
  3.5 0.0 collective-permute-done.arrived_ref
  3.5 0.6 copy-done.1
  4.1 0.6 merge_0.1
  4.7 5.9 %collective-permute-start.2 = (f32[12,48,128]{2,1,0:T(8,128)S(1)}, f32[12,48,128]{2,1,0:T(8,128)S(1)}, u32[]{:S(2)}, u32[]{:S(2)}) collective-permute-start(f32[12,48,128]{2,1,0:T(8,128)S(1)} %get-tuple-element.27), channel_id=1, source_target_pairs={{0,7},{1,0},{2,1},{3,2},{4,3},{5,4},{6,5},{7,6},{8,15},{9,8},{10,9... | collective-permute-start | bytes 884744 | tf_op jit(solution)/shard_map/ppermute | solution.py:302
  10.7 0.0 collective-permute-done.12.arrived_ref
  10.7 0.6 merge_1.1
  11.3 0.1 collective-permute-start.13
  11.4 0.1 collective-permute-start.1
  11.5 3.2 %collective-permute-start.14 = (f32[11,48,128]{2,1,0:T(8,128)S(1)}, f32[11,48,128]{2,1,0:T(8,128)S(1)}, u32[]{:S(2)}, u32[]{:S(2)}) collective-permute-start(f32[11,48,128]{2,1,0:T(8,128)S(1)} %get-tuple-element.36), channel_id=1, source_target_pairs={{0,7},{1,0},{2,1},{3,2},{4,3},{5,4},{6,5},{7,6},{8,15},{9,8},{10,9... | collective-permute-start | bytes 811016 | tf_op jit(solution)/shard_map/ppermute | solution.py:302
  14.7 3.4 %collective-permute-done.2.refs_2_ = f32[12,48,128]{2,1,0:T(8,128)S(1)} collective-permute-done((f32[12,48,128]{2,1,0:T(8,128)S(1)}, f32[12,48,128]{2,1,0:T(8,128)S(1)}, u32[]{:S(2)}, u32[]{:S(2)}) %collective-permute-start.2) | collective-permute-done | bytes 294944 | tf_op jit(solution)/shard_map/ppermute | solution.py:302
  18.1 3.8 %collective-permute-start.4 = (f32[11,48,128]{2,1,0:T(8,128)S(1)}, f32[11,48,128]{2,1,0:T(8,128)S(1)}, u32[]{:S(2)}, u32[]{:S(2)}) collective-permute-start(f32[11,48,128]{2,1,0:T(8,128)S(1)} %slice.53), channel_id=1, source_target_pairs={{0,7},{1,0},{2,1},{3,2},{4,3},{5,4},{6,5},{7,6},{8,15},{9,8},{10,9... | collective-permute-start | bytes 811016 | tf_op jit(solution)/shard_map/ppermute | solution.py:302
  21.8 0.6 stiff_out.1
  22.5 0.1 collective-permute-start.7
  22.6 0.1 collective-permute-start.15
  22.7 4.4 %collective-permute-done.1.refs_1_ = f32[11,48,128]{2,1,0:T(8,128)S(1)} collective-permute-done((f32[11,48,128]{2,1,0:T(8,128)S(1)}, f32[11,48,128]{2,1,0:T(8,128)S(1)}, u32[]{:S(2)}, u32[]{:S(2)}) %collective-permute-start.1) | collective-permute-done | bytes 270368 | tf_op jit(solution)/shard_map/ppermute | solution.py:302
  27.2 0.1 collective-permute-start.3
  27.3 3.3 %collective-permute-start.16 = (f32[10,48,128]{2,1,0:T(8,128)S(1)}, f32[10,48,128]{2,1,0:T(8,128)S(1)}, u32[]{:S(2)}, u32[]{:S(2)}) collective-permute-start(f32[10,48,128]{2,1,0:T(8,128)S(1)} %slice.59), channel_id=1, source_target_pairs={{0,7},{1,0},{2,1},{3,2},{4,3},{5,4},{6,5},{7,6},{8,15},{9,8},{10,9... | collective-permute-start | bytes 737288 | tf_op jit(solution)/shard_map/ppermute | solution.py:302
  30.6 0.0 collective-permute-done.4.refs_2_
  30.6 2.0 %collective-permute-start.6 = (f32[10,48,128]{2,1,0:T(8,128)S(1)}, f32[10,48,128]{2,1,0:T(8,128)S(1)}, u32[]{:S(2)}, u32[]{:S(2)}) collective-permute-start(f32[10,48,128]{2,1,0:T(8,128)S(1)} %slice.55), channel_id=1, source_target_pairs={{0,7},{1,0},{2,1},{3,2},{4,3},{5,4},{6,5},{7,6},{8,15},{9,8},{10,9... | collective-permute-start | bytes 737288 | tf_op jit(solution)/shard_map/ppermute | solution.py:302
  32.6 5.6 %collective-permute-done.3.refs_1_ = f32[10,48,128]{2,1,0:T(8,128)S(1)} collective-permute-done((f32[10,48,128]{2,1,0:T(8,128)S(1)}, f32[10,48,128]{2,1,0:T(8,128)S(1)}, u32[]{:S(2)}, u32[]{:S(2)}) %collective-permute-start.3) | collective-permute-done | bytes 245792 | tf_op jit(solution)/shard_map/ppermute | solution.py:302
  38.2 0.1 collective-permute-start.5
  38.3 0.0 collective-permute-done.15.refs_1_
  38.3 0.1 collective-permute-start.17
  38.4 3.3 %collective-permute-start.18 = (f32[5,48,128]{2,1,0:T(8,128)S(1)}, f32[5,48,128]{2,1,0:T(8,128)S(1)}, u32[]{:S(2)}, u32[]{:S(2)}) collective-permute-start(f32[5,48,128]{2,1,0:T(8,128)S(1)} %slice.61), channel_id=1, source_target_pairs={{0,7},{1,0},{2,1},{3,2},{4,3},{5,4},{6,5},{7,6},{8,15},{9,8},{10,9... | collective-permute-start | bytes 368648 | tf_op jit(solution)/shard_map/ppermute | solution.py:302
  41.7 8.1 %collective-permute-done.17.refs_0_.refs_1_ = f32[6,48,128]{2,1,0:T(8,128)S(1)} collective-permute-done((f32[6,48,128]{2,1,0:T(8,128)S(1)}, f32[6,48,128]{2,1,0:T(8,128)S(1)}, u32[]{:S(2)}, u32[]{:S(2)}) %collective-permute-start.17) | collective-permute-done | bytes 147488 | tf_op jit(solution)/shard_map/ppermute | solution.py:302
  49.8 0.0 collective-permute-start.22
  49.8 0.0 collective-permute-done.6.refs_2_
  49.8 2.1 %collective-permute-start.19 = (f32[5,48,128]{2,1,0:T(8,128)S(1)}, f32[5,48,128]{2,1,0:T(8,128)S(1)}, u32[]{:S(2)}, u32[]{:S(2)}) collective-permute-start(f32[5,48,128]{2,1,0:T(8,128)S(1)} %slice.62), channel_id=1, source_target_pairs={{0,1},{1,2},{2,3},{3,4},{4,5},{5,6},{6,7},{7,0},{8,9},{9,10},{10,1... | collective-permute-start | bytes 368648 | tf_op jit(solution)/shard_map/ppermute | solution.py:302
  51.9 1.3 %collective-permute-start.9 = (f32[5,48,128]{2,1,0:T(8,128)S(1)}, f32[5,48,128]{2,1,0:T(8,128)S(1)}, u32[]{:S(2)}, u32[]{:S(2)}) collective-permute-start(f32[5,48,128]{2,1,0:T(8,128)S(1)} %slice.57), channel_id=1, source_target_pairs={{0,7},{1,0},{2,1},{3,2},{4,3},{5,4},{6,5},{7,6},{8,15},{9,8},{10,9... | collective-permute-start | bytes 368648 | tf_op jit(solution)/shard_map/ppermute | solution.py:302
  53.2 0.9 %collective-permute-start.8 = (f32[4,48,128]{2,1,0:T(8,128)S(1)}, f32[4,48,128]{2,1,0:T(8,128)S(1)}, u32[]{:S(2)}, u32[]{:S(2)}) collective-permute-start(f32[4,48,128]{2,1,0:T(8,128)S(1)} %slice.56), channel_id=1, source_target_pairs={{0,1},{1,2},{2,3},{3,4},{4,5},{5,6},{6,7},{7,0},{8,9},{9,10},{10,1... | collective-permute-start | bytes 294920 | tf_op jit(solution)/shard_map/ppermute | solution.py:302
  54.1 1.2 %collective-permute-done.22.refs_2_ = f32[4,48,128]{2,1,0:T(8,128)S(1)} collective-permute-done((f32[4,48,128]{2,1,0:T(8,128)S(1)}, f32[4,48,128]{2,1,0:T(8,128)S(1)}, u32[]{:S(2)}, u32[]{:S(2)}) %collective-permute-start.22) | collective-permute-done | bytes 98336 | tf_op jit(solution)/shard_map/ppermute | solution.py:302
  55.3 0.0 collective-permute-start.21
  55.3 3.2 %collective-permute-start.23 = (f32[4,48,128]{2,1,0:T(8,128)S(1)}, f32[4,48,128]{2,1,0:T(8,128)S(1)}, u32[]{:S(2)}, u32[]{:S(2)}) collective-permute-start(f32[4,48,128]{2,1,0:T(8,128)S(1)} %collective-permute-done.22.refs_2_), channel_id=1, source_target_pairs={{0,7},{1,0},{2,1},{3,2},{4,3},{5,4},{6,5},{7,6},{8,15},{9,8},{10,9... | collective-permute-start | bytes 294920 | tf_op jit(solution)/shard_map/ppermute | solution.py:302
  58.6 0.3 chunks_0.4.refs_0_
  58.9 0.3 chunks_1.3.refs_0_
  59.1 0.6 stiff_merge.1.stiff_ref
  59.8 0.4 chunks_0.5.refs_0_
  60.1 0.4 chunks_1.4.refs_0_
  60.5 0.4 chunks_0.6.refs_0_
  60.9 0.4 chunks_1.5.total_ref
  61.2 0.4 chunks_0.7.total_ref
  61.6 0.0 collective-permute-done.19.refs_2_.refs_5_
  61.6 0.3 last_1a.1
  62.0 1.6 %collective-permute-start.20 = (f32[64,512]{1,0:T(8,128)S(1)}, f32[64,512]{1,0:T(8,128)S(1)}, u32[]{:S(2)}, u32[]{:S(2)}) collective-permute-start(f32[64,512]{1,0:T(8,128)S(1)} %get-tuple-element.38), channel_id=1, source_target_pairs={{0,8},{8,0},{1,9},{9,1},{2,10},{10,2},{3,11},{11,3},{4,12},{12,4},... | collective-permute-start | bytes 393224 | tf_op jit(solution)/shard_map/ppermute | solution.py:306
  63.5 0.0 collective-permute-done.8.refs_0_
  63.5 0.0 collective-permute-done.9.refs_1_.refs_0_
  63.5 0.3 last_0a.1
  63.8 0.6 collective-permute-start.10
  64.4 0.3 last_0b.1
  64.7 1.6 %collective-permute-start.11 = (f32[64,512]{1,0:T(8,128)S(1)}, f32[64,512]{1,0:T(8,128)S(1)}, u32[]{:S(2)}, u32[]{:S(2)}) collective-permute-start(f32[64,512]{1,0:T(8,128)S(1)} %get-tuple-element.31), channel_id=1, source_target_pairs={{0,8},{8,0},{1,9},{9,1},{2,10},{10,2},{3,11},{11,3},{4,12},{12,4},... | collective-permute-start | bytes 393224 | tf_op jit(solution)/shard_map/ppermute | solution.py:306
  66.3 0.0 collective-permute-done.23.refs_4_
  66.3 0.3 last_1b.1
  66.6 0.6 collective-permute-start.24
  67.3 2.3 %collective-permute-done.10.refs_1_ = f32[64,512]{1,0:T(8,128)S(1)} collective-permute-done((f32[64,512]{1,0:T(8,128)S(1)}, f32[64,512]{1,0:T(8,128)S(1)}, u32[]{:S(2)}, u32[]{:S(2)}) %collective-permute-start.10) | collective-permute-done | bytes 131104 | tf_op jit(solution)/shard_map/ppermute | solution.py:306
  69.5 1.4 %collective-permute-done.11.refs_3_ = f32[64,512]{1,0:T(8,128)S(1)} collective-permute-done((f32[64,512]{1,0:T(8,128)S(1)}, f32[64,512]{1,0:T(8,128)S(1)}, u32[]{:S(2)}, u32[]{:S(2)}) %collective-permute-start.11) | collective-permute-done | bytes 131104 | tf_op jit(solution)/shard_map/ppermute | solution.py:306
  70.9 0.7 %finish_0.1.refs_0_ = f32[2,64,1024]{2,1,0:T(8,128)} custom-call(f32[64,512]{1,0:T(8,128)S(1)} %get-tuple-element.28.refs_0_, f32[64,512]{1,0:T(8,128)S(1)} %collective-permute-done.10.refs_1_, f32[64,512]{1,0:T(8,128)S(1)} %get-tuple-element.30.refs_2_, f32[64,512]{1,0:T(8,128)S(1)} %collective-permute-done.11.refs_3_), custom_call_target="tpu_custom_call" | custom-call | tf_op jit(solution)/shard_map/finish_0/pallas_call | solution.py:288
  71.7 0.0 collective-permute-done.20.refs_2_
  71.7 0.6 collective-permute-done.24.refs_4_
  72.3 0.7 %finish_1.1 = f32[2,64,1024]{2,1,0:T(8,128)} custom-call(f32[2,64,1024]{2,1,0:T(8,128)} %finish_0.1.refs_0_, f32[64,512]{1,0:T(8,128)S(1)} %get-tuple-element.37.refs_1_, f32[64,512]{1,0:T(8,128)S(1)} %collective-permute-done.20.refs_2_, f32[64,512]{1,0:T(8,128)S(1)} %get-tuple-element.39.refs_3_, ...), custom_call_target="tpu_custom_call", output_to_operand_aliasing={{}: (0, {})} | custom-call | tf_op jit(solution)/shard_map/finish_1/pallas_call | solution.py:288
  (22 shorter events, 0.2 us)
Async XLA Ops:
  1.4 2.0 %collective-permute-start = (f32[16,48,128]{2,1,0:T(8,128)S(1)}, f32[16,48,128]{2,1,0:T(8,128)S(1)}, u32[]{:S(2)}, u32[]{:S(2)}) collective-permute-start(f32[16,48,128]{2,1,0:T(8,128)S(1)} %get-tuple-element.23), channel_id=1, source_target_pairs={{0,16},{16,0},{32,48},{48,32},{64,80},{80,64},{96,112},{112,96},{1... | collective-permute-start | bytes 1179656 | tf_op jit(solution)/shard_map/ppermute | solution.py:306
  1.5 9.1 %collective-permute-start.12 = (f32[16,48,128]{2,1,0:T(8,128)S(1)}, f32[16,48,128]{2,1,0:T(8,128)S(1)}, u32[]{:S(2)}, u32[]{:S(2)}) collective-permute-start(f32[16,48,128]{2,1,0:T(8,128)S(1)} %get-tuple-element.32), channel_id=1, source_target_pairs={{0,16},{16,0},{32,48},{48,32},{64,80},{80,64},{96,112},{112,96},{1... | collective-permute-start | bytes 1179656 | tf_op jit(solution)/shard_map/ppermute | solution.py:306
  3.5 0.7 copy-start.1
  4.1 17.7 %copy-start = (f32[4,64,1024]{2,1,0:T(8,128)S(1)}, f32[4,64,1024]{2,1,0:T(8,128)}, u32[]{:S(2)}) copy-start(f32[4,64,1024]{2,1,0:T(8,128)} %b_hbm.3) | copy-start | bytes 3145732
  4.7 13.3 %collective-permute-start.2 = (f32[12,48,128]{2,1,0:T(8,128)S(1)}, f32[12,48,128]{2,1,0:T(8,128)S(1)}, u32[]{:S(2)}, u32[]{:S(2)}) collective-permute-start(f32[12,48,128]{2,1,0:T(8,128)S(1)} %get-tuple-element.27), channel_id=1, source_target_pairs={{0,7},{1,0},{2,1},{3,2},{4,3},{5,4},{6,5},{7,6},{8,15},{9,8},{10,9... | collective-permute-start | bytes 884744 | tf_op jit(solution)/shard_map/ppermute | solution.py:302
  11.3 11.3 %collective-permute-start.13 = (f32[12,48,128]{2,1,0:T(8,128)S(1)}, f32[12,48,128]{2,1,0:T(8,128)S(1)}, u32[]{:S(2)}, u32[]{:S(2)}) collective-permute-start(f32[12,48,128]{2,1,0:T(8,128)S(1)} %get-tuple-element.34.refs_0_), channel_id=1, source_target_pairs={{0,1},{1,2},{2,3},{3,4},{4,5},{5,6},{6,7},{7,0},{8,9},{9,10},{10,1... | collective-permute-start | bytes 884744 | tf_op jit(solution)/shard_map/ppermute | solution.py:302
  11.4 15.8 %collective-permute-start.1 = (f32[11,48,128]{2,1,0:T(8,128)S(1)}, f32[11,48,128]{2,1,0:T(8,128)S(1)}, u32[]{:S(2)}, u32[]{:S(2)}) collective-permute-start(f32[11,48,128]{2,1,0:T(8,128)S(1)} %get-tuple-element.25.refs_0_), channel_id=1, source_target_pairs={{0,1},{1,2},{2,3},{3,4},{4,5},{5,6},{6,7},{7,0},{8,9},{9,10},{10,1... | collective-permute-start | bytes 811016 | tf_op jit(solution)/shard_map/ppermute | solution.py:302
  11.5 15.8 %collective-permute-start.14 = (f32[11,48,128]{2,1,0:T(8,128)S(1)}, f32[11,48,128]{2,1,0:T(8,128)S(1)}, u32[]{:S(2)}, u32[]{:S(2)}) collective-permute-start(f32[11,48,128]{2,1,0:T(8,128)S(1)} %get-tuple-element.36), channel_id=1, source_target_pairs={{0,7},{1,0},{2,1},{3,2},{4,3},{5,4},{6,5},{7,6},{8,15},{9,8},{10,9... | collective-permute-start | bytes 811016 | tf_op jit(solution)/shard_map/ppermute | solution.py:302
  18.1 12.5 %collective-permute-start.4 = (f32[11,48,128]{2,1,0:T(8,128)S(1)}, f32[11,48,128]{2,1,0:T(8,128)S(1)}, u32[]{:S(2)}, u32[]{:S(2)}) collective-permute-start(f32[11,48,128]{2,1,0:T(8,128)S(1)} %slice.53), channel_id=1, source_target_pairs={{0,7},{1,0},{2,1},{3,2},{4,3},{5,4},{6,5},{7,6},{8,15},{9,8},{10,9... | collective-permute-start | bytes 811016 | tf_op jit(solution)/shard_map/ppermute | solution.py:302
  22.5 30.8 %collective-permute-start.7 = (f32[2,64,1024]{2,1,0:T(8,128)S(1)}, f32[2,64,1024]{2,1,0:T(8,128)S(1)}, u32[]{:S(2)}, u32[]{:S(2)}) collective-permute-start(f32[2,64,1024]{2,1,0:T(8,128)S(1)} %stiff_out.1), channel_id=1, source_target_pairs={{0,16},{16,0},{32,48},{48,32},{64,80},{80,64},{96,112},{112,96},{1... | collective-permute-start | bytes 1572872 | tf_op jit(solution)/shard_map/ppermute | solution.py:306
  22.6 15.7 %collective-permute-start.15 = (f32[11,48,128]{2,1,0:T(8,128)S(1)}, f32[11,48,128]{2,1,0:T(8,128)S(1)}, u32[]{:S(2)}, u32[]{:S(2)}) collective-permute-start(f32[11,48,128]{2,1,0:T(8,128)S(1)} %slice.58), channel_id=1, source_target_pairs={{0,1},{1,2},{2,3},{3,4},{4,5},{5,6},{6,7},{7,0},{8,9},{9,10},{10,1... | collective-permute-start | bytes 811016 | tf_op jit(solution)/shard_map/ppermute | solution.py:302
  27.2 11.0 %collective-permute-start.3 = (f32[10,48,128]{2,1,0:T(8,128)S(1)}, f32[10,48,128]{2,1,0:T(8,128)S(1)}, u32[]{:S(2)}, u32[]{:S(2)}) collective-permute-start(f32[10,48,128]{2,1,0:T(8,128)S(1)} %slice.52), channel_id=1, source_target_pairs={{0,1},{1,2},{2,3},{3,4},{4,5},{5,6},{6,7},{7,0},{8,9},{9,10},{10,1... | collective-permute-start | bytes 737288 | tf_op jit(solution)/shard_map/ppermute | solution.py:302
  27.3 11.1 %collective-permute-start.16 = (f32[10,48,128]{2,1,0:T(8,128)S(1)}, f32[10,48,128]{2,1,0:T(8,128)S(1)}, u32[]{:S(2)}, u32[]{:S(2)}) collective-permute-start(f32[10,48,128]{2,1,0:T(8,128)S(1)} %slice.59), channel_id=1, source_target_pairs={{0,7},{1,0},{2,1},{3,2},{4,3},{5,4},{6,5},{7,6},{8,15},{9,8},{10,9... | collective-permute-start | bytes 737288 | tf_op jit(solution)/shard_map/ppermute | solution.py:302
  30.6 19.2 %collective-permute-start.6 = (f32[10,48,128]{2,1,0:T(8,128)S(1)}, f32[10,48,128]{2,1,0:T(8,128)S(1)}, u32[]{:S(2)}, u32[]{:S(2)}) collective-permute-start(f32[10,48,128]{2,1,0:T(8,128)S(1)} %slice.55), channel_id=1, source_target_pairs={{0,7},{1,0},{2,1},{3,2},{4,3},{5,4},{6,5},{7,6},{8,15},{9,8},{10,9... | collective-permute-start | bytes 737288 | tf_op jit(solution)/shard_map/ppermute | solution.py:302
  38.2 13.7 %collective-permute-start.5 = (f32[9,48,128]{2,1,0:T(8,128)S(1)}, f32[9,48,128]{2,1,0:T(8,128)S(1)}, u32[]{:S(2)}, u32[]{:S(2)}) collective-permute-start(f32[9,48,128]{2,1,0:T(8,128)S(1)} %slice.54), channel_id=1, source_target_pairs={{0,1},{1,2},{2,3},{3,4},{4,5},{5,6},{6,7},{7,0},{8,9},{9,10},{10,1... | collective-permute-start | bytes 663560 | tf_op jit(solution)/shard_map/ppermute | solution.py:302
  38.3 11.5 %collective-permute-start.17 = (f32[6,48,128]{2,1,0:T(8,128)S(1)}, f32[6,48,128]{2,1,0:T(8,128)S(1)}, u32[]{:S(2)}, u32[]{:S(2)}) collective-permute-start(f32[6,48,128]{2,1,0:T(8,128)S(1)} %slice.60), channel_id=1, source_target_pairs={{0,1},{1,2},{2,3},{3,4},{4,5},{5,6},{6,7},{7,0},{8,9},{9,10},{10,1... | collective-permute-start | bytes 442376 | tf_op jit(solution)/shard_map/ppermute | solution.py:302
  38.4 16.9 %collective-permute-start.18 = (f32[5,48,128]{2,1,0:T(8,128)S(1)}, f32[5,48,128]{2,1,0:T(8,128)S(1)}, u32[]{:S(2)}, u32[]{:S(2)}) collective-permute-start(f32[5,48,128]{2,1,0:T(8,128)S(1)} %slice.61), channel_id=1, source_target_pairs={{0,7},{1,0},{2,1},{3,2},{4,3},{5,4},{6,5},{7,6},{8,15},{9,8},{10,9... | collective-permute-start | bytes 368648 | tf_op jit(solution)/shard_map/ppermute | solution.py:302
  49.8 5.6 %collective-permute-start.22 = (f32[4,48,128]{2,1,0:T(8,128)S(1)}, f32[4,48,128]{2,1,0:T(8,128)S(1)}, u32[]{:S(2)}, u32[]{:S(2)}) collective-permute-start(f32[4,48,128]{2,1,0:T(8,128)S(1)} %slice.64), channel_id=1, source_target_pairs={{0,7},{1,0},{2,1},{3,2},{4,3},{5,4},{6,5},{7,6},{8,15},{9,8},{10,9... | collective-permute-start | bytes 294920 | tf_op jit(solution)/shard_map/ppermute | solution.py:302
  49.8 11.8 %collective-permute-start.19 = (f32[5,48,128]{2,1,0:T(8,128)S(1)}, f32[5,48,128]{2,1,0:T(8,128)S(1)}, u32[]{:S(2)}, u32[]{:S(2)}) collective-permute-start(f32[5,48,128]{2,1,0:T(8,128)S(1)} %slice.62), channel_id=1, source_target_pairs={{0,1},{1,2},{2,3},{3,4},{4,5},{5,6},{6,7},{7,0},{8,9},{9,10},{10,1... | collective-permute-start | bytes 368648 | tf_op jit(solution)/shard_map/ppermute | solution.py:302
  51.9 11.6 %collective-permute-start.9 = (f32[5,48,128]{2,1,0:T(8,128)S(1)}, f32[5,48,128]{2,1,0:T(8,128)S(1)}, u32[]{:S(2)}, u32[]{:S(2)}) collective-permute-start(f32[5,48,128]{2,1,0:T(8,128)S(1)} %slice.57), channel_id=1, source_target_pairs={{0,7},{1,0},{2,1},{3,2},{4,3},{5,4},{6,5},{7,6},{8,15},{9,8},{10,9... | collective-permute-start | bytes 368648 | tf_op jit(solution)/shard_map/ppermute | solution.py:302
  53.2 10.3 %collective-permute-start.8 = (f32[4,48,128]{2,1,0:T(8,128)S(1)}, f32[4,48,128]{2,1,0:T(8,128)S(1)}, u32[]{:S(2)}, u32[]{:S(2)}) collective-permute-start(f32[4,48,128]{2,1,0:T(8,128)S(1)} %slice.56), channel_id=1, source_target_pairs={{0,1},{1,2},{2,3},{3,4},{4,5},{5,6},{6,7},{7,0},{8,9},{9,10},{10,1... | collective-permute-start | bytes 294920 | tf_op jit(solution)/shard_map/ppermute | solution.py:302
  55.3 10.9 %collective-permute-start.21 = (f32[4,48,128]{2,1,0:T(8,128)S(1)}, f32[4,48,128]{2,1,0:T(8,128)S(1)}, u32[]{:S(2)}, u32[]{:S(2)}) collective-permute-start(f32[4,48,128]{2,1,0:T(8,128)S(1)} %slice.63), channel_id=1, source_target_pairs={{0,1},{1,2},{2,3},{3,4},{4,5},{5,6},{6,7},{7,0},{8,9},{9,10},{10,1... | collective-permute-start | bytes 294920 | tf_op jit(solution)/shard_map/ppermute | solution.py:302
  55.3 10.9 %collective-permute-start.23 = (f32[4,48,128]{2,1,0:T(8,128)S(1)}, f32[4,48,128]{2,1,0:T(8,128)S(1)}, u32[]{:S(2)}, u32[]{:S(2)}) collective-permute-start(f32[4,48,128]{2,1,0:T(8,128)S(1)} %collective-permute-done.22.refs_2_), channel_id=1, source_target_pairs={{0,7},{1,0},{2,1},{3,2},{4,3},{5,4},{6,5},{7,6},{8,15},{9,8},{10,9... | collective-permute-start | bytes 294920 | tf_op jit(solution)/shard_map/ppermute | solution.py:302
  62.0 9.7 %collective-permute-start.20 = (f32[64,512]{1,0:T(8,128)S(1)}, f32[64,512]{1,0:T(8,128)S(1)}, u32[]{:S(2)}, u32[]{:S(2)}) collective-permute-start(f32[64,512]{1,0:T(8,128)S(1)} %get-tuple-element.38), channel_id=1, source_target_pairs={{0,8},{8,0},{1,9},{9,1},{2,10},{10,2},{3,11},{11,3},{4,12},{12,4},... | collective-permute-start | bytes 393224 | tf_op jit(solution)/shard_map/ppermute | solution.py:306
  63.8 5.7 %collective-permute-start.10 = (f32[64,512]{1,0:T(8,128)S(1)}, f32[64,512]{1,0:T(8,128)S(1)}, u32[]{:S(2)}, u32[]{:S(2)}) collective-permute-start(f32[64,512]{1,0:T(8,128)S(1)} %get-tuple-element.29), channel_id=1, source_target_pairs={{0,8},{8,0},{1,9},{9,1},{2,10},{10,2},{3,11},{11,3},{4,12},{12,4},... | collective-permute-start | bytes 393224 | tf_op jit(solution)/shard_map/ppermute | solution.py:306
  64.7 6.2 %collective-permute-start.11 = (f32[64,512]{1,0:T(8,128)S(1)}, f32[64,512]{1,0:T(8,128)S(1)}, u32[]{:S(2)}, u32[]{:S(2)}) collective-permute-start(f32[64,512]{1,0:T(8,128)S(1)} %get-tuple-element.31), channel_id=1, source_target_pairs={{0,8},{8,0},{1,9},{9,1},{2,10},{10,2},{3,11},{11,3},{4,12},{12,4},... | collective-permute-start | bytes 393224 | tf_op jit(solution)/shard_map/ppermute | solution.py:306
  66.6 5.7 %collective-permute-start.24 = (f32[64,512]{1,0:T(8,128)S(1)}, f32[64,512]{1,0:T(8,128)S(1)}, u32[]{:S(2)}, u32[]{:S(2)}) collective-permute-start(f32[64,512]{1,0:T(8,128)S(1)} %get-tuple-element.40), channel_id=1, source_target_pairs={{0,8},{8,0},{1,9},{9,1},{2,10},{10,2},{3,11},{11,3},{4,12},{12,4},... | collective-permute-start | bytes 393224 | tf_op jit(solution)/shard_map/ppermute | solution.py:306

commit v3 on v2

--- a/solution.py
+++ b/solution.py
@@ -15,8 +15,13 @@
 HBM = pl.BlockSpec(memory_space=pltpu.HBM)
 
 
-def hops(slot):
-    return (3, 4) if slot == 0 else (4, 3)
+def hops(chain):
+    return (4, 3) if chain == 0 else (3, 4)
+
+
+def slot_of(chain):
+    column = lax.axis_index("tile_0")
+    return column if chain == 0 else 1 - column
 
 
 def locate(plan, group, wanted, home):
@@ -46,7 +51,7 @@
             copy.start()
         low = lax.broadcasted_iota(jnp.int32, (depth, LANES), 1) < LANES // 2
         copies[0].wait()
-        positions = [locate(plan_ref, group, owner * OWN + slot, home)[0] for slot in range(OWN)]
+        positions = [locate(plan_ref, group, owner * OWN + slot_of(slot), home)[0] for slot in range(OWN)]
         copies[1].wait()
         for slot in range(OWN):
             up = hops(slot)[0]
@@ -84,25 +89,23 @@
     )(plan, coupling, solve)
 
 
-def merge(plan, arrived, local, slot, home):
+def merge(plan, arrived, local, chain, home):
     total, depth, _ = arrived.shape
-    up, down = hops(slot)
+    up, down = hops(chain)
     blocks = total // 2
-    half = blocks // 2
 
     def kernel(plan_ref, arrived_ref, local_ref, up_ref, down_ref, own_ref):
         group = lax.axis_index("group")
-        _, here = locate(plan_ref, group, group * OWN + slot, home)
+        _, here = locate(plan_ref, group, group * OWN + slot_of(chain), home)
 
         def put(source):
             up_ref[...] = source[0 : up + blocks]
-            if slot == 0:
-                down_ref[...] = source[up : total - 1]
+            down_ref[...] = source[up : total - 1]
+            if chain == 0:
+                own_ref[0] = source[total - 1]
             else:
-                down_ref[0:half] = source[up + half : up + blocks]
-                down_ref[half:blocks] = source[up : up + half]
-                down_ref[blocks:] = source[up + blocks : total - 1]
-            own_ref[...] = source[total - 1]
+                own_ref[0:blocks] = source[up : up + blocks]
+                own_ref[blocks] = source[total - 1]
 
         @pl.when(here)
         def _():
@@ -117,12 +120,12 @@
         out_shape=(
             jax.ShapeDtypeStruct((up + blocks, depth, LANES), jnp.float32),
             jax.ShapeDtypeStruct((down + blocks, depth, LANES), jnp.float32),
-            jax.ShapeDtypeStruct((depth, LANES), jnp.float32),
+            jax.ShapeDtypeStruct((1 if chain == 0 else 1 + blocks, depth, LANES), jnp.float32),
         ),
         in_specs=[SMEM, VMEM, VMEM],
         out_specs=(VMEM, VMEM, VMEM),
         compiler_params=PARAMS,
-        name=f"merge_{slot}",
+        name=f"merge_{chain}",
     )(plan, arrived, local)
 
 
@@ -244,43 +247,38 @@
     )(*given, *arrays)
 
 
-def last_chunks(total, sources, stiff, slot, first, width, name):
-    rows = LANES // 2
+def last_chunks(total, sources):
+    rows, width = LANES // 2, total.shape[1]
     arrays, layout = gathered(sources)
-    columns = pl.ds(first, width)
-
-    def kernel(total_ref, stiff_ref, *refs):
+
+    def kernel(total_ref, *refs):
         send_ref, keep_ref, sum_ref = refs[-3:]
-        sum_ref[...] = total_ref[:, columns]
+        sum_ref[...] = total_ref[...]
         add_chunks(sum_ref, chunks_of(refs[:-3], layout), False)
         mine = lax.axis_index("tile_0")
         send_ref[...] = sum_ref[pl.ds(pl.multiple_of((1 - mine) * rows, rows), rows), :]
-        keep_ref[...] = stiff_ref[slot, :, columns] - sum_ref[pl.ds(pl.multiple_of(mine * rows, rows), rows), :]
+        keep_ref[...] = sum_ref[pl.ds(pl.multiple_of(mine * rows, rows), rows), :]
 
     half = jax.ShapeDtypeStruct((rows, width), jnp.float32)
     return pl.pallas_call(
         kernel,
         out_shape=(half, half),
-        in_specs=[VMEM] * (2 + len(arrays)),
+        in_specs=[VMEM] * (1 + len(arrays)),
         out_specs=(VMEM, VMEM),
         scratch_shapes=[pltpu.VMEM((LANES, width), jnp.float32)],
         compiler_params=PARAMS,
-        name=name,
-    )(total, stiff, *arrays)
-
-
-def finish(result, parts, slot, rows, width):
-    flat = [array for pair in parts for array in pair]
+        name="last_chunks",
+    )(total, *arrays)
+
+
+def finish(result, stiff, product, chain):
+    rows, width = product.shape
     given = [] if result is None else [result]
 
     def kernel(*refs):
-        ins = refs[len(given) : -3]
-        out_hbm, buf, sem = refs[-3:]
-        first = 0
-        for k in range(0, len(ins), 2):
-            columns = pl.ds(first, ins[k].shape[1])
-            buf[:, columns] = ins[k][...] - ins[k + 1][...]
-            first += ins[k].shape[1]
+        stiff_ref, product_ref, out_hbm, buf, sem = refs[len(given) :]
+        slot = slot_of(chain)
+        buf[...] = stiff_ref[slot] - product_ref[...]
         copy = pltpu.make_async_copy(buf, out_hbm.at[slot], sem)
         copy.start()
         copy.wait()
@@ -288,13 +286,13 @@
     return pl.pallas_call(
         kernel,
         out_shape=jax.ShapeDtypeStruct((OWN, rows, width), jnp.float32),
-        in_specs=[HBM] * len(given) + [VMEM] * len(flat),
+        in_specs=[HBM] * len(given) + [VMEM, VMEM],
         out_specs=HBM,
         scratch_shapes=[pltpu.VMEM((rows, width), jnp.float32), pltpu.SemaphoreType.DMA],
         input_output_aliases={0: 0} if given else {},
         compiler_params=PARAMS,
-        name=f"finish_{slot}",
-    )(*given, *flat)
+        name=f"finish_{chain}",
+    )(*given, stiff, product)
 
 
 def shifted(array, axis, distance):
@@ -306,72 +304,51 @@
     return lax.ppermute(array, axis, [(i, i ^ 1) for i in range(lax.axis_size(axis))])
 
 
-def up(array):
-    return shifted(array, "tile_1", 1)
-
-
-def down(array):
-    return shifted(array, "tile_1", -1)
+def crossed(array, distance):
+    size = lax.axis_size("tile_1")
+    pairs = [(x * size + z, (1 - x) * size + (z + distance) % size) for x in range(2) for z in range(size)]
+    return lax.ppermute(array, TILE, pairs)
 
 
 def body(coupling, interior_solve, boundary_stiffness, migration):
     home, depth, width = interior_solve.shape
-    rows = boundary_stiffness.shape[1]
     blocks = width // LANES
-    half = blocks // 2
     pieces = jnp.swapaxes(coupling, 1, 2)
     in_hbm = [pltpu.with_memory_space_constraint(a, pltpu.HBM) for a in (migration, pieces, interior_solve)]
     outgoing = pack(*in_hbm, True)
     arrived = [swapped(outgoing[0], "group"), swapped(outgoing[1], "group")]
     local = pack(*in_hbm, False)
-    up0, down0, own0 = merge(migration, arrived[0], local[0], 0, home)
-    up1, down1, own1 = merge(migration, arrived[1], local[1], 1, home)
+    ups, downs, owns = [None, None], [None, None], [None, None]
+    for chain in range(2):
+        ups[chain], downs[chain], owns[chain] = merge(migration, arrived[chain], local[chain], chain, home)
     stiff_arrived = swapped(stiff_out(migration, boundary_stiffness), "group")
     stiff = stiff_merge(migration, boundary_stiffness, stiff_arrived)
 
     def run(first):
         return list(range(first, first + blocks))
 
-    turned = list(range(half, blocks)) + list(range(half))
-    u0, d0, u1, d1 = up(up0), down(down0), up(up1), down(down1)
-    total0 = accumulate(None, [(up0, run(3), own0, None)], width, "chunks_0")
-    total1 = accumulate(None, [(up1, run(4), own1, None)], width, "chunks_1")
-    uu0, dd0 = up(u0[1:]), down(d0[:-1])
-    total0 = accumulate(total0, [(u0, run(3), u0, 0), (d0, run(0), d0, blocks + 3)], width, "chunks_0")
-    uu1, dd1 = up(u1[1:]), down(d1[:-1])
-    total1 = accumulate(total1, [(u1, run(4), u1, 0), (d1, turned, d1, blocks + 2)], width, "chunks_1")
-    uuu0, ddd0 = up(uu0[1:]), down(dd0[:-1])
-    total0 = accumulate(total0, [(uu0, run(2), uu0, 0), (dd0, run(0), dd0, blocks + 2)], width, "chunks_0")
-    uuu1a, ddd1a = up(uu1[1 : half + 3]), down(dd1[half : blocks + 1])
-    total1 = accumulate(total1, [(uu1, run(3), uu1, 0), (dd1, turned, dd1, blocks + 1)], width, "chunks_1")
-    far0a, far0b = up(uuu0[1 : half + 1]), down(ddd0[half : blocks + 1])
-    total0 = accumulate(total0, [(uuu0, run(1), uuu0, 0), (ddd0, run(0), ddd0, blocks + 1)], width, "chunks_0")
-    uuu1b, ddd1b = up(uu1[half + 3 :]), down(dd1[:half])
-    far1a, far1b = up(uuu1a[1:]), down(ddd1b)
-    left, right = list(range(half)), list(range(half, blocks))
-    wide = width // 2
-    send0a, keep0a = last_chunks(
-        total0, [(far0a, left, far0b, half)], stiff, 0, 0, wide, "last_0a"
-    )
-    send0b, keep0b = last_chunks(
-        total0, [(far0b, left, far0b, half)], stiff, 0, wide, wide, "last_0b"
-    )
-    del right
-    other0a, other0b = swapped(send0a, "tile_0"), swapped(send0b, "tile_0")
-    send1a, keep1a = last_chunks(
-        total1,
-        [(uuu1a, run(2)[:half], uuu1a, 0), (ddd1a, left, ddd1a, half), (far1a, run(1)[:half], far1a, 0)],
-        stiff, 1, 0, wide, "last_1a",
-    )
-    other1a = swapped(send1a, "tile_0")
-    send1b, keep1b = last_chunks(
-        total1,
-        [(uuu1b, left, uuu1a, 0), (ddd1b, left, ddd1a, half), (far1b, left, far1a, 0)],
-        stiff, 1, wide, wide, "last_1b",
-    )
-    other1b = swapped(send1b, "tile_0")
-    result = finish(None, [(keep0a, other0a), (keep0b, other0b)], 0, rows, width)
-    return finish(result, [(keep1a, other1a), (keep1b, other1b)], 1, rows, width)
+    crossed_own = crossed(owns[1], 0)
+    sources = [(ups[0], run(hops(0)[0]), owns[0], 0)]
+    total = None
+    for step in range(1, 4):
+        for chain in range(2):
+            if step == 1 and chain == 1:
+                ups[chain], downs[chain] = crossed(ups[chain], 1), crossed(downs[chain], -1)
+            else:
+                sent_up = ups[chain] if step == 1 else ups[chain][1:]
+                sent_down = downs[chain] if step == 1 else downs[chain][:-1]
+                ups[chain], downs[chain] = shifted(sent_up, "tile_1", 1), shifted(sent_down, "tile_1", -1)
+        total = accumulate(total, sources, width, f"chunks_{step}")
+        sources = [] if step > 1 else [(crossed_own, run(0), crossed_own, blocks)]
+        for chain in range(2):
+            left_up, left_down = hops(chain)[0] - step, hops(chain)[1] - step
+            sources.append((ups[chain], run(left_up + 1), ups[chain], 0))
+            sources.append((downs[chain], run(0), downs[chain], blocks + left_down))
+    far0, far1 = shifted(ups[0][1:], "tile_1", 1), shifted(downs[1][:-1], "tile_1", -1)
+    total = accumulate(total, sources, width, "chunks_4")
+    send, keep = last_chunks(total, [(far0, run(1), far0, 0), (far1, run(0), far1, blocks)])
+    other = swapped(send, "tile_0")
+    return finish(finish(None, stiff, keep, 0), stiff, other, 1)
 
 
 def solution(mesh):

time: 73.4 us -> 61.8 us (0.84)
  waiting for transfers between devices: 27 us -> 15.2 us
  starting transfers between devices: 34.6 us -> 36 us
  Pallas kernels: 10.3 us -> 9 us
    ppermute x18 -> x12, waiting for transfers between devices: 22.7 us -> 8.62 us  [shifted(): lax.ppermute(array, axis, [(i, (i + distance) % size) for i in range(size)])]
    ppermute x0 -> x3, starting transfers between devices: none -> 5.93 us  [crossed(): return lax.ppermute(array, TILE, pairs)]
    ppermute x7 -> x4, starting transfers between devices: 5.08 us -> 1.3 us  [swapped(): lax.ppermute(array, axis, [(i, i ^ 1) for i in range(lax.axis_size(axis))])]
    ppermute x0 -> x3, waiting for transfers between devices: none -> 2.09 us  [crossed(): return lax.ppermute(array, TILE, pairs)]
    pallas_call x4 -> x1, Pallas kernels: 1.21 us -> 0.4 us  [last_chunks(): pl.pallas_call(kernel, out_shape=(half, half), in_specs=[VMEM] * (1 + len...]
    ppermute x18 -> x12, starting transfers between devices: 29.5 us -> 28.8 us  [shifted(): lax.ppermute(array, axis, [(i, (i + distance) % size) for i in range(size)])]
    pallas_call x7 -> x4, Pallas kernels: 2.33 us -> 1.81 us  [accumulate(): pl.pallas_call(kernel, out_shape=jax.ShapeDtypeStruct((LANES, width), jnp...]
    ppermute x7 -> x4, waiting for transfers between devices: 4.31 us -> 4.46 us  [swapped(): lax.ppermute(array, axis, [(i, i ^ 1) for i in range(lax.axis_size(axis))])]
  transfers between devices with their start and end apart: 25 -> 19, of which waited for: 8 -> 10; matrix products, arithmetic and copies ran while one was open for 0% -> 0% of each run, Pallas kernels for 11% -> 11%
where the time goes in v3:
time: 61.8 us; the launch traced here: 61.4 us
  starting transfers between devices  36 us (58%)
  waiting for transfers between devices  15.2 us (25%)
  Pallas kernels  9 us (15%)
  local copies, waits for them, and re-layouts  0.81 us (1%)
    ppermute x12, starting transfers between devices, shifted(): lax.ppermute(array, axis, [(i, (i + distance) % size) for i in range(size)])  28.8 us
    ppermute x12, waiting for transfers between devices, shifted(): lax.ppermute(array, axis, [(i, (i + distance) % size) for i in range(size)])  8.62 us
    ppermute x3, starting transfers between devices, crossed(): return lax.ppermute(array, TILE, pairs)  5.93 us
    ppermute x4, waiting for transfers between devices, swapped(): lax.ppermute(array, axis, [(i, i ^ 1) for i in range(lax.axis_size(axis))])  4.46 us
    pallas_call x2, Pallas kernels, pack(): pl.pallas_call(kernel, out_shape=(packet, packet), in_specs=[HBM] * 3, ou...  2.85 us
    ppermute x3, waiting for transfers between devices, crossed(): return lax.ppermute(array, TILE, pairs)  2.09 us
    pallas_call x4, Pallas kernels, accumulate(): pl.pallas_call(kernel, out_shape=jax.ShapeDtypeStruct((LANES, width), jnp...  1.81 us
    pallas_call x2, Pallas kernels, finish(): pl.pallas_call(kernel, out_shape=jax.ShapeDtypeStruct((OWN, rows, width),...  1.48 us
  transfers between devices with their start and end apart: 19, of which 10 were waited for; matrix products, arithmetic and copies ran while one was open for 0% of the time, Pallas kernels for 11%

profile of v3, /device:TPU:24, one launch (start us, length us, event | category | flops | bytes accessed | tf_op | source)
XLA Modules:
  0.0 61.4 jit_solution(16931285596844055284)
XLA Ops:
  0.0 1.4 %pack_partner.1 = (f32[16,48,128]{2,1,0:T(8,128)S(1)}, f32[16,48,128]{2,1,0:T(8,128)S(1)}) custom-call(s32[64]{0:T(128)} %plan_ref.7, f32[4,48,1024]{2,1,0:T(8,128)} %bitcast.1, f32[4,48,1024]{2,1,0:T(8,128)} %x_hbm.3), custom_call_target="tpu_custom_call" | custom-call | tf_op jit(solution)/shard_map/pack_partner/pallas_call | solution.py:74
  1.4 0.1 collective-permute-start.1
  1.5 0.5 collective-permute-start.2
  2.0 1.4 %pack_own.1 = (f32[16,48,128]{2,1,0:T(8,128)S(1)}, f32[16,48,128]{2,1,0:T(8,128)S(1)}) custom-call(s32[64]{0:T(128)} %plan_ref.7, f32[4,48,1024]{2,1,0:T(8,128)} %bitcast.2, f32[4,48,1024]{2,1,0:T(8,128)} %x_hbm.3), custom_call_target="tpu_custom_call" | custom-call | tf_op jit(solution)/shard_map/pack_own/pallas_call | solution.py:74
  3.5 0.0 copy-start.1
  3.5 0.0 collective-permute-done.1.arrived_ref
  3.5 0.6 %copy-done.1 = s32[64]{0:T(128)S(1)} copy-done((s32[64]{0:T(128)S(1)}, s32[64]{0:T(128)}, u32[]{:S(2)}) %copy-start.1) | copy-done | bytes 280
  4.1 0.6 merge_0.1
  4.7 2.0 %collective-permute-start.4 = (f32[12,48,128]{2,1,0:T(8,128)S(1)}, f32[12,48,128]{2,1,0:T(8,128)S(1)}, u32[]{:S(2)}, u32[]{:S(2)}) collective-permute-start(f32[12,48,128]{2,1,0:T(8,128)S(1)} %get-tuple-element.19.refs_0_), channel_id=1, source_target_pairs={{0,1},{1,2},{2,3},{3,4},{4,5},{5,6},{6,7},{7,0},{8,9},{9,10},{10,1... | collective-permute-start | bytes 884744 | tf_op jit(solution)/shard_map/ppermute | solution.py:300
  6.7 0.0 collective-permute-done.2.arrived_ref
  6.7 0.6 merge_1.1
  7.3 5.0 %collective-permute-start.7 = (f32[12,48,128]{2,1,0:T(8,128)S(1)}, f32[12,48,128]{2,1,0:T(8,128)S(1)}, u32[]{:S(2)}, u32[]{:S(2)}) collective-permute-start(f32[12,48,128]{2,1,0:T(8,128)S(1)} %get-tuple-element.26), channel_id=1, source_target_pairs={{0,15},{1,8},{2,9},{3,10},{4,11},{5,12},{6,13},{7,14},{8,7},{9,0},... | collective-permute-start | bytes 884744 | tf_op jit(solution)/shard_map/ppermute | solution.py:310
  12.3 0.0 collective-permute-start.6
  12.3 3.2 %collective-permute-start.5 = (f32[11,48,128]{2,1,0:T(8,128)S(1)}, f32[11,48,128]{2,1,0:T(8,128)S(1)}, u32[]{:S(2)}, u32[]{:S(2)}) collective-permute-start(f32[11,48,128]{2,1,0:T(8,128)S(1)} %get-tuple-element.24), channel_id=1, source_target_pairs={{0,7},{1,0},{2,1},{3,2},{4,3},{5,4},{6,5},{7,6},{8,15},{9,8},{10,9... | collective-permute-start | bytes 811016 | tf_op jit(solution)/shard_map/ppermute | solution.py:300
  15.5 2.9 %collective-permute-done.4.refs_2_ = f32[12,48,128]{2,1,0:T(8,128)S(1)} collective-permute-done((f32[12,48,128]{2,1,0:T(8,128)S(1)}, f32[12,48,128]{2,1,0:T(8,128)S(1)}, u32[]{:S(2)}, u32[]{:S(2)}) %collective-permute-start.4) | collective-permute-done | bytes 294944 | tf_op jit(solution)/shard_map/ppermute | solution.py:300
  18.5 0.1 collective-permute-start.8
  18.6 1.4 %collective-permute-done.7.refs_5_ = f32[12,48,128]{2,1,0:T(8,128)S(1)} collective-permute-done((f32[12,48,128]{2,1,0:T(8,128)S(1)}, f32[12,48,128]{2,1,0:T(8,128)S(1)}, u32[]{:S(2)}, u32[]{:S(2)}) %collective-permute-start.7) | collective-permute-done | bytes 294944 | tf_op jit(solution)/shard_map/ppermute | solution.py:310
  20.0 0.0 copy-start
  20.0 4.5 %collective-permute-start.11 = (f32[11,48,128]{2,1,0:T(8,128)S(1)}, f32[11,48,128]{2,1,0:T(8,128)S(1)}, u32[]{:S(2)}, u32[]{:S(2)}) collective-permute-start(f32[11,48,128]{2,1,0:T(8,128)S(1)} %slice.43), channel_id=1, source_target_pairs={{0,7},{1,0},{2,1},{3,2},{4,3},{5,4},{6,5},{7,6},{8,15},{9,8},{10,9... | collective-permute-start | bytes 811016 | tf_op jit(solution)/shard_map/ppermute | solution.py:300
  24.5 0.7 %collective-permute-done.6.refs_4_ = f32[11,48,128]{2,1,0:T(8,128)S(1)} collective-permute-done((f32[11,48,128]{2,1,0:T(8,128)S(1)}, f32[11,48,128]{2,1,0:T(8,128)S(1)}, u32[]{:S(2)}, u32[]{:S(2)}) %collective-permute-start.6) | collective-permute-done | bytes 270368 | tf_op jit(solution)/shard_map/ppermute | solution.py:310
  25.2 0.7 %collective-permute-start.10 = (f32[10,48,128]{2,1,0:T(8,128)S(1)}, f32[10,48,128]{2,1,0:T(8,128)S(1)}, u32[]{:S(2)}, u32[]{:S(2)}) collective-permute-start(f32[10,48,128]{2,1,0:T(8,128)S(1)} %slice.42), channel_id=1, source_target_pairs={{0,1},{1,2},{2,3},{3,4},{4,5},{5,6},{6,7},{7,0},{8,9},{9,10},{10,1... | collective-permute-start | bytes 737288 | tf_op jit(solution)/shard_map/ppermute | solution.py:300
  25.9 0.0 collective-permute-done.5.refs_3_
  25.9 3.7 %collective-permute-start.9 = (f32[10,48,128]{2,1,0:T(8,128)S(1)}, f32[10,48,128]{2,1,0:T(8,128)S(1)}, u32[]{:S(2)}, u32[]{:S(2)}) collective-permute-start(f32[10,48,128]{2,1,0:T(8,128)S(1)} %slice.41), channel_id=1, source_target_pairs={{0,7},{1,0},{2,1},{3,2},{4,3},{5,4},{6,5},{7,6},{8,15},{9,8},{10,9... | collective-permute-start | bytes 737288 | tf_op jit(solution)/shard_map/ppermute | solution.py:300
  29.6 0.5 collective-permute-done.8.refs_1_
  30.1 1.2 %collective-permute-start.12 = (f32[10,48,128]{2,1,0:T(8,128)S(1)}, f32[10,48,128]{2,1,0:T(8,128)S(1)}, u32[]{:S(2)}, u32[]{:S(2)}) collective-permute-start(f32[10,48,128]{2,1,0:T(8,128)S(1)} %slice.44), channel_id=1, source_target_pairs={{0,1},{1,2},{2,3},{3,4},{4,5},{5,6},{6,7},{7,0},{8,9},{9,10},{10,1... | collective-permute-start | bytes 737288 | tf_op jit(solution)/shard_map/ppermute | solution.py:300
  31.3 0.3 collective-permute-done.11.refs_4_
  31.6 3.8 %collective-permute-start.15 = (f32[10,48,128]{2,1,0:T(8,128)S(1)}, f32[10,48,128]{2,1,0:T(8,128)S(1)}, u32[]{:S(2)}, u32[]{:S(2)}) collective-permute-start(f32[10,48,128]{2,1,0:T(8,128)S(1)} %slice.47), channel_id=1, source_target_pairs={{0,7},{1,0},{2,1},{3,2},{4,3},{5,4},{6,5},{7,6},{8,15},{9,8},{10,9... | collective-permute-start | bytes 737288 | tf_op jit(solution)/shard_map/ppermute | solution.py:300
  35.3 1.0 %collective-permute-start.3 = (f32[9,48,128]{2,1,0:T(8,128)S(1)}, f32[9,48,128]{2,1,0:T(8,128)S(1)}, u32[]{:S(2)}, u32[]{:S(2)}) collective-permute-start(f32[9,48,128]{2,1,0:T(8,128)S(1)} %get-tuple-element.23), channel_id=1, source_target_pairs={{0,8},{1,9},{2,10},{3,11},{4,12},{5,13},{6,14},{7,15},{8,0},{9,1},... | collective-permute-start | bytes 663560 | tf_op jit(solution)/shard_map/ppermute | solution.py:310
  36.3 0.0 copy-done
  36.3 0.6 %stiff_out.1 = f32[2,64,1024]{2,1,0:T(8,128)S(1)} custom-call(s32[64]{0:T(128)S(1)} %copy-done.1, f32[4,64,1024]{2,1,0:T(8,128)S(1)} %copy-done), custom_call_target="tpu_custom_call" | custom-call | tf_op jit(solution)/shard_map/stiff_out/pallas_call | solution.py:146
  36.9 0.0 collective-permute-done.10.refs_3_
  37.0 0.1 collective-permute-start
  37.1 0.0 collective-permute-done.9.refs_2_
  37.1 0.9 %collective-permute-start.14 = (f32[9,48,128]{2,1,0:T(8,128)S(1)}, f32[9,48,128]{2,1,0:T(8,128)S(1)}, u32[]{:S(2)}, u32[]{:S(2)}) collective-permute-start(f32[9,48,128]{2,1,0:T(8,128)S(1)} %slice.46), channel_id=1, source_target_pairs={{0,1},{1,2},{2,3},{3,4},{4,5},{5,6},{6,7},{7,0},{8,9},{9,10},{10,1... | collective-permute-start | bytes 663560 | tf_op jit(solution)/shard_map/ppermute | solution.py:300
  38.0 2.0 %collective-permute-done.12.refs_1_ = f32[10,48,128]{2,1,0:T(8,128)S(1)} collective-permute-done((f32[10,48,128]{2,1,0:T(8,128)S(1)}, f32[10,48,128]{2,1,0:T(8,128)S(1)}, u32[]{:S(2)}, u32[]{:S(2)}) %collective-permute-start.12) | collective-permute-done | bytes 245792 | tf_op jit(solution)/shard_map/ppermute | solution.py:300
  40.1 5.4 %collective-permute-start.13 = (f32[9,48,128]{2,1,0:T(8,128)S(1)}, f32[9,48,128]{2,1,0:T(8,128)S(1)}, u32[]{:S(2)}, u32[]{:S(2)}) collective-permute-start(f32[9,48,128]{2,1,0:T(8,128)S(1)} %slice.45), channel_id=1, source_target_pairs={{0,7},{1,0},{2,1},{3,2},{4,3},{5,4},{6,5},{7,6},{8,15},{9,8},{10,9... | collective-permute-start | bytes 663560 | tf_op jit(solution)/shard_map/ppermute | solution.py:300
  45.5 0.0 collective-permute-done.15.refs_4_
  45.5 0.1 collective-permute-start.16
  45.6 0.0 collective-permute-done.3.refs_1_
  45.6 3.3 %collective-permute-start.17 = (f32[9,48,128]{2,1,0:T(8,128)S(1)}, f32[9,48,128]{2,1,0:T(8,128)S(1)}, u32[]{:S(2)}, u32[]{:S(2)}) collective-permute-start(f32[9,48,128]{2,1,0:T(8,128)S(1)} %slice.49), channel_id=1, source_target_pairs={{0,7},{1,0},{2,1},{3,2},{4,3},{5,4},{6,5},{7,6},{8,15},{9,8},{10,9... | collective-permute-start | bytes 663560 | tf_op jit(solution)/shard_map/ppermute | solution.py:300
  48.9 0.3 chunks_1.1.refs_0_
  49.2 0.6 chunks_2.1.refs_0_
  49.7 0.5 chunks_3.1.refs_0_
  50.2 0.0 collective-permute-done.14.refs_3_
  50.2 0.7 %collective-permute-done.13.refs_2_ = f32[9,48,128]{2,1,0:T(8,128)S(1)} collective-permute-done((f32[9,48,128]{2,1,0:T(8,128)S(1)}, f32[9,48,128]{2,1,0:T(8,128)S(1)}, u32[]{:S(2)}, u32[]{:S(2)}) %collective-permute-start.13) | collective-permute-done | bytes 221216 | tf_op jit(solution)/shard_map/ppermute | solution.py:300
  50.9 0.5 chunks_4.1.total_ref
  51.4 1.3 %collective-permute-done.16.refs_0_ = f32[9,48,128]{2,1,0:T(8,128)S(1)} collective-permute-done((f32[9,48,128]{2,1,0:T(8,128)S(1)}, f32[9,48,128]{2,1,0:T(8,128)S(1)}, u32[]{:S(2)}, u32[]{:S(2)}) %collective-permute-start.16) | collective-permute-done | bytes 221216 | tf_op jit(solution)/shard_map/ppermute | solution.py:300
  52.7 0.9 %collective-permute-done.17.refs_1_ = f32[9,48,128]{2,1,0:T(8,128)S(1)} collective-permute-done((f32[9,48,128]{2,1,0:T(8,128)S(1)}, f32[9,48,128]{2,1,0:T(8,128)S(1)}, u32[]{:S(2)}, u32[]{:S(2)}) %collective-permute-start.17) | collective-permute-done | bytes 221216 | tf_op jit(solution)/shard_map/ppermute | solution.py:300
  53.6 0.4 last_chunks.1
  54.0 0.6 %collective-permute-start.18 = (f32[64,1024]{1,0:T(8,128)S(1)}, f32[64,1024]{1,0:T(8,128)S(1)}, u32[]{:S(2)}, u32[]{:S(2)}) collective-permute-start(f32[64,1024]{1,0:T(8,128)S(1)} %get-tuple-element.28), channel_id=1, source_target_pairs={{0,8},{8,0},{1,9},{9,1},{2,10},{10,2},{3,11},{11,3},{4,12},{12,4},... | collective-permute-start | bytes 786440 | tf_op jit(solution)/shard_map/ppermute | solution.py:304
  54.7 0.0 collective-permute-done.arrived_ref
  54.7 0.6 %stiff_merge.1.refs_0_.refs_1_ = f32[2,64,1024]{2,1,0:T(8,128)S(1)} custom-call(s32[64]{0:T(128)S(1)} %copy-done.1, f32[4,64,1024]{2,1,0:T(8,128)S(1)} %copy-done, f32[2,64,1024]{2,1,0:T(8,128)S(1)} %collective-permute-done.arrived_ref), custom_call_target="tpu_custom_call" | custom-call | tf_op jit(solution)/shard_map/stiff_merge/pallas_call | solution.py:175
  55.3 0.7 %finish_0.1.refs_0_ = f32[2,64,1024]{2,1,0:T(8,128)} custom-call(f32[2,64,1024]{2,1,0:T(8,128)S(1)} %stiff_merge.1.refs_0_.refs_1_, f32[64,1024]{1,0:T(8,128)S(1)} %get-tuple-element.27.refs_1_), custom_call_target="tpu_custom_call" | custom-call | tf_op jit(solution)/shard_map/finish_0/pallas_call | solution.py:286
  56.1 4.4 %collective-permute-done.18.refs_2_ = f32[64,1024]{1,0:T(8,128)S(1)} collective-permute-done((f32[64,1024]{1,0:T(8,128)S(1)}, f32[64,1024]{1,0:T(8,128)S(1)}, u32[]{:S(2)}, u32[]{:S(2)}) %collective-permute-start.18) | collective-permute-done | bytes 262176 | tf_op jit(solution)/shard_map/ppermute | solution.py:304
  60.5 0.7 %finish_1.1 = f32[2,64,1024]{2,1,0:T(8,128)} custom-call(f32[2,64,1024]{2,1,0:T(8,128)} %finish_0.1.refs_0_, f32[2,64,1024]{2,1,0:T(8,128)S(1)} %stiff_merge.1.refs_0_.refs_1_, f32[64,1024]{1,0:T(8,128)S(1)} %collective-permute-done.18.refs_2_), custom_call_target="tpu_custom_call", output_to_operand_aliasing={{}: (0, {})} | custom-call | tf_op jit(solution)/shard_map/finish_1/pallas_call | solution.py:286
  (10 shorter events, 0.2 us)
Async XLA Ops:
  1.4 2.0 %collective-permute-start.1 = (f32[16,48,128]{2,1,0:T(8,128)S(1)}, f32[16,48,128]{2,1,0:T(8,128)S(1)}, u32[]{:S(2)}, u32[]{:S(2)}) collective-permute-start(f32[16,48,128]{2,1,0:T(8,128)S(1)} %get-tuple-element.17), channel_id=1, source_target_pairs={{0,16},{16,0},{32,48},{48,32},{64,80},{80,64},{96,112},{112,96},{1... | collective-permute-start | bytes 1179656 | tf_op jit(solution)/shard_map/ppermute | solution.py:304
  1.5 5.2 %collective-permute-start.2 = (f32[16,48,128]{2,1,0:T(8,128)S(1)}, f32[16,48,128]{2,1,0:T(8,128)S(1)}, u32[]{:S(2)}, u32[]{:S(2)}) collective-permute-start(f32[16,48,128]{2,1,0:T(8,128)S(1)} %get-tuple-element.21), channel_id=1, source_target_pairs={{0,16},{16,0},{32,48},{48,32},{64,80},{80,64},{96,112},{112,96},{1... | collective-permute-start | bytes 1179656 | tf_op jit(solution)/shard_map/ppermute | solution.py:304
  3.5 0.7 %copy-start.1 = (s32[64]{0:T(128)S(1)}, s32[64]{0:T(128)}, u32[]{:S(2)}) copy-start(s32[64]{0:T(128)} %plan_ref.7) | copy-start | bytes 772
  4.7 13.7 %collective-permute-start.4 = (f32[12,48,128]{2,1,0:T(8,128)S(1)}, f32[12,48,128]{2,1,0:T(8,128)S(1)}, u32[]{:S(2)}, u32[]{:S(2)}) collective-permute-start(f32[12,48,128]{2,1,0:T(8,128)S(1)} %get-tuple-element.19.refs_0_), channel_id=1, source_target_pairs={{0,1},{1,2},{2,3},{3,4},{4,5},{5,6},{6,7},{7,0},{8,9},{9,10},{10,1... | collective-permute-start | bytes 884744 | tf_op jit(solution)/shard_map/ppermute | solution.py:300
  7.3 12.6 %collective-permute-start.7 = (f32[12,48,128]{2,1,0:T(8,128)S(1)}, f32[12,48,128]{2,1,0:T(8,128)S(1)}, u32[]{:S(2)}, u32[]{:S(2)}) collective-permute-start(f32[12,48,128]{2,1,0:T(8,128)S(1)} %get-tuple-element.26), channel_id=1, source_target_pairs={{0,15},{1,8},{2,9},{3,10},{4,11},{5,12},{6,13},{7,14},{8,7},{9,0},... | collective-permute-start | bytes 884744 | tf_op jit(solution)/shard_map/ppermute | solution.py:310
  12.3 12.9 %collective-permute-start.6 = (f32[11,48,128]{2,1,0:T(8,128)S(1)}, f32[11,48,128]{2,1,0:T(8,128)S(1)}, u32[]{:S(2)}, u32[]{:S(2)}) collective-permute-start(f32[11,48,128]{2,1,0:T(8,128)S(1)} %get-tuple-element.25), channel_id=1, source_target_pairs={{0,9},{1,10},{2,11},{3,12},{4,13},{5,14},{6,15},{7,8},{8,1},{9,2},... | collective-permute-start | bytes 811016 | tf_op jit(solution)/shard_map/ppermute | solution.py:310
  12.3 13.5 %collective-permute-start.5 = (f32[11,48,128]{2,1,0:T(8,128)S(1)}, f32[11,48,128]{2,1,0:T(8,128)S(1)}, u32[]{:S(2)}, u32[]{:S(2)}) collective-permute-start(f32[11,48,128]{2,1,0:T(8,128)S(1)} %get-tuple-element.24), channel_id=1, source_target_pairs={{0,7},{1,0},{2,1},{3,2},{4,3},{5,4},{6,5},{7,6},{8,15},{9,8},{10,9... | collective-permute-start | bytes 811016 | tf_op jit(solution)/shard_map/ppermute | solution.py:300
  18.5 11.6 %collective-permute-start.8 = (f32[11,48,128]{2,1,0:T(8,128)S(1)}, f32[11,48,128]{2,1,0:T(8,128)S(1)}, u32[]{:S(2)}, u32[]{:S(2)}) collective-permute-start(f32[11,48,128]{2,1,0:T(8,128)S(1)} %slice.40), channel_id=1, source_target_pairs={{0,1},{1,2},{2,3},{3,4},{4,5},{5,6},{6,7},{7,0},{8,9},{9,10},{10,1... | collective-permute-start | bytes 811016 | tf_op jit(solution)/shard_map/ppermute | solution.py:300
  20.0 16.3 %copy-start = (f32[4,64,1024]{2,1,0:T(8,128)S(1)}, f32[4,64,1024]{2,1,0:T(8,128)}, u32[]{:S(2)}) copy-start(f32[4,64,1024]{2,1,0:T(8,128)} %b_hbm.3) | copy-start | bytes 3145732
  20.0 11.6 %collective-permute-start.11 = (f32[11,48,128]{2,1,0:T(8,128)S(1)}, f32[11,48,128]{2,1,0:T(8,128)S(1)}, u32[]{:S(2)}, u32[]{:S(2)}) collective-permute-start(f32[11,48,128]{2,1,0:T(8,128)S(1)} %slice.43), channel_id=1, source_target_pairs={{0,7},{1,0},{2,1},{3,2},{4,3},{5,4},{6,5},{7,6},{8,15},{9,8},{10,9... | collective-permute-start | bytes 811016 | tf_op jit(solution)/shard_map/ppermute | solution.py:300
  25.2 11.7 %collective-permute-start.10 = (f32[10,48,128]{2,1,0:T(8,128)S(1)}, f32[10,48,128]{2,1,0:T(8,128)S(1)}, u32[]{:S(2)}, u32[]{:S(2)}) collective-permute-start(f32[10,48,128]{2,1,0:T(8,128)S(1)} %slice.42), channel_id=1, source_target_pairs={{0,1},{1,2},{2,3},{3,4},{4,5},{5,6},{6,7},{7,0},{8,9},{9,10},{10,1... | collective-permute-start | bytes 737288 | tf_op jit(solution)/shard_map/ppermute | solution.py:300
  25.9 11.2 %collective-permute-start.9 = (f32[10,48,128]{2,1,0:T(8,128)S(1)}, f32[10,48,128]{2,1,0:T(8,128)S(1)}, u32[]{:S(2)}, u32[]{:S(2)}) collective-permute-start(f32[10,48,128]{2,1,0:T(8,128)S(1)} %slice.41), channel_id=1, source_target_pairs={{0,7},{1,0},{2,1},{3,2},{4,3},{5,4},{6,5},{7,6},{8,15},{9,8},{10,9... | collective-permute-start | bytes 737288 | tf_op jit(solution)/shard_map/ppermute | solution.py:300
  30.1 10.0 %collective-permute-start.12 = (f32[10,48,128]{2,1,0:T(8,128)S(1)}, f32[10,48,128]{2,1,0:T(8,128)S(1)}, u32[]{:S(2)}, u32[]{:S(2)}) collective-permute-start(f32[10,48,128]{2,1,0:T(8,128)S(1)} %slice.44), channel_id=1, source_target_pairs={{0,1},{1,2},{2,3},{3,4},{4,5},{5,6},{6,7},{7,0},{8,9},{9,10},{10,1... | collective-permute-start | bytes 737288 | tf_op jit(solution)/shard_map/ppermute | solution.py:300
  31.6 13.9 %collective-permute-start.15 = (f32[10,48,128]{2,1,0:T(8,128)S(1)}, f32[10,48,128]{2,1,0:T(8,128)S(1)}, u32[]{:S(2)}, u32[]{:S(2)}) collective-permute-start(f32[10,48,128]{2,1,0:T(8,128)S(1)} %slice.47), channel_id=1, source_target_pairs={{0,7},{1,0},{2,1},{3,2},{4,3},{5,4},{6,5},{7,6},{8,15},{9,8},{10,9... | collective-permute-start | bytes 737288 | tf_op jit(solution)/shard_map/ppermute | solution.py:300
  35.3 10.2 %collective-permute-start.3 = (f32[9,48,128]{2,1,0:T(8,128)S(1)}, f32[9,48,128]{2,1,0:T(8,128)S(1)}, u32[]{:S(2)}, u32[]{:S(2)}) collective-permute-start(f32[9,48,128]{2,1,0:T(8,128)S(1)} %get-tuple-element.23), channel_id=1, source_target_pairs={{0,8},{1,9},{2,10},{3,11},{4,12},{5,13},{6,14},{7,15},{8,0},{9,1},... | collective-permute-start | bytes 663560 | tf_op jit(solution)/shard_map/ppermute | solution.py:310
  37.0 17.7 %collective-permute-start = (f32[2,64,1024]{2,1,0:T(8,128)S(1)}, f32[2,64,1024]{2,1,0:T(8,128)S(1)}, u32[]{:S(2)}, u32[]{:S(2)}) collective-permute-start(f32[2,64,1024]{2,1,0:T(8,128)S(1)} %stiff_out.1), channel_id=1, source_target_pairs={{0,16},{16,0},{32,48},{48,32},{64,80},{80,64},{96,112},{112,96},{1... | collective-permute-start | bytes 1572872 | tf_op jit(solution)/shard_map/ppermute | solution.py:304
  37.1 13.1 %collective-permute-start.14 = (f32[9,48,128]{2,1,0:T(8,128)S(1)}, f32[9,48,128]{2,1,0:T(8,128)S(1)}, u32[]{:S(2)}, u32[]{:S(2)}) collective-permute-start(f32[9,48,128]{2,1,0:T(8,128)S(1)} %slice.46), channel_id=1, source_target_pairs={{0,1},{1,2},{2,3},{3,4},{4,5},{5,6},{6,7},{7,0},{8,9},{9,10},{10,1... | collective-permute-start | bytes 663560 | tf_op jit(solution)/shard_map/ppermute | solution.py:300
  40.1 10.9 %collective-permute-start.13 = (f32[9,48,128]{2,1,0:T(8,128)S(1)}, f32[9,48,128]{2,1,0:T(8,128)S(1)}, u32[]{:S(2)}, u32[]{:S(2)}) collective-permute-start(f32[9,48,128]{2,1,0:T(8,128)S(1)} %slice.45), channel_id=1, source_target_pairs={{0,7},{1,0},{2,1},{3,2},{4,3},{5,4},{6,5},{7,6},{8,15},{9,8},{10,9... | collective-permute-start | bytes 663560 | tf_op jit(solution)/shard_map/ppermute | solution.py:300
  45.5 7.2 %collective-permute-start.16 = (f32[9,48,128]{2,1,0:T(8,128)S(1)}, f32[9,48,128]{2,1,0:T(8,128)S(1)}, u32[]{:S(2)}, u32[]{:S(2)}) collective-permute-start(f32[9,48,128]{2,1,0:T(8,128)S(1)} %slice.48), channel_id=1, source_target_pairs={{0,1},{1,2},{2,3},{3,4},{4,5},{5,6},{6,7},{7,0},{8,9},{9,10},{10,1... | collective-permute-start | bytes 663560 | tf_op jit(solution)/shard_map/ppermute | solution.py:300
  45.6 8.0 %collective-permute-start.17 = (f32[9,48,128]{2,1,0:T(8,128)S(1)}, f32[9,48,128]{2,1,0:T(8,128)S(1)}, u32[]{:S(2)}, u32[]{:S(2)}) collective-permute-start(f32[9,48,128]{2,1,0:T(8,128)S(1)} %slice.49), channel_id=1, source_target_pairs={{0,7},{1,0},{2,1},{3,2},{4,3},{5,4},{6,5},{7,6},{8,15},{9,8},{10,9... | collective-permute-start | bytes 663560 | tf_op jit(solution)/shard_map/ppermute | solution.py:300
  54.0 6.5 %collective-permute-start.18 = (f32[64,1024]{1,0:T(8,128)S(1)}, f32[64,1024]{1,0:T(8,128)S(1)}, u32[]{:S(2)}, u32[]{:S(2)}) collective-permute-start(f32[64,1024]{1,0:T(8,128)S(1)} %get-tuple-element.28), channel_id=1, source_target_pairs={{0,8},{8,0},{1,9},{9,1},{2,10},{10,2},{3,11},{11,3},{4,12},{12,4},... | collective-permute-start | bytes 786440 | tf_op jit(solution)/shard_map/ppermute | solution.py:304

commit v4 on v3

--- a/solution.py
+++ b/solution.py
@@ -129,38 +129,50 @@
     )(plan, arrived, local)
 
 
-def stiff_out(plan, stiff):
+FIRST_ROWS = 16
+
+
+def stiff_out(plan, stiff, part):
     home, rows, width = stiff.shape
+    total = rows + FIRST_ROWS if part == 0 else rows - FIRST_ROWS
 
     def kernel(plan_ref, b_hbm, out_ref, sem):
         group = lax.axis_index("group")
-        copies = []
-        for slot in range(OWN):
-            position, _ = locate(plan_ref, group, jnp.bitwise_xor(group, 1) * OWN + slot, home)
-            copy = pltpu.make_async_copy(b_hbm.at[position], out_ref.at[slot], sem.at[slot])
+        partner = jnp.bitwise_xor(group, 1)
+        places = [locate(plan_ref, group, partner * OWN + slot, home)[0] for slot in range(OWN)]
+        if part == 0:
+            copies = [
+                pltpu.make_async_copy(b_hbm.at[places[0]], out_ref.at[pl.ds(0, rows)], sem.at[0]),
+                pltpu.make_async_copy(
+                    b_hbm.at[places[1], pl.ds(0, FIRST_ROWS)], out_ref.at[pl.ds(rows, FIRST_ROWS)], sem.at[1]
+                ),
+            ]
+        else:
+            copies = [pltpu.make_async_copy(b_hbm.at[places[1], pl.ds(FIRST_ROWS, total)], out_ref, sem.at[0])]
+        for copy in copies:
             copy.start()
-            copies.append(copy)
         for copy in copies:
             copy.wait()
 
     return pl.pallas_call(
         kernel,
-        out_shape=jax.ShapeDtypeStruct((OWN, rows, width), jnp.float32),
+        out_shape=jax.ShapeDtypeStruct((total, width), jnp.float32),
         in_specs=[SMEM, HBM],
         out_specs=VMEM,
-        scratch_shapes=[pltpu.SemaphoreType.DMA((OWN,))],
-        compiler_params=PARAMS,
-        name="stiff_out",
+        scratch_shapes=[pltpu.SemaphoreType.DMA((2,))],
+        compiler_params=PARAMS,
+        name=f"stiff_out_{part}",
     )(plan, stiff)
 
 
 def stiff_merge(plan, stiff, arrived):
     home, rows, width = stiff.shape
 
-    def kernel(plan_ref, b_hbm, arrived_ref, out_ref, sem):
+    def kernel(plan_ref, b_hbm, part0, part1, out_ref, sem):
         group = lax.axis_index("group")
+        places = [locate(plan_ref, group, group * OWN + slot, home) for slot in range(OWN)]
         for slot in range(OWN):
-            position, here = locate(plan_ref, group, group * OWN + slot, home)
+            position, here = places[slot]
 
             @pl.when(here)
             def _():
@@ -170,17 +182,21 @@
 
             @pl.when(jnp.logical_not(here))
             def _():
-                out_ref[slot] = arrived_ref[slot]
+                if slot == 0:
+                    out_ref[0] = part0[0:rows]
+                else:
+                    out_ref[1, 0:FIRST_ROWS] = part0[rows:]
+                    out_ref[1, FIRST_ROWS:] = part1[...]
 
     return pl.pallas_call(
         kernel,
         out_shape=jax.ShapeDtypeStruct((OWN, rows, width), jnp.float32),
-        in_specs=[SMEM, HBM, VMEM],
+        in_specs=[SMEM, HBM, VMEM, VMEM],
         out_specs=VMEM,
         scratch_shapes=[pltpu.SemaphoreType.DMA((OWN,))],
         compiler_params=PARAMS,
         name="stiff_merge",
-    )(plan, stiff, arrived)
+    )(plan, stiff, *arrived)
 
 
 def split(value):
@@ -310,6 +326,10 @@
     return lax.ppermute(array, TILE, pairs)
 
 
+def after(array, *earlier):
+    return lax.optimization_barrier((array, *earlier))[0]
+
+
 def body(coupling, interior_solve, boundary_stiffness, migration):
     home, depth, width = interior_solve.shape
     blocks = width // LANES
@@ -318,35 +338,42 @@
     outgoing = pack(*in_hbm, True)
     arrived = [swapped(outgoing[0], "group"), swapped(outgoing[1], "group")]
     local = pack(*in_hbm, False)
-    ups, downs, owns = [None, None], [None, None], [None, None]
-    for chain in range(2):
-        ups[chain], downs[chain], owns[chain] = merge(migration, arrived[chain], local[chain], chain, home)
-    stiff_arrived = swapped(stiff_out(migration, boundary_stiffness), "group")
-    stiff = stiff_merge(migration, boundary_stiffness, stiff_arrived)
+    up0, down0, own0 = merge(migration, arrived[0], local[0], 0, home)
+    up1, down1, own1 = merge(migration, after(arrived[1], up0), local[1], 1, home)
 
     def run(first):
         return list(range(first, first + blocks))
 
-    crossed_own = crossed(owns[1], 0)
-    sources = [(ups[0], run(hops(0)[0]), owns[0], 0)]
-    total = None
-    for step in range(1, 4):
-        for chain in range(2):
-            if step == 1 and chain == 1:
-                ups[chain], downs[chain] = crossed(ups[chain], 1), crossed(downs[chain], -1)
-            else:
-                sent_up = ups[chain] if step == 1 else ups[chain][1:]
-                sent_down = downs[chain] if step == 1 else downs[chain][:-1]
-                ups[chain], downs[chain] = shifted(sent_up, "tile_1", 1), shifted(sent_down, "tile_1", -1)
+    def onward(arrays, crossing):
+        sent = [None] * 4
+        for k in (3, 2, 1, 0):
+            if arrays[k] is not None:
+                distance = 1 if k % 2 == 0 else -1
+                sent[k] = crossed(arrays[k], distance) if crossing and k > 1 else shifted(arrays[k], "tile_1", distance)
+        return sent
+
+    came = onward([up0, down0, up1, down1], True)
+    stiff1 = swapped(stiff_out(migration, boundary_stiffness, 1), "group")
+    total = accumulate(None, [(up0, run(hops(0)[0]), own0, 0)], width, "chunks_1")
+    left = [hops(0)[0] - 1, hops(0)[1] - 1, hops(1)[0] - 1, hops(1)[1] - 1]
+    for step in range(2, 5):
+        sources, sent = [], []
+        for k in range(4):
+            upward = k % 2 == 0
+            sources.append((came[k], run(left[k] + 1) if upward else run(0), came[k], 0 if upward else blocks + left[k]))
+            sent.append((came[k][1:] if upward else came[k][:-1]) if left[k] else None)
+            left[k] -= 1
         total = accumulate(total, sources, width, f"chunks_{step}")
-        sources = [] if step > 1 else [(crossed_own, run(0), crossed_own, blocks)]
-        for chain in range(2):
-            left_up, left_down = hops(chain)[0] - step, hops(chain)[1] - step
-            sources.append((ups[chain], run(left_up + 1), ups[chain], 0))
-            sources.append((downs[chain], run(0), downs[chain], blocks + left_down))
-    far0, far1 = shifted(ups[0][1:], "tile_1", 1), shifted(downs[1][:-1], "tile_1", -1)
-    total = accumulate(total, sources, width, "chunks_4")
-    send, keep = last_chunks(total, [(far0, run(1), far0, 0), (far1, run(0), far1, blocks)])
+        if step == 4:
+            stiff0 = swapped(stiff_out(after(migration, came[1]), boundary_stiffness, 0), "group")
+            crossed_own = crossed(after(own1, came[2], stiff1), 0)
+        came = onward(sent, False)
+    stiff = stiff_merge(migration, boundary_stiffness, (stiff0, stiff1))
+    far0 = after(came[0], stiff0)
+    total = accumulate(total, [(far0, run(1), far0, 0)], width, "chunks_5")
+    send, keep = last_chunks(
+        total, [(crossed_own, run(0), crossed_own, blocks), (came[3], run(0), came[3], blocks)]
+    )
     other = swapped(send, "tile_0")
     return finish(finish(None, stiff, keep, 0), stiff, other, 1)
 

time: 61.8 us -> 65.5 us (1.060)
  waiting for transfers between devices: 15.2 us -> 20.4 us
  starting transfers between devices: 36 us -> 33.6 us
  Pallas kernels: 9 us -> 10.1 us
    ppermute x12, waiting for transfers between devices: 8.62 us -> 11.9 us  [shifted(): lax.ppermute(array, axis, [(i, (i + distance) % size) for i in range(size)])]
    ppermute x12, starting transfers between devices: 28.8 us -> 27.2 us  [shifted(): lax.ppermute(array, axis, [(i, (i + distance) % size) for i in range(size)])]
    ppermute x3, waiting for transfers between devices: 2.09 us -> 3.59 us  [crossed(): return lax.ppermute(array, TILE, pairs)]
    ppermute x3, starting transfers between devices: 5.93 us -> 4.73 us  [crossed(): return lax.ppermute(array, TILE, pairs)]
    pallas_call x1 -> x2, Pallas kernels: 0.62 us -> 1.52 us  [stiff_out(): pl.pallas_call(kernel, out_shape=jax.ShapeDtypeStruct((total, width), jnp...]
    ppermute x4 -> x5, waiting for transfers between devices: 4.46 us -> 4.84 us  [swapped(): lax.ppermute(array, axis, [(i, i ^ 1) for i in range(lax.axis_size(axis))])]
    ppermute x4 -> x5, starting transfers between devices: 1.3 us -> 1.68 us  [swapped(): lax.ppermute(array, axis, [(i, i ^ 1) for i in range(lax.axis_size(axis))])]
    pallas_call x4 -> x5, Pallas kernels: 1.81 us -> 2.03 us  [accumulate(): pl.pallas_call(kernel, out_shape=jax.ShapeDtypeStruct((LANES, width), jnp...]
  transfers between devices with their start and end apart: 19 -> 20, of which waited for: 10 -> 8; matrix products, arithmetic and copies ran while one was open for 0% -> 0% of each run, Pallas kernels for 11% -> 12%
where the time goes in v4:
time: 65.5 us; the launch traced here: 65.3 us
  starting transfers between devices  33.6 us (51%)
  waiting for transfers between devices  20.4 us (31%)
  Pallas kernels  10.1 us (15%)
  local copies, waits for them, and re-layouts  0.81 us (1%)
    ppermute x12, starting transfers between devices, shifted(): lax.ppermute(array, axis, [(i, (i + distance) % size) for i in range(size)])  27.2 us
    ppermute x12, waiting for transfers between devices, shifted(): lax.ppermute(array, axis, [(i, (i + distance) % size) for i in range(size)])  11.9 us
    ppermute x5, waiting for transfers between devices, swapped(): lax.ppermute(array, axis, [(i, i ^ 1) for i in range(lax.axis_size(axis))])  4.84 us
    ppermute x3, starting transfers between devices, crossed(): return lax.ppermute(array, TILE, pairs)  4.73 us
    ppermute x3, waiting for transfers between devices, crossed(): return lax.ppermute(array, TILE, pairs)  3.59 us
    pallas_call x2, Pallas kernels, pack(): pl.pallas_call(kernel, out_shape=(packet, packet), in_specs=[HBM] * 3, ou...  2.85 us
    pallas_call x5, Pallas kernels, accumulate(): pl.pallas_call(kernel, out_shape=jax.ShapeDtypeStruct((LANES, width), jnp...  2.03 us
    ppermute x5, starting transfers between devices, swapped(): lax.ppermute(array, axis, [(i, i ^ 1) for i in range(lax.axis_size(axis))])  1.68 us
  transfers between devices with their start and end apart: 20, of which 8 were waited for; matrix products, arithmetic and copies ran while one was open for 0% of the time, Pallas kernels for 12%

profile of v4, /device:TPU:24, one launch (start us, length us, event | category | flops | bytes accessed | tf_op | source)
XLA Modules:
  0.0 65.3 jit_solution(8511377031208029326)
XLA Ops:
  0.0 1.4 %pack_partner.1 = (f32[16,48,128]{2,1,0:T(8,128)S(1)}, f32[16,48,128]{2,1,0:T(8,128)S(1)}) custom-call(s32[64]{0:T(128)} %plan_ref.8, f32[4,48,1024]{2,1,0:T(8,128)} %bitcast.1, f32[4,48,1024]{2,1,0:T(8,128)} %x_hbm.3), custom_call_target="tpu_custom_call" | custom-call | tf_op jit(solution)/shard_map/pack_partner/pallas_call | solution.py:74
  1.4 0.1 collective-permute-start
  1.5 0.5 collective-permute-start.7
  2.0 1.4 %pack_own.1 = (f32[16,48,128]{2,1,0:T(8,128)S(1)}, f32[16,48,128]{2,1,0:T(8,128)S(1)}) custom-call(s32[64]{0:T(128)} %plan_ref.8, f32[4,48,1024]{2,1,0:T(8,128)} %bitcast.2, f32[4,48,1024]{2,1,0:T(8,128)} %x_hbm.3), custom_call_target="tpu_custom_call" | custom-call | tf_op jit(solution)/shard_map/pack_own/pallas_call | solution.py:74
  3.5 0.0 copy-start.1
  3.5 0.0 collective-permute-done.arrived_ref
  3.5 0.6 copy-done.1
  4.1 0.6 merge_0.1
  4.7 5.9 %collective-permute-start.1 = (f32[11,48,128]{2,1,0:T(8,128)S(1)}, f32[11,48,128]{2,1,0:T(8,128)S(1)}, u32[]{:S(2)}, u32[]{:S(2)}) collective-permute-start(f32[11,48,128]{2,1,0:T(8,128)S(1)} %get-tuple-element.23), channel_id=1, source_target_pairs={{0,7},{1,0},{2,1},{3,2},{4,3},{5,4},{6,5},{7,6},{8,15},{9,8},{10,9... | collective-permute-start | bytes 811016 | tf_op jit(solution)/shard_map/ppermute | solution.py:316
  10.7 0.0 collective-permute-start.6
  10.7 0.0 collective-permute-done.7.arrived_ref
  10.7 0.6 merge_1.1
  11.3 4.2 %collective-permute-start.9 = (f32[12,48,128]{2,1,0:T(8,128)S(1)}, f32[12,48,128]{2,1,0:T(8,128)S(1)}, u32[]{:S(2)}, u32[]{:S(2)}) collective-permute-start(f32[12,48,128]{2,1,0:T(8,128)S(1)} %get-tuple-element.31), channel_id=1, source_target_pairs={{0,15},{1,8},{2,9},{3,10},{4,11},{5,12},{6,13},{7,14},{8,7},{9,0},... | collective-permute-start | bytes 884744 | tf_op jit(solution)/shard_map/ppermute | solution.py:326
  15.5 0.0 collective-permute-start.8
  15.5 2.0 %collective-permute-done.1.refs_2_ = f32[11,48,128]{2,1,0:T(8,128)S(1)} collective-permute-done((f32[11,48,128]{2,1,0:T(8,128)S(1)}, f32[11,48,128]{2,1,0:T(8,128)S(1)}, u32[]{:S(2)}, u32[]{:S(2)}) %collective-permute-start.1) | collective-permute-done | bytes 270368 | tf_op jit(solution)/shard_map/ppermute | solution.py:316
  17.5 3.8 %collective-permute-start.2 = (f32[10,48,128]{2,1,0:T(8,128)S(1)}, f32[10,48,128]{2,1,0:T(8,128)S(1)}, u32[]{:S(2)}, u32[]{:S(2)}) collective-permute-start(f32[10,48,128]{2,1,0:T(8,128)S(1)} %slice.40), channel_id=1, source_target_pairs={{0,7},{1,0},{2,1},{3,2},{4,3},{5,4},{6,5},{7,6},{8,15},{9,8},{10,9... | collective-permute-start | bytes 737288 | tf_op jit(solution)/shard_map/ppermute | solution.py:316
  21.3 0.5 collective-permute-done.6.refs_1_
  21.8 0.1 collective-permute-start.10
  21.9 3.6 %collective-permute-done.9.refs_4_ = f32[12,48,128]{2,1,0:T(8,128)S(1)} collective-permute-done((f32[12,48,128]{2,1,0:T(8,128)S(1)}, f32[12,48,128]{2,1,0:T(8,128)S(1)}, u32[]{:S(2)}, u32[]{:S(2)}) %collective-permute-start.9) | collective-permute-done | bytes 294944 | tf_op jit(solution)/shard_map/ppermute | solution.py:326
  25.5 6.0 %collective-permute-start.12 = (f32[11,48,128]{2,1,0:T(8,128)S(1)}, f32[11,48,128]{2,1,0:T(8,128)S(1)}, u32[]{:S(2)}, u32[]{:S(2)}) collective-permute-start(f32[11,48,128]{2,1,0:T(8,128)S(1)} %slice.44), channel_id=1, source_target_pairs={{0,7},{1,0},{2,1},{3,2},{4,3},{5,4},{6,5},{7,6},{8,15},{9,8},{10,9... | collective-permute-start | bytes 811016 | tf_op jit(solution)/shard_map/ppermute | solution.py:316
  31.5 0.0 collective-permute-done.8.refs_3_
  31.6 0.0 copy-start
  31.6 0.1 collective-permute-start.11
  31.7 0.0 collective-permute-done.2.refs_2_
  31.7 3.3 %collective-permute-start.3 = (f32[9,48,128]{2,1,0:T(8,128)S(1)}, f32[9,48,128]{2,1,0:T(8,128)S(1)}, u32[]{:S(2)}, u32[]{:S(2)}) collective-permute-start(f32[9,48,128]{2,1,0:T(8,128)S(1)} %slice.41), channel_id=1, source_target_pairs={{0,7},{1,0},{2,1},{3,2},{4,3},{5,4},{6,5},{7,6},{8,15},{9,8},{10,9... | collective-permute-start | bytes 663560 | tf_op jit(solution)/shard_map/ppermute | solution.py:316
  35.0 0.0 collective-permute-done.10.refs_1_
  35.0 0.1 collective-permute-start.13
  35.1 3.4 %collective-permute-done.12.refs_4_ = f32[11,48,128]{2,1,0:T(8,128)S(1)} collective-permute-done((f32[11,48,128]{2,1,0:T(8,128)S(1)}, f32[11,48,128]{2,1,0:T(8,128)S(1)}, u32[]{:S(2)}, u32[]{:S(2)}) %collective-permute-start.12) | collective-permute-done | bytes 270368 | tf_op jit(solution)/shard_map/ppermute | solution.py:316
  38.5 3.8 %collective-permute-start.15 = (f32[10,48,128]{2,1,0:T(8,128)S(1)}, f32[10,48,128]{2,1,0:T(8,128)S(1)}, u32[]{:S(2)}, u32[]{:S(2)}) collective-permute-start(f32[10,48,128]{2,1,0:T(8,128)S(1)} %slice.47), channel_id=1, source_target_pairs={{0,7},{1,0},{2,1},{3,2},{4,3},{5,4},{6,5},{7,6},{8,15},{9,8},{10,9... | collective-permute-start | bytes 737288 | tf_op jit(solution)/shard_map/ppermute | solution.py:316
  42.2 0.0 collective-permute-done.11.refs_3_
  42.3 0.1 collective-permute-start.14
  42.4 0.0 copy-done
  42.4 0.8 %stiff_out_1.1 = f32[48,1024]{1,0:T(8,128)S(1)} custom-call(s32[64]{0:T(128)S(1)} %copy-done.1, f32[4,64,1024]{2,1,0:T(8,128)S(1)} %copy-done), custom_call_target="tpu_custom_call" | custom-call | tf_op jit(solution)/shard_map/stiff_out_1/pallas_call | solution.py:157
  43.2 0.1 collective-permute-start.5
  43.3 0.0 collective-permute-done.3.refs_2_
  43.3 0.7 %stiff_out_0.1 = f32[80,1024]{1,0:T(8,128)S(1)} custom-call(s32[64]{0:T(128)S(1)} %copy-done.1, f32[4,64,1024]{2,1,0:T(8,128)S(1)} %copy-done), custom_call_target="tpu_custom_call" | custom-call | tf_op jit(solution)/shard_map/stiff_out_0/pallas_call | solution.py:157
  44.0 0.8 %collective-permute-start.4 = (f32[80,1024]{1,0:T(8,128)S(1)}, f32[80,1024]{1,0:T(8,128)S(1)}, u32[]{:S(2)}, u32[]{:S(2)}) collective-permute-start(f32[80,1024]{1,0:T(8,128)S(1)} %stiff_out_0.1), channel_id=1, source_target_pairs={{0,16},{16,0},{32,48},{48,32},{64,80},{80,64},{96,112},{112,96},{1... | collective-permute-start | bytes 983048 | tf_op jit(solution)/shard_map/ppermute | solution.py:320
  44.8 1.9 %collective-permute-done.13.refs_1_ = f32[10,48,128]{2,1,0:T(8,128)S(1)} collective-permute-done((f32[10,48,128]{2,1,0:T(8,128)S(1)}, f32[10,48,128]{2,1,0:T(8,128)S(1)}, u32[]{:S(2)}, u32[]{:S(2)}) %collective-permute-start.13) | collective-permute-done | bytes 245792 | tf_op jit(solution)/shard_map/ppermute | solution.py:316
  46.7 0.1 collective-permute-start.16
  46.8 0.0 collective-permute-done.5.part1
  46.8 2.8 %collective-permute-done.14.refs_3_ = f32[9,48,128]{2,1,0:T(8,128)S(1)} collective-permute-done((f32[9,48,128]{2,1,0:T(8,128)S(1)}, f32[9,48,128]{2,1,0:T(8,128)S(1)}, u32[]{:S(2)}, u32[]{:S(2)}) %collective-permute-start.14) | collective-permute-done | bytes 221216 | tf_op jit(solution)/shard_map/ppermute | solution.py:316
  49.7 0.5 collective-permute-start.17
  50.1 0.0 collective-permute-done.15.refs_4_
  50.2 3.9 %collective-permute-start.18 = (f32[9,48,128]{2,1,0:T(8,128)S(1)}, f32[9,48,128]{2,1,0:T(8,128)S(1)}, u32[]{:S(2)}, u32[]{:S(2)}) collective-permute-start(f32[9,48,128]{2,1,0:T(8,128)S(1)} %slice.49), channel_id=1, source_target_pairs={{0,7},{1,0},{2,1},{3,2},{4,3},{5,4},{6,5},{7,6},{8,15},{9,8},{10,9... | collective-permute-start | bytes 663560 | tf_op jit(solution)/shard_map/ppermute | solution.py:316
  54.1 0.3 chunks_1.1.refs_0_
  54.4 0.5 chunks_2.1.refs_0_
  54.9 0.5 chunks_3.1.refs_0_
  55.4 0.5 chunks_4.1.refs_0_
  55.9 0.0 collective-permute-done.16.refs_1_
  55.9 0.0 collective-permute-done.4.part0
  55.9 0.3 chunks_5.1.total_ref
  56.2 0.0 collective-permute-done.17.refs_0_
  56.2 1.4 %collective-permute-done.18.refs_1_ = f32[9,48,128]{2,1,0:T(8,128)S(1)} collective-permute-done((f32[9,48,128]{2,1,0:T(8,128)S(1)}, f32[9,48,128]{2,1,0:T(8,128)S(1)}, u32[]{:S(2)}, u32[]{:S(2)}) %collective-permute-start.18) | collective-permute-done | bytes 221216 | tf_op jit(solution)/shard_map/ppermute | solution.py:316
  57.6 0.4 last_chunks.1
  58.0 0.2 collective-permute-start.19
  58.2 0.6 stiff_merge.1.refs_0_.refs_1_
  58.8 0.7 %finish_0.1.refs_0_ = f32[2,64,1024]{2,1,0:T(8,128)} custom-call(f32[2,64,1024]{2,1,0:T(8,128)S(1)} %stiff_merge.1.refs_0_.refs_1_, f32[64,1024]{1,0:T(8,128)S(1)} %get-tuple-element.35.refs_1_), custom_call_target="tpu_custom_call" | custom-call | tf_op jit(solution)/shard_map/finish_0/pallas_call | solution.py:302
  59.6 4.8 %collective-permute-done.19.refs_2_ = f32[64,1024]{1,0:T(8,128)S(1)} collective-permute-done((f32[64,1024]{1,0:T(8,128)S(1)}, f32[64,1024]{1,0:T(8,128)S(1)}, u32[]{:S(2)}, u32[]{:S(2)}) %collective-permute-start.19) | collective-permute-done | bytes 262176 | tf_op jit(solution)/shard_map/ppermute | solution.py:320
  64.4 0.7 %finish_1.1 = f32[2,64,1024]{2,1,0:T(8,128)} custom-call(f32[2,64,1024]{2,1,0:T(8,128)} %finish_0.1.refs_0_, f32[2,64,1024]{2,1,0:T(8,128)S(1)} %stiff_merge.1.refs_0_.refs_1_, f32[64,1024]{1,0:T(8,128)S(1)} %collective-permute-done.19.refs_2_), custom_call_target="tpu_custom_call", output_to_operand_aliasing={{}: (0, {})} | custom-call | tf_op jit(solution)/shard_map/finish_1/pallas_call | solution.py:302
  (10 shorter events, 0.2 us)
Async XLA Ops:
  1.4 2.0 %collective-permute-start = (f32[16,48,128]{2,1,0:T(8,128)S(1)}, f32[16,48,128]{2,1,0:T(8,128)S(1)}, u32[]{:S(2)}, u32[]{:S(2)}) collective-permute-start(f32[16,48,128]{2,1,0:T(8,128)S(1)} %get-tuple-element.21), channel_id=1, source_target_pairs={{0,16},{16,0},{32,48},{48,32},{64,80},{80,64},{96,112},{112,96},{1... | collective-permute-start | bytes 1179656 | tf_op jit(solution)/shard_map/ppermute | solution.py:320
  1.5 9.1 %collective-permute-start.7 = (f32[16,48,128]{2,1,0:T(8,128)S(1)}, f32[16,48,128]{2,1,0:T(8,128)S(1)}, u32[]{:S(2)}, u32[]{:S(2)}) collective-permute-start(f32[16,48,128]{2,1,0:T(8,128)S(1)} %get-tuple-element.27), channel_id=1, source_target_pairs={{0,16},{16,0},{32,48},{48,32},{64,80},{80,64},{96,112},{112,96},{1... | collective-permute-start | bytes 1179656 | tf_op jit(solution)/shard_map/ppermute | solution.py:320
  3.5 0.7 %copy-start.1 = (s32[64]{0:T(128)S(1)}, s32[64]{0:T(128)}, u32[]{:S(2)}) copy-start(s32[64]{0:T(128)} %plan_ref.8) | copy-start | bytes 772
  4.7 12.8 %collective-permute-start.1 = (f32[11,48,128]{2,1,0:T(8,128)S(1)}, f32[11,48,128]{2,1,0:T(8,128)S(1)}, u32[]{:S(2)}, u32[]{:S(2)}) collective-permute-start(f32[11,48,128]{2,1,0:T(8,128)S(1)} %get-tuple-element.23), channel_id=1, source_target_pairs={{0,7},{1,0},{2,1},{3,2},{4,3},{5,4},{6,5},{7,6},{8,15},{9,8},{10,9... | collective-permute-start | bytes 811016 | tf_op jit(solution)/shard_map/ppermute | solution.py:316
  10.7 11.1 %collective-permute-start.6 = (f32[12,48,128]{2,1,0:T(8,128)S(1)}, f32[12,48,128]{2,1,0:T(8,128)S(1)}, u32[]{:S(2)}, u32[]{:S(2)}) collective-permute-start(f32[12,48,128]{2,1,0:T(8,128)S(1)} %get-tuple-element.25.refs_0_), channel_id=1, source_target_pairs={{0,1},{1,2},{2,3},{3,4},{4,5},{5,6},{6,7},{7,0},{8,9},{9,10},{10,1... | collective-permute-start | bytes 884744 | tf_op jit(solution)/shard_map/ppermute | solution.py:316
  11.3 14.2 %collective-permute-start.9 = (f32[12,48,128]{2,1,0:T(8,128)S(1)}, f32[12,48,128]{2,1,0:T(8,128)S(1)}, u32[]{:S(2)}, u32[]{:S(2)}) collective-permute-start(f32[12,48,128]{2,1,0:T(8,128)S(1)} %get-tuple-element.31), channel_id=1, source_target_pairs={{0,15},{1,8},{2,9},{3,10},{4,11},{5,12},{6,13},{7,14},{8,7},{9,0},... | collective-permute-start | bytes 884744 | tf_op jit(solution)/shard_map/ppermute | solution.py:326
  15.5 16.0 %collective-permute-start.8 = (f32[11,48,128]{2,1,0:T(8,128)S(1)}, f32[11,48,128]{2,1,0:T(8,128)S(1)}, u32[]{:S(2)}, u32[]{:S(2)}) collective-permute-start(f32[11,48,128]{2,1,0:T(8,128)S(1)} %get-tuple-element.30), channel_id=1, source_target_pairs={{0,9},{1,10},{2,11},{3,12},{4,13},{5,14},{6,15},{7,8},{8,1},{9,2},... | collective-permute-start | bytes 811016 | tf_op jit(solution)/shard_map/ppermute | solution.py:326
  17.5 14.1 %collective-permute-start.2 = (f32[10,48,128]{2,1,0:T(8,128)S(1)}, f32[10,48,128]{2,1,0:T(8,128)S(1)}, u32[]{:S(2)}, u32[]{:S(2)}) collective-permute-start(f32[10,48,128]{2,1,0:T(8,128)S(1)} %slice.40), channel_id=1, source_target_pairs={{0,7},{1,0},{2,1},{3,2},{4,3},{5,4},{6,5},{7,6},{8,15},{9,8},{10,9... | collective-permute-start | bytes 737288 | tf_op jit(solution)/shard_map/ppermute | solution.py:316
  21.8 13.2 %collective-permute-start.10 = (f32[11,48,128]{2,1,0:T(8,128)S(1)}, f32[11,48,128]{2,1,0:T(8,128)S(1)}, u32[]{:S(2)}, u32[]{:S(2)}) collective-permute-start(f32[11,48,128]{2,1,0:T(8,128)S(1)} %slice.42), channel_id=1, source_target_pairs={{0,1},{1,2},{2,3},{3,4},{4,5},{5,6},{6,7},{7,0},{8,9},{9,10},{10,1... | collective-permute-start | bytes 811016 | tf_op jit(solution)/shard_map/ppermute | solution.py:316
  25.5 13.0 %collective-permute-start.12 = (f32[11,48,128]{2,1,0:T(8,128)S(1)}, f32[11,48,128]{2,1,0:T(8,128)S(1)}, u32[]{:S(2)}, u32[]{:S(2)}) collective-permute-start(f32[11,48,128]{2,1,0:T(8,128)S(1)} %slice.44), channel_id=1, source_target_pairs={{0,7},{1,0},{2,1},{3,2},{4,3},{5,4},{6,5},{7,6},{8,15},{9,8},{10,9... | collective-permute-start | bytes 811016 | tf_op jit(solution)/shard_map/ppermute | solution.py:316
  31.6 10.8 %copy-start = (f32[4,64,1024]{2,1,0:T(8,128)S(1)}, f32[4,64,1024]{2,1,0:T(8,128)}, u32[]{:S(2)}) copy-start(f32[4,64,1024]{2,1,0:T(8,128)} %b_hbm.5) | copy-start | bytes 3145732
  31.6 10.7 %collective-permute-start.11 = (f32[10,48,128]{2,1,0:T(8,128)S(1)}, f32[10,48,128]{2,1,0:T(8,128)S(1)}, u32[]{:S(2)}, u32[]{:S(2)}) collective-permute-start(f32[10,48,128]{2,1,0:T(8,128)S(1)} %slice.43), channel_id=1, source_target_pairs={{0,1},{1,2},{2,3},{3,4},{4,5},{5,6},{6,7},{7,0},{8,9},{9,10},{10,1... | collective-permute-start | bytes 737288 | tf_op jit(solution)/shard_map/ppermute | solution.py:316
  31.7 11.6 %collective-permute-start.3 = (f32[9,48,128]{2,1,0:T(8,128)S(1)}, f32[9,48,128]{2,1,0:T(8,128)S(1)}, u32[]{:S(2)}, u32[]{:S(2)}) collective-permute-start(f32[9,48,128]{2,1,0:T(8,128)S(1)} %slice.41), channel_id=1, source_target_pairs={{0,7},{1,0},{2,1},{3,2},{4,3},{5,4},{6,5},{7,6},{8,15},{9,8},{10,9... | collective-permute-start | bytes 663560 | tf_op jit(solution)/shard_map/ppermute | solution.py:316
  35.0 11.7 %collective-permute-start.13 = (f32[10,48,128]{2,1,0:T(8,128)S(1)}, f32[10,48,128]{2,1,0:T(8,128)S(1)}, u32[]{:S(2)}, u32[]{:S(2)}) collective-permute-start(f32[10,48,128]{2,1,0:T(8,128)S(1)} %slice.45), channel_id=1, source_target_pairs={{0,1},{1,2},{2,3},{3,4},{4,5},{5,6},{6,7},{7,0},{8,9},{9,10},{10,1... | collective-permute-start | bytes 737288 | tf_op jit(solution)/shard_map/ppermute | solution.py:316
  38.5 11.7 %collective-permute-start.15 = (f32[10,48,128]{2,1,0:T(8,128)S(1)}, f32[10,48,128]{2,1,0:T(8,128)S(1)}, u32[]{:S(2)}, u32[]{:S(2)}) collective-permute-start(f32[10,48,128]{2,1,0:T(8,128)S(1)} %slice.47), channel_id=1, source_target_pairs={{0,7},{1,0},{2,1},{3,2},{4,3},{5,4},{6,5},{7,6},{8,15},{9,8},{10,9... | collective-permute-start | bytes 737288 | tf_op jit(solution)/shard_map/ppermute | solution.py:316
  42.3 7.4 %collective-permute-start.14 = (f32[9,48,128]{2,1,0:T(8,128)S(1)}, f32[9,48,128]{2,1,0:T(8,128)S(1)}, u32[]{:S(2)}, u32[]{:S(2)}) collective-permute-start(f32[9,48,128]{2,1,0:T(8,128)S(1)} %slice.46), channel_id=1, source_target_pairs={{0,1},{1,2},{2,3},{3,4},{4,5},{5,6},{6,7},{7,0},{8,9},{9,10},{10,1... | collective-permute-start | bytes 663560 | tf_op jit(solution)/shard_map/ppermute | solution.py:316
  43.2 3.6 %collective-permute-start.5 = (f32[48,1024]{1,0:T(8,128)S(1)}, f32[48,1024]{1,0:T(8,128)S(1)}, u32[]{:S(2)}, u32[]{:S(2)}) collective-permute-start(f32[48,1024]{1,0:T(8,128)S(1)} %stiff_out_1.1), channel_id=1, source_target_pairs={{0,16},{16,0},{32,48},{48,32},{64,80},{80,64},{96,112},{112,96},{1... | collective-permute-start | bytes 589832 | tf_op jit(solution)/shard_map/ppermute | solution.py:320
  44.0 11.9 %collective-permute-start.4 = (f32[80,1024]{1,0:T(8,128)S(1)}, f32[80,1024]{1,0:T(8,128)S(1)}, u32[]{:S(2)}, u32[]{:S(2)}) collective-permute-start(f32[80,1024]{1,0:T(8,128)S(1)} %stiff_out_0.1), channel_id=1, source_target_pairs={{0,16},{16,0},{32,48},{48,32},{64,80},{80,64},{96,112},{112,96},{1... | collective-permute-start | bytes 983048 | tf_op jit(solution)/shard_map/ppermute | solution.py:320
  46.7 9.2 %collective-permute-start.16 = (f32[9,48,128]{2,1,0:T(8,128)S(1)}, f32[9,48,128]{2,1,0:T(8,128)S(1)}, u32[]{:S(2)}, u32[]{:S(2)}) collective-permute-start(f32[9,48,128]{2,1,0:T(8,128)S(1)} %slice.48), channel_id=1, source_target_pairs={{0,1},{1,2},{2,3},{3,4},{4,5},{5,6},{6,7},{7,0},{8,9},{9,10},{10,1... | collective-permute-start | bytes 663560 | tf_op jit(solution)/shard_map/ppermute | solution.py:316
  49.7 6.5 %collective-permute-start.17 = (f32[9,48,128]{2,1,0:T(8,128)S(1)}, f32[9,48,128]{2,1,0:T(8,128)S(1)}, u32[]{:S(2)}, u32[]{:S(2)}) collective-permute-start(f32[9,48,128]{2,1,0:T(8,128)S(1)} %get-tuple-element.34), channel_id=1, source_target_pairs={{0,8},{1,9},{2,10},{3,11},{4,12},{5,13},{6,14},{7,15},{8,0},{9,1},... | collective-permute-start | bytes 663560 | tf_op jit(solution)/shard_map/ppermute | solution.py:326
  50.2 7.4 %collective-permute-start.18 = (f32[9,48,128]{2,1,0:T(8,128)S(1)}, f32[9,48,128]{2,1,0:T(8,128)S(1)}, u32[]{:S(2)}, u32[]{:S(2)}) collective-permute-start(f32[9,48,128]{2,1,0:T(8,128)S(1)} %slice.49), channel_id=1, source_target_pairs={{0,7},{1,0},{2,1},{3,2},{4,3},{5,4},{6,5},{7,6},{8,15},{9,8},{10,9... | collective-permute-start | bytes 663560 | tf_op jit(solution)/shard_map/ppermute | solution.py:316
  58.0 6.5 %collective-permute-start.19 = (f32[64,1024]{1,0:T(8,128)S(1)}, f32[64,1024]{1,0:T(8,128)S(1)}, u32[]{:S(2)}, u32[]{:S(2)}) collective-permute-start(f32[64,1024]{1,0:T(8,128)S(1)} %get-tuple-element.36), channel_id=1, source_target_pairs={{0,8},{8,0},{1,9},{9,1},{2,10},{10,2},{3,11},{11,3},{4,12},{12,4},... | collective-permute-start | bytes 786440 | tf_op jit(solution)/shard_map/ppermute | solution.py:320

commit v5 on v2

--- a/solution.py
+++ b/solution.py
@@ -32,22 +32,27 @@
     home, depth, width = solve.shape
     blocks = width // LANES
 
-    def kernel(plan_hbm, c_hbm, x_hbm, out0, out1, plan_ref, c_buf, x_buf, plan_sem, c_sem, x_sem):
+    def kernel(plan_given, c_hbm, x_hbm, out0, out1, plan_buf, c_buf, x_buf, plan_sem, c_sem, x_sem):
         group = lax.axis_index("group")
         place = lax.axis_index("tile_1")
         owner = jnp.bitwise_xor(group, 1) if for_partner else group
         outs = (out0, out1)
         copies = [
-            pltpu.make_async_copy(plan_hbm, plan_ref, plan_sem),
             pltpu.make_async_copy(c_hbm, c_buf, c_sem),
             pltpu.make_async_copy(x_hbm, x_buf, x_sem),
         ]
         for copy in copies:
             copy.start()
+        plan_ref = plan_given
+        if for_partner:
+            plan_copy = pltpu.make_async_copy(plan_given, plan_buf, plan_sem)
+            plan_copy.start()
+            plan_ref = plan_buf
         low = lax.broadcasted_iota(jnp.int32, (depth, LANES), 1) < LANES // 2
+        if for_partner:
+            plan_copy.wait()
+        positions = [locate(plan_ref, group, owner * OWN + slot, home)[0] for slot in range(OWN)]
         copies[0].wait()
-        positions = [locate(plan_ref, group, owner * OWN + slot, home)[0] for slot in range(OWN)]
-        copies[1].wait()
         for slot in range(OWN):
             up = hops(slot)[0]
             for m in range(blocks // 2):
@@ -59,7 +64,7 @@
                     ahead = jnp.bitwise_and(to - place, blocks - 1)
                     spot = jnp.where(ahead == 0, 15, jnp.where(ahead <= up, ahead - 1, ahead + 7))
                     outs[slot][spot] = piece
-        copies[2].wait()
+        copies[1].wait()
         for slot in range(OWN):
             up = hops(slot)[0]
             for n in range(blocks):
@@ -69,7 +74,7 @@
     return pl.pallas_call(
         kernel,
         out_shape=(packet, packet),
-        in_specs=[HBM] * 3,
+        in_specs=[HBM if for_partner else SMEM, HBM, HBM],
         out_specs=(VMEM, VMEM),
         scratch_shapes=[
             pltpu.SMEM(plan.shape, jnp.int32),
@@ -186,10 +191,12 @@
 
 
 def add_chunks(total_ref, chunks, start):
-    for packet, places, piece in chunks:
+    for packets, places, piece in chunks:
         c_high, c_low = split(piece)
         left = jnp.concatenate([c_high, c_high, c_low], axis=0)
+        each = len(places) // len(packets)
         for n in range(0, len(places), 2):
+            packet = packets[n // each]
             x = jnp.concatenate([packet[places[n]], packet[places[n + 1]]], axis=1)
             x_high, x_low = split(x)
             right = jnp.concatenate([x_high, x_low, x_high], axis=0)
@@ -209,15 +216,16 @@
         arrays.append(array)
         return len(arrays) - 1
 
-    for packet, places, holder, index in sources:
-        layout.append((place(packet), places, place(holder), index))
+    for packets, places, holder, index in sources:
+        packets = packets if isinstance(packets, tuple) else (packets,)
+        layout.append((tuple(place(p) for p in packets), places, place(holder), index))
     return arrays, layout
 
 
 def chunks_of(refs, layout):
     return [
-        (refs[k], places, refs[holder][...] if index is None else refs[holder][index])
-        for k, places, holder, index in layout
+        ([refs[k] for k in ks], places, refs[holder][...] if index is None else refs[holder][index])
+        for ks, places, holder, index in layout
     ]
 
 
@@ -244,42 +252,42 @@
     )(*given, *arrays)
 
 
-def last_chunks(total, sources, stiff, slot, first, width, name):
+def last_chunks(total, sources, first, width, name):
     rows = LANES // 2
     arrays, layout = gathered(sources)
-    columns = pl.ds(first, width)
-
-    def kernel(total_ref, stiff_ref, *refs):
+
+    def kernel(total_ref, *refs):
         send_ref, keep_ref, sum_ref = refs[-3:]
-        sum_ref[...] = total_ref[:, columns]
+        sum_ref[...] = total_ref[:, pl.ds(first, width)]
         add_chunks(sum_ref, chunks_of(refs[:-3], layout), False)
         mine = lax.axis_index("tile_0")
         send_ref[...] = sum_ref[pl.ds(pl.multiple_of((1 - mine) * rows, rows), rows), :]
-        keep_ref[...] = stiff_ref[slot, :, columns] - sum_ref[pl.ds(pl.multiple_of(mine * rows, rows), rows), :]
+        keep_ref[...] = sum_ref[pl.ds(pl.multiple_of(mine * rows, rows), rows), :]
 
     half = jax.ShapeDtypeStruct((rows, width), jnp.float32)
     return pl.pallas_call(
         kernel,
         out_shape=(half, half),
-        in_specs=[VMEM] * (2 + len(arrays)),
+        in_specs=[VMEM] * (1 + len(arrays)),
         out_specs=(VMEM, VMEM),
         scratch_shapes=[pltpu.VMEM((LANES, width), jnp.float32)],
         compiler_params=PARAMS,
         name=name,
-    )(total, stiff, *arrays)
-
-
-def finish(result, parts, slot, rows, width):
+    )(total, *arrays)
+
+
+def finish(result, stiff, parts, slot):
     flat = [array for pair in parts for array in pair]
     given = [] if result is None else [result]
+    rows, width = stiff.shape[1:]
 
     def kernel(*refs):
-        ins = refs[len(given) : -3]
+        stiff_ref, *ins = refs[len(given) : -3]
         out_hbm, buf, sem = refs[-3:]
         first = 0
         for k in range(0, len(ins), 2):
             columns = pl.ds(first, ins[k].shape[1])
-            buf[:, columns] = ins[k][...] - ins[k + 1][...]
+            buf[:, columns] = stiff_ref[slot, :, columns] - (ins[k][...] + ins[k + 1][...])
             first += ins[k].shape[1]
         copy = pltpu.make_async_copy(buf, out_hbm.at[slot], sem)
         copy.start()
@@ -288,13 +296,13 @@
     return pl.pallas_call(
         kernel,
         out_shape=jax.ShapeDtypeStruct((OWN, rows, width), jnp.float32),
-        in_specs=[HBM] * len(given) + [VMEM] * len(flat),
+        in_specs=[HBM] * len(given) + [VMEM] * (1 + len(flat)),
         out_specs=HBM,
         scratch_shapes=[pltpu.VMEM((rows, width), jnp.float32), pltpu.SemaphoreType.DMA],
         input_output_aliases={0: 0} if given else {},
         compiler_params=PARAMS,
         name=f"finish_{slot}",
-    )(*given, *flat)
+    )(*given, stiff, *flat)
 
 
 def shifted(array, axis, distance):
@@ -323,7 +331,7 @@
     in_hbm = [pltpu.with_memory_space_constraint(a, pltpu.HBM) for a in (migration, pieces, interior_solve)]
     outgoing = pack(*in_hbm, True)
     arrived = [swapped(outgoing[0], "group"), swapped(outgoing[1], "group")]
-    local = pack(*in_hbm, False)
+    local = pack(migration, *in_hbm[1:], False)
     up0, down0, own0 = merge(migration, arrived[0], local[0], 0, home)
     up1, down1, own1 = merge(migration, arrived[1], local[1], 1, home)
     stiff_arrived = swapped(stiff_out(migration, boundary_stiffness), "group")
@@ -345,33 +353,29 @@
     uuu1a, ddd1a = up(uu1[1 : half + 3]), down(dd1[half : blocks + 1])
     total1 = accumulate(total1, [(uu1, run(3), uu1, 0), (dd1, turned, dd1, blocks + 1)], width, "chunks_1")
     far0a, far0b = up(uuu0[1 : half + 1]), down(ddd0[half : blocks + 1])
-    total0 = accumulate(total0, [(uuu0, run(1), uuu0, 0), (ddd0, run(0), ddd0, blocks + 1)], width, "chunks_0")
     uuu1b, ddd1b = up(uu1[half + 3 :]), down(dd1[:half])
     far1a, far1b = up(uuu1a[1:]), down(ddd1b)
-    left, right = list(range(half)), list(range(half, blocks))
+    left = list(range(half))
     wide = width // 2
-    send0a, keep0a = last_chunks(
-        total0, [(far0a, left, far0b, half)], stiff, 0, 0, wide, "last_0a"
+    total0 = accumulate(total0, [(uuu0, run(1), uuu0, 0), (ddd0, run(0), ddd0, blocks + 1)], width, "chunks_0")
+    send0, keep0 = last_chunks(
+        total0, [((far0a, far0b), left + left, far0b, half)], 0, width, "last_0"
     )
-    send0b, keep0b = last_chunks(
-        total0, [(far0b, left, far0b, half)], stiff, 0, wide, wide, "last_0b"
-    )
-    del right
-    other0a, other0b = swapped(send0a, "tile_0"), swapped(send0b, "tile_0")
+    other0 = swapped(send0, "tile_0")
     send1a, keep1a = last_chunks(
         total1,
         [(uuu1a, run(2)[:half], uuu1a, 0), (ddd1a, left, ddd1a, half), (far1a, run(1)[:half], far1a, 0)],
-        stiff, 1, 0, wide, "last_1a",
+        0, wide, "last_1a",
     )
     other1a = swapped(send1a, "tile_0")
     send1b, keep1b = last_chunks(
         total1,
         [(uuu1b, left, uuu1a, 0), (ddd1b, left, ddd1a, half), (far1b, left, far1a, 0)],
-        stiff, 1, wide, wide, "last_1b",
+        wide, wide, "last_1b",
     )
     other1b = swapped(send1b, "tile_0")
-    result = finish(None, [(keep0a, other0a), (keep0b, other0b)], 0, rows, width)
-    return finish(result, [(keep1a, other1a), (keep1b, other1b)], 1, rows, width)
+    result = finish(None, stiff, [(keep0, other0)], 0)
+    return finish(result, stiff, [(keep1a, other1a), (keep1b, other1b)], 1)
 
 
 def solution(mesh):

time: 73.4 us -> 67.8 us (0.924)
  waiting for transfers between devices: 27 us -> 23.9 us
  starting transfers between devices: 34.6 us -> 32.4 us
    ppermute x7 -> x6, waiting for transfers between devices: 4.31 us -> 2.5 us  [swapped(): lax.ppermute(array, axis, [(i, i ^ 1) for i in range(lax.axis_size(axis))])]
    ppermute x18, starting transfers between devices: 29.5 us -> 27.9 us  [shifted(): lax.ppermute(array, axis, [(i, (i + distance) % size) for i in range(size)])]
    ppermute x18, waiting for transfers between devices: 22.7 us -> 21.4 us  [shifted(): lax.ppermute(array, axis, [(i, (i + distance) % size) for i in range(size)])]
    ppermute x7 -> x6, starting transfers between devices: 5.08 us -> 4.46 us  [swapped(): lax.ppermute(array, axis, [(i, i ^ 1) for i in range(lax.axis_size(axis))])]
    pallas_call x6 -> x5, Pallas kernels: 4.05 us -> 4.37 us  [the longest x2 3.38 us: pack(): pl.pallas_call(kernel, out_shape=(packet, packet), in_specs=[HBM if for_p...]
  transfers between devices with their start and end apart: 25 -> 24, of which waited for: 8 -> 9; matrix products, arithmetic and copies ran while one was open for 0% -> 0% of each run, Pallas kernels for 11% -> 13%
where the time goes in v5:
time: 67.8 us; the launch traced here: 67.6 us
  starting transfers between devices  32.4 us (48%)
  waiting for transfers between devices  23.9 us (35%)
  Pallas kernels  10.7 us (16%)
    ppermute x18, starting transfers between devices, shifted(): lax.ppermute(array, axis, [(i, (i + distance) % size) for i in range(size)])  27.9 us
    ppermute x18, waiting for transfers between devices, shifted(): lax.ppermute(array, axis, [(i, (i + distance) % size) for i in range(size)])  21.4 us
    ppermute x6, starting transfers between devices, swapped(): lax.ppermute(array, axis, [(i, i ^ 1) for i in range(lax.axis_size(axis))])  4.46 us
    pallas_call x2, Pallas kernels, pack(): pl.pallas_call(kernel, out_shape=(packet, packet), in_specs=[HBM if for_p...  3.38 us
    ppermute x6, waiting for transfers between devices, swapped(): lax.ppermute(array, axis, [(i, i ^ 1) for i in range(lax.axis_size(axis))])  2.5 us
    pallas_call x7, Pallas kernels, accumulate(): pl.pallas_call(kernel, out_shape=jax.ShapeDtypeStruct((LANES, width), jnp...  2.33 us
    pallas_call x2, Pallas kernels, finish(): pl.pallas_call(kernel, out_shape=jax.ShapeDtypeStruct((OWN, rows, width),...  1.54 us
  transfers between devices with their start and end apart: 24, of which 9 were waited for; matrix products, arithmetic and copies ran while one was open for 0% of the time, Pallas kernels for 13%

profile of v5, /device:TPU:24, one launch (start us, length us, event | category | flops | bytes accessed | tf_op | source)
XLA Modules:
  0.0 67.6 jit_solution(12267233954980418349)
XLA Ops:
  0.0 1.4 %pack_partner.1 = (f32[16,48,128]{2,1,0:T(8,128)S(1)}, f32[16,48,128]{2,1,0:T(8,128)S(1)}) custom-call(s32[64]{0:T(128)} %plan_ref.7, f32[4,48,1024]{2,1,0:T(8,128)} %bitcast.1, f32[4,48,1024]{2,1,0:T(8,128)} %x_hbm.3), custom_call_target="tpu_custom_call" | custom-call | tf_op jit(solution)/shard_map/pack_partner/pallas_call | solution.py:74
  1.4 0.0 copy-start.1
  1.4 0.1 collective-permute-start.1
  1.5 0.5 collective-permute-start.11
  2.0 0.0 copy-done.1
  2.1 2.0 %pack_own.1 = (f32[16,48,128]{2,1,0:T(8,128)S(1)}, f32[16,48,128]{2,1,0:T(8,128)S(1)}) custom-call(s32[64]{0:T(128)S(1)} %copy-done.1, f32[4,48,1024]{2,1,0:T(8,128)} %bitcast.2, f32[4,48,1024]{2,1,0:T(8,128)} %x_hbm.3), custom_call_target="tpu_custom_call" | custom-call | tf_op jit(solution)/shard_map/pack_own/pallas_call | solution.py:74
  4.1 0.0 collective-permute-done.1.arrived_ref
  4.1 0.6 merge_0.1
  4.7 5.9 %collective-permute-start.3 = (f32[12,48,128]{2,1,0:T(8,128)S(1)}, f32[12,48,128]{2,1,0:T(8,128)S(1)}, u32[]{:S(2)}, u32[]{:S(2)}) collective-permute-start(f32[12,48,128]{2,1,0:T(8,128)S(1)} %get-tuple-element.25), channel_id=1, source_target_pairs={{0,7},{1,0},{2,1},{3,2},{4,3},{5,4},{6,5},{7,6},{8,15},{9,8},{10,9... | collective-permute-start | bytes 884744 | tf_op jit(solution)/shard_map/ppermute | solution.py:310
  10.6 0.0 collective-permute-start.2
  10.6 0.0 collective-permute-done.11.arrived_ref
  10.6 0.6 merge_1.1
  11.2 0.1 collective-permute-start.12
  11.3 5.8 %collective-permute-done.3.refs_2_ = f32[12,48,128]{2,1,0:T(8,128)S(1)} collective-permute-done((f32[12,48,128]{2,1,0:T(8,128)S(1)}, f32[12,48,128]{2,1,0:T(8,128)S(1)}, u32[]{:S(2)}, u32[]{:S(2)}) %collective-permute-start.3) | collective-permute-done | bytes 294944 | tf_op jit(solution)/shard_map/ppermute | solution.py:310
  17.1 3.8 %collective-permute-start.5 = (f32[11,48,128]{2,1,0:T(8,128)S(1)}, f32[11,48,128]{2,1,0:T(8,128)S(1)}, u32[]{:S(2)}, u32[]{:S(2)}) collective-permute-start(f32[11,48,128]{2,1,0:T(8,128)S(1)} %slice.53), channel_id=1, source_target_pairs={{0,7},{1,0},{2,1},{3,2},{4,3},{5,4},{6,5},{7,6},{8,15},{9,8},{10,9... | collective-permute-start | bytes 811016 | tf_op jit(solution)/shard_map/ppermute | solution.py:310
  20.9 0.3 collective-permute-done.2.refs_1_
  21.2 0.0 copy-start
  21.2 0.1 collective-permute-start.4
  21.3 3.2 %collective-permute-start.13 = (f32[11,48,128]{2,1,0:T(8,128)S(1)}, f32[11,48,128]{2,1,0:T(8,128)S(1)}, u32[]{:S(2)}, u32[]{:S(2)}) collective-permute-start(f32[11,48,128]{2,1,0:T(8,128)S(1)} %get-tuple-element.32), channel_id=1, source_target_pairs={{0,7},{1,0},{2,1},{3,2},{4,3},{5,4},{6,5},{7,6},{8,15},{9,8},{10,9... | collective-permute-start | bytes 811016 | tf_op jit(solution)/shard_map/ppermute | solution.py:310
  24.6 3.0 %collective-permute-done.12.refs_1_ = f32[12,48,128]{2,1,0:T(8,128)S(1)} collective-permute-done((f32[12,48,128]{2,1,0:T(8,128)S(1)}, f32[12,48,128]{2,1,0:T(8,128)S(1)}, u32[]{:S(2)}, u32[]{:S(2)}) %collective-permute-start.12) | collective-permute-done | bytes 294944 | tf_op jit(solution)/shard_map/ppermute | solution.py:310
  27.5 0.1 collective-permute-start.14
  27.6 5.2 %collective-permute-done.4.refs_1_ = f32[10,48,128]{2,1,0:T(8,128)S(1)} collective-permute-done((f32[10,48,128]{2,1,0:T(8,128)S(1)}, f32[10,48,128]{2,1,0:T(8,128)S(1)}, u32[]{:S(2)}, u32[]{:S(2)}) %collective-permute-start.4) | collective-permute-done | bytes 245792 | tf_op jit(solution)/shard_map/ppermute | solution.py:310
  32.8 0.1 collective-permute-start.6
  32.9 0.0 collective-permute-done.5.refs_2_
  32.9 3.3 %collective-permute-start.7 = (f32[10,48,128]{2,1,0:T(8,128)S(1)}, f32[10,48,128]{2,1,0:T(8,128)S(1)}, u32[]{:S(2)}, u32[]{:S(2)}) collective-permute-start(f32[10,48,128]{2,1,0:T(8,128)S(1)} %slice.55), channel_id=1, source_target_pairs={{0,7},{1,0},{2,1},{3,2},{4,3},{5,4},{6,5},{7,6},{8,15},{9,8},{10,9... | collective-permute-start | bytes 737288 | tf_op jit(solution)/shard_map/ppermute | solution.py:310
  36.2 0.0 collective-permute-done.13.refs_2_
  36.2 0.1 collective-permute-start.15
  36.4 0.6 stiff_out.1
  37.0 0.1 collective-permute-start
  37.1 5.0 %collective-permute-done.6.refs_1_ = f32[9,48,128]{2,1,0:T(8,128)S(1)} collective-permute-done((f32[9,48,128]{2,1,0:T(8,128)S(1)}, f32[9,48,128]{2,1,0:T(8,128)S(1)}, u32[]{:S(2)}, u32[]{:S(2)}) %collective-permute-start.6) | collective-permute-done | bytes 221216 | tf_op jit(solution)/shard_map/ppermute | solution.py:310
  42.1 0.1 collective-permute-start.8
  42.2 0.0 collective-permute-done.14.refs_1_
  42.2 0.1 collective-permute-start.16
  42.3 0.0 collective-permute-done.7.refs_2_
  42.4 3.5 %collective-permute-start.9 = (f32[5,48,128]{2,1,0:T(8,128)S(1)}, f32[5,48,128]{2,1,0:T(8,128)S(1)}, u32[]{:S(2)}, u32[]{:S(2)}) collective-permute-start(f32[5,48,128]{2,1,0:T(8,128)S(1)} %slice.57), channel_id=1, source_target_pairs={{0,7},{1,0},{2,1},{3,2},{4,3},{5,4},{6,5},{7,6},{8,15},{9,8},{10,9... | collective-permute-start | bytes 368648 | tf_op jit(solution)/shard_map/ppermute | solution.py:310
  45.8 0.0 collective-permute-done.15.refs_2_
  45.8 2.2 %collective-permute-start.17 = (f32[5,48,128]{2,1,0:T(8,128)S(1)}, f32[5,48,128]{2,1,0:T(8,128)S(1)}, u32[]{:S(2)}, u32[]{:S(2)}) collective-permute-start(f32[5,48,128]{2,1,0:T(8,128)S(1)} %slice.61), channel_id=1, source_target_pairs={{0,7},{1,0},{2,1},{3,2},{4,3},{5,4},{6,5},{7,6},{8,15},{9,8},{10,9... | collective-permute-start | bytes 368648 | tf_op jit(solution)/shard_map/ppermute | solution.py:310
  48.0 0.5 collective-permute-done.8.refs_0_
  48.6 0.0 collective-permute-start.21
  48.6 0.3 chunks_0.4.refs_0_
  48.8 0.4 chunks_0.5.refs_0_
  49.2 0.4 chunks_0.6.refs_0_
  49.6 0.4 chunks_0.7.total_ref
  49.9 0.0 collective-permute-done.9.refs_1_
  50.0 0.3 last_0.1
  50.3 1.6 %collective-permute-start.10 = (f32[64,1024]{1,0:T(8,128)S(1)}, f32[64,1024]{1,0:T(8,128)S(1)}, u32[]{:S(2)}, u32[]{:S(2)}) collective-permute-start(f32[64,1024]{1,0:T(8,128)S(1)} %get-tuple-element.27), channel_id=1, source_target_pairs={{0,8},{8,0},{1,9},{9,1},{2,10},{10,2},{3,11},{11,3},{4,12},{12,4},... | collective-permute-start | bytes 786440 | tf_op jit(solution)/shard_map/ppermute | solution.py:314
  51.9 0.0 collective-permute-done.16.refs_0_.refs_1_
  51.9 2.1 %collective-permute-start.18 = (f32[5,48,128]{2,1,0:T(8,128)S(1)}, f32[5,48,128]{2,1,0:T(8,128)S(1)}, u32[]{:S(2)}, u32[]{:S(2)}) collective-permute-start(f32[5,48,128]{2,1,0:T(8,128)S(1)} %slice.62), channel_id=1, source_target_pairs={{0,1},{1,2},{2,3},{3,4},{4,5},{5,6},{6,7},{7,0},{8,9},{9,10},{10,1... | collective-permute-start | bytes 368648 | tf_op jit(solution)/shard_map/ppermute | solution.py:310
  54.0 0.0 collective-permute-done.21.refs_2_
  54.0 0.3 collective-permute-start.20
  54.3 3.0 %collective-permute-start.22 = (f32[4,48,128]{2,1,0:T(8,128)S(1)}, f32[4,48,128]{2,1,0:T(8,128)S(1)}, u32[]{:S(2)}, u32[]{:S(2)}) collective-permute-start(f32[4,48,128]{2,1,0:T(8,128)S(1)} %collective-permute-done.21.refs_2_), channel_id=1, source_target_pairs={{0,7},{1,0},{2,1},{3,2},{4,3},{5,4},{6,5},{7,6},{8,15},{9,8},{10,9... | collective-permute-start | bytes 294920 | tf_op jit(solution)/shard_map/ppermute | solution.py:310
  57.3 0.3 chunks_1.3.refs_0_
  57.6 0.4 chunks_1.4.refs_0_
  58.0 0.4 chunks_1.5.total_ref
  58.3 1.6 %collective-permute-done.20.refs_0_ = f32[4,48,128]{2,1,0:T(8,128)S(1)} collective-permute-done((f32[4,48,128]{2,1,0:T(8,128)S(1)}, f32[4,48,128]{2,1,0:T(8,128)S(1)}, u32[]{:S(2)}, u32[]{:S(2)}) %collective-permute-start.20) | collective-permute-done | bytes 98336 | tf_op jit(solution)/shard_map/ppermute | solution.py:310
  59.9 0.3 last_1b.1
  60.3 0.7 %collective-permute-start.23 = (f32[64,512]{1,0:T(8,128)S(1)}, f32[64,512]{1,0:T(8,128)S(1)}, u32[]{:S(2)}, u32[]{:S(2)}) collective-permute-start(f32[64,512]{1,0:T(8,128)S(1)} %get-tuple-element.36), channel_id=1, source_target_pairs={{0,8},{8,0},{1,9},{9,1},{2,10},{10,2},{3,11},{11,3},{4,12},{12,4},... | collective-permute-start | bytes 393224 | tf_op jit(solution)/shard_map/ppermute | solution.py:314
  60.9 0.3 last_1a.1
  61.3 1.5 %collective-permute-start.19 = (f32[64,512]{1,0:T(8,128)S(1)}, f32[64,512]{1,0:T(8,128)S(1)}, u32[]{:S(2)}, u32[]{:S(2)}) collective-permute-start(f32[64,512]{1,0:T(8,128)S(1)} %get-tuple-element.34), channel_id=1, source_target_pairs={{0,8},{8,0},{1,9},{9,1},{2,10},{10,2},{3,11},{11,3},{4,12},{12,4},... | collective-permute-start | bytes 393224 | tf_op jit(solution)/shard_map/ppermute | solution.py:314
  62.8 0.6 stiff_merge.1.refs_0_.refs_1_
  63.4 0.8 %finish_0.1.refs_0_ = f32[2,64,1024]{2,1,0:T(8,128)} custom-call(f32[2,64,1024]{2,1,0:T(8,128)S(1)} %stiff_merge.1.refs_0_.refs_1_, f32[64,1024]{1,0:T(8,128)S(1)} %get-tuple-element.26.refs_1_, f32[64,1024]{1,0:T(8,128)S(1)} %collective-permute-done.10.refs_2_), custom_call_target="tpu_custom_call" | custom-call | tf_op jit(solution)/shard_map/finish_0/pallas_call | solution.py:296
  64.2 1.1 %collective-permute-done.23.refs_5_ = f32[64,512]{1,0:T(8,128)S(1)} collective-permute-done((f32[64,512]{1,0:T(8,128)S(1)}, f32[64,512]{1,0:T(8,128)S(1)}, u32[]{:S(2)}, u32[]{:S(2)}) %collective-permute-start.23) | collective-permute-done | bytes 131104 | tf_op jit(solution)/shard_map/ppermute | solution.py:314
  65.3 1.4 %collective-permute-done.19.refs_3_ = f32[64,512]{1,0:T(8,128)S(1)} collective-permute-done((f32[64,512]{1,0:T(8,128)S(1)}, f32[64,512]{1,0:T(8,128)S(1)}, u32[]{:S(2)}, u32[]{:S(2)}) %collective-permute-start.19) | collective-permute-done | bytes 131104 | tf_op jit(solution)/shard_map/ppermute | solution.py:314
  66.7 0.8 %finish_1.1 = f32[2,64,1024]{2,1,0:T(8,128)} custom-call(f32[2,64,1024]{2,1,0:T(8,128)} %finish_0.1.refs_0_, f32[2,64,1024]{2,1,0:T(8,128)S(1)} %stiff_merge.1.refs_0_.refs_1_, f32[64,512]{1,0:T(8,128)S(1)} %get-tuple-element.33.refs_2_, f32[64,512]{1,0:T(8,128)S(1)} %collective-permute-done.19.refs_3_, ...), custom_call_target="tpu_custom_call", output_to_operand_aliasing={{}: (0, {})} | custom-call | tf_op jit(solution)/shard_map/finish_1/pallas_call | solution.py:296
  (19 shorter events, 0.2 us)
Async XLA Ops:
  1.4 0.7 copy-start.1
  1.4 2.6 %collective-permute-start.1 = (f32[16,48,128]{2,1,0:T(8,128)S(1)}, f32[16,48,128]{2,1,0:T(8,128)S(1)}, u32[]{:S(2)}, u32[]{:S(2)}) collective-permute-start(f32[16,48,128]{2,1,0:T(8,128)S(1)} %get-tuple-element.21), channel_id=1, source_target_pairs={{0,16},{16,0},{32,48},{48,32},{64,80},{80,64},{96,112},{112,96},{1... | collective-permute-start | bytes 1179656 | tf_op jit(solution)/shard_map/ppermute | solution.py:314
  1.5 9.1 %collective-permute-start.11 = (f32[16,48,128]{2,1,0:T(8,128)S(1)}, f32[16,48,128]{2,1,0:T(8,128)S(1)}, u32[]{:S(2)}, u32[]{:S(2)}) collective-permute-start(f32[16,48,128]{2,1,0:T(8,128)S(1)} %get-tuple-element.28), channel_id=1, source_target_pairs={{0,16},{16,0},{32,48},{48,32},{64,80},{80,64},{96,112},{112,96},{1... | collective-permute-start | bytes 1179656 | tf_op jit(solution)/shard_map/ppermute | solution.py:314
  4.7 12.4 %collective-permute-start.3 = (f32[12,48,128]{2,1,0:T(8,128)S(1)}, f32[12,48,128]{2,1,0:T(8,128)S(1)}, u32[]{:S(2)}, u32[]{:S(2)}) collective-permute-start(f32[12,48,128]{2,1,0:T(8,128)S(1)} %get-tuple-element.25), channel_id=1, source_target_pairs={{0,7},{1,0},{2,1},{3,2},{4,3},{5,4},{6,5},{7,6},{8,15},{9,8},{10,9... | collective-permute-start | bytes 884744 | tf_op jit(solution)/shard_map/ppermute | solution.py:310
  10.6 10.6 %collective-permute-start.2 = (f32[11,48,128]{2,1,0:T(8,128)S(1)}, f32[11,48,128]{2,1,0:T(8,128)S(1)}, u32[]{:S(2)}, u32[]{:S(2)}) collective-permute-start(f32[11,48,128]{2,1,0:T(8,128)S(1)} %get-tuple-element.23.refs_0_), channel_id=1, source_target_pairs={{0,1},{1,2},{2,3},{3,4},{4,5},{5,6},{6,7},{7,0},{8,9},{9,10},{10,1... | collective-permute-start | bytes 811016 | tf_op jit(solution)/shard_map/ppermute | solution.py:310
  11.2 16.3 %collective-permute-start.12 = (f32[12,48,128]{2,1,0:T(8,128)S(1)}, f32[12,48,128]{2,1,0:T(8,128)S(1)}, u32[]{:S(2)}, u32[]{:S(2)}) collective-permute-start(f32[12,48,128]{2,1,0:T(8,128)S(1)} %get-tuple-element.30.refs_0_), channel_id=1, source_target_pairs={{0,1},{1,2},{2,3},{3,4},{4,5},{5,6},{6,7},{7,0},{8,9},{9,10},{10,1... | collective-permute-start | bytes 884744 | tf_op jit(solution)/shard_map/ppermute | solution.py:310
  17.1 15.8 %collective-permute-start.5 = (f32[11,48,128]{2,1,0:T(8,128)S(1)}, f32[11,48,128]{2,1,0:T(8,128)S(1)}, u32[]{:S(2)}, u32[]{:S(2)}) collective-permute-start(f32[11,48,128]{2,1,0:T(8,128)S(1)} %slice.53), channel_id=1, source_target_pairs={{0,7},{1,0},{2,1},{3,2},{4,3},{5,4},{6,5},{7,6},{8,15},{9,8},{10,9... | collective-permute-start | bytes 811016 | tf_op jit(solution)/shard_map/ppermute | solution.py:310
  21.2 15.1 %copy-start = (f32[4,64,1024]{2,1,0:T(8,128)S(1)}, f32[4,64,1024]{2,1,0:T(8,128)}, u32[]{:S(2)}) copy-start(f32[4,64,1024]{2,1,0:T(8,128)} %b_hbm.3) | copy-start | bytes 3145732
  21.2 11.6 %collective-permute-start.4 = (f32[10,48,128]{2,1,0:T(8,128)S(1)}, f32[10,48,128]{2,1,0:T(8,128)S(1)}, u32[]{:S(2)}, u32[]{:S(2)}) collective-permute-start(f32[10,48,128]{2,1,0:T(8,128)S(1)} %slice.52), channel_id=1, source_target_pairs={{0,1},{1,2},{2,3},{3,4},{4,5},{5,6},{6,7},{7,0},{8,9},{9,10},{10,1... | collective-permute-start | bytes 737288 | tf_op jit(solution)/shard_map/ppermute | solution.py:310
  21.3 14.9 %collective-permute-start.13 = (f32[11,48,128]{2,1,0:T(8,128)S(1)}, f32[11,48,128]{2,1,0:T(8,128)S(1)}, u32[]{:S(2)}, u32[]{:S(2)}) collective-permute-start(f32[11,48,128]{2,1,0:T(8,128)S(1)} %get-tuple-element.32), channel_id=1, source_target_pairs={{0,7},{1,0},{2,1},{3,2},{4,3},{5,4},{6,5},{7,6},{8,15},{9,8},{10,9... | collective-permute-start | bytes 811016 | tf_op jit(solution)/shard_map/ppermute | solution.py:310
  27.5 14.7 %collective-permute-start.14 = (f32[11,48,128]{2,1,0:T(8,128)S(1)}, f32[11,48,128]{2,1,0:T(8,128)S(1)}, u32[]{:S(2)}, u32[]{:S(2)}) collective-permute-start(f32[11,48,128]{2,1,0:T(8,128)S(1)} %slice.58), channel_id=1, source_target_pairs={{0,1},{1,2},{2,3},{3,4},{4,5},{5,6},{6,7},{7,0},{8,9},{9,10},{10,1... | collective-permute-start | bytes 811016 | tf_op jit(solution)/shard_map/ppermute | solution.py:310
  32.8 9.3 %collective-permute-start.6 = (f32[9,48,128]{2,1,0:T(8,128)S(1)}, f32[9,48,128]{2,1,0:T(8,128)S(1)}, u32[]{:S(2)}, u32[]{:S(2)}) collective-permute-start(f32[9,48,128]{2,1,0:T(8,128)S(1)} %slice.54), channel_id=1, source_target_pairs={{0,1},{1,2},{2,3},{3,4},{4,5},{5,6},{6,7},{7,0},{8,9},{9,10},{10,1... | collective-permute-start | bytes 663560 | tf_op jit(solution)/shard_map/ppermute | solution.py:310
  32.9 9.4 %collective-permute-start.7 = (f32[10,48,128]{2,1,0:T(8,128)S(1)}, f32[10,48,128]{2,1,0:T(8,128)S(1)}, u32[]{:S(2)}, u32[]{:S(2)}) collective-permute-start(f32[10,48,128]{2,1,0:T(8,128)S(1)} %slice.55), channel_id=1, source_target_pairs={{0,7},{1,0},{2,1},{3,2},{4,3},{5,4},{6,5},{7,6},{8,15},{9,8},{10,9... | collective-permute-start | bytes 737288 | tf_op jit(solution)/shard_map/ppermute | solution.py:310
  36.2 9.6 %collective-permute-start.15 = (f32[10,48,128]{2,1,0:T(8,128)S(1)}, f32[10,48,128]{2,1,0:T(8,128)S(1)}, u32[]{:S(2)}, u32[]{:S(2)}) collective-permute-start(f32[10,48,128]{2,1,0:T(8,128)S(1)} %slice.59), channel_id=1, source_target_pairs={{0,7},{1,0},{2,1},{3,2},{4,3},{5,4},{6,5},{7,6},{8,15},{9,8},{10,9... | collective-permute-start | bytes 737288 | tf_op jit(solution)/shard_map/ppermute | solution.py:310
  37.0 25.8 %collective-permute-start = (f32[2,64,1024]{2,1,0:T(8,128)S(1)}, f32[2,64,1024]{2,1,0:T(8,128)S(1)}, u32[]{:S(2)}, u32[]{:S(2)}) collective-permute-start(f32[2,64,1024]{2,1,0:T(8,128)S(1)} %stiff_out.1), channel_id=1, source_target_pairs={{0,16},{16,0},{32,48},{48,32},{64,80},{80,64},{96,112},{112,96},{1... | collective-permute-start | bytes 1572872 | tf_op jit(solution)/shard_map/ppermute | solution.py:314
  42.1 6.5 %collective-permute-start.8 = (f32[4,48,128]{2,1,0:T(8,128)S(1)}, f32[4,48,128]{2,1,0:T(8,128)S(1)}, u32[]{:S(2)}, u32[]{:S(2)}) collective-permute-start(f32[4,48,128]{2,1,0:T(8,128)S(1)} %slice.56), channel_id=1, source_target_pairs={{0,1},{1,2},{2,3},{3,4},{4,5},{5,6},{6,7},{7,0},{8,9},{9,10},{10,1... | collective-permute-start | bytes 294920 | tf_op jit(solution)/shard_map/ppermute | solution.py:310
  42.2 9.6 %collective-permute-start.16 = (f32[6,48,128]{2,1,0:T(8,128)S(1)}, f32[6,48,128]{2,1,0:T(8,128)S(1)}, u32[]{:S(2)}, u32[]{:S(2)}) collective-permute-start(f32[6,48,128]{2,1,0:T(8,128)S(1)} %slice.60), channel_id=1, source_target_pairs={{0,1},{1,2},{2,3},{3,4},{4,5},{5,6},{6,7},{7,0},{8,9},{9,10},{10,1... | collective-permute-start | bytes 442376 | tf_op jit(solution)/shard_map/ppermute | solution.py:310
  42.4 7.6 %collective-permute-start.9 = (f32[5,48,128]{2,1,0:T(8,128)S(1)}, f32[5,48,128]{2,1,0:T(8,128)S(1)}, u32[]{:S(2)}, u32[]{:S(2)}) collective-permute-start(f32[5,48,128]{2,1,0:T(8,128)S(1)} %slice.57), channel_id=1, source_target_pairs={{0,7},{1,0},{2,1},{3,2},{4,3},{5,4},{6,5},{7,6},{8,15},{9,8},{10,9... | collective-permute-start | bytes 368648 | tf_op jit(solution)/shard_map/ppermute | solution.py:310
  45.8 8.4 %collective-permute-start.17 = (f32[5,48,128]{2,1,0:T(8,128)S(1)}, f32[5,48,128]{2,1,0:T(8,128)S(1)}, u32[]{:S(2)}, u32[]{:S(2)}) collective-permute-start(f32[5,48,128]{2,1,0:T(8,128)S(1)} %slice.61), channel_id=1, source_target_pairs={{0,7},{1,0},{2,1},{3,2},{4,3},{5,4},{6,5},{7,6},{8,15},{9,8},{10,9... | collective-permute-start | bytes 368648 | tf_op jit(solution)/shard_map/ppermute | solution.py:310
  48.6 5.4 %collective-permute-start.21 = (f32[4,48,128]{2,1,0:T(8,128)S(1)}, f32[4,48,128]{2,1,0:T(8,128)S(1)}, u32[]{:S(2)}, u32[]{:S(2)}) collective-permute-start(f32[4,48,128]{2,1,0:T(8,128)S(1)} %slice.64), channel_id=1, source_target_pairs={{0,7},{1,0},{2,1},{3,2},{4,3},{5,4},{6,5},{7,6},{8,15},{9,8},{10,9... | collective-permute-start | bytes 294920 | tf_op jit(solution)/shard_map/ppermute | solution.py:310
  50.3 13.2 %collective-permute-start.10 = (f32[64,1024]{1,0:T(8,128)S(1)}, f32[64,1024]{1,0:T(8,128)S(1)}, u32[]{:S(2)}, u32[]{:S(2)}) collective-permute-start(f32[64,1024]{1,0:T(8,128)S(1)} %get-tuple-element.27), channel_id=1, source_target_pairs={{0,8},{8,0},{1,9},{9,1},{2,10},{10,2},{3,11},{11,3},{4,12},{12,4},... | collective-permute-start | bytes 786440 | tf_op jit(solution)/shard_map/ppermute | solution.py:314
  51.9 8.0 %collective-permute-start.18 = (f32[5,48,128]{2,1,0:T(8,128)S(1)}, f32[5,48,128]{2,1,0:T(8,128)S(1)}, u32[]{:S(2)}, u32[]{:S(2)}) collective-permute-start(f32[5,48,128]{2,1,0:T(8,128)S(1)} %slice.62), channel_id=1, source_target_pairs={{0,1},{1,2},{2,3},{3,4},{4,5},{5,6},{6,7},{7,0},{8,9},{9,10},{10,1... | collective-permute-start | bytes 368648 | tf_op jit(solution)/shard_map/ppermute | solution.py:310
  54.0 5.9 %collective-permute-start.20 = (f32[4,48,128]{2,1,0:T(8,128)S(1)}, f32[4,48,128]{2,1,0:T(8,128)S(1)}, u32[]{:S(2)}, u32[]{:S(2)}) collective-permute-start(f32[4,48,128]{2,1,0:T(8,128)S(1)} %slice.63), channel_id=1, source_target_pairs={{0,1},{1,2},{2,3},{3,4},{4,5},{5,6},{6,7},{7,0},{8,9},{9,10},{10,1... | collective-permute-start | bytes 294920 | tf_op jit(solution)/shard_map/ppermute | solution.py:310
  54.3 5.6 %collective-permute-start.22 = (f32[4,48,128]{2,1,0:T(8,128)S(1)}, f32[4,48,128]{2,1,0:T(8,128)S(1)}, u32[]{:S(2)}, u32[]{:S(2)}) collective-permute-start(f32[4,48,128]{2,1,0:T(8,128)S(1)} %collective-permute-done.21.refs_2_), channel_id=1, source_target_pairs={{0,7},{1,0},{2,1},{3,2},{4,3},{5,4},{6,5},{7,6},{8,15},{9,8},{10,9... | collective-permute-start | bytes 294920 | tf_op jit(solution)/shard_map/ppermute | solution.py:310
  60.3 5.1 %collective-permute-start.23 = (f32[64,512]{1,0:T(8,128)S(1)}, f32[64,512]{1,0:T(8,128)S(1)}, u32[]{:S(2)}, u32[]{:S(2)}) collective-permute-start(f32[64,512]{1,0:T(8,128)S(1)} %get-tuple-element.36), channel_id=1, source_target_pairs={{0,8},{8,0},{1,9},{9,1},{2,10},{10,2},{3,11},{11,3},{4,12},{12,4},... | collective-permute-start | bytes 393224 | tf_op jit(solution)/shard_map/ppermute | solution.py:314
  61.3 5.4 %collective-permute-start.19 = (f32[64,512]{1,0:T(8,128)S(1)}, f32[64,512]{1,0:T(8,128)S(1)}, u32[]{:S(2)}, u32[]{:S(2)}) collective-permute-start(f32[64,512]{1,0:T(8,128)S(1)} %get-tuple-element.34), channel_id=1, source_target_pairs={{0,8},{8,0},{1,9},{9,1},{2,10},{10,2},{3,11},{11,3},{4,12},{12,4},... | collective-permute-start | bytes 393224 | tf_op jit(solution)/shard_map/ppermute | solution.py:314

commit v6 on v5

--- a/solution.py
+++ b/solution.py
@@ -16,7 +16,7 @@
 
 
 def hops(slot):
-    return (3, 4) if slot == 0 else (4, 3)
+    return (4, 3) if slot == 0 else (3, 4)
 
 
 def locate(plan, group, wanted, home):
@@ -93,7 +93,6 @@
     total, depth, _ = arrived.shape
     up, down = hops(slot)
     blocks = total // 2
-    half = blocks // 2
 
     def kernel(plan_ref, arrived_ref, local_ref, up_ref, down_ref, own_ref):
         group = lax.axis_index("group")
@@ -101,12 +100,7 @@
 
         def put(source):
             up_ref[...] = source[0 : up + blocks]
-            if slot == 0:
-                down_ref[...] = source[up : total - 1]
-            else:
-                down_ref[0:half] = source[up + half : up + blocks]
-                down_ref[half:blocks] = source[up : up + half]
-                down_ref[blocks:] = source[up + blocks : total - 1]
+            down_ref[...] = source[up : total - 1]
             own_ref[...] = source[total - 1]
 
         @pl.when(here)
@@ -245,7 +239,6 @@
         out_shape=jax.ShapeDtypeStruct((LANES, width), jnp.float32),
         in_specs=[VMEM] * (n_given + len(arrays)),
         out_specs=VMEM,
-        input_output_aliases={0: 0} if n_given else {},
         compiler_params=PARAMS,
         cost_estimate=pl.CostEstimate(flops=2 * 144 * 128 * 1024, bytes_accessed=1 << 20, transcendentals=0),
         name=name,
@@ -312,6 +305,10 @@
 
 def swapped(array, axis):
     return lax.ppermute(array, axis, [(i, i ^ 1) for i in range(lax.axis_size(axis))])
+
+
+def after(array, *earlier):
+    return lax.optimization_barrier((array, *earlier))[0]
 
 
 def up(array):
@@ -340,42 +337,45 @@
     def run(first):
         return list(range(first, first + blocks))
 
-    turned = list(range(half, blocks)) + list(range(half))
+    left = list(range(half))
     u0, d0, u1, d1 = up(up0), down(down0), up(up1), down(down1)
-    total0 = accumulate(None, [(up0, run(3), own0, None)], width, "chunks_0")
-    total1 = accumulate(None, [(up1, run(4), own1, None)], width, "chunks_1")
     uu0, dd0 = up(u0[1:]), down(d0[:-1])
-    total0 = accumulate(total0, [(u0, run(3), u0, 0), (d0, run(0), d0, blocks + 3)], width, "chunks_0")
     uu1, dd1 = up(u1[1:]), down(d1[:-1])
-    total1 = accumulate(total1, [(u1, run(4), u1, 0), (d1, turned, d1, blocks + 2)], width, "chunks_1")
+    total0 = accumulate(
+        None, [(up0, run(4), own0, None), (u0, run(4), u0, 0), (d0, run(0), d0, blocks + 2)], width, "chunks_0"
+    )
     uuu0, ddd0 = up(uu0[1:]), down(dd0[:-1])
-    total0 = accumulate(total0, [(uu0, run(2), uu0, 0), (dd0, run(0), dd0, blocks + 2)], width, "chunks_0")
-    uuu1a, ddd1a = up(uu1[1 : half + 3]), down(dd1[half : blocks + 1])
-    total1 = accumulate(total1, [(uu1, run(3), uu1, 0), (dd1, turned, dd1, blocks + 1)], width, "chunks_1")
-    far0a, far0b = up(uuu0[1 : half + 1]), down(ddd0[half : blocks + 1])
-    uuu1b, ddd1b = up(uu1[half + 3 :]), down(dd1[:half])
-    far1a, far1b = up(uuu1a[1:]), down(ddd1b)
-    left = list(range(half))
-    wide = width // 2
-    total0 = accumulate(total0, [(uuu0, run(1), uuu0, 0), (ddd0, run(0), ddd0, blocks + 1)], width, "chunks_0")
+    total1 = accumulate(
+        None, [(up1, run(3), own1, None), (u1, run(3), u1, 0), (d1, run(0), d1, blocks + 3)], width, "chunks_1"
+    )
+    uuu1a, ddd1b = up(after(uu1[1 : half + 2], total0)), down(dd1[half : blocks + 2])
+    ready0 = accumulate(total0, [(uu0, run(3), uu0, 0), (dd0, run(0), dd0, blocks + 1)], width, "chunks_0")
+    far0a, far0b = up(after(uuu0[1 : half + 2], total1)), down(ddd0[half:blocks])
+    far1a, far1b = up(uuu1a[1:]), down(after(ddd1b[: half + 1], ready0))
+    ready1 = accumulate(total1, [(uu1, run(2), uu1, 0), (dd1, run(0), dd1, blocks + 2)], width, "chunks_1")
+    uuu1b, ddd1a = up(after(uu1[half + 2 :], ready1)), down(dd1[:half])
     send0, keep0 = last_chunks(
-        total0, [((far0a, far0b), left + left, far0b, half)], 0, width, "last_0"
+        ready0,
+        [
+            (uuu0, run(2), uuu0, 0),
+            (ddd0, run(0), ddd0, blocks),
+            ((far0a, far0b), [1, 2, 3, 4, 0, 1, 2, 3], far0a, 0),
+        ],
+        0, width, "last_0",
     )
     other0 = swapped(send0, "tile_0")
-    send1a, keep1a = last_chunks(
-        total1,
-        [(uuu1a, run(2)[:half], uuu1a, 0), (ddd1a, left, ddd1a, half), (far1a, run(1)[:half], far1a, 0)],
-        0, wide, "last_1a",
+    send1, keep1 = last_chunks(
+        ready1,
+        [
+            ((uuu1a, uuu1b), [1, 2, 3, 4, 0, 1, 2, 3], uuu1a, 0),
+            ((ddd1a, ddd1b), left + left, ddd1b, half + 1),
+            ((far1a, far1b), left + left, far1b, half),
+        ],
+        0, width, "last_1",
     )
-    other1a = swapped(send1a, "tile_0")
-    send1b, keep1b = last_chunks(
-        total1,
-        [(uuu1b, left, uuu1a, 0), (ddd1b, left, ddd1a, half), (far1b, left, far1a, 0)],
-        wide, wide, "last_1b",
-    )
-    other1b = swapped(send1b, "tile_0")
+    other1 = swapped(send1, "tile_0")
     result = finish(None, stiff, [(keep0, other0)], 0)
-    return finish(result, stiff, [(keep1a, other1a), (keep1b, other1b)], 1)
+    return finish(result, stiff, [(keep1, other1)], 1)
 
 
 def solution(mesh):

time: 67.8 us -> 66.8 us (0.985)
  waiting for transfers between devices: 23.9 us -> 20.8 us
  starting transfers between devices: 32.4 us -> 35.3 us
  Pallas kernels: 10.7 us -> 9.82 us
    ppermute x18, waiting for transfers between devices: 21.4 us -> 15.6 us  [shifted(): lax.ppermute(array, axis, [(i, (i + distance) % size) for i in range(size)])]
    ppermute x18, starting transfers between devices: 27.9 us -> 31.6 us  [shifted(): lax.ppermute(array, axis, [(i, (i + distance) % size) for i in range(size)])]
    ppermute x6 -> x5, waiting for transfers between devices: 2.5 us -> 5.22 us  [swapped(): lax.ppermute(array, axis, [(i, i ^ 1) for i in range(lax.axis_size(axis))])]
    pallas_call x7 -> x4, Pallas kernels: 2.33 us -> 1.53 us  [accumulate(): pl.pallas_call(kernel, out_shape=jax.ShapeDtypeStruct((LANES, width), jnp...]
    ppermute x6 -> x5, starting transfers between devices: 4.46 us -> 3.75 us  [swapped(): lax.ppermute(array, axis, [(i, i ^ 1) for i in range(lax.axis_size(axis))])]
  transfers between devices with their start and end apart: 24 -> 23, of which waited for: 9 -> 9; matrix products, arithmetic and copies ran while one was open for 0% -> 0% of each run, Pallas kernels for 13% -> 11%
where the time goes in v6:
time: 66.8 us; the launch traced here: 66.7 us
  starting transfers between devices  35.3 us (53%)
  waiting for transfers between devices  20.8 us (31%)
  Pallas kernels  9.82 us (15%)
    ppermute x18, starting transfers between devices, shifted(): lax.ppermute(array, axis, [(i, (i + distance) % size) for i in range(size)])  31.6 us
    ppermute x18, waiting for transfers between devices, shifted(): lax.ppermute(array, axis, [(i, (i + distance) % size) for i in range(size)])  15.6 us
    ppermute x5, waiting for transfers between devices, swapped(): lax.ppermute(array, axis, [(i, i ^ 1) for i in range(lax.axis_size(axis))])  5.22 us
    ppermute x5, starting transfers between devices, swapped(): lax.ppermute(array, axis, [(i, i ^ 1) for i in range(lax.axis_size(axis))])  3.75 us
    pallas_call x2, Pallas kernels, pack(): pl.pallas_call(kernel, out_shape=(packet, packet), in_specs=[HBM if for_p...  3.38 us
    pallas_call x4, Pallas kernels, accumulate(): pl.pallas_call(kernel, out_shape=jax.ShapeDtypeStruct((LANES, width), jnp...  1.53 us
    pallas_call x2, Pallas kernels, finish(): pl.pallas_call(kernel, out_shape=jax.ShapeDtypeStruct((OWN, rows, width),...  1.5 us
  transfers between devices with their start and end apart: 23, of which 9 were waited for; matrix products, arithmetic and copies ran while one was open for 0% of the time, Pallas kernels for 11%

profile of v6, /device:TPU:24, one launch (start us, length us, event | category | flops | bytes accessed | tf_op | source)
XLA Modules:
  0.0 66.7 jit_solution(2084703277413376311)
XLA Ops:
  0.0 1.4 %pack_partner.1 = (f32[16,48,128]{2,1,0:T(8,128)S(1)}, f32[16,48,128]{2,1,0:T(8,128)S(1)}) custom-call(s32[64]{0:T(128)} %plan_ref.7, f32[4,48,1024]{2,1,0:T(8,128)} %bitcast.1, f32[4,48,1024]{2,1,0:T(8,128)} %x_hbm.3), custom_call_target="tpu_custom_call" | custom-call | tf_op jit(solution)/shard_map/pack_partner/pallas_call | solution.py:74
  1.4 0.0 copy-start.1
  1.4 0.1 collective-permute-start.1
  1.5 0.5 collective-permute-start.8
  2.0 0.0 copy-done.1
  2.1 2.0 %pack_own.1 = (f32[16,48,128]{2,1,0:T(8,128)S(1)}, f32[16,48,128]{2,1,0:T(8,128)S(1)}) custom-call(s32[64]{0:T(128)S(1)} %copy-done.1, f32[4,48,1024]{2,1,0:T(8,128)} %bitcast.2, f32[4,48,1024]{2,1,0:T(8,128)} %x_hbm.3), custom_call_target="tpu_custom_call" | custom-call | tf_op jit(solution)/shard_map/pack_own/pallas_call | solution.py:74
  4.1 0.0 collective-permute-done.1.arrived_ref
  4.1 0.6 merge_0.1
  4.7 2.0 %collective-permute-start.2 = (f32[12,48,128]{2,1,0:T(8,128)S(1)}, f32[12,48,128]{2,1,0:T(8,128)S(1)}, u32[]{:S(2)}, u32[]{:S(2)}) collective-permute-start(f32[12,48,128]{2,1,0:T(8,128)S(1)} %get-tuple-element.25.refs_0_), channel_id=1, source_target_pairs={{0,1},{1,2},{2,3},{3,4},{4,5},{5,6},{6,7},{7,0},{8,9},{9,10},{10,1... | collective-permute-start | bytes 884744 | tf_op jit(solution)/shard_map/ppermute | solution.py:303
  6.7 4.0 %collective-permute-start.3 = (f32[11,48,128]{2,1,0:T(8,128)S(1)}, f32[11,48,128]{2,1,0:T(8,128)S(1)}, u32[]{:S(2)}, u32[]{:S(2)}) collective-permute-start(f32[11,48,128]{2,1,0:T(8,128)S(1)} %get-tuple-element.27), channel_id=1, source_target_pairs={{0,7},{1,0},{2,1},{3,2},{4,3},{5,4},{6,5},{7,6},{8,15},{9,8},{10,9... | collective-permute-start | bytes 811016 | tf_op jit(solution)/shard_map/ppermute | solution.py:303
  10.7 0.0 collective-permute-done.8.arrived_ref
  10.7 0.6 merge_1.1
  11.3 2.0 %collective-permute-start.10 = (f32[12,48,128]{2,1,0:T(8,128)S(1)}, f32[12,48,128]{2,1,0:T(8,128)S(1)}, u32[]{:S(2)}, u32[]{:S(2)}) collective-permute-start(f32[12,48,128]{2,1,0:T(8,128)S(1)} %get-tuple-element.32), channel_id=1, source_target_pairs={{0,7},{1,0},{2,1},{3,2},{4,3},{5,4},{6,5},{7,6},{8,15},{9,8},{10,9... | collective-permute-start | bytes 884744 | tf_op jit(solution)/shard_map/ppermute | solution.py:303
  13.3 0.1 collective-permute-start.9
  13.4 5.0 %collective-permute-done.2.refs_2_ = f32[12,48,128]{2,1,0:T(8,128)S(1)} collective-permute-done((f32[12,48,128]{2,1,0:T(8,128)S(1)}, f32[12,48,128]{2,1,0:T(8,128)S(1)}, u32[]{:S(2)}, u32[]{:S(2)}) %collective-permute-start.2) | collective-permute-done | bytes 294944 | tf_op jit(solution)/shard_map/ppermute | solution.py:303
  18.4 0.1 collective-permute-start.4
  18.5 0.0 collective-permute-done.3.refs_3_
  18.6 0.0 copy-start
  18.6 3.3 %collective-permute-start.5 = (f32[10,48,128]{2,1,0:T(8,128)S(1)}, f32[10,48,128]{2,1,0:T(8,128)S(1)}, u32[]{:S(2)}, u32[]{:S(2)}) collective-permute-start(f32[10,48,128]{2,1,0:T(8,128)S(1)} %slice.57), channel_id=1, source_target_pairs={{0,7},{1,0},{2,1},{3,2},{4,3},{5,4},{6,5},{7,6},{8,15},{9,8},{10,9... | collective-permute-start | bytes 737288 | tf_op jit(solution)/shard_map/ppermute | solution.py:303
  21.9 2.0 %collective-permute-done.10.refs_3_ = f32[12,48,128]{2,1,0:T(8,128)S(1)} collective-permute-done((f32[12,48,128]{2,1,0:T(8,128)S(1)}, f32[12,48,128]{2,1,0:T(8,128)S(1)}, u32[]{:S(2)}, u32[]{:S(2)}) %collective-permute-start.10) | collective-permute-done | bytes 294944 | tf_op jit(solution)/shard_map/ppermute | solution.py:303
  23.9 3.8 %collective-permute-start.15 = (f32[11,48,128]{2,1,0:T(8,128)S(1)}, f32[11,48,128]{2,1,0:T(8,128)S(1)}, u32[]{:S(2)}, u32[]{:S(2)}) collective-permute-start(f32[11,48,128]{2,1,0:T(8,128)S(1)} %slice.63), channel_id=1, source_target_pairs={{0,7},{1,0},{2,1},{3,2},{4,3},{5,4},{6,5},{7,6},{8,15},{9,8},{10,9... | collective-permute-start | bytes 811016 | tf_op jit(solution)/shard_map/ppermute | solution.py:303
  27.7 0.0 collective-permute-done.9.refs_2_
  27.7 0.1 collective-permute-start.14
  27.8 1.6 %collective-permute-done.4.refs_1_ = f32[11,48,128]{2,1,0:T(8,128)S(1)} collective-permute-done((f32[11,48,128]{2,1,0:T(8,128)S(1)}, f32[11,48,128]{2,1,0:T(8,128)S(1)}, u32[]{:S(2)}, u32[]{:S(2)}) %collective-permute-start.4) | collective-permute-done | bytes 270368 | tf_op jit(solution)/shard_map/ppermute | solution.py:303
  29.4 0.1 collective-permute-start.6
  29.5 0.0 collective-permute-done.5.refs_2_
  29.6 3.4 %collective-permute-start.7 = (f32[9,48,128]{2,1,0:T(8,128)S(1)}, f32[9,48,128]{2,1,0:T(8,128)S(1)}, u32[]{:S(2)}, u32[]{:S(2)}) collective-permute-start(f32[9,48,128]{2,1,0:T(8,128)S(1)} %slice.59), channel_id=1, source_target_pairs={{0,7},{1,0},{2,1},{3,2},{4,3},{5,4},{6,5},{7,6},{8,15},{9,8},{10,9... | collective-permute-start | bytes 663560 | tf_op jit(solution)/shard_map/ppermute | solution.py:303
  32.9 2.0 %collective-permute-done.15.refs_2_ = f32[11,48,128]{2,1,0:T(8,128)S(1)} collective-permute-done((f32[11,48,128]{2,1,0:T(8,128)S(1)}, f32[11,48,128]{2,1,0:T(8,128)S(1)}, u32[]{:S(2)}, u32[]{:S(2)}) %collective-permute-start.15) | collective-permute-done | bytes 270368 | tf_op jit(solution)/shard_map/ppermute | solution.py:303
  35.0 3.8 %collective-permute-start.19 = (f32[6,48,128]{2,1,0:T(8,128)S(1)}, f32[6,48,128]{2,1,0:T(8,128)S(1)}, u32[]{:S(2)}, u32[]{:S(2)}) collective-permute-start(f32[6,48,128]{2,1,0:T(8,128)S(1)} %slice.67), channel_id=1, source_target_pairs={{0,7},{1,0},{2,1},{3,2},{4,3},{5,4},{6,5},{7,6},{8,15},{9,8},{10,9... | collective-permute-start | bytes 442376 | tf_op jit(solution)/shard_map/ppermute | solution.py:303
  38.7 0.0 copy-done
  38.7 0.6 stiff_out.1
  39.4 0.1 collective-permute-start
  39.5 0.4 chunks_1.2.refs_0_
  39.9 0.4 chunks_0.2.refs_0_
  40.3 0.0 collective-permute-done.14.refs_1_
  40.3 0.3 collective-permute-start.16
  40.6 0.0 collective-permute-done.6.refs_0_
  40.6 0.1 collective-permute-start.11
  40.7 0.0 collective-permute-done.7.refs_1_
  40.8 3.3 %collective-permute-start.12 = (f32[4,48,128]{2,1,0:T(8,128)S(1)}, f32[4,48,128]{2,1,0:T(8,128)S(1)}, u32[]{:S(2)}, u32[]{:S(2)}) collective-permute-start(f32[4,48,128]{2,1,0:T(8,128)S(1)} %slice.61), channel_id=1, source_target_pairs={{0,7},{1,0},{2,1},{3,2},{4,3},{5,4},{6,5},{7,6},{8,15},{9,8},{10,9... | collective-permute-start | bytes 294920 | tf_op jit(solution)/shard_map/ppermute | solution.py:303
  44.1 0.3 chunks_0.3.total_ref
  44.4 0.0 collective-permute-done.19.refs_3_
  44.4 2.1 %collective-permute-start.21 = (f32[5,48,128]{2,1,0:T(8,128)S(1)}, f32[5,48,128]{2,1,0:T(8,128)S(1)}, u32[]{:S(2)}, u32[]{:S(2)}) collective-permute-start(f32[5,48,128]{2,1,0:T(8,128)S(1)} %slice.69), channel_id=1, source_target_pairs={{0,7},{1,0},{2,1},{3,2},{4,3},{5,4},{6,5},{7,6},{8,15},{9,8},{10,9... | collective-permute-start | bytes 368648 | tf_op jit(solution)/shard_map/ppermute | solution.py:303
  46.5 0.3 chunks_1.3.total_ref
  46.9 1.0 %collective-permute-done.16.refs_0_ = f32[5,48,128]{2,1,0:T(8,128)S(1)} collective-permute-done((f32[5,48,128]{2,1,0:T(8,128)S(1)}, f32[5,48,128]{2,1,0:T(8,128)S(1)}, u32[]{:S(2)}, u32[]{:S(2)}) %collective-permute-start.16) | collective-permute-done | bytes 122912 | tf_op jit(solution)/shard_map/ppermute | solution.py:303
  47.9 0.0 collective-permute-start.17
  47.9 0.0 collective-permute-done.12.refs_3_
  47.9 3.3 %collective-permute-start.18 = (f32[4,48,128]{2,1,0:T(8,128)S(1)}, f32[4,48,128]{2,1,0:T(8,128)S(1)}, u32[]{:S(2)}, u32[]{:S(2)}) collective-permute-start(f32[4,48,128]{2,1,0:T(8,128)S(1)} %slice.66), channel_id=1, source_target_pairs={{0,7},{1,0},{2,1},{3,2},{4,3},{5,4},{6,5},{7,6},{8,15},{9,8},{10,9... | collective-permute-start | bytes 294920 | tf_op jit(solution)/shard_map/ppermute | solution.py:303
  51.2 0.0 collective-permute-done.11.refs_2_
  51.2 0.0 collective-permute-start.20
  51.3 0.5 last_0.1
  51.7 2.0 %collective-permute-done.17.refs_1_ = f32[4,48,128]{2,1,0:T(8,128)S(1)} collective-permute-done((f32[4,48,128]{2,1,0:T(8,128)S(1)}, f32[4,48,128]{2,1,0:T(8,128)S(1)}, u32[]{:S(2)}, u32[]{:S(2)}) %collective-permute-start.17) | collective-permute-done | bytes 98336 | tf_op jit(solution)/shard_map/ppermute | solution.py:303
  53.7 1.5 %collective-permute-start.13 = (f32[64,1024]{1,0:T(8,128)S(1)}, f32[64,1024]{1,0:T(8,128)S(1)}, u32[]{:S(2)}, u32[]{:S(2)}) collective-permute-start(f32[64,1024]{1,0:T(8,128)S(1)} %get-tuple-element.35), channel_id=1, source_target_pairs={{0,8},{8,0},{1,9},{9,1},{2,10},{10,2},{3,11},{11,3},{4,12},{12,4},... | collective-permute-start | bytes 786440 | tf_op jit(solution)/shard_map/ppermute | solution.py:307
  55.2 0.0 collective-permute-done.18.refs_2_
  55.2 1.8 %collective-permute-done.20.refs_4_ = f32[4,48,128]{2,1,0:T(8,128)S(1)} collective-permute-done((f32[4,48,128]{2,1,0:T(8,128)S(1)}, f32[4,48,128]{2,1,0:T(8,128)S(1)}, u32[]{:S(2)}, u32[]{:S(2)}) %collective-permute-start.20) | collective-permute-done | bytes 98336 | tf_op jit(solution)/shard_map/ppermute | solution.py:303
  57.1 0.0 collective-permute-done.21.refs_5_
  57.1 0.5 last_1.1
  57.6 1.6 %collective-permute-start.22 = (f32[64,1024]{1,0:T(8,128)S(1)}, f32[64,1024]{1,0:T(8,128)S(1)}, u32[]{:S(2)}, u32[]{:S(2)}) collective-permute-start(f32[64,1024]{1,0:T(8,128)S(1)} %get-tuple-element.40), channel_id=1, source_target_pairs={{0,8},{8,0},{1,9},{9,1},{2,10},{10,2},{3,11},{11,3},{4,12},{12,4},... | collective-permute-start | bytes 786440 | tf_op jit(solution)/shard_map/ppermute | solution.py:307
  59.1 0.0 collective-permute-done.arrived_ref
  59.1 0.6 stiff_merge.1.refs_0_.refs_1_
  59.8 2.7 %collective-permute-done.13.refs_2_ = f32[64,1024]{1,0:T(8,128)S(1)} collective-permute-done((f32[64,1024]{1,0:T(8,128)S(1)}, f32[64,1024]{1,0:T(8,128)S(1)}, u32[]{:S(2)}, u32[]{:S(2)}) %collective-permute-start.13) | collective-permute-done | bytes 262176 | tf_op jit(solution)/shard_map/ppermute | solution.py:307
  62.5 0.7 %finish_0.1.refs_0_ = f32[2,64,1024]{2,1,0:T(8,128)} custom-call(f32[2,64,1024]{2,1,0:T(8,128)S(1)} %stiff_merge.1.refs_0_.refs_1_, f32[64,1024]{1,0:T(8,128)S(1)} %get-tuple-element.34.refs_1_, f32[64,1024]{1,0:T(8,128)S(1)} %collective-permute-done.13.refs_2_), custom_call_target="tpu_custom_call" | custom-call | tf_op jit(solution)/shard_map/finish_0/pallas_call | solution.py:289
  63.2 2.5 %collective-permute-done.22.refs_3_ = f32[64,1024]{1,0:T(8,128)S(1)} collective-permute-done((f32[64,1024]{1,0:T(8,128)S(1)}, f32[64,1024]{1,0:T(8,128)S(1)}, u32[]{:S(2)}, u32[]{:S(2)}) %collective-permute-start.22) | collective-permute-done | bytes 262176 | tf_op jit(solution)/shard_map/ppermute | solution.py:307
  65.8 0.7 %finish_1.1 = f32[2,64,1024]{2,1,0:T(8,128)} custom-call(f32[2,64,1024]{2,1,0:T(8,128)} %finish_0.1.refs_0_, f32[2,64,1024]{2,1,0:T(8,128)S(1)} %stiff_merge.1.refs_0_.refs_1_, f32[64,1024]{1,0:T(8,128)S(1)} %get-tuple-element.39.refs_2_, f32[64,1024]{1,0:T(8,128)S(1)} %collective-permute-done.22.refs_3_), custom_call_target="tpu_custom_call", output_to_operand_aliasing={{}: (0, {})} | custom-call | tf_op jit(solution)/shard_map/finish_1/pallas_call | solution.py:289
  (14 shorter events, 0.2 us)
Async XLA Ops:
  1.4 0.7 copy-start.1
  1.4 2.6 %collective-permute-start.1 = (f32[16,48,128]{2,1,0:T(8,128)S(1)}, f32[16,48,128]{2,1,0:T(8,128)S(1)}, u32[]{:S(2)}, u32[]{:S(2)}) collective-permute-start(f32[16,48,128]{2,1,0:T(8,128)S(1)} %get-tuple-element.23), channel_id=1, source_target_pairs={{0,16},{16,0},{32,48},{48,32},{64,80},{80,64},{96,112},{112,96},{1... | collective-permute-start | bytes 1179656 | tf_op jit(solution)/shard_map/ppermute | solution.py:307
  1.5 9.2 %collective-permute-start.8 = (f32[16,48,128]{2,1,0:T(8,128)S(1)}, f32[16,48,128]{2,1,0:T(8,128)S(1)}, u32[]{:S(2)}, u32[]{:S(2)}) collective-permute-start(f32[16,48,128]{2,1,0:T(8,128)S(1)} %get-tuple-element.28), channel_id=1, source_target_pairs={{0,16},{16,0},{32,48},{48,32},{64,80},{80,64},{96,112},{112,96},{1... | collective-permute-start | bytes 1179656 | tf_op jit(solution)/shard_map/ppermute | solution.py:307
  4.7 13.7 %collective-permute-start.2 = (f32[12,48,128]{2,1,0:T(8,128)S(1)}, f32[12,48,128]{2,1,0:T(8,128)S(1)}, u32[]{:S(2)}, u32[]{:S(2)}) collective-permute-start(f32[12,48,128]{2,1,0:T(8,128)S(1)} %get-tuple-element.25.refs_0_), channel_id=1, source_target_pairs={{0,1},{1,2},{2,3},{3,4},{4,5},{5,6},{6,7},{7,0},{8,9},{9,10},{10,1... | collective-permute-start | bytes 884744 | tf_op jit(solution)/shard_map/ppermute | solution.py:303
  6.7 11.9 %collective-permute-start.3 = (f32[11,48,128]{2,1,0:T(8,128)S(1)}, f32[11,48,128]{2,1,0:T(8,128)S(1)}, u32[]{:S(2)}, u32[]{:S(2)}) collective-permute-start(f32[11,48,128]{2,1,0:T(8,128)S(1)} %get-tuple-element.27), channel_id=1, source_target_pairs={{0,7},{1,0},{2,1},{3,2},{4,3},{5,4},{6,5},{7,6},{8,15},{9,8},{10,9... | collective-permute-start | bytes 811016 | tf_op jit(solution)/shard_map/ppermute | solution.py:303
  11.3 12.6 %collective-permute-start.10 = (f32[12,48,128]{2,1,0:T(8,128)S(1)}, f32[12,48,128]{2,1,0:T(8,128)S(1)}, u32[]{:S(2)}, u32[]{:S(2)}) collective-permute-start(f32[12,48,128]{2,1,0:T(8,128)S(1)} %get-tuple-element.32), channel_id=1, source_target_pairs={{0,7},{1,0},{2,1},{3,2},{4,3},{5,4},{6,5},{7,6},{8,15},{9,8},{10,9... | collective-permute-start | bytes 884744 | tf_op jit(solution)/shard_map/ppermute | solution.py:303
  13.3 14.3 %collective-permute-start.9 = (f32[11,48,128]{2,1,0:T(8,128)S(1)}, f32[11,48,128]{2,1,0:T(8,128)S(1)}, u32[]{:S(2)}, u32[]{:S(2)}) collective-permute-start(f32[11,48,128]{2,1,0:T(8,128)S(1)} %get-tuple-element.30.refs_0_), channel_id=1, source_target_pairs={{0,1},{1,2},{2,3},{3,4},{4,5},{5,6},{6,7},{7,0},{8,9},{9,10},{10,1... | collective-permute-start | bytes 811016 | tf_op jit(solution)/shard_map/ppermute | solution.py:303
  18.4 11.0 %collective-permute-start.4 = (f32[11,48,128]{2,1,0:T(8,128)S(1)}, f32[11,48,128]{2,1,0:T(8,128)S(1)}, u32[]{:S(2)}, u32[]{:S(2)}) collective-permute-start(f32[11,48,128]{2,1,0:T(8,128)S(1)} %slice.56), channel_id=1, source_target_pairs={{0,1},{1,2},{2,3},{3,4},{4,5},{5,6},{6,7},{7,0},{8,9},{9,10},{10,1... | collective-permute-start | bytes 811016 | tf_op jit(solution)/shard_map/ppermute | solution.py:303
  18.6 20.2 %copy-start = (f32[4,64,1024]{2,1,0:T(8,128)S(1)}, f32[4,64,1024]{2,1,0:T(8,128)}, u32[]{:S(2)}) copy-start(f32[4,64,1024]{2,1,0:T(8,128)} %b_hbm.3) | copy-start | bytes 3145732
  18.6 11.0 %collective-permute-start.5 = (f32[10,48,128]{2,1,0:T(8,128)S(1)}, f32[10,48,128]{2,1,0:T(8,128)S(1)}, u32[]{:S(2)}, u32[]{:S(2)}) collective-permute-start(f32[10,48,128]{2,1,0:T(8,128)S(1)} %slice.57), channel_id=1, source_target_pairs={{0,7},{1,0},{2,1},{3,2},{4,3},{5,4},{6,5},{7,6},{8,15},{9,8},{10,9... | collective-permute-start | bytes 737288 | tf_op jit(solution)/shard_map/ppermute | solution.py:303
  23.9 11.0 %collective-permute-start.15 = (f32[11,48,128]{2,1,0:T(8,128)S(1)}, f32[11,48,128]{2,1,0:T(8,128)S(1)}, u32[]{:S(2)}, u32[]{:S(2)}) collective-permute-start(f32[11,48,128]{2,1,0:T(8,128)S(1)} %slice.63), channel_id=1, source_target_pairs={{0,7},{1,0},{2,1},{3,2},{4,3},{5,4},{6,5},{7,6},{8,15},{9,8},{10,9... | collective-permute-start | bytes 811016 | tf_op jit(solution)/shard_map/ppermute | solution.py:303
  27.7 12.6 %collective-permute-start.14 = (f32[10,48,128]{2,1,0:T(8,128)S(1)}, f32[10,48,128]{2,1,0:T(8,128)S(1)}, u32[]{:S(2)}, u32[]{:S(2)}) collective-permute-start(f32[10,48,128]{2,1,0:T(8,128)S(1)} %slice.62), channel_id=1, source_target_pairs={{0,1},{1,2},{2,3},{3,4},{4,5},{5,6},{6,7},{7,0},{8,9},{9,10},{10,1... | collective-permute-start | bytes 737288 | tf_op jit(solution)/shard_map/ppermute | solution.py:303
  29.4 11.2 %collective-permute-start.6 = (f32[10,48,128]{2,1,0:T(8,128)S(1)}, f32[10,48,128]{2,1,0:T(8,128)S(1)}, u32[]{:S(2)}, u32[]{:S(2)}) collective-permute-start(f32[10,48,128]{2,1,0:T(8,128)S(1)} %slice.58), channel_id=1, source_target_pairs={{0,1},{1,2},{2,3},{3,4},{4,5},{5,6},{6,7},{7,0},{8,9},{9,10},{10,1... | collective-permute-start | bytes 737288 | tf_op jit(solution)/shard_map/ppermute | solution.py:303
  29.6 11.2 %collective-permute-start.7 = (f32[9,48,128]{2,1,0:T(8,128)S(1)}, f32[9,48,128]{2,1,0:T(8,128)S(1)}, u32[]{:S(2)}, u32[]{:S(2)}) collective-permute-start(f32[9,48,128]{2,1,0:T(8,128)S(1)} %slice.59), channel_id=1, source_target_pairs={{0,7},{1,0},{2,1},{3,2},{4,3},{5,4},{6,5},{7,6},{8,15},{9,8},{10,9... | collective-permute-start | bytes 663560 | tf_op jit(solution)/shard_map/ppermute | solution.py:303
  35.0 9.5 %collective-permute-start.19 = (f32[6,48,128]{2,1,0:T(8,128)S(1)}, f32[6,48,128]{2,1,0:T(8,128)S(1)}, u32[]{:S(2)}, u32[]{:S(2)}) collective-permute-start(f32[6,48,128]{2,1,0:T(8,128)S(1)} %slice.67), channel_id=1, source_target_pairs={{0,7},{1,0},{2,1},{3,2},{4,3},{5,4},{6,5},{7,6},{8,15},{9,8},{10,9... | collective-permute-start | bytes 442376 | tf_op jit(solution)/shard_map/ppermute | solution.py:303
  39.4 19.8 %collective-permute-start = (f32[2,64,1024]{2,1,0:T(8,128)S(1)}, f32[2,64,1024]{2,1,0:T(8,128)S(1)}, u32[]{:S(2)}, u32[]{:S(2)}) collective-permute-start(f32[2,64,1024]{2,1,0:T(8,128)S(1)} %stiff_out.1), channel_id=1, source_target_pairs={{0,16},{16,0},{32,48},{48,32},{64,80},{80,64},{96,112},{112,96},{1... | collective-permute-start | bytes 1572872 | tf_op jit(solution)/shard_map/ppermute | solution.py:307
  40.3 7.6 %collective-permute-start.16 = (f32[5,48,128]{2,1,0:T(8,128)S(1)}, f32[5,48,128]{2,1,0:T(8,128)S(1)}, u32[]{:S(2)}, u32[]{:S(2)}) collective-permute-start(f32[5,48,128]{2,1,0:T(8,128)S(1)} %slice.64), channel_id=1, source_target_pairs={{0,1},{1,2},{2,3},{3,4},{4,5},{5,6},{6,7},{7,0},{8,9},{9,10},{10,1... | collective-permute-start | bytes 368648 | tf_op jit(solution)/shard_map/ppermute | solution.py:303
  40.6 10.6 %collective-permute-start.11 = (f32[5,48,128]{2,1,0:T(8,128)S(1)}, f32[5,48,128]{2,1,0:T(8,128)S(1)}, u32[]{:S(2)}, u32[]{:S(2)}) collective-permute-start(f32[5,48,128]{2,1,0:T(8,128)S(1)} %slice.60), channel_id=1, source_target_pairs={{0,1},{1,2},{2,3},{3,4},{4,5},{5,6},{6,7},{7,0},{8,9},{9,10},{10,1... | collective-permute-start | bytes 368648 | tf_op jit(solution)/shard_map/ppermute | solution.py:303
  40.8 7.2 %collective-permute-start.12 = (f32[4,48,128]{2,1,0:T(8,128)S(1)}, f32[4,48,128]{2,1,0:T(8,128)S(1)}, u32[]{:S(2)}, u32[]{:S(2)}) collective-permute-start(f32[4,48,128]{2,1,0:T(8,128)S(1)} %slice.61), channel_id=1, source_target_pairs={{0,7},{1,0},{2,1},{3,2},{4,3},{5,4},{6,5},{7,6},{8,15},{9,8},{10,9... | collective-permute-start | bytes 294920 | tf_op jit(solution)/shard_map/ppermute | solution.py:303
  44.4 12.6 %collective-permute-start.21 = (f32[5,48,128]{2,1,0:T(8,128)S(1)}, f32[5,48,128]{2,1,0:T(8,128)S(1)}, u32[]{:S(2)}, u32[]{:S(2)}) collective-permute-start(f32[5,48,128]{2,1,0:T(8,128)S(1)} %slice.69), channel_id=1, source_target_pairs={{0,7},{1,0},{2,1},{3,2},{4,3},{5,4},{6,5},{7,6},{8,15},{9,8},{10,9... | collective-permute-start | bytes 368648 | tf_op jit(solution)/shard_map/ppermute | solution.py:303
  47.9 5.8 %collective-permute-start.17 = (f32[4,48,128]{2,1,0:T(8,128)S(1)}, f32[4,48,128]{2,1,0:T(8,128)S(1)}, u32[]{:S(2)}, u32[]{:S(2)}) collective-permute-start(f32[4,48,128]{2,1,0:T(8,128)S(1)} %slice.65), channel_id=1, source_target_pairs={{0,1},{1,2},{2,3},{3,4},{4,5},{5,6},{6,7},{7,0},{8,9},{9,10},{10,1... | collective-permute-start | bytes 294920 | tf_op jit(solution)/shard_map/ppermute | solution.py:303
  47.9 7.3 %collective-permute-start.18 = (f32[4,48,128]{2,1,0:T(8,128)S(1)}, f32[4,48,128]{2,1,0:T(8,128)S(1)}, u32[]{:S(2)}, u32[]{:S(2)}) collective-permute-start(f32[4,48,128]{2,1,0:T(8,128)S(1)} %slice.66), channel_id=1, source_target_pairs={{0,7},{1,0},{2,1},{3,2},{4,3},{5,4},{6,5},{7,6},{8,15},{9,8},{10,9... | collective-permute-start | bytes 294920 | tf_op jit(solution)/shard_map/ppermute | solution.py:303
  51.2 5.8 %collective-permute-start.20 = (f32[4,48,128]{2,1,0:T(8,128)S(1)}, f32[4,48,128]{2,1,0:T(8,128)S(1)}, u32[]{:S(2)}, u32[]{:S(2)}) collective-permute-start(f32[4,48,128]{2,1,0:T(8,128)S(1)} %slice.68), channel_id=1, source_target_pairs={{0,1},{1,2},{2,3},{3,4},{4,5},{5,6},{6,7},{7,0},{8,9},{9,10},{10,1... | collective-permute-start | bytes 294920 | tf_op jit(solution)/shard_map/ppermute | solution.py:303
  53.7 8.7 %collective-permute-start.13 = (f32[64,1024]{1,0:T(8,128)S(1)}, f32[64,1024]{1,0:T(8,128)S(1)}, u32[]{:S(2)}, u32[]{:S(2)}) collective-permute-start(f32[64,1024]{1,0:T(8,128)S(1)} %get-tuple-element.35), channel_id=1, source_target_pairs={{0,8},{8,0},{1,9},{9,1},{2,10},{10,2},{3,11},{11,3},{4,12},{12,4},... | collective-permute-start | bytes 786440 | tf_op jit(solution)/shard_map/ppermute | solution.py:307
  57.6 8.2 %collective-permute-start.22 = (f32[64,1024]{1,0:T(8,128)S(1)}, f32[64,1024]{1,0:T(8,128)S(1)}, u32[]{:S(2)}, u32[]{:S(2)}) collective-permute-start(f32[64,1024]{1,0:T(8,128)S(1)} %get-tuple-element.40), channel_id=1, source_target_pairs={{0,8},{8,0},{1,9},{9,1},{2,10},{10,2},{3,11},{11,3},{4,12},{12,4},... | collective-permute-start | bytes 786440 | tf_op jit(solution)/shard_map/ppermute | solution.py:307

commit v7 on v6

--- a/solution.py
+++ b/solution.py
@@ -15,8 +15,13 @@
 HBM = pl.BlockSpec(memory_space=pltpu.HBM)
 
 
-def hops(slot):
-    return (4, 3) if slot == 0 else (3, 4)
+def hops(chain):
+    return (4, 3) if chain == 0 else (3, 4)
+
+
+def slot_of(chain):
+    column = lax.axis_index("tile_0")
+    return column if chain == 0 else 1 - column
 
 
 def locate(plan, group, wanted, home):
@@ -51,7 +56,7 @@
         low = lax.broadcasted_iota(jnp.int32, (depth, LANES), 1) < LANES // 2
         if for_partner:
             plan_copy.wait()
-        positions = [locate(plan_ref, group, owner * OWN + slot, home)[0] for slot in range(OWN)]
+        positions = [locate(plan_ref, group, owner * OWN + slot_of(slot), home)[0] for slot in range(OWN)]
         copies[0].wait()
         for slot in range(OWN):
             up = hops(slot)[0]
@@ -89,39 +94,26 @@
     )(plan, coupling, solve)
 
 
-def merge(plan, arrived, local, slot, home):
-    total, depth, _ = arrived.shape
-    up, down = hops(slot)
-    blocks = total // 2
-
-    def kernel(plan_ref, arrived_ref, local_ref, up_ref, down_ref, own_ref):
+def merge(plan, arrived, local, chain, home):
+    def kernel(plan_ref, arrived_ref, local_ref, out_ref):
         group = lax.axis_index("group")
-        _, here = locate(plan_ref, group, group * OWN + slot, home)
-
-        def put(source):
-            up_ref[...] = source[0 : up + blocks]
-            down_ref[...] = source[up : total - 1]
-            own_ref[...] = source[total - 1]
+        _, here = locate(plan_ref, group, group * OWN + slot_of(chain), home)
 
         @pl.when(here)
         def _():
-            put(local_ref)
+            out_ref[...] = local_ref[...]
 
         @pl.when(jnp.logical_not(here))
         def _():
-            put(arrived_ref)
-
-    return pl.pallas_call(
-        kernel,
-        out_shape=(
-            jax.ShapeDtypeStruct((up + blocks, depth, LANES), jnp.float32),
-            jax.ShapeDtypeStruct((down + blocks, depth, LANES), jnp.float32),
-            jax.ShapeDtypeStruct((depth, LANES), jnp.float32),
-        ),
+            out_ref[...] = arrived_ref[...]
+
+    return pl.pallas_call(
+        kernel,
+        out_shape=jax.ShapeDtypeStruct(arrived.shape, jnp.float32),
         in_specs=[SMEM, VMEM, VMEM],
-        out_specs=(VMEM, VMEM, VMEM),
-        compiler_params=PARAMS,
-        name=f"merge_{slot}",
+        out_specs=VMEM,
+        compiler_params=PARAMS,
+        name=f"merge_{chain}",
     )(plan, arrived, local)
 
 
@@ -245,13 +237,13 @@
     )(*given, *arrays)
 
 
-def last_chunks(total, sources, first, width, name):
-    rows = LANES // 2
+def last_chunks(total, sources):
+    rows, width = LANES // 2, total.shape[1]
     arrays, layout = gathered(sources)
 
     def kernel(total_ref, *refs):
         send_ref, keep_ref, sum_ref = refs[-3:]
-        sum_ref[...] = total_ref[:, pl.ds(first, width)]
+        sum_ref[...] = total_ref[...]
         add_chunks(sum_ref, chunks_of(refs[:-3], layout), False)
         mine = lax.axis_index("tile_0")
         send_ref[...] = sum_ref[pl.ds(pl.multiple_of((1 - mine) * rows, rows), rows), :]
@@ -265,23 +257,18 @@
         out_specs=(VMEM, VMEM),
         scratch_shapes=[pltpu.VMEM((LANES, width), jnp.float32)],
         compiler_params=PARAMS,
-        name=name,
+        name="last_chunks",
     )(total, *arrays)
 
 
-def finish(result, stiff, parts, slot):
-    flat = [array for pair in parts for array in pair]
+def finish(result, stiff, product, chain):
+    rows, width = product.shape
     given = [] if result is None else [result]
-    rows, width = stiff.shape[1:]
 
     def kernel(*refs):
-        stiff_ref, *ins = refs[len(given) : -3]
-        out_hbm, buf, sem = refs[-3:]
-        first = 0
-        for k in range(0, len(ins), 2):
-            columns = pl.ds(first, ins[k].shape[1])
-            buf[:, columns] = stiff_ref[slot, :, columns] - (ins[k][...] + ins[k + 1][...])
-            first += ins[k].shape[1]
+        stiff_ref, product_ref, out_hbm, buf, sem = refs[len(given) :]
+        slot = slot_of(chain)
+        buf[...] = stiff_ref[slot] - product_ref[...]
         copy = pltpu.make_async_copy(buf, out_hbm.at[slot], sem)
         copy.start()
         copy.wait()
@@ -289,13 +276,13 @@
     return pl.pallas_call(
         kernel,
         out_shape=jax.ShapeDtypeStruct((OWN, rows, width), jnp.float32),
-        in_specs=[HBM] * len(given) + [VMEM] * (1 + len(flat)),
+        in_specs=[HBM] * len(given) + [VMEM, VMEM],
         out_specs=HBM,
         scratch_shapes=[pltpu.VMEM((rows, width), jnp.float32), pltpu.SemaphoreType.DMA],
         input_output_aliases={0: 0} if given else {},
         compiler_params=PARAMS,
-        name=f"finish_{slot}",
-    )(*given, stiff, *flat)
+        name=f"finish_{chain}",
+    )(*given, stiff, product)
 
 
 def shifted(array, axis, distance):
@@ -321,61 +308,63 @@
 
 def body(coupling, interior_solve, boundary_stiffness, migration):
     home, depth, width = interior_solve.shape
-    rows = boundary_stiffness.shape[1]
     blocks = width // LANES
     half = blocks // 2
+    last = 2 * blocks - 1
     pieces = jnp.swapaxes(coupling, 1, 2)
     in_hbm = [pltpu.with_memory_space_constraint(a, pltpu.HBM) for a in (migration, pieces, interior_solve)]
     outgoing = pack(*in_hbm, True)
     arrived = [swapped(outgoing[0], "group"), swapped(outgoing[1], "group")]
     local = pack(migration, *in_hbm[1:], False)
-    up0, down0, own0 = merge(migration, arrived[0], local[0], 0, home)
-    up1, down1, own1 = merge(migration, arrived[1], local[1], 1, home)
-    stiff_arrived = swapped(stiff_out(migration, boundary_stiffness), "group")
-    stiff = stiff_merge(migration, boundary_stiffness, stiff_arrived)
+    packet1 = swapped(merge(migration, arrived[1], local[1], 1, home), "tile_0")
+    packet0 = merge(migration, arrived[0], local[0], 0, home)
 
     def run(first):
         return list(range(first, first + blocks))
 
     left = list(range(half))
-    u0, d0, u1, d1 = up(up0), down(down0), up(up1), down(down1)
-    uu0, dd0 = up(u0[1:]), down(d0[:-1])
+    u0, d0 = up(packet0[0 : 4 + blocks]), down(packet0[4:last])
+    stiff_arrived = swapped(stiff_out(after(migration, packet0), boundary_stiffness), "group")
+    stiff = stiff_merge(migration, boundary_stiffness, stiff_arrived)
+    u1, d1 = up(after(packet1[0 : 3 + blocks], u0, d0)), down(after(packet1[3:last], u0, d0))
+    uu0, dd0 = up(after(u0[1:], stiff_arrived)), down(d0[:-1])
+    total = accumulate(
+        None, [(packet0, run(4), packet0, last), (u0, run(4), u0, 0), (d0, run(0), d0, blocks + 2)], width, "chunks_1"
+    )
     uu1, dd1 = up(u1[1:]), down(d1[:-1])
-    total0 = accumulate(
-        None, [(up0, run(4), own0, None), (u0, run(4), u0, 0), (d0, run(0), d0, blocks + 2)], width, "chunks_0"
-    )
-    uuu0, ddd0 = up(uu0[1:]), down(dd0[:-1])
-    total1 = accumulate(
-        None, [(up1, run(3), own1, None), (u1, run(3), u1, 0), (d1, run(0), d1, blocks + 3)], width, "chunks_1"
-    )
-    uuu1a, ddd1b = up(after(uu1[1 : half + 2], total0)), down(dd1[half : blocks + 2])
-    ready0 = accumulate(total0, [(uu0, run(3), uu0, 0), (dd0, run(0), dd0, blocks + 1)], width, "chunks_0")
-    far0a, far0b = up(after(uuu0[1 : half + 2], total1)), down(ddd0[half:blocks])
-    far1a, far1b = up(uuu1a[1:]), down(after(ddd1b[: half + 1], ready0))
-    ready1 = accumulate(total1, [(uu1, run(2), uu1, 0), (dd1, run(0), dd1, blocks + 2)], width, "chunks_1")
-    uuu1b, ddd1a = up(after(uu1[half + 2 :], ready1)), down(dd1[:half])
-    send0, keep0 = last_chunks(
-        ready0,
+    uuu0, ddd0 = up(after(uu0[1:], total)), down(dd0[:-1])
+    total = accumulate(
+        total,
+        [(packet1, run(3), packet1, last), (u1, run(3), u1, 0), (d1, run(0), d1, blocks + 3)], width, "chunks_2",
+    )
+    uuu1, ddd1 = up(uu1[1:]), down(after(dd1[:-1], total))
+    total = accumulate(
+        total,
         [
-            (uuu0, run(2), uuu0, 0),
-            (ddd0, run(0), ddd0, blocks),
+            (uu0, run(3), uu0, 0), (dd0, run(0), dd0, blocks + 1),
+            (uu1, run(2), uu1, 0), (dd1, run(0), dd1, blocks + 2),
+        ],
+        width, "chunks_3",
+    )
+    far0a, far0b = up(uuu0[1 : half + 2]), down(ddd0[half:blocks])
+    far1a, far1b = up(uuu1[1 : half + 1]), down(after(ddd1[half : blocks + 1], total))
+    total = accumulate(
+        total,
+        [
+            (uuu0, run(2), uuu0, 0), (ddd0, run(0), ddd0, blocks),
+            (uuu1, run(1), uuu1, 0), (ddd1, run(0), ddd1, blocks + 1),
+        ],
+        width, "chunks_4",
+    )
+    send, keep = last_chunks(
+        total,
+        [
             ((far0a, far0b), [1, 2, 3, 4, 0, 1, 2, 3], far0a, 0),
-        ],
-        0, width, "last_0",
-    )
-    other0 = swapped(send0, "tile_0")
-    send1, keep1 = last_chunks(
-        ready1,
-        [
-            ((uuu1a, uuu1b), [1, 2, 3, 4, 0, 1, 2, 3], uuu1a, 0),
-            ((ddd1a, ddd1b), left + left, ddd1b, half + 1),
             ((far1a, far1b), left + left, far1b, half),
         ],
-        0, width, "last_1",
-    )
-    other1 = swapped(send1, "tile_0")
-    result = finish(None, stiff, [(keep0, other0)], 0)
-    return finish(result, stiff, [(keep1, other1)], 1)
+    )
+    other = swapped(send, "tile_0")
+    return finish(finish(None, stiff, keep, 0), stiff, other, 1)
 
 
 def solution(mesh):

time: 66.8 us -> 69.8 us (1.045)
  waiting for transfers between devices: 20.8 us -> 28 us
  starting transfers between devices: 35.3 us -> 31.4 us
    ppermute x18 -> x16, waiting for transfers between devices: 15.6 us -> 22.2 us  [shifted(): lax.ppermute(array, axis, [(i, (i + distance) % size) for i in range(size)])]
    ppermute x18 -> x16, starting transfers between devices: 31.6 us -> 27.7 us  [shifted(): lax.ppermute(array, axis, [(i, (i + distance) % size) for i in range(size)])]
  transfers between devices with their start and end apart: 23 -> 21, of which waited for: 9 -> 11; matrix products, arithmetic and copies ran while one was open for 0% -> 0% of each run, Pallas kernels for 11% -> 10%
where the time goes in v7:
time: 69.8 us; the launch traced here: 69.6 us
  starting transfers between devices  31.4 us (45%)
  waiting for transfers between devices  28 us (40%)
  Pallas kernels  9.51 us (14%)
    ppermute x16, starting transfers between devices, shifted(): lax.ppermute(array, axis, [(i, (i + distance) % size) for i in range(size)])  27.7 us
    ppermute x16, waiting for transfers between devices, shifted(): lax.ppermute(array, axis, [(i, (i + distance) % size) for i in range(size)])  22.2 us
    ppermute x5, waiting for transfers between devices, swapped(): lax.ppermute(array, axis, [(i, i ^ 1) for i in range(lax.axis_size(axis))])  5.83 us
    ppermute x5, starting transfers between devices, swapped(): lax.ppermute(array, axis, [(i, i ^ 1) for i in range(lax.axis_size(axis))])  3.68 us
    pallas_call x2, Pallas kernels, pack(): pl.pallas_call(kernel, out_shape=(packet, packet), in_specs=[HBM if for_p...  3.38 us
    pallas_call x4, Pallas kernels, accumulate(): pl.pallas_call(kernel, out_shape=jax.ShapeDtypeStruct((LANES, width), jnp...  1.82 us
    pallas_call x2, Pallas kernels, finish(): pl.pallas_call(kernel, out_shape=jax.ShapeDtypeStruct((OWN, rows, width),...  1.48 us
  transfers between devices with their start and end apart: 21, of which 11 were waited for; matrix products, arithmetic and copies ran while one was open for 0% of the time, Pallas kernels for 10%

profile of v7, /device:TPU:24, one launch (start us, length us, event | category | flops | bytes accessed | tf_op | source)
XLA Modules:
  0.0 69.6 jit_solution(8184226192691334078)
XLA Ops:
  0.0 1.4 %pack_partner.1 = (f32[16,48,128]{2,1,0:T(8,128)S(1)}, f32[16,48,128]{2,1,0:T(8,128)S(1)}) custom-call(s32[64]{0:T(128)} %plan_ref.6, f32[4,48,1024]{2,1,0:T(8,128)} %bitcast.1, f32[4,48,1024]{2,1,0:T(8,128)} %x_hbm.3), custom_call_target="tpu_custom_call" | custom-call | tf_op jit(solution)/shard_map/pack_partner/pallas_call | solution.py:79
  1.4 0.0 copy-start.1
  1.4 0.1 collective-permute-start.4
  1.5 0.5 collective-permute-start
  2.0 0.0 copy-done.1
  2.1 2.0 %pack_own.1 = (f32[16,48,128]{2,1,0:T(8,128)S(1)}, f32[16,48,128]{2,1,0:T(8,128)S(1)}) custom-call(s32[64]{0:T(128)S(1)} %copy-done.1, f32[4,48,1024]{2,1,0:T(8,128)} %bitcast.2, f32[4,48,1024]{2,1,0:T(8,128)} %x_hbm.3), custom_call_target="tpu_custom_call" | custom-call | tf_op jit(solution)/shard_map/pack_own/pallas_call | solution.py:79
  4.1 0.0 collective-permute-done.4.arrived_ref
  4.1 0.6 merge_1.1
  4.7 1.6 %collective-permute-start.5 = (f32[16,48,128]{2,1,0:T(8,128)S(1)}, f32[16,48,128]{2,1,0:T(8,128)S(1)}, u32[]{:S(2)}, u32[]{:S(2)}) collective-permute-start(f32[16,48,128]{2,1,0:T(8,128)S(1)} %merge_1.1), channel_id=1, source_target_pairs={{0,8},{8,0},{1,9},{9,1},{2,10},{10,2},{3,11},{11,3},{4,12},{12,4},... | collective-permute-start | bytes 1179656 | tf_op jit(solution)/shard_map/ppermute | solution.py:294
  6.2 0.0 collective-permute-done.arrived_ref
  6.2 0.0 copy-start
  6.2 0.6 merge_0.1.refs_0_
  6.9 2.0 %collective-permute-start.2 = (f32[12,48,128]{2,1,0:T(8,128)S(1)}, f32[12,48,128]{2,1,0:T(8,128)S(1)}, u32[]{:S(2)}, u32[]{:S(2)}) collective-permute-start(f32[12,48,128]{2,1,0:T(8,128)S(1)} %slice.64), channel_id=1, source_target_pairs={{0,1},{1,2},{2,3},{3,4},{4,5},{5,6},{6,7},{7,0},{8,9},{9,10},{10,1... | collective-permute-start | bytes 884744 | tf_op jit(solution)/shard_map/ppermute | solution.py:290
  8.9 4.0 %collective-permute-start.3 = (f32[11,48,128]{2,1,0:T(8,128)S(1)}, f32[11,48,128]{2,1,0:T(8,128)S(1)}, u32[]{:S(2)}, u32[]{:S(2)}) collective-permute-start(f32[11,48,128]{2,1,0:T(8,128)S(1)} %slice.65), channel_id=1, source_target_pairs={{0,7},{1,0},{2,1},{3,2},{4,3},{5,4},{6,5},{7,6},{8,15},{9,8},{10,9... | collective-permute-start | bytes 811016 | tf_op jit(solution)/shard_map/ppermute | solution.py:290
  12.9 0.0 copy-done
  12.9 0.6 stiff_out.1
  13.6 0.1 collective-permute-start.1
  13.7 2.2 %collective-permute-done.5.refs_1_ = f32[16,48,128]{2,1,0:T(8,128)S(1)} collective-permute-done((f32[16,48,128]{2,1,0:T(8,128)S(1)}, f32[16,48,128]{2,1,0:T(8,128)S(1)}, u32[]{:S(2)}, u32[]{:S(2)}) %collective-permute-start.5) | collective-permute-done | bytes 393248 | tf_op jit(solution)/shard_map/ppermute | solution.py:294
  15.9 2.8 %collective-permute-done.3.refs_2_ = f32[11,48,128]{2,1,0:T(8,128)S(1)} collective-permute-done((f32[11,48,128]{2,1,0:T(8,128)S(1)}, f32[11,48,128]{2,1,0:T(8,128)S(1)}, u32[]{:S(2)}, u32[]{:S(2)}) %collective-permute-start.3) | collective-permute-done | bytes 270368 | tf_op jit(solution)/shard_map/ppermute | solution.py:290
  18.6 1.1 %collective-permute-done.2.refs_1_ = f32[12,48,128]{2,1,0:T(8,128)S(1)} collective-permute-done((f32[12,48,128]{2,1,0:T(8,128)S(1)}, f32[12,48,128]{2,1,0:T(8,128)S(1)}, u32[]{:S(2)}, u32[]{:S(2)}) %collective-permute-start.2) | collective-permute-done | bytes 294944 | tf_op jit(solution)/shard_map/ppermute | solution.py:290
  19.8 2.5 %collective-permute-start.7 = (f32[12,48,128]{2,1,0:T(8,128)S(1)}, f32[12,48,128]{2,1,0:T(8,128)S(1)}, u32[]{:S(2)}, u32[]{:S(2)}) collective-permute-start(f32[12,48,128]{2,1,0:T(8,128)S(1)} %slice.67), channel_id=1, source_target_pairs={{0,7},{1,0},{2,1},{3,2},{4,3},{5,4},{6,5},{7,6},{8,15},{9,8},{10,9... | collective-permute-start | bytes 884744 | tf_op jit(solution)/shard_map/ppermute | solution.py:290
  22.3 0.1 collective-permute-start.6
  22.4 0.0 collective-permute-done.1.arrived_ref
  22.4 0.1 collective-permute-start.8
  22.5 5.3 %collective-permute-done.7.refs_3_ = f32[12,48,128]{2,1,0:T(8,128)S(1)} collective-permute-done((f32[12,48,128]{2,1,0:T(8,128)S(1)}, f32[12,48,128]{2,1,0:T(8,128)S(1)}, u32[]{:S(2)}, u32[]{:S(2)}) %collective-permute-start.7) | collective-permute-done | bytes 294944 | tf_op jit(solution)/shard_map/ppermute | solution.py:290
  27.9 3.5 %collective-permute-start.11 = (f32[11,48,128]{2,1,0:T(8,128)S(1)}, f32[11,48,128]{2,1,0:T(8,128)S(1)}, u32[]{:S(2)}, u32[]{:S(2)}) collective-permute-start(f32[11,48,128]{2,1,0:T(8,128)S(1)} %slice.71), channel_id=1, source_target_pairs={{0,7},{1,0},{2,1},{3,2},{4,3},{5,4},{6,5},{7,6},{8,15},{9,8},{10,9... | collective-permute-start | bytes 811016 | tf_op jit(solution)/shard_map/ppermute | solution.py:290
  31.4 0.1 collective-permute-start.9
  31.5 1.5 %collective-permute-done.6.refs_2_ = f32[11,48,128]{2,1,0:T(8,128)S(1)} collective-permute-done((f32[11,48,128]{2,1,0:T(8,128)S(1)}, f32[11,48,128]{2,1,0:T(8,128)S(1)}, u32[]{:S(2)}, u32[]{:S(2)}) %collective-permute-start.6) | collective-permute-done | bytes 270368 | tf_op jit(solution)/shard_map/ppermute | solution.py:290
  33.0 0.6 collective-permute-start.10
  33.6 0.4 chunks_1.1.refs_0_
  34.1 0.4 chunks_2.1.refs_0_
  34.5 4.3 %collective-permute-done.8.refs_1_ = f32[11,48,128]{2,1,0:T(8,128)S(1)} collective-permute-done((f32[11,48,128]{2,1,0:T(8,128)S(1)}, f32[11,48,128]{2,1,0:T(8,128)S(1)}, u32[]{:S(2)}, u32[]{:S(2)}) %collective-permute-start.8) | collective-permute-done | bytes 270368 | tf_op jit(solution)/shard_map/ppermute | solution.py:290
  38.8 0.1 collective-permute-start.12
  38.9 0.0 collective-permute-done.11.refs_4_
  39.0 3.3 %collective-permute-start.15 = (f32[10,48,128]{2,1,0:T(8,128)S(1)}, f32[10,48,128]{2,1,0:T(8,128)S(1)}, u32[]{:S(2)}, u32[]{:S(2)}) collective-permute-start(f32[10,48,128]{2,1,0:T(8,128)S(1)} %slice.75), channel_id=1, source_target_pairs={{0,7},{1,0},{2,1},{3,2},{4,3},{5,4},{6,5},{7,6},{8,15},{9,8},{10,9... | collective-permute-start | bytes 737288 | tf_op jit(solution)/shard_map/ppermute | solution.py:290
  42.3 1.4 %collective-permute-done.9.refs_2_ = f32[10,48,128]{2,1,0:T(8,128)S(1)} collective-permute-done((f32[10,48,128]{2,1,0:T(8,128)S(1)}, f32[10,48,128]{2,1,0:T(8,128)S(1)}, u32[]{:S(2)}, u32[]{:S(2)}) %collective-permute-start.9) | collective-permute-done | bytes 245792 | tf_op jit(solution)/shard_map/ppermute | solution.py:290
  43.6 3.8 %collective-permute-start.13 = (f32[9,48,128]{2,1,0:T(8,128)S(1)}, f32[9,48,128]{2,1,0:T(8,128)S(1)}, u32[]{:S(2)}, u32[]{:S(2)}) collective-permute-start(f32[9,48,128]{2,1,0:T(8,128)S(1)} %slice.73), channel_id=1, source_target_pairs={{0,7},{1,0},{2,1},{3,2},{4,3},{5,4},{6,5},{7,6},{8,15},{9,8},{10,9... | collective-permute-start | bytes 663560 | tf_op jit(solution)/shard_map/ppermute | solution.py:290
  47.4 0.0 collective-permute-done.10.refs_3_
  47.4 0.3 collective-permute-start.14
  47.7 0.5 chunks_3.1.refs_0_
  48.2 0.4 collective-permute-done.12.refs_1_
  48.6 0.1 collective-permute-start.16
  48.7 0.0 collective-permute-done.15.refs_4_
  48.7 3.5 %collective-permute-start.19 = (f32[5,48,128]{2,1,0:T(8,128)S(1)}, f32[5,48,128]{2,1,0:T(8,128)S(1)}, u32[]{:S(2)}, u32[]{:S(2)}) collective-permute-start(f32[5,48,128]{2,1,0:T(8,128)S(1)} %slice.79), channel_id=1, source_target_pairs={{0,7},{1,0},{2,1},{3,2},{4,3},{5,4},{6,5},{7,6},{8,15},{9,8},{10,9... | collective-permute-start | bytes 368648 | tf_op jit(solution)/shard_map/ppermute | solution.py:290
  52.2 0.0 collective-permute-done.13.refs_2_
  52.2 3.7 %collective-permute-start.17 = (f32[4,48,128]{2,1,0:T(8,128)S(1)}, f32[4,48,128]{2,1,0:T(8,128)S(1)}, u32[]{:S(2)}, u32[]{:S(2)}) collective-permute-start(f32[4,48,128]{2,1,0:T(8,128)S(1)} %slice.77), channel_id=1, source_target_pairs={{0,7},{1,0},{2,1},{3,2},{4,3},{5,4},{6,5},{7,6},{8,15},{9,8},{10,9... | collective-permute-start | bytes 294920 | tf_op jit(solution)/shard_map/ppermute | solution.py:290
  56.0 0.0 collective-permute-done.14.refs_3_
  56.0 0.1 collective-permute-start.18
  56.1 0.5 chunks_4.1.total_ref
  56.6 1.6 %collective-permute-done.17.refs_1_ = f32[4,48,128]{2,1,0:T(8,128)S(1)} collective-permute-done((f32[4,48,128]{2,1,0:T(8,128)S(1)}, f32[4,48,128]{2,1,0:T(8,128)S(1)}, u32[]{:S(2)}, u32[]{:S(2)}) %collective-permute-start.17) | collective-permute-done | bytes 98336 | tf_op jit(solution)/shard_map/ppermute | solution.py:290
  58.2 0.0 collective-permute-done.16.refs_0_
  58.2 3.7 %collective-permute-done.18.refs_2_ = f32[4,48,128]{2,1,0:T(8,128)S(1)} collective-permute-done((f32[4,48,128]{2,1,0:T(8,128)S(1)}, f32[4,48,128]{2,1,0:T(8,128)S(1)}, u32[]{:S(2)}, u32[]{:S(2)}) %collective-permute-start.18) | collective-permute-done | bytes 98336 | tf_op jit(solution)/shard_map/ppermute | solution.py:290
  61.9 0.0 collective-permute-done.19.refs_3_
  61.9 0.4 last_chunks.1
  62.3 1.4 %collective-permute-start.20 = (f32[64,1024]{1,0:T(8,128)S(1)}, f32[64,1024]{1,0:T(8,128)S(1)}, u32[]{:S(2)}, u32[]{:S(2)}) collective-permute-start(f32[64,1024]{1,0:T(8,128)S(1)} %get-tuple-element.30), channel_id=1, source_target_pairs={{0,8},{8,0},{1,9},{9,1},{2,10},{10,2},{3,11},{11,3},{4,12},{12,4},... | collective-permute-start | bytes 786440 | tf_op jit(solution)/shard_map/ppermute | solution.py:294
  63.7 0.6 stiff_merge.1.refs_0_.refs_1_
  64.3 0.7 %finish_0.1.refs_0_ = f32[2,64,1024]{2,1,0:T(8,128)} custom-call(f32[2,64,1024]{2,1,0:T(8,128)S(1)} %stiff_merge.1.refs_0_.refs_1_, f32[64,1024]{1,0:T(8,128)S(1)} %get-tuple-element.29.refs_1_), custom_call_target="tpu_custom_call" | custom-call | tf_op jit(solution)/shard_map/finish_0/pallas_call | solution.py:276
  65.1 3.7 %collective-permute-done.20.refs_2_ = f32[64,1024]{1,0:T(8,128)S(1)} collective-permute-done((f32[64,1024]{1,0:T(8,128)S(1)}, f32[64,1024]{1,0:T(8,128)S(1)}, u32[]{:S(2)}, u32[]{:S(2)}) %collective-permute-start.20) | collective-permute-done | bytes 262176 | tf_op jit(solution)/shard_map/ppermute | solution.py:294
  68.7 0.7 %finish_1.1 = f32[2,64,1024]{2,1,0:T(8,128)} custom-call(f32[2,64,1024]{2,1,0:T(8,128)} %finish_0.1.refs_0_, f32[2,64,1024]{2,1,0:T(8,128)S(1)} %stiff_merge.1.refs_0_.refs_1_, f32[64,1024]{1,0:T(8,128)S(1)} %collective-permute-done.20.refs_2_), custom_call_target="tpu_custom_call", output_to_operand_aliasing={{}: (0, {})} | custom-call | tf_op jit(solution)/shard_map/finish_1/pallas_call | solution.py:276
  (16 shorter events, 0.2 us)
Async XLA Ops:
  1.4 0.7 copy-start.1
  1.4 2.6 %collective-permute-start.4 = (f32[16,48,128]{2,1,0:T(8,128)S(1)}, f32[16,48,128]{2,1,0:T(8,128)S(1)}, u32[]{:S(2)}, u32[]{:S(2)}) collective-permute-start(f32[16,48,128]{2,1,0:T(8,128)S(1)} %get-tuple-element.21), channel_id=1, source_target_pairs={{0,16},{16,0},{32,48},{48,32},{64,80},{80,64},{96,112},{112,96},{1... | collective-permute-start | bytes 1179656 | tf_op jit(solution)/shard_map/ppermute | solution.py:294
  1.5 4.7 %collective-permute-start = (f32[16,48,128]{2,1,0:T(8,128)S(1)}, f32[16,48,128]{2,1,0:T(8,128)S(1)}, u32[]{:S(2)}, u32[]{:S(2)}) collective-permute-start(f32[16,48,128]{2,1,0:T(8,128)S(1)} %get-tuple-element.18), channel_id=1, source_target_pairs={{0,16},{16,0},{32,48},{48,32},{64,80},{80,64},{96,112},{112,96},{1... | collective-permute-start | bytes 1179656 | tf_op jit(solution)/shard_map/ppermute | solution.py:294
  4.7 11.2 %collective-permute-start.5 = (f32[16,48,128]{2,1,0:T(8,128)S(1)}, f32[16,48,128]{2,1,0:T(8,128)S(1)}, u32[]{:S(2)}, u32[]{:S(2)}) collective-permute-start(f32[16,48,128]{2,1,0:T(8,128)S(1)} %merge_1.1), channel_id=1, source_target_pairs={{0,8},{8,0},{1,9},{9,1},{2,10},{10,2},{3,11},{11,3},{4,12},{12,4},... | collective-permute-start | bytes 1179656 | tf_op jit(solution)/shard_map/ppermute | solution.py:294
  6.2 6.7 %copy-start = (f32[4,64,1024]{2,1,0:T(8,128)S(1)}, f32[4,64,1024]{2,1,0:T(8,128)}, u32[]{:S(2)}) copy-start(f32[4,64,1024]{2,1,0:T(8,128)} %b_hbm.3) | copy-start | bytes 3145732
  6.9 12.9 %collective-permute-start.2 = (f32[12,48,128]{2,1,0:T(8,128)S(1)}, f32[12,48,128]{2,1,0:T(8,128)S(1)}, u32[]{:S(2)}, u32[]{:S(2)}) collective-permute-start(f32[12,48,128]{2,1,0:T(8,128)S(1)} %slice.64), channel_id=1, source_target_pairs={{0,1},{1,2},{2,3},{3,4},{4,5},{5,6},{6,7},{7,0},{8,9},{9,10},{10,1... | collective-permute-start | bytes 884744 | tf_op jit(solution)/shard_map/ppermute | solution.py:290
  8.9 9.7 %collective-permute-start.3 = (f32[11,48,128]{2,1,0:T(8,128)S(1)}, f32[11,48,128]{2,1,0:T(8,128)S(1)}, u32[]{:S(2)}, u32[]{:S(2)}) collective-permute-start(f32[11,48,128]{2,1,0:T(8,128)S(1)} %slice.65), channel_id=1, source_target_pairs={{0,7},{1,0},{2,1},{3,2},{4,3},{5,4},{6,5},{7,6},{8,15},{9,8},{10,9... | collective-permute-start | bytes 811016 | tf_op jit(solution)/shard_map/ppermute | solution.py:290
  13.6 8.9 %collective-permute-start.1 = (f32[2,64,1024]{2,1,0:T(8,128)S(1)}, f32[2,64,1024]{2,1,0:T(8,128)S(1)}, u32[]{:S(2)}, u32[]{:S(2)}) collective-permute-start(f32[2,64,1024]{2,1,0:T(8,128)S(1)} %stiff_out.1), channel_id=1, source_target_pairs={{0,16},{16,0},{32,48},{48,32},{64,80},{80,64},{96,112},{112,96},{1... | collective-permute-start | bytes 1572872 | tf_op jit(solution)/shard_map/ppermute | solution.py:294
  19.8 8.1 %collective-permute-start.7 = (f32[12,48,128]{2,1,0:T(8,128)S(1)}, f32[12,48,128]{2,1,0:T(8,128)S(1)}, u32[]{:S(2)}, u32[]{:S(2)}) collective-permute-start(f32[12,48,128]{2,1,0:T(8,128)S(1)} %slice.67), channel_id=1, source_target_pairs={{0,7},{1,0},{2,1},{3,2},{4,3},{5,4},{6,5},{7,6},{8,15},{9,8},{10,9... | collective-permute-start | bytes 884744 | tf_op jit(solution)/shard_map/ppermute | solution.py:290
  22.3 10.7 %collective-permute-start.6 = (f32[11,48,128]{2,1,0:T(8,128)S(1)}, f32[11,48,128]{2,1,0:T(8,128)S(1)}, u32[]{:S(2)}, u32[]{:S(2)}) collective-permute-start(f32[11,48,128]{2,1,0:T(8,128)S(1)} %slice.66), channel_id=1, source_target_pairs={{0,1},{1,2},{2,3},{3,4},{4,5},{5,6},{6,7},{7,0},{8,9},{9,10},{10,1... | collective-permute-start | bytes 811016 | tf_op jit(solution)/shard_map/ppermute | solution.py:290
  22.4 16.4 %collective-permute-start.8 = (f32[11,48,128]{2,1,0:T(8,128)S(1)}, f32[11,48,128]{2,1,0:T(8,128)S(1)}, u32[]{:S(2)}, u32[]{:S(2)}) collective-permute-start(f32[11,48,128]{2,1,0:T(8,128)S(1)} %slice.68), channel_id=1, source_target_pairs={{0,1},{1,2},{2,3},{3,4},{4,5},{5,6},{6,7},{7,0},{8,9},{9,10},{10,1... | collective-permute-start | bytes 811016 | tf_op jit(solution)/shard_map/ppermute | solution.py:290
  27.9 11.0 %collective-permute-start.11 = (f32[11,48,128]{2,1,0:T(8,128)S(1)}, f32[11,48,128]{2,1,0:T(8,128)S(1)}, u32[]{:S(2)}, u32[]{:S(2)}) collective-permute-start(f32[11,48,128]{2,1,0:T(8,128)S(1)} %slice.71), channel_id=1, source_target_pairs={{0,7},{1,0},{2,1},{3,2},{4,3},{5,4},{6,5},{7,6},{8,15},{9,8},{10,9... | collective-permute-start | bytes 811016 | tf_op jit(solution)/shard_map/ppermute | solution.py:290
  31.4 12.2 %collective-permute-start.9 = (f32[10,48,128]{2,1,0:T(8,128)S(1)}, f32[10,48,128]{2,1,0:T(8,128)S(1)}, u32[]{:S(2)}, u32[]{:S(2)}) collective-permute-start(f32[10,48,128]{2,1,0:T(8,128)S(1)} %slice.69), channel_id=1, source_target_pairs={{0,7},{1,0},{2,1},{3,2},{4,3},{5,4},{6,5},{7,6},{8,15},{9,8},{10,9... | collective-permute-start | bytes 737288 | tf_op jit(solution)/shard_map/ppermute | solution.py:290
  33.0 14.4 %collective-permute-start.10 = (f32[10,48,128]{2,1,0:T(8,128)S(1)}, f32[10,48,128]{2,1,0:T(8,128)S(1)}, u32[]{:S(2)}, u32[]{:S(2)}) collective-permute-start(f32[10,48,128]{2,1,0:T(8,128)S(1)} %slice.70), channel_id=1, source_target_pairs={{0,1},{1,2},{2,3},{3,4},{4,5},{5,6},{6,7},{7,0},{8,9},{9,10},{10,1... | collective-permute-start | bytes 737288 | tf_op jit(solution)/shard_map/ppermute | solution.py:290
  38.8 9.8 %collective-permute-start.12 = (f32[10,48,128]{2,1,0:T(8,128)S(1)}, f32[10,48,128]{2,1,0:T(8,128)S(1)}, u32[]{:S(2)}, u32[]{:S(2)}) collective-permute-start(f32[10,48,128]{2,1,0:T(8,128)S(1)} %slice.72), channel_id=1, source_target_pairs={{0,1},{1,2},{2,3},{3,4},{4,5},{5,6},{6,7},{7,0},{8,9},{9,10},{10,1... | collective-permute-start | bytes 737288 | tf_op jit(solution)/shard_map/ppermute | solution.py:290
  39.0 9.7 %collective-permute-start.15 = (f32[10,48,128]{2,1,0:T(8,128)S(1)}, f32[10,48,128]{2,1,0:T(8,128)S(1)}, u32[]{:S(2)}, u32[]{:S(2)}) collective-permute-start(f32[10,48,128]{2,1,0:T(8,128)S(1)} %slice.75), channel_id=1, source_target_pairs={{0,7},{1,0},{2,1},{3,2},{4,3},{5,4},{6,5},{7,6},{8,15},{9,8},{10,9... | collective-permute-start | bytes 737288 | tf_op jit(solution)/shard_map/ppermute | solution.py:290
  43.6 8.6 %collective-permute-start.13 = (f32[9,48,128]{2,1,0:T(8,128)S(1)}, f32[9,48,128]{2,1,0:T(8,128)S(1)}, u32[]{:S(2)}, u32[]{:S(2)}) collective-permute-start(f32[9,48,128]{2,1,0:T(8,128)S(1)} %slice.73), channel_id=1, source_target_pairs={{0,7},{1,0},{2,1},{3,2},{4,3},{5,4},{6,5},{7,6},{8,15},{9,8},{10,9... | collective-permute-start | bytes 663560 | tf_op jit(solution)/shard_map/ppermute | solution.py:290
  47.4 8.5 %collective-permute-start.14 = (f32[9,48,128]{2,1,0:T(8,128)S(1)}, f32[9,48,128]{2,1,0:T(8,128)S(1)}, u32[]{:S(2)}, u32[]{:S(2)}) collective-permute-start(f32[9,48,128]{2,1,0:T(8,128)S(1)} %slice.74), channel_id=1, source_target_pairs={{0,1},{1,2},{2,3},{3,4},{4,5},{5,6},{6,7},{7,0},{8,9},{9,10},{10,1... | collective-permute-start | bytes 663560 | tf_op jit(solution)/shard_map/ppermute | solution.py:290
  48.6 9.6 %collective-permute-start.16 = (f32[5,48,128]{2,1,0:T(8,128)S(1)}, f32[5,48,128]{2,1,0:T(8,128)S(1)}, u32[]{:S(2)}, u32[]{:S(2)}) collective-permute-start(f32[5,48,128]{2,1,0:T(8,128)S(1)} %slice.76), channel_id=1, source_target_pairs={{0,1},{1,2},{2,3},{3,4},{4,5},{5,6},{6,7},{7,0},{8,9},{9,10},{10,1... | collective-permute-start | bytes 368648 | tf_op jit(solution)/shard_map/ppermute | solution.py:290
  48.7 13.1 %collective-permute-start.19 = (f32[5,48,128]{2,1,0:T(8,128)S(1)}, f32[5,48,128]{2,1,0:T(8,128)S(1)}, u32[]{:S(2)}, u32[]{:S(2)}) collective-permute-start(f32[5,48,128]{2,1,0:T(8,128)S(1)} %slice.79), channel_id=1, source_target_pairs={{0,7},{1,0},{2,1},{3,2},{4,3},{5,4},{6,5},{7,6},{8,15},{9,8},{10,9... | collective-permute-start | bytes 368648 | tf_op jit(solution)/shard_map/ppermute | solution.py:290
  52.2 5.9 %collective-permute-start.17 = (f32[4,48,128]{2,1,0:T(8,128)S(1)}, f32[4,48,128]{2,1,0:T(8,128)S(1)}, u32[]{:S(2)}, u32[]{:S(2)}) collective-permute-start(f32[4,48,128]{2,1,0:T(8,128)S(1)} %slice.77), channel_id=1, source_target_pairs={{0,7},{1,0},{2,1},{3,2},{4,3},{5,4},{6,5},{7,6},{8,15},{9,8},{10,9... | collective-permute-start | bytes 294920 | tf_op jit(solution)/shard_map/ppermute | solution.py:290
  56.0 5.9 %collective-permute-start.18 = (f32[4,48,128]{2,1,0:T(8,128)S(1)}, f32[4,48,128]{2,1,0:T(8,128)S(1)}, u32[]{:S(2)}, u32[]{:S(2)}) collective-permute-start(f32[4,48,128]{2,1,0:T(8,128)S(1)} %slice.78), channel_id=1, source_target_pairs={{0,1},{1,2},{2,3},{3,4},{4,5},{5,6},{6,7},{7,0},{8,9},{9,10},{10,1... | collective-permute-start | bytes 294920 | tf_op jit(solution)/shard_map/ppermute | solution.py:290
  62.3 6.5 %collective-permute-start.20 = (f32[64,1024]{1,0:T(8,128)S(1)}, f32[64,1024]{1,0:T(8,128)S(1)}, u32[]{:S(2)}, u32[]{:S(2)}) collective-permute-start(f32[64,1024]{1,0:T(8,128)S(1)} %get-tuple-element.30), channel_id=1, source_target_pairs={{0,8},{8,0},{1,9},{9,1},{2,10},{10,2},{3,11},{11,3},{4,12},{12,4},... | collective-permute-start | bytes 786440 | tf_op jit(solution)/shard_map/ppermute | solution.py:294

commit v8 on v3

--- a/solution.py
+++ b/solution.py
@@ -33,26 +33,42 @@
     return position, here
 
 
-def pack(plan, coupling, solve, for_partner):
+def pack(plan, coupling, solve, stiff=None):
     home, depth, width = solve.shape
     blocks = width // LANES
-
-    def kernel(plan_hbm, c_hbm, x_hbm, out0, out1, plan_ref, c_buf, x_buf, plan_sem, c_sem, x_sem):
+    for_partner = stiff is not None
+
+    def kernel(plan_given, c_hbm, x_hbm, *refs):
+        if for_partner:
+            b_hbm, out0, out1, out_b, plan_buf, c_buf, x_buf, plan_sem, c_sem, x_sem, b_sem = refs
+        else:
+            out0, out1, c_buf, x_buf, c_sem, x_sem = refs
         group = lax.axis_index("group")
         place = lax.axis_index("tile_1")
         owner = jnp.bitwise_xor(group, 1) if for_partner else group
         outs = (out0, out1)
         copies = [
-            pltpu.make_async_copy(plan_hbm, plan_ref, plan_sem),
             pltpu.make_async_copy(c_hbm, c_buf, c_sem),
             pltpu.make_async_copy(x_hbm, x_buf, x_sem),
         ]
         for copy in copies:
             copy.start()
+        plan_ref = plan_given
+        if for_partner:
+            plan_copy = pltpu.make_async_copy(plan_given, plan_buf, plan_sem)
+            plan_copy.start()
+            plan_ref = plan_buf
         low = lax.broadcasted_iota(jnp.int32, (depth, LANES), 1) < LANES // 2
+        if for_partner:
+            plan_copy.wait()
+        positions = [locate(plan_ref, group, owner * OWN + slot_of(slot), home)[0] for slot in range(OWN)]
+        b_copies = []
+        if for_partner:
+            for slot in range(OWN):
+                place_b, _ = locate(plan_ref, group, owner * OWN + slot, home)
+                b_copies.append(pltpu.make_async_copy(b_hbm.at[place_b], out_b.at[slot], b_sem.at[slot]))
+                b_copies[slot].start()
         copies[0].wait()
-        positions = [locate(plan_ref, group, owner * OWN + slot_of(slot), home)[0] for slot in range(OWN)]
-        copies[1].wait()
         for slot in range(OWN):
             up = hops(slot)[0]
             for m in range(blocks // 2):
@@ -64,29 +80,42 @@
                     ahead = jnp.bitwise_and(to - place, blocks - 1)
                     spot = jnp.where(ahead == 0, 15, jnp.where(ahead <= up, ahead - 1, ahead + 7))
                     outs[slot][spot] = piece
-        copies[2].wait()
+        copies[1].wait()
         for slot in range(OWN):
             up = hops(slot)[0]
             for n in range(blocks):
                 outs[slot][up + n] = x_buf[positions[slot], :, pl.ds(n * LANES, LANES)]
+        for copy in b_copies:
+            copy.wait()
 
     packet = jax.ShapeDtypeStruct((2 * blocks, depth, LANES), jnp.float32)
-    return pl.pallas_call(
-        kernel,
-        out_shape=(packet, packet),
-        in_specs=[HBM] * 3,
-        out_specs=(VMEM, VMEM),
+    staging = [pltpu.VMEM((home, depth, width), jnp.float32)] * 2
+    semaphores = [pltpu.SemaphoreType.DMA] * 2
+    if not for_partner:
+        return pl.pallas_call(
+            kernel,
+            out_shape=(packet, packet),
+            in_specs=[SMEM, HBM, HBM],
+            out_specs=(VMEM, VMEM),
+            scratch_shapes=[*staging, *semaphores],
+            compiler_params=PARAMS,
+            name="pack_own",
+        )(plan, coupling, solve)
+    return pl.pallas_call(
+        kernel,
+        out_shape=(packet, packet, jax.ShapeDtypeStruct((OWN, *stiff.shape[1:]), jnp.float32)),
+        in_specs=[HBM] * 4,
+        out_specs=(VMEM, VMEM, VMEM),
         scratch_shapes=[
             pltpu.SMEM(plan.shape, jnp.int32),
-            pltpu.VMEM((home, depth, width), jnp.float32),
-            pltpu.VMEM((home, depth, width), jnp.float32),
+            *staging,
             pltpu.SemaphoreType.DMA,
-            pltpu.SemaphoreType.DMA,
-            pltpu.SemaphoreType.DMA,
+            *semaphores,
+            pltpu.SemaphoreType.DMA((OWN,)),
         ],
         compiler_params=PARAMS,
-        name="pack_partner" if for_partner else "pack_own",
-    )(plan, coupling, solve)
+        name="pack_partner",
+    )(plan, coupling, solve, stiff)
 
 
 def merge(plan, arrived, local, chain, home):
@@ -127,31 +156,6 @@
         compiler_params=PARAMS,
         name=f"merge_{chain}",
     )(plan, arrived, local)
-
-
-def stiff_out(plan, stiff):
-    home, rows, width = stiff.shape
-
-    def kernel(plan_ref, b_hbm, out_ref, sem):
-        group = lax.axis_index("group")
-        copies = []
-        for slot in range(OWN):
-            position, _ = locate(plan_ref, group, jnp.bitwise_xor(group, 1) * OWN + slot, home)
-            copy = pltpu.make_async_copy(b_hbm.at[position], out_ref.at[slot], sem.at[slot])
-            copy.start()
-            copies.append(copy)
-        for copy in copies:
-            copy.wait()
-
-    return pl.pallas_call(
-        kernel,
-        out_shape=jax.ShapeDtypeStruct((OWN, rows, width), jnp.float32),
-        in_specs=[SMEM, HBM],
-        out_specs=VMEM,
-        scratch_shapes=[pltpu.SemaphoreType.DMA((OWN,))],
-        compiler_params=PARAMS,
-        name="stiff_out",
-    )(plan, stiff)
 
 
 def stiff_merge(plan, stiff, arrived):
@@ -304,6 +308,10 @@
     return lax.ppermute(array, axis, [(i, i ^ 1) for i in range(lax.axis_size(axis))])
 
 
+def after(array, *earlier):
+    return lax.optimization_barrier((array, *earlier))[0]
+
+
 def crossed(array, distance):
     size = lax.axis_size("tile_1")
     pairs = [(x * size + z, (1 - x) * size + (z + distance) % size) for x in range(2) for z in range(size)]
@@ -314,14 +322,14 @@
     home, depth, width = interior_solve.shape
     blocks = width // LANES
     pieces = jnp.swapaxes(coupling, 1, 2)
-    in_hbm = [pltpu.with_memory_space_constraint(a, pltpu.HBM) for a in (migration, pieces, interior_solve)]
-    outgoing = pack(*in_hbm, True)
+    in_hbm = [pltpu.with_memory_space_constraint(a, pltpu.HBM) for a in (migration, pieces, interior_solve, boundary_stiffness)]
+    outgoing = pack(*in_hbm)
     arrived = [swapped(outgoing[0], "group"), swapped(outgoing[1], "group")]
-    local = pack(*in_hbm, False)
+    stiff_arrived = swapped(outgoing[2], "group")
+    local = pack(migration, *in_hbm[1:3])
     ups, downs, owns = [None, None], [None, None], [None, None]
     for chain in range(2):
         ups[chain], downs[chain], owns[chain] = merge(migration, arrived[chain], local[chain], chain, home)
-    stiff_arrived = swapped(stiff_out(migration, boundary_stiffness), "group")
     stiff = stiff_merge(migration, boundary_stiffness, stiff_arrived)
 
     def run(first):
@@ -333,7 +341,8 @@
     for step in range(1, 4):
         for chain in range(2):
             if step == 1 and chain == 1:
-                ups[chain], downs[chain] = crossed(ups[chain], 1), crossed(downs[chain], -1)
+                ups[chain] = crossed(after(ups[chain], stiff_arrived), 1)
+                downs[chain] = crossed(downs[chain], -1)
             else:
                 sent_up = ups[chain] if step == 1 else ups[chain][1:]
                 sent_down = downs[chain] if step == 1 else downs[chain][:-1]

time: 61.8 us -> 63.2 us (1.023)
  the two profiles are of different devices: /device:TPU:24 before, /device:TPU:112 now
where the time goes in v8:
time: 63.2 us; the launch traced here: 63 us
  waiting for transfers between devices  29.1 us (46%)
  starting transfers between devices  23.8 us (38%)
  Pallas kernels  9.5 us (15%)
    ppermute x12, waiting for transfers between devices, shifted(): lax.ppermute(array, axis, [(i, (i + distance) % size) for i in range(size)])  19.2 us
    ppermute x12, starting transfers between devices, shifted(): lax.ppermute(array, axis, [(i, (i + distance) % size) for i in range(size)])  16.4 us
    ppermute x3, starting transfers between devices, crossed(): return lax.ppermute(array, TILE, pairs)  6.24 us
    ppermute x4, waiting for transfers between devices, swapped(): lax.ppermute(array, axis, [(i, i ^ 1) for i in range(lax.axis_size(axis))])  5.62 us
    ppermute x3, waiting for transfers between devices, crossed(): return lax.ppermute(array, TILE, pairs)  4.31 us
    pallas_call x1, Pallas kernels, pack(): pl.pallas_call(kernel, out_shape=(packet, packet, jax.ShapeDtypeStruct((O...  2 us
    pallas_call x1, Pallas kernels, pack(): pl.pallas_call(kernel, out_shape=(packet, packet), in_specs=[SMEM, HBM, H...  1.95 us
    pallas_call x4, Pallas kernels, accumulate(): pl.pallas_call(kernel, out_shape=jax.ShapeDtypeStruct((LANES, width), jnp...  1.82 us
  transfers between devices with their start and end apart: 19, of which 10 were waited for; matrix products, arithmetic and copies ran while one was open for 0% of the time, Pallas kernels for 10%

profile of v8, /device:TPU:112, one launch (start us, length us, event | category | flops | bytes accessed | tf_op | source)
XLA Modules:
  0.0 63.0 jit_solution(16893336679140693925)
XLA Ops:
  0.0 2.0 %pack_partner.1 = (f32[16,48,128]{2,1,0:T(8,128)S(1)}, f32[16,48,128]{2,1,0:T(8,128)S(1)}, f32[2,64,1024]{2,1,0:T(8,128)S(1)}) custom-call(s32[64]{0:T(128)} %plan_ref.5, f32[4,48,1024]{2,1,0:T(8,128)} %bitcast.1, f32[4,48,1024]{2,1,0:T(8,128)} %x_hbm.3, f32[4,64,1024]{2,1,0:T(8,128)} %b_hbm.1), custom_call_target="tpu_custom_call" | custom-call | tf_op jit(solution)/shard_map/pack_partner/pallas_call | solution.py:104
  2.0 0.1 collective-permute-start.1
  2.1 0.0 copy-start.1
  2.1 0.5 collective-permute-start.2
  2.6 0.1 collective-permute-start
  2.7 0.0 copy-done.1
  2.8 2.0 %pack_own.1 = (f32[16,48,128]{2,1,0:T(8,128)S(1)}, f32[16,48,128]{2,1,0:T(8,128)S(1)}) custom-call(s32[64]{0:T(128)S(1)} %copy-done.1, f32[4,48,1024]{2,1,0:T(8,128)} %bitcast.2, f32[4,48,1024]{2,1,0:T(8,128)} %x_hbm.3), custom_call_target="tpu_custom_call" | custom-call | tf_op jit(solution)/shard_map/pack_own/pallas_call | solution.py:95
  4.7 0.0 collective-permute-done.1.arrived_ref
  4.7 0.6 merge_0.1
  5.3 3.2 %collective-permute-start.4 = (f32[12,48,128]{2,1,0:T(8,128)S(1)}, f32[12,48,128]{2,1,0:T(8,128)S(1)}, u32[]{:S(2)}, u32[]{:S(2)}) collective-permute-start(f32[12,48,128]{2,1,0:T(8,128)S(1)} %get-tuple-element.22.refs_0_), channel_id=1, source_target_pairs={{0,1},{1,2},{2,3},{3,4},{4,5},{5,6},{6,7},{7,0},{8,9},{9,10},{10,1... | collective-permute-start | bytes 884744 | tf_op jit(solution)/shard_map/ppermute | solution.py:304
  8.6 0.0 collective-permute-done.2.arrived_ref
  8.6 0.6 merge_1.1
  9.2 0.1 collective-permute-start.7
  9.3 0.1 collective-permute-start.5
  9.4 0.0 collective-permute-done.arrived_ref
  9.4 4.1 %collective-permute-start.6 = (f32[11,48,128]{2,1,0:T(8,128)S(1)}, f32[11,48,128]{2,1,0:T(8,128)S(1)}, u32[]{:S(2)}, u32[]{:S(2)}) collective-permute-start(f32[11,48,128]{2,1,0:T(8,128)S(1)} %get-tuple-element.29), channel_id=1, source_target_pairs={{0,9},{1,10},{2,11},{3,12},{4,13},{5,14},{6,15},{7,8},{8,1},{9,2},... | collective-permute-start | bytes 811016 | tf_op jit(solution)/shard_map/ppermute | solution.py:318
  13.5 2.4 %collective-permute-done.4.refs_2_ = f32[12,48,128]{2,1,0:T(8,128)S(1)} collective-permute-done((f32[12,48,128]{2,1,0:T(8,128)S(1)}, f32[12,48,128]{2,1,0:T(8,128)S(1)}, u32[]{:S(2)}, u32[]{:S(2)}) %collective-permute-start.4) | collective-permute-done | bytes 294944 | tf_op jit(solution)/shard_map/ppermute | solution.py:304
  15.9 3.8 %collective-permute-start.8 = (f32[11,48,128]{2,1,0:T(8,128)S(1)}, f32[11,48,128]{2,1,0:T(8,128)S(1)}, u32[]{:S(2)}, u32[]{:S(2)}) collective-permute-start(f32[11,48,128]{2,1,0:T(8,128)S(1)} %slice.40), channel_id=1, source_target_pairs={{0,1},{1,2},{2,3},{3,4},{4,5},{5,6},{6,7},{7,0},{8,9},{9,10},{10,1... | collective-permute-start | bytes 811016 | tf_op jit(solution)/shard_map/ppermute | solution.py:304
  19.7 4.3 %collective-permute-done.7.refs_5_ = f32[12,48,128]{2,1,0:T(8,128)S(1)} collective-permute-done((f32[12,48,128]{2,1,0:T(8,128)S(1)}, f32[12,48,128]{2,1,0:T(8,128)S(1)}, u32[]{:S(2)}, u32[]{:S(2)}) %collective-permute-start.7) | collective-permute-done | bytes 294944 | tf_op jit(solution)/shard_map/ppermute | solution.py:318
  24.0 0.1 collective-permute-start.11
  24.1 5.0 %collective-permute-done.5.refs_3_ = f32[11,48,128]{2,1,0:T(8,128)S(1)} collective-permute-done((f32[11,48,128]{2,1,0:T(8,128)S(1)}, f32[11,48,128]{2,1,0:T(8,128)S(1)}, u32[]{:S(2)}, u32[]{:S(2)}) %collective-permute-start.5) | collective-permute-done | bytes 270368 | tf_op jit(solution)/shard_map/ppermute | solution.py:304
  29.2 0.1 collective-permute-start.9
  29.2 0.0 collective-permute-done.6.refs_4_
  29.3 3.3 %collective-permute-start.10 = (f32[10,48,128]{2,1,0:T(8,128)S(1)}, f32[10,48,128]{2,1,0:T(8,128)S(1)}, u32[]{:S(2)}, u32[]{:S(2)}) collective-permute-start(f32[10,48,128]{2,1,0:T(8,128)S(1)} %slice.42), channel_id=1, source_target_pairs={{0,1},{1,2},{2,3},{3,4},{4,5},{5,6},{6,7},{7,0},{8,9},{9,10},{10,1... | collective-permute-start | bytes 737288 | tf_op jit(solution)/shard_map/ppermute | solution.py:304
  32.6 0.0 collective-permute-done.8.refs_1_
  32.6 0.1 collective-permute-start.12
  32.7 2.2 %collective-permute-done.11.refs_4_ = f32[11,48,128]{2,1,0:T(8,128)S(1)} collective-permute-done((f32[11,48,128]{2,1,0:T(8,128)S(1)}, f32[11,48,128]{2,1,0:T(8,128)S(1)}, u32[]{:S(2)}, u32[]{:S(2)}) %collective-permute-start.11) | collective-permute-done | bytes 270368 | tf_op jit(solution)/shard_map/ppermute | solution.py:304
  34.9 0.1 collective-permute-start.15
  35.0 2.0 %collective-permute-start.3 = (f32[9,48,128]{2,1,0:T(8,128)S(1)}, f32[9,48,128]{2,1,0:T(8,128)S(1)}, u32[]{:S(2)}, u32[]{:S(2)}) collective-permute-start(f32[9,48,128]{2,1,0:T(8,128)S(1)} %get-tuple-element.26), channel_id=1, source_target_pairs={{0,8},{1,9},{2,10},{3,11},{4,12},{5,13},{6,14},{7,15},{8,0},{9,1},... | collective-permute-start | bytes 663560 | tf_op jit(solution)/shard_map/ppermute | solution.py:318
  37.1 3.1 %collective-permute-done.9.refs_2_ = f32[10,48,128]{2,1,0:T(8,128)S(1)} collective-permute-done((f32[10,48,128]{2,1,0:T(8,128)S(1)}, f32[10,48,128]{2,1,0:T(8,128)S(1)}, u32[]{:S(2)}, u32[]{:S(2)}) %collective-permute-start.9) | collective-permute-done | bytes 245792 | tf_op jit(solution)/shard_map/ppermute | solution.py:304
  40.2 0.1 collective-permute-start.13
  40.3 0.0 collective-permute-done.10.refs_3_
  40.3 3.5 %collective-permute-start.14 = (f32[9,48,128]{2,1,0:T(8,128)S(1)}, f32[9,48,128]{2,1,0:T(8,128)S(1)}, u32[]{:S(2)}, u32[]{:S(2)}) collective-permute-start(f32[9,48,128]{2,1,0:T(8,128)S(1)} %slice.46), channel_id=1, source_target_pairs={{0,1},{1,2},{2,3},{3,4},{4,5},{5,6},{6,7},{7,0},{8,9},{9,10},{10,1... | collective-permute-start | bytes 663560 | tf_op jit(solution)/shard_map/ppermute | solution.py:304
  43.8 0.0 collective-permute-done.12.refs_1_
  43.8 1.6 %collective-permute-start.16 = (f32[9,48,128]{2,1,0:T(8,128)S(1)}, f32[9,48,128]{2,1,0:T(8,128)S(1)}, u32[]{:S(2)}, u32[]{:S(2)}) collective-permute-start(f32[9,48,128]{2,1,0:T(8,128)S(1)} %slice.48), channel_id=1, source_target_pairs={{0,1},{1,2},{2,3},{3,4},{4,5},{5,6},{6,7},{7,0},{8,9},{9,10},{10,1... | collective-permute-start | bytes 663560 | tf_op jit(solution)/shard_map/ppermute | solution.py:304
  45.4 0.1 collective-permute-done.15.refs_4_
  45.5 0.6 collective-permute-start.17
  46.0 0.3 chunks_1.1.refs_0_
  46.3 0.0 collective-permute-done.3.refs_1_
  46.3 0.6 chunks_2.1.refs_0_
  46.9 0.5 chunks_3.1.refs_0_
  47.4 0.0 copy-start
  47.4 2.8 %collective-permute-done.13.refs_2_ = f32[9,48,128]{2,1,0:T(8,128)S(1)} collective-permute-done((f32[9,48,128]{2,1,0:T(8,128)S(1)}, f32[9,48,128]{2,1,0:T(8,128)S(1)}, u32[]{:S(2)}, u32[]{:S(2)}) %collective-permute-start.13) | collective-permute-done | bytes 221216 | tf_op jit(solution)/shard_map/ppermute | solution.py:304
  50.2 0.0 collective-permute-done.14.refs_3_
  50.2 0.5 chunks_4.1.total_ref
  50.7 1.4 %collective-permute-done.16.refs_0_ = f32[9,48,128]{2,1,0:T(8,128)S(1)} collective-permute-done((f32[9,48,128]{2,1,0:T(8,128)S(1)}, f32[9,48,128]{2,1,0:T(8,128)S(1)}, u32[]{:S(2)}, u32[]{:S(2)}) %collective-permute-start.16) | collective-permute-done | bytes 221216 | tf_op jit(solution)/shard_map/ppermute | solution.py:304
  52.1 2.2 %collective-permute-done.17.refs_1_ = f32[9,48,128]{2,1,0:T(8,128)S(1)} collective-permute-done((f32[9,48,128]{2,1,0:T(8,128)S(1)}, f32[9,48,128]{2,1,0:T(8,128)S(1)}, u32[]{:S(2)}, u32[]{:S(2)}) %collective-permute-start.17) | collective-permute-done | bytes 221216 | tf_op jit(solution)/shard_map/ppermute | solution.py:304
  54.2 0.4 last_chunks.1
  54.6 0.5 collective-permute-start.18
  55.1 0.0 copy-done
  55.1 0.6 %stiff_merge.1.refs_0_.refs_1_ = f32[2,64,1024]{2,1,0:T(8,128)S(1)} custom-call(s32[64]{0:T(128)S(1)} %copy-done.1, f32[4,64,1024]{2,1,0:T(8,128)S(1)} %copy-done, f32[2,64,1024]{2,1,0:T(8,128)S(1)} %collective-permute-done.arrived_ref), custom_call_target="tpu_custom_call" | custom-call | tf_op jit(solution)/shard_map/stiff_merge/pallas_call | solution.py:179
  55.8 0.7 %finish_0.1.refs_0_ = f32[2,64,1024]{2,1,0:T(8,128)} custom-call(f32[2,64,1024]{2,1,0:T(8,128)S(1)} %stiff_merge.1.refs_0_.refs_1_, f32[64,1024]{1,0:T(8,128)S(1)} %get-tuple-element.31.refs_1_), custom_call_target="tpu_custom_call" | custom-call | tf_op jit(solution)/shard_map/finish_0/pallas_call | solution.py:290
  56.5 5.6 %collective-permute-done.18.refs_2_ = f32[64,1024]{1,0:T(8,128)S(1)} collective-permute-done((f32[64,1024]{1,0:T(8,128)S(1)}, f32[64,1024]{1,0:T(8,128)S(1)}, u32[]{:S(2)}, u32[]{:S(2)}) %collective-permute-start.18) | collective-permute-done | bytes 262176 | tf_op jit(solution)/shard_map/ppermute | solution.py:308
  62.1 0.7 %finish_1.1 = f32[2,64,1024]{2,1,0:T(8,128)} custom-call(f32[2,64,1024]{2,1,0:T(8,128)} %finish_0.1.refs_0_, f32[2,64,1024]{2,1,0:T(8,128)S(1)} %stiff_merge.1.refs_0_.refs_1_, f32[64,1024]{1,0:T(8,128)S(1)} %collective-permute-done.18.refs_2_), custom_call_target="tpu_custom_call", output_to_operand_aliasing={{}: (0, {})} | custom-call | tf_op jit(solution)/shard_map/finish_1/pallas_call | solution.py:290
  (10 shorter events, 0.2 us)
Async XLA Ops:
  2.0 2.7 %collective-permute-start.1 = (f32[16,48,128]{2,1,0:T(8,128)S(1)}, f32[16,48,128]{2,1,0:T(8,128)S(1)}, u32[]{:S(2)}, u32[]{:S(2)}) collective-permute-start(f32[16,48,128]{2,1,0:T(8,128)S(1)} %get-tuple-element.20), channel_id=1, source_target_pairs={{0,16},{16,0},{32,48},{48,32},{64,80},{80,64},{96,112},{112,96},{1... | collective-permute-start | bytes 1179656 | tf_op jit(solution)/shard_map/ppermute | solution.py:308
  2.1 0.7 %copy-start.1 = (s32[64]{0:T(128)S(1)}, s32[64]{0:T(128)}, u32[]{:S(2)}) copy-start(s32[64]{0:T(128)} %plan_ref.5) | copy-start | bytes 772
  2.1 6.4 %collective-permute-start.2 = (f32[16,48,128]{2,1,0:T(8,128)S(1)}, f32[16,48,128]{2,1,0:T(8,128)S(1)}, u32[]{:S(2)}, u32[]{:S(2)}) collective-permute-start(f32[16,48,128]{2,1,0:T(8,128)S(1)} %get-tuple-element.24), channel_id=1, source_target_pairs={{0,16},{16,0},{32,48},{48,32},{64,80},{80,64},{96,112},{112,96},{1... | collective-permute-start | bytes 1179656 | tf_op jit(solution)/shard_map/ppermute | solution.py:308
  2.6 6.8 %collective-permute-start = (f32[2,64,1024]{2,1,0:T(8,128)S(1)}, f32[2,64,1024]{2,1,0:T(8,128)S(1)}, u32[]{:S(2)}, u32[]{:S(2)}) collective-permute-start(f32[2,64,1024]{2,1,0:T(8,128)S(1)} %get-tuple-element.19), channel_id=1, source_target_pairs={{0,16},{16,0},{32,48},{48,32},{64,80},{80,64},{96,112},{112,96},{1... | collective-permute-start | bytes 1572872 | tf_op jit(solution)/shard_map/ppermute | solution.py:308
  5.3 10.5 %collective-permute-start.4 = (f32[12,48,128]{2,1,0:T(8,128)S(1)}, f32[12,48,128]{2,1,0:T(8,128)S(1)}, u32[]{:S(2)}, u32[]{:S(2)}) collective-permute-start(f32[12,48,128]{2,1,0:T(8,128)S(1)} %get-tuple-element.22.refs_0_), channel_id=1, source_target_pairs={{0,1},{1,2},{2,3},{3,4},{4,5},{5,6},{6,7},{7,0},{8,9},{9,10},{10,1... | collective-permute-start | bytes 884744 | tf_op jit(solution)/shard_map/ppermute | solution.py:304
  9.2 14.8 %collective-permute-start.7 = (f32[12,48,128]{2,1,0:T(8,128)S(1)}, f32[12,48,128]{2,1,0:T(8,128)S(1)}, u32[]{:S(2)}, u32[]{:S(2)}) collective-permute-start(f32[12,48,128]{2,1,0:T(8,128)S(1)} %get-tuple-element.30), channel_id=1, source_target_pairs={{0,15},{1,8},{2,9},{3,10},{4,11},{5,12},{6,13},{7,14},{8,7},{9,0},... | collective-permute-start | bytes 884744 | tf_op jit(solution)/shard_map/ppermute | solution.py:318
  9.3 19.9 %collective-permute-start.5 = (f32[11,48,128]{2,1,0:T(8,128)S(1)}, f32[11,48,128]{2,1,0:T(8,128)S(1)}, u32[]{:S(2)}, u32[]{:S(2)}) collective-permute-start(f32[11,48,128]{2,1,0:T(8,128)S(1)} %get-tuple-element.27), channel_id=1, source_target_pairs={{0,7},{1,0},{2,1},{3,2},{4,3},{5,4},{6,5},{7,6},{8,15},{9,8},{10,9... | collective-permute-start | bytes 811016 | tf_op jit(solution)/shard_map/ppermute | solution.py:304
  9.4 19.9 %collective-permute-start.6 = (f32[11,48,128]{2,1,0:T(8,128)S(1)}, f32[11,48,128]{2,1,0:T(8,128)S(1)}, u32[]{:S(2)}, u32[]{:S(2)}) collective-permute-start(f32[11,48,128]{2,1,0:T(8,128)S(1)} %get-tuple-element.29), channel_id=1, source_target_pairs={{0,9},{1,10},{2,11},{3,12},{4,13},{5,14},{6,15},{7,8},{8,1},{9,2},... | collective-permute-start | bytes 811016 | tf_op jit(solution)/shard_map/ppermute | solution.py:318
  15.9 16.7 %collective-permute-start.8 = (f32[11,48,128]{2,1,0:T(8,128)S(1)}, f32[11,48,128]{2,1,0:T(8,128)S(1)}, u32[]{:S(2)}, u32[]{:S(2)}) collective-permute-start(f32[11,48,128]{2,1,0:T(8,128)S(1)} %slice.40), channel_id=1, source_target_pairs={{0,1},{1,2},{2,3},{3,4},{4,5},{5,6},{6,7},{7,0},{8,9},{9,10},{10,1... | collective-permute-start | bytes 811016 | tf_op jit(solution)/shard_map/ppermute | solution.py:304
  24.0 10.9 %collective-permute-start.11 = (f32[11,48,128]{2,1,0:T(8,128)S(1)}, f32[11,48,128]{2,1,0:T(8,128)S(1)}, u32[]{:S(2)}, u32[]{:S(2)}) collective-permute-start(f32[11,48,128]{2,1,0:T(8,128)S(1)} %slice.43), channel_id=1, source_target_pairs={{0,7},{1,0},{2,1},{3,2},{4,3},{5,4},{6,5},{7,6},{8,15},{9,8},{10,9... | collective-permute-start | bytes 811016 | tf_op jit(solution)/shard_map/ppermute | solution.py:304
  29.2 11.0 %collective-permute-start.9 = (f32[10,48,128]{2,1,0:T(8,128)S(1)}, f32[10,48,128]{2,1,0:T(8,128)S(1)}, u32[]{:S(2)}, u32[]{:S(2)}) collective-permute-start(f32[10,48,128]{2,1,0:T(8,128)S(1)} %slice.41), channel_id=1, source_target_pairs={{0,7},{1,0},{2,1},{3,2},{4,3},{5,4},{6,5},{7,6},{8,15},{9,8},{10,9... | collective-permute-start | bytes 737288 | tf_op jit(solution)/shard_map/ppermute | solution.py:304
  29.3 11.0 %collective-permute-start.10 = (f32[10,48,128]{2,1,0:T(8,128)S(1)}, f32[10,48,128]{2,1,0:T(8,128)S(1)}, u32[]{:S(2)}, u32[]{:S(2)}) collective-permute-start(f32[10,48,128]{2,1,0:T(8,128)S(1)} %slice.42), channel_id=1, source_target_pairs={{0,1},{1,2},{2,3},{3,4},{4,5},{5,6},{6,7},{7,0},{8,9},{9,10},{10,1... | collective-permute-start | bytes 737288 | tf_op jit(solution)/shard_map/ppermute | solution.py:304
  32.6 11.2 %collective-permute-start.12 = (f32[10,48,128]{2,1,0:T(8,128)S(1)}, f32[10,48,128]{2,1,0:T(8,128)S(1)}, u32[]{:S(2)}, u32[]{:S(2)}) collective-permute-start(f32[10,48,128]{2,1,0:T(8,128)S(1)} %slice.44), channel_id=1, source_target_pairs={{0,1},{1,2},{2,3},{3,4},{4,5},{5,6},{6,7},{7,0},{8,9},{9,10},{10,1... | collective-permute-start | bytes 737288 | tf_op jit(solution)/shard_map/ppermute | solution.py:304
  34.9 10.5 %collective-permute-start.15 = (f32[10,48,128]{2,1,0:T(8,128)S(1)}, f32[10,48,128]{2,1,0:T(8,128)S(1)}, u32[]{:S(2)}, u32[]{:S(2)}) collective-permute-start(f32[10,48,128]{2,1,0:T(8,128)S(1)} %slice.47), channel_id=1, source_target_pairs={{0,7},{1,0},{2,1},{3,2},{4,3},{5,4},{6,5},{7,6},{8,15},{9,8},{10,9... | collective-permute-start | bytes 737288 | tf_op jit(solution)/shard_map/ppermute | solution.py:304
  35.0 11.3 %collective-permute-start.3 = (f32[9,48,128]{2,1,0:T(8,128)S(1)}, f32[9,48,128]{2,1,0:T(8,128)S(1)}, u32[]{:S(2)}, u32[]{:S(2)}) collective-permute-start(f32[9,48,128]{2,1,0:T(8,128)S(1)} %get-tuple-element.26), channel_id=1, source_target_pairs={{0,8},{1,9},{2,10},{3,11},{4,12},{5,13},{6,14},{7,15},{8,0},{9,1},... | collective-permute-start | bytes 663560 | tf_op jit(solution)/shard_map/ppermute | solution.py:318
  40.2 10.0 %collective-permute-start.13 = (f32[9,48,128]{2,1,0:T(8,128)S(1)}, f32[9,48,128]{2,1,0:T(8,128)S(1)}, u32[]{:S(2)}, u32[]{:S(2)}) collective-permute-start(f32[9,48,128]{2,1,0:T(8,128)S(1)} %slice.45), channel_id=1, source_target_pairs={{0,7},{1,0},{2,1},{3,2},{4,3},{5,4},{6,5},{7,6},{8,15},{9,8},{10,9... | collective-permute-start | bytes 663560 | tf_op jit(solution)/shard_map/ppermute | solution.py:304
  40.3 9.9 %collective-permute-start.14 = (f32[9,48,128]{2,1,0:T(8,128)S(1)}, f32[9,48,128]{2,1,0:T(8,128)S(1)}, u32[]{:S(2)}, u32[]{:S(2)}) collective-permute-start(f32[9,48,128]{2,1,0:T(8,128)S(1)} %slice.46), channel_id=1, source_target_pairs={{0,1},{1,2},{2,3},{3,4},{4,5},{5,6},{6,7},{7,0},{8,9},{9,10},{10,1... | collective-permute-start | bytes 663560 | tf_op jit(solution)/shard_map/ppermute | solution.py:304
  43.8 8.2 %collective-permute-start.16 = (f32[9,48,128]{2,1,0:T(8,128)S(1)}, f32[9,48,128]{2,1,0:T(8,128)S(1)}, u32[]{:S(2)}, u32[]{:S(2)}) collective-permute-start(f32[9,48,128]{2,1,0:T(8,128)S(1)} %slice.48), channel_id=1, source_target_pairs={{0,1},{1,2},{2,3},{3,4},{4,5},{5,6},{6,7},{7,0},{8,9},{9,10},{10,1... | collective-permute-start | bytes 663560 | tf_op jit(solution)/shard_map/ppermute | solution.py:304
  45.5 8.7 %collective-permute-start.17 = (f32[9,48,128]{2,1,0:T(8,128)S(1)}, f32[9,48,128]{2,1,0:T(8,128)S(1)}, u32[]{:S(2)}, u32[]{:S(2)}) collective-permute-start(f32[9,48,128]{2,1,0:T(8,128)S(1)} %slice.49), channel_id=1, source_target_pairs={{0,7},{1,0},{2,1},{3,2},{4,3},{5,4},{6,5},{7,6},{8,15},{9,8},{10,9... | collective-permute-start | bytes 663560 | tf_op jit(solution)/shard_map/ppermute | solution.py:304
  47.4 7.7 %copy-start = (f32[4,64,1024]{2,1,0:T(8,128)S(1)}, f32[4,64,1024]{2,1,0:T(8,128)}, u32[]{:S(2)}) copy-start(f32[4,64,1024]{2,1,0:T(8,128)} %b_hbm.1) | copy-start | bytes 3145732
  54.6 7.5 %collective-permute-start.18 = (f32[64,1024]{1,0:T(8,128)S(1)}, f32[64,1024]{1,0:T(8,128)S(1)}, u32[]{:S(2)}, u32[]{:S(2)}) collective-permute-start(f32[64,1024]{1,0:T(8,128)S(1)} %get-tuple-element.32), channel_id=1, source_target_pairs={{0,8},{8,0},{1,9},{9,1},{2,10},{10,2},{3,11},{11,3},{4,12},{12,4},... | collective-permute-start | bytes 786440 | tf_op jit(solution)/shard_map/ppermute | solution.py:308

commit v9 on v3

--- a/solution.py
+++ b/solution.py
@@ -33,70 +33,81 @@
     return position, here
 
 
-def pack(plan, coupling, solve, for_partner):
+def write_pieces(out, c_buf, position, chain, blocks):
+    place = lax.axis_index("tile_1")
+    low = lax.broadcasted_iota(jnp.int32, out.shape[1:], 1) < LANES // 2
+    going_up = hops(chain)[0]
+    for m in range(blocks // 2):
+        first = c_buf[position, :, pl.ds(m * LANES, LANES)]
+        second = c_buf[position, :, pl.ds((m + blocks // 2) * LANES, LANES)]
+        even = jnp.where(low, first, pltpu.roll(second, LANES // 2, 1))
+        odd = jnp.where(low, pltpu.roll(first, LANES // 2, 1), second)
+        for to, piece in ((2 * m, even), (2 * m + 1, odd)):
+            ahead = jnp.bitwise_and(to - place, blocks - 1)
+            out[jnp.where(ahead == 0, 15, jnp.where(ahead <= going_up, ahead - 1, ahead + 7))] = piece
+
+
+def write_panel(out, x_buf, position, chain, blocks):
+    going_up = hops(chain)[0]
+    for n in range(blocks):
+        out[going_up + n] = x_buf[position, :, pl.ds(n * LANES, LANES)]
+
+
+def find(plan, wanted, home):
+    position, here = jnp.int32(0), jnp.bool_(False)
+    for k in range(home):
+        match = plan[k] == wanted
+        position = jnp.where(match, jnp.int32(k), position)
+        here = jnp.logical_or(here, match)
+    return position, here
+
+
+def pack_partner(plan, coupling, solve):
     home, depth, width = solve.shape
     blocks = width // LANES
 
-    def kernel(plan_hbm, c_hbm, x_hbm, out0, out1, plan_ref, c_buf, x_buf, plan_sem, c_sem, x_sem):
+    def kernel(plan_hbm, c_hbm, x_hbm, out0, out1, c_buf, x_buf, plan_out, plan_ref, plan_sem, c_sem, x_sem):
         group = lax.axis_index("group")
-        place = lax.axis_index("tile_1")
-        owner = jnp.bitwise_xor(group, 1) if for_partner else group
-        outs = (out0, out1)
-        copies = [
-            pltpu.make_async_copy(plan_hbm, plan_ref, plan_sem),
-            pltpu.make_async_copy(c_hbm, c_buf, c_sem),
-            pltpu.make_async_copy(x_hbm, x_buf, x_sem),
-        ]
-        for copy in copies:
-            copy.start()
-        low = lax.broadcasted_iota(jnp.int32, (depth, LANES), 1) < LANES // 2
-        copies[0].wait()
-        positions = [locate(plan_ref, group, owner * OWN + slot_of(slot), home)[0] for slot in range(OWN)]
-        copies[1].wait()
-        for slot in range(OWN):
-            up = hops(slot)[0]
-            for m in range(blocks // 2):
-                first = c_buf[positions[slot], :, pl.ds(m * LANES, LANES)]
-                second = c_buf[positions[slot], :, pl.ds((m + blocks // 2) * LANES, LANES)]
-                even = jnp.where(low, first, pltpu.roll(second, LANES // 2, 1))
-                odd = jnp.where(low, pltpu.roll(first, LANES // 2, 1), second)
-                for to, piece in ((2 * m, even), (2 * m + 1, odd)):
-                    ahead = jnp.bitwise_and(to - place, blocks - 1)
-                    spot = jnp.where(ahead == 0, 15, jnp.where(ahead <= up, ahead - 1, ahead + 7))
-                    outs[slot][spot] = piece
-        copies[2].wait()
-        for slot in range(OWN):
-            up = hops(slot)[0]
-            for n in range(blocks):
-                outs[slot][up + n] = x_buf[positions[slot], :, pl.ds(n * LANES, LANES)]
+        plan_copy = pltpu.make_async_copy(plan_hbm, plan_ref, plan_sem)
+        c_copy = pltpu.make_async_copy(c_hbm, c_buf, c_sem)
+        x_copy = pltpu.make_async_copy(x_hbm, x_buf, x_sem)
+        plan_copy.start()
+        c_copy.start()
+        x_copy.start()
+        plan_copy.wait()
+        for k in range(home):
+            plan_out[k] = plan_ref[group * home + k]
+        partner = jnp.bitwise_xor(group, 1)
+        positions = [locate(plan_ref, group, partner * OWN + slot_of(chain), home)[0] for chain in range(2)]
+        c_copy.wait()
+        for chain, out in enumerate((out0, out1)):
+            write_pieces(out, c_buf, positions[chain], chain, blocks)
+        x_copy.wait()
+        for chain, out in enumerate((out0, out1)):
+            write_panel(out, x_buf, positions[chain], chain, blocks)
 
     packet = jax.ShapeDtypeStruct((2 * blocks, depth, LANES), jnp.float32)
-    return pl.pallas_call(
-        kernel,
-        out_shape=(packet, packet),
+    staging = jax.ShapeDtypeStruct(solve.shape, jnp.float32)
+    return pl.pallas_call(
+        kernel,
+        out_shape=(packet, packet, staging, staging, jax.ShapeDtypeStruct((home,), jnp.int32)),
         in_specs=[HBM] * 3,
-        out_specs=(VMEM, VMEM),
-        scratch_shapes=[
-            pltpu.SMEM(plan.shape, jnp.int32),
-            pltpu.VMEM((home, depth, width), jnp.float32),
-            pltpu.VMEM((home, depth, width), jnp.float32),
-            pltpu.SemaphoreType.DMA,
-            pltpu.SemaphoreType.DMA,
-            pltpu.SemaphoreType.DMA,
-        ],
-        compiler_params=PARAMS,
-        name="pack_partner" if for_partner else "pack_own",
+        out_specs=(VMEM, VMEM, VMEM, VMEM, SMEM),
+        scratch_shapes=[pltpu.SMEM(plan.shape, jnp.int32)] + [pltpu.SemaphoreType.DMA] * 3,
+        compiler_params=PARAMS,
+        name="pack_partner",
     )(plan, coupling, solve)
 
 
-def merge(plan, arrived, local, chain, home):
+def merge(plan, arrived, coupling, solve, chain):
     total, depth, _ = arrived.shape
     up, down = hops(chain)
     blocks = total // 2
-
-    def kernel(plan_ref, arrived_ref, local_ref, up_ref, down_ref, own_ref):
+    home = solve.shape[0]
+
+    def kernel(plan_ref, arrived_ref, c_ref, x_ref, up_ref, down_ref, own_ref, packed):
         group = lax.axis_index("group")
-        _, here = locate(plan_ref, group, group * OWN + slot_of(chain), home)
+        position, here = find(plan_ref, group * OWN + slot_of(chain), home)
 
         def put(source):
             up_ref[...] = source[0 : up + blocks]
@@ -109,7 +120,9 @@
 
         @pl.when(here)
         def _():
-            put(local_ref)
+            write_pieces(packed, c_ref, position, chain, blocks)
+            write_panel(packed, x_ref, position, chain, blocks)
+            put(packed)
 
         @pl.when(jnp.logical_not(here))
         def _():
@@ -122,11 +135,12 @@
             jax.ShapeDtypeStruct((down + blocks, depth, LANES), jnp.float32),
             jax.ShapeDtypeStruct((1 if chain == 0 else 1 + blocks, depth, LANES), jnp.float32),
         ),
-        in_specs=[SMEM, VMEM, VMEM],
+        in_specs=[SMEM, VMEM, VMEM, VMEM],
         out_specs=(VMEM, VMEM, VMEM),
+        scratch_shapes=[pltpu.VMEM(arrived.shape, jnp.float32)],
         compiler_params=PARAMS,
         name=f"merge_{chain}",
-    )(plan, arrived, local)
+    )(plan, arrived, coupling, solve)
 
 
 def stiff_out(plan, stiff):
@@ -304,6 +318,10 @@
     return lax.ppermute(array, axis, [(i, i ^ 1) for i in range(lax.axis_size(axis))])
 
 
+def after(array, *earlier):
+    return lax.optimization_barrier((array, *earlier))[0]
+
+
 def crossed(array, distance):
     size = lax.axis_size("tile_1")
     pairs = [(x * size + z, (1 - x) * size + (z + distance) % size) for x in range(2) for z in range(size)]
@@ -315,12 +333,11 @@
     blocks = width // LANES
     pieces = jnp.swapaxes(coupling, 1, 2)
     in_hbm = [pltpu.with_memory_space_constraint(a, pltpu.HBM) for a in (migration, pieces, interior_solve)]
-    outgoing = pack(*in_hbm, True)
-    arrived = [swapped(outgoing[0], "group"), swapped(outgoing[1], "group")]
-    local = pack(*in_hbm, False)
+    out0, out1, c_home, x_home, home_plan = pack_partner(*in_hbm)
+    arrived = [swapped(out0, "group"), swapped(out1, "group")]
     ups, downs, owns = [None, None], [None, None], [None, None]
     for chain in range(2):
-        ups[chain], downs[chain], owns[chain] = merge(migration, arrived[chain], local[chain], chain, home)
+        ups[chain], downs[chain], owns[chain] = merge(home_plan, arrived[chain], c_home, x_home, chain)
     stiff_arrived = swapped(stiff_out(migration, boundary_stiffness), "group")
     stiff = stiff_merge(migration, boundary_stiffness, stiff_arrived)
 

time: 61.8 us -> 61.9 us (level)
  waiting for transfers between devices: 15.2 us -> 16.5 us
  Pallas kernels: 9 us -> 8.35 us
  local copies, waits for them, and re-layouts: 0.81 us -> 0.18 us
    ppermute x4, waiting for transfers between devices: 4.46 us -> 5.66 us  [swapped(): lax.ppermute(array, axis, [(i, i ^ 1) for i in range(lax.axis_size(axis))])]
    pallas_call x2 -> x1, Pallas kernels: 2.85 us -> 1.99 us  [pack_partner(): pl.pallas_call(kernel, out_shape=(packet, packet, staging, staging, jax.S...]
    unnamed x4, local copies, waits for them, and re-layouts: 0.65 us -> 0.01 us
  transfers between devices with their start and end apart: 19 -> 19, of which waited for: 10 -> 11; matrix products, arithmetic and copies ran while one was open for 0% -> 0% of each run, Pallas kernels for 11% -> 9%
where the time goes in v9:
time: 61.9 us; the launch traced here: 61.2 us
  starting transfers between devices  35.8 us (58%)
  waiting for transfers between devices  16.5 us (27%)
  Pallas kernels  8.35 us (13%)
    ppermute x12, starting transfers between devices, shifted(): lax.ppermute(array, axis, [(i, (i + distance) % size) for i in range(size)])  28.6 us
    ppermute x12, waiting for transfers between devices, shifted(): lax.ppermute(array, axis, [(i, (i + distance) % size) for i in range(size)])  8.72 us
    ppermute x3, starting transfers between devices, crossed(): return lax.ppermute(array, TILE, pairs)  5.88 us
    ppermute x4, waiting for transfers between devices, swapped(): lax.ppermute(array, axis, [(i, i ^ 1) for i in range(lax.axis_size(axis))])  5.66 us
    ppermute x3, waiting for transfers between devices, crossed(): return lax.ppermute(array, TILE, pairs)  2.08 us
    pallas_call x1, Pallas kernels, pack_partner(): pl.pallas_call(kernel, out_shape=(packet, packet, staging, staging, jax.S...  1.99 us
    pallas_call x4, Pallas kernels, accumulate(): pl.pallas_call(kernel, out_shape=jax.ShapeDtypeStruct((LANES, width), jnp...  1.82 us
    pallas_call x2, Pallas kernels, finish(): pl.pallas_call(kernel, out_shape=jax.ShapeDtypeStruct((OWN, rows, width),...  1.48 us
  transfers between devices with their start and end apart: 19, of which 11 were waited for; matrix products, arithmetic and copies ran while one was open for 0% of the time, Pallas kernels for 9%

profile of v9, /device:TPU:24, one launch (start us, length us, event | category | flops | bytes accessed | tf_op | source)
XLA Modules:
  0.0 61.2 jit_solution(18425748068448831744)
XLA Ops:
  0.0 2.0 %pack_partner.1 = (f32[16,48,128]{2,1,0:T(8,128)S(1)}, f32[16,48,128]{2,1,0:T(8,128)S(1)}, f32[4,48,1024]{2,1,0:T(8,128)S(1)}, f32[4,48,1024]{2,1,0:T(8,128)S(1)}, s32[4]{0:T(128)S(1)}) custom-call(s32[64]{0:T(128)} %plan_hbm.1, f32[4,48,1024]{2,1,0:T(8,128)} %bitcast.1, f32[4,48,1024]{2,1,0:T(8,128)} %x_hbm.1), custom_call_target="tpu_custom_call" | custom-call | tf_op jit(solution)/shard_map/pack_partner/pallas_call | solution.py:91
  2.0 0.1 collective-permute-start.1
  2.1 0.5 collective-permute-start.2
  2.6 1.2 %collective-permute-done.1.arrived_ref = f32[16,48,128]{2,1,0:T(8,128)S(1)} collective-permute-done((f32[16,48,128]{2,1,0:T(8,128)S(1)}, f32[16,48,128]{2,1,0:T(8,128)S(1)}, u32[]{:S(2)}, u32[]{:S(2)}) %collective-permute-start.1) | collective-permute-done | bytes 393248 | tf_op jit(solution)/shard_map/ppermute | solution.py:318
  3.8 0.7 %merge_0.1 = (f32[12,48,128]{2,1,0:T(8,128)S(1)}, f32[11,48,128]{2,1,0:T(8,128)S(1)}, f32[1,48,128]{2,1,0:T(8,128)S(1)}) custom-call(s32[4]{0:T(128)S(1)} %get-tuple-element.18.plan_ref, f32[16,48,128]{2,1,0:T(8,128)S(1)} %collective-permute-done.1.arrived_ref, f32[4,48,1024]{2,1,0:T(8,128)S(1)} %get-tuple-element.20.c_ref, ...), custom_call_target="tpu_custom_call" | custom-call | tf_op jit(solution)/shard_map/merge_0/pallas_call | solution.py:131
  4.5 2.0 %collective-permute-start.4 = (f32[12,48,128]{2,1,0:T(8,128)S(1)}, f32[12,48,128]{2,1,0:T(8,128)S(1)}, u32[]{:S(2)}, u32[]{:S(2)}) collective-permute-start(f32[12,48,128]{2,1,0:T(8,128)S(1)} %get-tuple-element.22.refs_0_), channel_id=1, source_target_pairs={{0,1},{1,2},{2,3},{3,4},{4,5},{5,6},{6,7},{7,0},{8,9},{9,10},{10,1... | collective-permute-start | bytes 884744 | tf_op jit(solution)/shard_map/ppermute | solution.py:314
  6.5 0.0 collective-permute-done.2.arrived_ref
  6.5 0.7 %merge_1.1 = (f32[11,48,128]{2,1,0:T(8,128)S(1)}, f32[12,48,128]{2,1,0:T(8,128)S(1)}, f32[9,48,128]{2,1,0:T(8,128)S(1)}) custom-call(s32[4]{0:T(128)S(1)} %get-tuple-element.18.plan_ref, f32[16,48,128]{2,1,0:T(8,128)S(1)} %collective-permute-done.2.arrived_ref, f32[4,48,1024]{2,1,0:T(8,128)S(1)} %get-tuple-element.20.c_ref, ...), custom_call_target="tpu_custom_call" | custom-call | tf_op jit(solution)/shard_map/merge_1/pallas_call | solution.py:131
  7.2 5.0 %collective-permute-start.7 = (f32[12,48,128]{2,1,0:T(8,128)S(1)}, f32[12,48,128]{2,1,0:T(8,128)S(1)}, u32[]{:S(2)}, u32[]{:S(2)}) collective-permute-start(f32[12,48,128]{2,1,0:T(8,128)S(1)} %get-tuple-element.28), channel_id=1, source_target_pairs={{0,15},{1,8},{2,9},{3,10},{4,11},{5,12},{6,13},{7,14},{8,7},{9,0},... | collective-permute-start | bytes 884744 | tf_op jit(solution)/shard_map/ppermute | solution.py:328
  12.2 0.0 collective-permute-start.6
  12.2 3.2 %collective-permute-start.5 = (f32[11,48,128]{2,1,0:T(8,128)S(1)}, f32[11,48,128]{2,1,0:T(8,128)S(1)}, u32[]{:S(2)}, u32[]{:S(2)}) collective-permute-start(f32[11,48,128]{2,1,0:T(8,128)S(1)} %get-tuple-element.26), channel_id=1, source_target_pairs={{0,7},{1,0},{2,1},{3,2},{4,3},{5,4},{6,5},{7,6},{8,15},{9,8},{10,9... | collective-permute-start | bytes 811016 | tf_op jit(solution)/shard_map/ppermute | solution.py:314
  15.4 2.9 %collective-permute-done.4.refs_2_ = f32[12,48,128]{2,1,0:T(8,128)S(1)} collective-permute-done((f32[12,48,128]{2,1,0:T(8,128)S(1)}, f32[12,48,128]{2,1,0:T(8,128)S(1)}, u32[]{:S(2)}, u32[]{:S(2)}) %collective-permute-start.4) | collective-permute-done | bytes 294944 | tf_op jit(solution)/shard_map/ppermute | solution.py:314
  18.3 0.1 collective-permute-start.8
  18.4 1.5 %collective-permute-done.7.refs_5_ = f32[12,48,128]{2,1,0:T(8,128)S(1)} collective-permute-done((f32[12,48,128]{2,1,0:T(8,128)S(1)}, f32[12,48,128]{2,1,0:T(8,128)S(1)}, u32[]{:S(2)}, u32[]{:S(2)}) %collective-permute-start.7) | collective-permute-done | bytes 294944 | tf_op jit(solution)/shard_map/ppermute | solution.py:328
  19.8 0.0 copy-start
  19.9 4.5 %collective-permute-start.11 = (f32[11,48,128]{2,1,0:T(8,128)S(1)}, f32[11,48,128]{2,1,0:T(8,128)S(1)}, u32[]{:S(2)}, u32[]{:S(2)}) collective-permute-start(f32[11,48,128]{2,1,0:T(8,128)S(1)} %slice.43), channel_id=1, source_target_pairs={{0,7},{1,0},{2,1},{3,2},{4,3},{5,4},{6,5},{7,6},{8,15},{9,8},{10,9... | collective-permute-start | bytes 811016 | tf_op jit(solution)/shard_map/ppermute | solution.py:314
  24.4 0.6 %collective-permute-done.6.refs_4_ = f32[11,48,128]{2,1,0:T(8,128)S(1)} collective-permute-done((f32[11,48,128]{2,1,0:T(8,128)S(1)}, f32[11,48,128]{2,1,0:T(8,128)S(1)}, u32[]{:S(2)}, u32[]{:S(2)}) %collective-permute-start.6) | collective-permute-done | bytes 270368 | tf_op jit(solution)/shard_map/ppermute | solution.py:328
  25.0 0.7 %collective-permute-start.10 = (f32[10,48,128]{2,1,0:T(8,128)S(1)}, f32[10,48,128]{2,1,0:T(8,128)S(1)}, u32[]{:S(2)}, u32[]{:S(2)}) collective-permute-start(f32[10,48,128]{2,1,0:T(8,128)S(1)} %slice.42), channel_id=1, source_target_pairs={{0,1},{1,2},{2,3},{3,4},{4,5},{5,6},{6,7},{7,0},{8,9},{9,10},{10,1... | collective-permute-start | bytes 737288 | tf_op jit(solution)/shard_map/ppermute | solution.py:314
  25.7 0.0 collective-permute-done.5.refs_3_
  25.7 3.7 %collective-permute-start.9 = (f32[10,48,128]{2,1,0:T(8,128)S(1)}, f32[10,48,128]{2,1,0:T(8,128)S(1)}, u32[]{:S(2)}, u32[]{:S(2)}) collective-permute-start(f32[10,48,128]{2,1,0:T(8,128)S(1)} %slice.41), channel_id=1, source_target_pairs={{0,7},{1,0},{2,1},{3,2},{4,3},{5,4},{6,5},{7,6},{8,15},{9,8},{10,9... | collective-permute-start | bytes 737288 | tf_op jit(solution)/shard_map/ppermute | solution.py:314
  29.4 0.4 collective-permute-done.8.refs_1_
  29.9 1.1 %collective-permute-start.12 = (f32[10,48,128]{2,1,0:T(8,128)S(1)}, f32[10,48,128]{2,1,0:T(8,128)S(1)}, u32[]{:S(2)}, u32[]{:S(2)}) collective-permute-start(f32[10,48,128]{2,1,0:T(8,128)S(1)} %slice.44), channel_id=1, source_target_pairs={{0,1},{1,2},{2,3},{3,4},{4,5},{5,6},{6,7},{7,0},{8,9},{9,10},{10,1... | collective-permute-start | bytes 737288 | tf_op jit(solution)/shard_map/ppermute | solution.py:314
  31.0 0.4 collective-permute-done.11.refs_4_
  31.4 0.0 copy-start.1
  31.4 3.8 %collective-permute-start.15 = (f32[10,48,128]{2,1,0:T(8,128)S(1)}, f32[10,48,128]{2,1,0:T(8,128)S(1)}, u32[]{:S(2)}, u32[]{:S(2)}) collective-permute-start(f32[10,48,128]{2,1,0:T(8,128)S(1)} %slice.47), channel_id=1, source_target_pairs={{0,7},{1,0},{2,1},{3,2},{4,3},{5,4},{6,5},{7,6},{8,15},{9,8},{10,9... | collective-permute-start | bytes 737288 | tf_op jit(solution)/shard_map/ppermute | solution.py:314
  35.2 0.9 %collective-permute-start.3 = (f32[9,48,128]{2,1,0:T(8,128)S(1)}, f32[9,48,128]{2,1,0:T(8,128)S(1)}, u32[]{:S(2)}, u32[]{:S(2)}) collective-permute-start(f32[9,48,128]{2,1,0:T(8,128)S(1)} %get-tuple-element.25), channel_id=1, source_target_pairs={{0,8},{1,9},{2,10},{3,11},{4,12},{5,13},{6,14},{7,15},{8,0},{9,1},... | collective-permute-start | bytes 663560 | tf_op jit(solution)/shard_map/ppermute | solution.py:328
  36.1 0.0 copy-done
  36.1 0.0 copy-done.1
  36.1 0.6 %stiff_out.1 = f32[2,64,1024]{2,1,0:T(8,128)S(1)} custom-call(s32[64]{0:T(128)S(1)} %copy-done.1, f32[4,64,1024]{2,1,0:T(8,128)S(1)} %copy-done), custom_call_target="tpu_custom_call" | custom-call | tf_op jit(solution)/shard_map/stiff_out/pallas_call | solution.py:160
  36.8 0.0 collective-permute-done.10.refs_3_
  36.8 0.1 collective-permute-start
  36.9 0.0 collective-permute-done.9.refs_2_
  36.9 0.7 %collective-permute-start.14 = (f32[9,48,128]{2,1,0:T(8,128)S(1)}, f32[9,48,128]{2,1,0:T(8,128)S(1)}, u32[]{:S(2)}, u32[]{:S(2)}) collective-permute-start(f32[9,48,128]{2,1,0:T(8,128)S(1)} %slice.46), channel_id=1, source_target_pairs={{0,1},{1,2},{2,3},{3,4},{4,5},{5,6},{6,7},{7,0},{8,9},{9,10},{10,1... | collective-permute-start | bytes 663560 | tf_op jit(solution)/shard_map/ppermute | solution.py:314
  37.6 2.1 %collective-permute-done.12.refs_1_ = f32[10,48,128]{2,1,0:T(8,128)S(1)} collective-permute-done((f32[10,48,128]{2,1,0:T(8,128)S(1)}, f32[10,48,128]{2,1,0:T(8,128)S(1)}, u32[]{:S(2)}, u32[]{:S(2)}) %collective-permute-start.12) | collective-permute-done | bytes 245792 | tf_op jit(solution)/shard_map/ppermute | solution.py:314
  39.8 5.5 %collective-permute-start.13 = (f32[9,48,128]{2,1,0:T(8,128)S(1)}, f32[9,48,128]{2,1,0:T(8,128)S(1)}, u32[]{:S(2)}, u32[]{:S(2)}) collective-permute-start(f32[9,48,128]{2,1,0:T(8,128)S(1)} %slice.45), channel_id=1, source_target_pairs={{0,7},{1,0},{2,1},{3,2},{4,3},{5,4},{6,5},{7,6},{8,15},{9,8},{10,9... | collective-permute-start | bytes 663560 | tf_op jit(solution)/shard_map/ppermute | solution.py:314
  45.3 0.0 collective-permute-done.15.refs_4_
  45.3 0.1 collective-permute-start.16
  45.4 0.0 collective-permute-done.3.refs_1_
  45.4 3.3 %collective-permute-start.17 = (f32[9,48,128]{2,1,0:T(8,128)S(1)}, f32[9,48,128]{2,1,0:T(8,128)S(1)}, u32[]{:S(2)}, u32[]{:S(2)}) collective-permute-start(f32[9,48,128]{2,1,0:T(8,128)S(1)} %slice.49), channel_id=1, source_target_pairs={{0,7},{1,0},{2,1},{3,2},{4,3},{5,4},{6,5},{7,6},{8,15},{9,8},{10,9... | collective-permute-start | bytes 663560 | tf_op jit(solution)/shard_map/ppermute | solution.py:314
  48.7 0.3 chunks_1.1.refs_0_
  49.0 0.6 chunks_2.1.refs_0_
  49.5 0.5 chunks_3.1.refs_0_
  50.0 0.0 collective-permute-done.14.refs_3_
  50.1 0.8 %collective-permute-done.13.refs_2_ = f32[9,48,128]{2,1,0:T(8,128)S(1)} collective-permute-done((f32[9,48,128]{2,1,0:T(8,128)S(1)}, f32[9,48,128]{2,1,0:T(8,128)S(1)}, u32[]{:S(2)}, u32[]{:S(2)}) %collective-permute-start.13) | collective-permute-done | bytes 221216 | tf_op jit(solution)/shard_map/ppermute | solution.py:314
  50.9 0.5 chunks_4.1.total_ref
  51.4 1.1 %collective-permute-done.16.refs_0_ = f32[9,48,128]{2,1,0:T(8,128)S(1)} collective-permute-done((f32[9,48,128]{2,1,0:T(8,128)S(1)}, f32[9,48,128]{2,1,0:T(8,128)S(1)}, u32[]{:S(2)}, u32[]{:S(2)}) %collective-permute-start.16) | collective-permute-done | bytes 221216 | tf_op jit(solution)/shard_map/ppermute | solution.py:314
  52.5 0.9 %collective-permute-done.17.refs_1_ = f32[9,48,128]{2,1,0:T(8,128)S(1)} collective-permute-done((f32[9,48,128]{2,1,0:T(8,128)S(1)}, f32[9,48,128]{2,1,0:T(8,128)S(1)}, u32[]{:S(2)}, u32[]{:S(2)}) %collective-permute-start.17) | collective-permute-done | bytes 221216 | tf_op jit(solution)/shard_map/ppermute | solution.py:314
  53.4 0.4 last_chunks.1
  53.8 0.6 %collective-permute-start.18 = (f32[64,1024]{1,0:T(8,128)S(1)}, f32[64,1024]{1,0:T(8,128)S(1)}, u32[]{:S(2)}, u32[]{:S(2)}) collective-permute-start(f32[64,1024]{1,0:T(8,128)S(1)} %get-tuple-element.30), channel_id=1, source_target_pairs={{0,8},{8,0},{1,9},{9,1},{2,10},{10,2},{3,11},{11,3},{4,12},{12,4},... | collective-permute-start | bytes 786440 | tf_op jit(solution)/shard_map/ppermute | solution.py:318
  54.5 0.0 collective-permute-done.arrived_ref
  54.5 0.6 %stiff_merge.1.refs_0_.refs_1_ = f32[2,64,1024]{2,1,0:T(8,128)S(1)} custom-call(s32[64]{0:T(128)S(1)} %copy-done.1, f32[4,64,1024]{2,1,0:T(8,128)S(1)} %copy-done, f32[2,64,1024]{2,1,0:T(8,128)S(1)} %collective-permute-done.arrived_ref), custom_call_target="tpu_custom_call" | custom-call | tf_op jit(solution)/shard_map/stiff_merge/pallas_call | solution.py:189
  55.1 0.7 %finish_0.1.refs_0_ = f32[2,64,1024]{2,1,0:T(8,128)} custom-call(f32[2,64,1024]{2,1,0:T(8,128)S(1)} %stiff_merge.1.refs_0_.refs_1_, f32[64,1024]{1,0:T(8,128)S(1)} %get-tuple-element.29.refs_1_), custom_call_target="tpu_custom_call" | custom-call | tf_op jit(solution)/shard_map/finish_0/pallas_call | solution.py:300
  55.9 4.4 %collective-permute-done.18.refs_2_ = f32[64,1024]{1,0:T(8,128)S(1)} collective-permute-done((f32[64,1024]{1,0:T(8,128)S(1)}, f32[64,1024]{1,0:T(8,128)S(1)}, u32[]{:S(2)}, u32[]{:S(2)}) %collective-permute-start.18) | collective-permute-done | bytes 262176 | tf_op jit(solution)/shard_map/ppermute | solution.py:318
  60.3 0.7 %finish_1.1 = f32[2,64,1024]{2,1,0:T(8,128)} custom-call(f32[2,64,1024]{2,1,0:T(8,128)} %finish_0.1.refs_0_, f32[2,64,1024]{2,1,0:T(8,128)S(1)} %stiff_merge.1.refs_0_.refs_1_, f32[64,1024]{1,0:T(8,128)S(1)} %collective-permute-done.18.refs_2_), custom_call_target="tpu_custom_call", output_to_operand_aliasing={{}: (0, {})} | custom-call | tf_op jit(solution)/shard_map/finish_1/pallas_call | solution.py:300
  (10 shorter events, 0.2 us)
Async XLA Ops:
  2.0 1.8 %collective-permute-start.1 = (f32[16,48,128]{2,1,0:T(8,128)S(1)}, f32[16,48,128]{2,1,0:T(8,128)S(1)}, u32[]{:S(2)}, u32[]{:S(2)}) collective-permute-start(f32[16,48,128]{2,1,0:T(8,128)S(1)} %get-tuple-element.19), channel_id=1, source_target_pairs={{0,16},{16,0},{32,48},{48,32},{64,80},{80,64},{96,112},{112,96},{1... | collective-permute-start | bytes 1179656 | tf_op jit(solution)/shard_map/ppermute | solution.py:318
  2.1 4.4 %collective-permute-start.2 = (f32[16,48,128]{2,1,0:T(8,128)S(1)}, f32[16,48,128]{2,1,0:T(8,128)S(1)}, u32[]{:S(2)}, u32[]{:S(2)}) collective-permute-start(f32[16,48,128]{2,1,0:T(8,128)S(1)} %get-tuple-element.24), channel_id=1, source_target_pairs={{0,16},{16,0},{32,48},{48,32},{64,80},{80,64},{96,112},{112,96},{1... | collective-permute-start | bytes 1179656 | tf_op jit(solution)/shard_map/ppermute | solution.py:318
  4.5 13.7 %collective-permute-start.4 = (f32[12,48,128]{2,1,0:T(8,128)S(1)}, f32[12,48,128]{2,1,0:T(8,128)S(1)}, u32[]{:S(2)}, u32[]{:S(2)}) collective-permute-start(f32[12,48,128]{2,1,0:T(8,128)S(1)} %get-tuple-element.22.refs_0_), channel_id=1, source_target_pairs={{0,1},{1,2},{2,3},{3,4},{4,5},{5,6},{6,7},{7,0},{8,9},{9,10},{10,1... | collective-permute-start | bytes 884744 | tf_op jit(solution)/shard_map/ppermute | solution.py:314
  7.2 12.6 %collective-permute-start.7 = (f32[12,48,128]{2,1,0:T(8,128)S(1)}, f32[12,48,128]{2,1,0:T(8,128)S(1)}, u32[]{:S(2)}, u32[]{:S(2)}) collective-permute-start(f32[12,48,128]{2,1,0:T(8,128)S(1)} %get-tuple-element.28), channel_id=1, source_target_pairs={{0,15},{1,8},{2,9},{3,10},{4,11},{5,12},{6,13},{7,14},{8,7},{9,0},... | collective-permute-start | bytes 884744 | tf_op jit(solution)/shard_map/ppermute | solution.py:328
  12.2 12.8 %collective-permute-start.6 = (f32[11,48,128]{2,1,0:T(8,128)S(1)}, f32[11,48,128]{2,1,0:T(8,128)S(1)}, u32[]{:S(2)}, u32[]{:S(2)}) collective-permute-start(f32[11,48,128]{2,1,0:T(8,128)S(1)} %get-tuple-element.27), channel_id=1, source_target_pairs={{0,9},{1,10},{2,11},{3,12},{4,13},{5,14},{6,15},{7,8},{8,1},{9,2},... | collective-permute-start | bytes 811016 | tf_op jit(solution)/shard_map/ppermute | solution.py:328
  12.2 13.5 %collective-permute-start.5 = (f32[11,48,128]{2,1,0:T(8,128)S(1)}, f32[11,48,128]{2,1,0:T(8,128)S(1)}, u32[]{:S(2)}, u32[]{:S(2)}) collective-permute-start(f32[11,48,128]{2,1,0:T(8,128)S(1)} %get-tuple-element.26), channel_id=1, source_target_pairs={{0,7},{1,0},{2,1},{3,2},{4,3},{5,4},{6,5},{7,6},{8,15},{9,8},{10,9... | collective-permute-start | bytes 811016 | tf_op jit(solution)/shard_map/ppermute | solution.py:314
  18.3 11.6 %collective-permute-start.8 = (f32[11,48,128]{2,1,0:T(8,128)S(1)}, f32[11,48,128]{2,1,0:T(8,128)S(1)}, u32[]{:S(2)}, u32[]{:S(2)}) collective-permute-start(f32[11,48,128]{2,1,0:T(8,128)S(1)} %slice.40), channel_id=1, source_target_pairs={{0,1},{1,2},{2,3},{3,4},{4,5},{5,6},{6,7},{7,0},{8,9},{9,10},{10,1... | collective-permute-start | bytes 811016 | tf_op jit(solution)/shard_map/ppermute | solution.py:314
  19.8 16.3 %copy-start = (f32[4,64,1024]{2,1,0:T(8,128)S(1)}, f32[4,64,1024]{2,1,0:T(8,128)}, u32[]{:S(2)}) copy-start(f32[4,64,1024]{2,1,0:T(8,128)} %b_hbm.3) | copy-start | bytes 3145732
  19.9 11.6 %collective-permute-start.11 = (f32[11,48,128]{2,1,0:T(8,128)S(1)}, f32[11,48,128]{2,1,0:T(8,128)S(1)}, u32[]{:S(2)}, u32[]{:S(2)}) collective-permute-start(f32[11,48,128]{2,1,0:T(8,128)S(1)} %slice.43), channel_id=1, source_target_pairs={{0,7},{1,0},{2,1},{3,2},{4,3},{5,4},{6,5},{7,6},{8,15},{9,8},{10,9... | collective-permute-start | bytes 811016 | tf_op jit(solution)/shard_map/ppermute | solution.py:314
  25.0 11.8 %collective-permute-start.10 = (f32[10,48,128]{2,1,0:T(8,128)S(1)}, f32[10,48,128]{2,1,0:T(8,128)S(1)}, u32[]{:S(2)}, u32[]{:S(2)}) collective-permute-start(f32[10,48,128]{2,1,0:T(8,128)S(1)} %slice.42), channel_id=1, source_target_pairs={{0,1},{1,2},{2,3},{3,4},{4,5},{5,6},{6,7},{7,0},{8,9},{9,10},{10,1... | collective-permute-start | bytes 737288 | tf_op jit(solution)/shard_map/ppermute | solution.py:314
  25.7 11.2 %collective-permute-start.9 = (f32[10,48,128]{2,1,0:T(8,128)S(1)}, f32[10,48,128]{2,1,0:T(8,128)S(1)}, u32[]{:S(2)}, u32[]{:S(2)}) collective-permute-start(f32[10,48,128]{2,1,0:T(8,128)S(1)} %slice.41), channel_id=1, source_target_pairs={{0,7},{1,0},{2,1},{3,2},{4,3},{5,4},{6,5},{7,6},{8,15},{9,8},{10,9... | collective-permute-start | bytes 737288 | tf_op jit(solution)/shard_map/ppermute | solution.py:314
  29.9 9.9 %collective-permute-start.12 = (f32[10,48,128]{2,1,0:T(8,128)S(1)}, f32[10,48,128]{2,1,0:T(8,128)S(1)}, u32[]{:S(2)}, u32[]{:S(2)}) collective-permute-start(f32[10,48,128]{2,1,0:T(8,128)S(1)} %slice.44), channel_id=1, source_target_pairs={{0,1},{1,2},{2,3},{3,4},{4,5},{5,6},{6,7},{7,0},{8,9},{9,10},{10,1... | collective-permute-start | bytes 737288 | tf_op jit(solution)/shard_map/ppermute | solution.py:314
  31.4 4.7 %copy-start.1 = (s32[64]{0:T(128)S(1)}, s32[64]{0:T(128)}, u32[]{:S(2)}) copy-start(s32[64]{0:T(128)} %plan_hbm.1) | copy-start | bytes 772
  31.4 13.8 %collective-permute-start.15 = (f32[10,48,128]{2,1,0:T(8,128)S(1)}, f32[10,48,128]{2,1,0:T(8,128)S(1)}, u32[]{:S(2)}, u32[]{:S(2)}) collective-permute-start(f32[10,48,128]{2,1,0:T(8,128)S(1)} %slice.47), channel_id=1, source_target_pairs={{0,7},{1,0},{2,1},{3,2},{4,3},{5,4},{6,5},{7,6},{8,15},{9,8},{10,9... | collective-permute-start | bytes 737288 | tf_op jit(solution)/shard_map/ppermute | solution.py:314
  35.2 10.2 %collective-permute-start.3 = (f32[9,48,128]{2,1,0:T(8,128)S(1)}, f32[9,48,128]{2,1,0:T(8,128)S(1)}, u32[]{:S(2)}, u32[]{:S(2)}) collective-permute-start(f32[9,48,128]{2,1,0:T(8,128)S(1)} %get-tuple-element.25), channel_id=1, source_target_pairs={{0,8},{1,9},{2,10},{3,11},{4,12},{5,13},{6,14},{7,15},{8,0},{9,1},... | collective-permute-start | bytes 663560 | tf_op jit(solution)/shard_map/ppermute | solution.py:328
  36.8 17.7 %collective-permute-start = (f32[2,64,1024]{2,1,0:T(8,128)S(1)}, f32[2,64,1024]{2,1,0:T(8,128)S(1)}, u32[]{:S(2)}, u32[]{:S(2)}) collective-permute-start(f32[2,64,1024]{2,1,0:T(8,128)S(1)} %stiff_out.1), channel_id=1, source_target_pairs={{0,16},{16,0},{32,48},{48,32},{64,80},{80,64},{96,112},{112,96},{1... | collective-permute-start | bytes 1572872 | tf_op jit(solution)/shard_map/ppermute | solution.py:318
  36.9 13.1 %collective-permute-start.14 = (f32[9,48,128]{2,1,0:T(8,128)S(1)}, f32[9,48,128]{2,1,0:T(8,128)S(1)}, u32[]{:S(2)}, u32[]{:S(2)}) collective-permute-start(f32[9,48,128]{2,1,0:T(8,128)S(1)} %slice.46), channel_id=1, source_target_pairs={{0,1},{1,2},{2,3},{3,4},{4,5},{5,6},{6,7},{7,0},{8,9},{9,10},{10,1... | collective-permute-start | bytes 663560 | tf_op jit(solution)/shard_map/ppermute | solution.py:314
  39.8 11.1 %collective-permute-start.13 = (f32[9,48,128]{2,1,0:T(8,128)S(1)}, f32[9,48,128]{2,1,0:T(8,128)S(1)}, u32[]{:S(2)}, u32[]{:S(2)}) collective-permute-start(f32[9,48,128]{2,1,0:T(8,128)S(1)} %slice.45), channel_id=1, source_target_pairs={{0,7},{1,0},{2,1},{3,2},{4,3},{5,4},{6,5},{7,6},{8,15},{9,8},{10,9... | collective-permute-start | bytes 663560 | tf_op jit(solution)/shard_map/ppermute | solution.py:314
  45.3 7.2 %collective-permute-start.16 = (f32[9,48,128]{2,1,0:T(8,128)S(1)}, f32[9,48,128]{2,1,0:T(8,128)S(1)}, u32[]{:S(2)}, u32[]{:S(2)}) collective-permute-start(f32[9,48,128]{2,1,0:T(8,128)S(1)} %slice.48), channel_id=1, source_target_pairs={{0,1},{1,2},{2,3},{3,4},{4,5},{5,6},{6,7},{7,0},{8,9},{9,10},{10,1... | collective-permute-start | bytes 663560 | tf_op jit(solution)/shard_map/ppermute | solution.py:314
  45.4 8.0 %collective-permute-start.17 = (f32[9,48,128]{2,1,0:T(8,128)S(1)}, f32[9,48,128]{2,1,0:T(8,128)S(1)}, u32[]{:S(2)}, u32[]{:S(2)}) collective-permute-start(f32[9,48,128]{2,1,0:T(8,128)S(1)} %slice.49), channel_id=1, source_target_pairs={{0,7},{1,0},{2,1},{3,2},{4,3},{5,4},{6,5},{7,6},{8,15},{9,8},{10,9... | collective-permute-start | bytes 663560 | tf_op jit(solution)/shard_map/ppermute | solution.py:314
  53.8 6.5 %collective-permute-start.18 = (f32[64,1024]{1,0:T(8,128)S(1)}, f32[64,1024]{1,0:T(8,128)S(1)}, u32[]{:S(2)}, u32[]{:S(2)}) collective-permute-start(f32[64,1024]{1,0:T(8,128)S(1)} %get-tuple-element.30), channel_id=1, source_target_pairs={{0,8},{8,0},{1,9},{9,1},{2,10},{10,2},{3,11},{11,3},{4,12},{12,4},... | collective-permute-start | bytes 786440 | tf_op jit(solution)/shard_map/ppermute | solution.py:318

commit v10 on v3

--- a/solution.py
+++ b/solution.py
@@ -37,7 +37,8 @@
     home, depth, width = solve.shape
     blocks = width // LANES
 
-    def kernel(plan_hbm, c_hbm, x_hbm, out0, out1, plan_ref, c_buf, x_buf, plan_sem, c_sem, x_sem):
+    def kernel(plan_hbm, c_hbm, x_hbm, out0, out1, *refs):
+        plan_ref, c_buf, x_buf, plan_sem, c_sem, x_sem = refs[-6:]
         group = lax.axis_index("group")
         place = lax.axis_index("tile_1")
         owner = jnp.bitwise_xor(group, 1) if for_partner else group
@@ -52,6 +53,10 @@
         low = lax.broadcasted_iota(jnp.int32, (depth, LANES), 1) < LANES // 2
         copies[0].wait()
         positions = [locate(plan_ref, group, owner * OWN + slot_of(slot), home)[0] for slot in range(OWN)]
+        if for_partner:
+            for chain in range(2):
+                _, here = locate(plan_ref, group, group * OWN + slot_of(chain), home)
+                refs[0][chain] = jnp.broadcast_to(here.astype(jnp.int32), refs[0].shape[1:])
         copies[1].wait()
         for slot in range(OWN):
             up = hops(slot)[0]
@@ -73,9 +78,9 @@
     packet = jax.ShapeDtypeStruct((2 * blocks, depth, LANES), jnp.float32)
     return pl.pallas_call(
         kernel,
-        out_shape=(packet, packet),
+        out_shape=(packet, packet) + ((jax.ShapeDtypeStruct((2, 8, LANES), jnp.int32),) if for_partner else ()),
         in_specs=[HBM] * 3,
-        out_specs=(VMEM, VMEM),
+        out_specs=(VMEM, VMEM) + ((VMEM,) if for_partner else ()),
         scratch_shapes=[
             pltpu.SMEM(plan.shape, jnp.int32),
             pltpu.VMEM((home, depth, width), jnp.float32),
@@ -89,31 +94,23 @@
     )(plan, coupling, solve)
 
 
-def merge(plan, arrived, local, chain, home):
+def merge(at_home, arrived, local, chain):
     total, depth, _ = arrived.shape
     up, down = hops(chain)
     blocks = total // 2
 
-    def kernel(plan_ref, arrived_ref, local_ref, up_ref, down_ref, own_ref):
-        group = lax.axis_index("group")
-        _, here = locate(plan_ref, group, group * OWN + slot_of(chain), home)
-
-        def put(source):
-            up_ref[...] = source[0 : up + blocks]
-            down_ref[...] = source[up : total - 1]
-            if chain == 0:
-                own_ref[0] = source[total - 1]
-            else:
-                own_ref[0:blocks] = source[up : up + blocks]
-                own_ref[blocks] = source[total - 1]
-
-        @pl.when(here)
-        def _():
-            put(local_ref)
-
-        @pl.when(jnp.logical_not(here))
-        def _():
-            put(arrived_ref)
+    def kernel(home_ref, arrived_ref, local_ref, up_ref, down_ref, own_ref):
+        here = jnp.broadcast_to(home_ref[chain, 0:1, :], (depth, LANES)) != 0
+        for k in range(total):
+            block = jnp.where(here, local_ref[k], arrived_ref[k])
+            if k < up + blocks:
+                up_ref[k] = block
+            if up <= k < total - 1:
+                down_ref[k - up] = block
+            if chain == 1 and up <= k < up + blocks:
+                own_ref[k - up] = block
+            if k == total - 1:
+                own_ref[blocks if chain else 0] = block
 
     return pl.pallas_call(
         kernel,
@@ -122,11 +119,11 @@
             jax.ShapeDtypeStruct((down + blocks, depth, LANES), jnp.float32),
             jax.ShapeDtypeStruct((1 if chain == 0 else 1 + blocks, depth, LANES), jnp.float32),
         ),
-        in_specs=[SMEM, VMEM, VMEM],
+        in_specs=[VMEM, VMEM, VMEM],
         out_specs=(VMEM, VMEM, VMEM),
         compiler_params=PARAMS,
         name=f"merge_{chain}",
-    )(plan, arrived, local)
+    )(at_home, arrived, local)
 
 
 def stiff_out(plan, stiff):
@@ -320,7 +317,7 @@
     local = pack(*in_hbm, False)
     ups, downs, owns = [None, None], [None, None], [None, None]
     for chain in range(2):
-        ups[chain], downs[chain], owns[chain] = merge(migration, arrived[chain], local[chain], chain, home)
+        ups[chain], downs[chain], owns[chain] = merge(outgoing[2], arrived[chain], local[chain], chain)
     stiff_arrived = swapped(stiff_out(migration, boundary_stiffness), "group")
     stiff = stiff_merge(migration, boundary_stiffness, stiff_arrived)
 

time: 61.8 us -> 60.4 us (0.977)
  waiting for transfers between devices: 15.2 us -> 17 us
  starting transfers between devices: 36 us -> 34.3 us
  Pallas kernels: 9 us -> 7.91 us
  local copies, waits for them, and re-layouts: 0.81 us -> 0.18 us
    ppermute x12, starting transfers between devices: 28.8 us -> 26.7 us  [shifted(): lax.ppermute(array, axis, [(i, (i + distance) % size) for i in range(size)])]
    ppermute x12, waiting for transfers between devices: 8.62 us -> 10.5 us  [shifted(): lax.ppermute(array, axis, [(i, (i + distance) % size) for i in range(size)])]
    pallas_call x2, Pallas kernels: 1.21 us -> 0.11 us  [merge(): pl.pallas_call(kernel, out_shape=(jax.ShapeDtypeStruct((up + blocks, dept...]
    unnamed x4, local copies, waits for them, and re-layouts: 0.65 us -> 0.01 us
  transfers between devices with their start and end apart: 19 -> 19, of which waited for: 10 -> 10; matrix products, arithmetic and copies ran while one was open for 0% -> 0% of each run, Pallas kernels for 11% -> 10%
where the time goes in v10:
time: 60.4 us; the launch traced here: 59.9 us
  starting transfers between devices  34.3 us (57%)
  waiting for transfers between devices  17 us (28%)
  Pallas kernels  7.91 us (13%)
    ppermute x12, starting transfers between devices, shifted(): lax.ppermute(array, axis, [(i, (i + distance) % size) for i in range(size)])  26.7 us
    ppermute x12, waiting for transfers between devices, shifted(): lax.ppermute(array, axis, [(i, (i + distance) % size) for i in range(size)])  10.5 us
    ppermute x3, starting transfers between devices, crossed(): return lax.ppermute(array, TILE, pairs)  6.3 us
    ppermute x4, waiting for transfers between devices, swapped(): lax.ppermute(array, axis, [(i, i ^ 1) for i in range(lax.axis_size(axis))])  4.45 us
    pallas_call x2, Pallas kernels, pack(): pl.pallas_call(kernel, out_shape=(packet, packet) + ((jax.ShapeDtypeStruc...  2.85 us
    ppermute x3, waiting for transfers between devices, crossed(): return lax.ppermute(array, TILE, pairs)  2.05 us
    pallas_call x4, Pallas kernels, accumulate(): pl.pallas_call(kernel, out_shape=jax.ShapeDtypeStruct((LANES, width), jnp...  1.82 us
    pallas_call x2, Pallas kernels, finish(): pl.pallas_call(kernel, out_shape=jax.ShapeDtypeStruct((OWN, rows, width),...  1.48 us
  transfers between devices with their start and end apart: 19, of which 10 were waited for; matrix products, arithmetic and copies ran while one was open for 0% of the time, Pallas kernels for 10%

profile of v10, /device:TPU:24, one launch (start us, length us, event | category | flops | bytes accessed | tf_op | source)
XLA Modules:
  0.0 59.9 jit_solution(12958337282650193551)
XLA Ops:
  0.0 1.4 %pack_partner.1 = (f32[16,48,128]{2,1,0:T(8,128)S(1)}, f32[16,48,128]{2,1,0:T(8,128)S(1)}, s32[2,8,128]{2,1,0:T(8,128)S(1)}) custom-call(s32[64]{0:T(128)} %plan_hbm.3, f32[4,48,1024]{2,1,0:T(8,128)} %bitcast.1, f32[4,48,1024]{2,1,0:T(8,128)} %x_hbm.3), custom_call_target="tpu_custom_call" | custom-call | tf_op jit(solution)/shard_map/pack_partner/pallas_call | solution.py:79
  1.4 0.1 collective-permute-start.1
  1.5 0.5 collective-permute-start.2
  2.0 1.4 %pack_own.1 = (f32[16,48,128]{2,1,0:T(8,128)S(1)}, f32[16,48,128]{2,1,0:T(8,128)S(1)}) custom-call(s32[64]{0:T(128)} %plan_hbm.3, f32[4,48,1024]{2,1,0:T(8,128)} %bitcast.2, f32[4,48,1024]{2,1,0:T(8,128)} %x_hbm.3), custom_call_target="tpu_custom_call" | custom-call | tf_op jit(solution)/shard_map/pack_own/pallas_call | solution.py:79
  3.5 0.0 collective-permute-done.1.arrived_ref
  3.5 0.1 merge_0.1
  3.5 2.0 %collective-permute-start.4 = (f32[12,48,128]{2,1,0:T(8,128)S(1)}, f32[12,48,128]{2,1,0:T(8,128)S(1)}, u32[]{:S(2)}, u32[]{:S(2)}) collective-permute-start(f32[12,48,128]{2,1,0:T(8,128)S(1)} %get-tuple-element.21.refs_0_), channel_id=1, source_target_pairs={{0,1},{1,2},{2,3},{3,4},{4,5},{5,6},{6,7},{7,0},{8,9},{9,10},{10,1... | collective-permute-start | bytes 884744 | tf_op jit(solution)/shard_map/ppermute | solution.py:297
  5.5 0.0 collective-permute-done.2.arrived_ref
  5.5 0.1 merge_1.1
  5.6 5.1 %collective-permute-start.7 = (f32[12,48,128]{2,1,0:T(8,128)S(1)}, f32[12,48,128]{2,1,0:T(8,128)S(1)}, u32[]{:S(2)}, u32[]{:S(2)}) collective-permute-start(f32[12,48,128]{2,1,0:T(8,128)S(1)} %get-tuple-element.28), channel_id=1, source_target_pairs={{0,15},{1,8},{2,9},{3,10},{4,11},{5,12},{6,13},{7,14},{8,7},{9,0},... | collective-permute-start | bytes 884744 | tf_op jit(solution)/shard_map/ppermute | solution.py:307
  10.7 0.0 collective-permute-start.6
  10.7 3.2 %collective-permute-start.5 = (f32[11,48,128]{2,1,0:T(8,128)S(1)}, f32[11,48,128]{2,1,0:T(8,128)S(1)}, u32[]{:S(2)}, u32[]{:S(2)}) collective-permute-start(f32[11,48,128]{2,1,0:T(8,128)S(1)} %get-tuple-element.26), channel_id=1, source_target_pairs={{0,7},{1,0},{2,1},{3,2},{4,3},{5,4},{6,5},{7,6},{8,15},{9,8},{10,9... | collective-permute-start | bytes 811016 | tf_op jit(solution)/shard_map/ppermute | solution.py:297
  13.9 3.3 %collective-permute-done.4.refs_2_ = f32[12,48,128]{2,1,0:T(8,128)S(1)} collective-permute-done((f32[12,48,128]{2,1,0:T(8,128)S(1)}, f32[12,48,128]{2,1,0:T(8,128)S(1)}, u32[]{:S(2)}, u32[]{:S(2)}) %collective-permute-start.4) | collective-permute-done | bytes 294944 | tf_op jit(solution)/shard_map/ppermute | solution.py:297
  17.3 0.1 collective-permute-start.8
  17.4 0.9 %collective-permute-done.7.refs_5_ = f32[12,48,128]{2,1,0:T(8,128)S(1)} collective-permute-done((f32[12,48,128]{2,1,0:T(8,128)S(1)}, f32[12,48,128]{2,1,0:T(8,128)S(1)}, u32[]{:S(2)}, u32[]{:S(2)}) %collective-permute-start.7) | collective-permute-done | bytes 294944 | tf_op jit(solution)/shard_map/ppermute | solution.py:307
  18.2 0.0 copy-start
  18.3 4.5 %collective-permute-start.11 = (f32[11,48,128]{2,1,0:T(8,128)S(1)}, f32[11,48,128]{2,1,0:T(8,128)S(1)}, u32[]{:S(2)}, u32[]{:S(2)}) collective-permute-start(f32[11,48,128]{2,1,0:T(8,128)S(1)} %slice.43), channel_id=1, source_target_pairs={{0,7},{1,0},{2,1},{3,2},{4,3},{5,4},{6,5},{7,6},{8,15},{9,8},{10,9... | collective-permute-start | bytes 811016 | tf_op jit(solution)/shard_map/ppermute | solution.py:297
  22.8 1.2 %collective-permute-done.6.refs_4_ = f32[11,48,128]{2,1,0:T(8,128)S(1)} collective-permute-done((f32[11,48,128]{2,1,0:T(8,128)S(1)}, f32[11,48,128]{2,1,0:T(8,128)S(1)}, u32[]{:S(2)}, u32[]{:S(2)}) %collective-permute-start.6) | collective-permute-done | bytes 270368 | tf_op jit(solution)/shard_map/ppermute | solution.py:307
  24.0 0.1 collective-permute-start.10
  24.1 0.0 collective-permute-done.5.refs_3_
  24.1 3.7 %collective-permute-start.9 = (f32[10,48,128]{2,1,0:T(8,128)S(1)}, f32[10,48,128]{2,1,0:T(8,128)S(1)}, u32[]{:S(2)}, u32[]{:S(2)}) collective-permute-start(f32[10,48,128]{2,1,0:T(8,128)S(1)} %slice.41), channel_id=1, source_target_pairs={{0,7},{1,0},{2,1},{3,2},{4,3},{5,4},{6,5},{7,6},{8,15},{9,8},{10,9... | collective-permute-start | bytes 737288 | tf_op jit(solution)/shard_map/ppermute | solution.py:297
  27.8 1.0 %collective-permute-done.8.refs_1_ = f32[11,48,128]{2,1,0:T(8,128)S(1)} collective-permute-done((f32[11,48,128]{2,1,0:T(8,128)S(1)}, f32[11,48,128]{2,1,0:T(8,128)S(1)}, u32[]{:S(2)}, u32[]{:S(2)}) %collective-permute-start.8) | collective-permute-done | bytes 270368 | tf_op jit(solution)/shard_map/ppermute | solution.py:297
  28.9 0.8 %collective-permute-start.12 = (f32[10,48,128]{2,1,0:T(8,128)S(1)}, f32[10,48,128]{2,1,0:T(8,128)S(1)}, u32[]{:S(2)}, u32[]{:S(2)}) collective-permute-start(f32[10,48,128]{2,1,0:T(8,128)S(1)} %slice.44), channel_id=1, source_target_pairs={{0,1},{1,2},{2,3},{3,4},{4,5},{5,6},{6,7},{7,0},{8,9},{9,10},{10,1... | collective-permute-start | bytes 737288 | tf_op jit(solution)/shard_map/ppermute | solution.py:297
  29.7 0.1 collective-permute-done.11.refs_4_
  29.8 0.0 copy-start.1
  29.8 3.8 %collective-permute-start.15 = (f32[10,48,128]{2,1,0:T(8,128)S(1)}, f32[10,48,128]{2,1,0:T(8,128)S(1)}, u32[]{:S(2)}, u32[]{:S(2)}) collective-permute-start(f32[10,48,128]{2,1,0:T(8,128)S(1)} %slice.47), channel_id=1, source_target_pairs={{0,7},{1,0},{2,1},{3,2},{4,3},{5,4},{6,5},{7,6},{8,15},{9,8},{10,9... | collective-permute-start | bytes 737288 | tf_op jit(solution)/shard_map/ppermute | solution.py:297
  33.6 1.2 %collective-permute-start.3 = (f32[9,48,128]{2,1,0:T(8,128)S(1)}, f32[9,48,128]{2,1,0:T(8,128)S(1)}, u32[]{:S(2)}, u32[]{:S(2)}) collective-permute-start(f32[9,48,128]{2,1,0:T(8,128)S(1)} %get-tuple-element.25), channel_id=1, source_target_pairs={{0,8},{1,9},{2,10},{3,11},{4,12},{5,13},{6,14},{7,15},{8,0},{9,1},... | collective-permute-start | bytes 663560 | tf_op jit(solution)/shard_map/ppermute | solution.py:307
  34.8 0.0 copy-done
  34.8 0.0 copy-done.1
  34.8 0.6 %stiff_out.1 = f32[2,64,1024]{2,1,0:T(8,128)S(1)} custom-call(s32[64]{0:T(128)S(1)} %copy-done.1, f32[4,64,1024]{2,1,0:T(8,128)S(1)} %copy-done), custom_call_target="tpu_custom_call" | custom-call | tf_op jit(solution)/shard_map/stiff_out/pallas_call | solution.py:143
  35.4 0.0 collective-permute-done.10.refs_3_
  35.4 0.1 collective-permute-start
  35.5 0.0 collective-permute-done.9.refs_2_
  35.6 0.1 collective-permute-start.14
  35.7 3.2 %collective-permute-done.12.refs_1_ = f32[10,48,128]{2,1,0:T(8,128)S(1)} collective-permute-done((f32[10,48,128]{2,1,0:T(8,128)S(1)}, f32[10,48,128]{2,1,0:T(8,128)S(1)}, u32[]{:S(2)}, u32[]{:S(2)}) %collective-permute-start.12) | collective-permute-done | bytes 245792 | tf_op jit(solution)/shard_map/ppermute | solution.py:297
  38.9 5.0 %collective-permute-start.13 = (f32[9,48,128]{2,1,0:T(8,128)S(1)}, f32[9,48,128]{2,1,0:T(8,128)S(1)}, u32[]{:S(2)}, u32[]{:S(2)}) collective-permute-start(f32[9,48,128]{2,1,0:T(8,128)S(1)} %slice.45), channel_id=1, source_target_pairs={{0,7},{1,0},{2,1},{3,2},{4,3},{5,4},{6,5},{7,6},{8,15},{9,8},{10,9... | collective-permute-start | bytes 663560 | tf_op jit(solution)/shard_map/ppermute | solution.py:297
  43.9 0.0 collective-permute-done.15.refs_4_
  43.9 0.1 collective-permute-start.16
  44.0 0.0 collective-permute-done.3.refs_1_
  44.0 3.3 %collective-permute-start.17 = (f32[9,48,128]{2,1,0:T(8,128)S(1)}, f32[9,48,128]{2,1,0:T(8,128)S(1)}, u32[]{:S(2)}, u32[]{:S(2)}) collective-permute-start(f32[9,48,128]{2,1,0:T(8,128)S(1)} %slice.49), channel_id=1, source_target_pairs={{0,7},{1,0},{2,1},{3,2},{4,3},{5,4},{6,5},{7,6},{8,15},{9,8},{10,9... | collective-permute-start | bytes 663560 | tf_op jit(solution)/shard_map/ppermute | solution.py:297
  47.3 0.3 chunks_1.1.refs_0_
  47.6 0.6 chunks_2.1.refs_0_
  48.2 0.5 chunks_3.1.refs_0_
  48.7 0.0 collective-permute-done.14.refs_3_
  48.7 0.7 %collective-permute-done.13.refs_2_ = f32[9,48,128]{2,1,0:T(8,128)S(1)} collective-permute-done((f32[9,48,128]{2,1,0:T(8,128)S(1)}, f32[9,48,128]{2,1,0:T(8,128)S(1)}, u32[]{:S(2)}, u32[]{:S(2)}) %collective-permute-start.13) | collective-permute-done | bytes 221216 | tf_op jit(solution)/shard_map/ppermute | solution.py:297
  49.4 0.5 chunks_4.1.total_ref
  49.9 1.3 %collective-permute-done.16.refs_0_ = f32[9,48,128]{2,1,0:T(8,128)S(1)} collective-permute-done((f32[9,48,128]{2,1,0:T(8,128)S(1)}, f32[9,48,128]{2,1,0:T(8,128)S(1)}, u32[]{:S(2)}, u32[]{:S(2)}) %collective-permute-start.16) | collective-permute-done | bytes 221216 | tf_op jit(solution)/shard_map/ppermute | solution.py:297
  51.1 0.9 %collective-permute-done.17.refs_1_ = f32[9,48,128]{2,1,0:T(8,128)S(1)} collective-permute-done((f32[9,48,128]{2,1,0:T(8,128)S(1)}, f32[9,48,128]{2,1,0:T(8,128)S(1)}, u32[]{:S(2)}, u32[]{:S(2)}) %collective-permute-start.17) | collective-permute-done | bytes 221216 | tf_op jit(solution)/shard_map/ppermute | solution.py:297
  52.1 0.4 last_chunks.1
  52.5 0.6 %collective-permute-start.18 = (f32[64,1024]{1,0:T(8,128)S(1)}, f32[64,1024]{1,0:T(8,128)S(1)}, u32[]{:S(2)}, u32[]{:S(2)}) collective-permute-start(f32[64,1024]{1,0:T(8,128)S(1)} %get-tuple-element.30), channel_id=1, source_target_pairs={{0,8},{8,0},{1,9},{9,1},{2,10},{10,2},{3,11},{11,3},{4,12},{12,4},... | collective-permute-start | bytes 786440 | tf_op jit(solution)/shard_map/ppermute | solution.py:301
  53.1 0.0 collective-permute-done.arrived_ref
  53.1 0.6 %stiff_merge.1.refs_0_.refs_1_ = f32[2,64,1024]{2,1,0:T(8,128)S(1)} custom-call(s32[64]{0:T(128)S(1)} %copy-done.1, f32[4,64,1024]{2,1,0:T(8,128)S(1)} %copy-done, f32[2,64,1024]{2,1,0:T(8,128)S(1)} %collective-permute-done.arrived_ref), custom_call_target="tpu_custom_call" | custom-call | tf_op jit(solution)/shard_map/stiff_merge/pallas_call | solution.py:172
  53.8 0.7 %finish_0.1.refs_0_ = f32[2,64,1024]{2,1,0:T(8,128)} custom-call(f32[2,64,1024]{2,1,0:T(8,128)S(1)} %stiff_merge.1.refs_0_.refs_1_, f32[64,1024]{1,0:T(8,128)S(1)} %get-tuple-element.29.refs_1_), custom_call_target="tpu_custom_call" | custom-call | tf_op jit(solution)/shard_map/finish_0/pallas_call | solution.py:283
  54.5 4.4 %collective-permute-done.18.refs_2_ = f32[64,1024]{1,0:T(8,128)S(1)} collective-permute-done((f32[64,1024]{1,0:T(8,128)S(1)}, f32[64,1024]{1,0:T(8,128)S(1)}, u32[]{:S(2)}, u32[]{:S(2)}) %collective-permute-start.18) | collective-permute-done | bytes 262176 | tf_op jit(solution)/shard_map/ppermute | solution.py:301
  59.0 0.7 %finish_1.1 = f32[2,64,1024]{2,1,0:T(8,128)} custom-call(f32[2,64,1024]{2,1,0:T(8,128)} %finish_0.1.refs_0_, f32[2,64,1024]{2,1,0:T(8,128)S(1)} %stiff_merge.1.refs_0_.refs_1_, f32[64,1024]{1,0:T(8,128)S(1)} %collective-permute-done.18.refs_2_), custom_call_target="tpu_custom_call", output_to_operand_aliasing={{}: (0, {})} | custom-call | tf_op jit(solution)/shard_map/finish_1/pallas_call | solution.py:283
  (10 shorter events, 0.2 us)
Async XLA Ops:
  1.4 2.0 %collective-permute-start.1 = (f32[16,48,128]{2,1,0:T(8,128)S(1)}, f32[16,48,128]{2,1,0:T(8,128)S(1)}, u32[]{:S(2)}, u32[]{:S(2)}) collective-permute-start(f32[16,48,128]{2,1,0:T(8,128)S(1)} %get-tuple-element.19), channel_id=1, source_target_pairs={{0,16},{16,0},{32,48},{48,32},{64,80},{80,64},{96,112},{112,96},{1... | collective-permute-start | bytes 1179656 | tf_op jit(solution)/shard_map/ppermute | solution.py:301
  1.5 4.0 %collective-permute-start.2 = (f32[16,48,128]{2,1,0:T(8,128)S(1)}, f32[16,48,128]{2,1,0:T(8,128)S(1)}, u32[]{:S(2)}, u32[]{:S(2)}) collective-permute-start(f32[16,48,128]{2,1,0:T(8,128)S(1)} %get-tuple-element.23), channel_id=1, source_target_pairs={{0,16},{16,0},{32,48},{48,32},{64,80},{80,64},{96,112},{112,96},{1... | collective-permute-start | bytes 1179656 | tf_op jit(solution)/shard_map/ppermute | solution.py:301
  3.5 13.7 %collective-permute-start.4 = (f32[12,48,128]{2,1,0:T(8,128)S(1)}, f32[12,48,128]{2,1,0:T(8,128)S(1)}, u32[]{:S(2)}, u32[]{:S(2)}) collective-permute-start(f32[12,48,128]{2,1,0:T(8,128)S(1)} %get-tuple-element.21.refs_0_), channel_id=1, source_target_pairs={{0,1},{1,2},{2,3},{3,4},{4,5},{5,6},{6,7},{7,0},{8,9},{9,10},{10,1... | collective-permute-start | bytes 884744 | tf_op jit(solution)/shard_map/ppermute | solution.py:297
  5.6 12.6 %collective-permute-start.7 = (f32[12,48,128]{2,1,0:T(8,128)S(1)}, f32[12,48,128]{2,1,0:T(8,128)S(1)}, u32[]{:S(2)}, u32[]{:S(2)}) collective-permute-start(f32[12,48,128]{2,1,0:T(8,128)S(1)} %get-tuple-element.28), channel_id=1, source_target_pairs={{0,15},{1,8},{2,9},{3,10},{4,11},{5,12},{6,13},{7,14},{8,7},{9,0},... | collective-permute-start | bytes 884744 | tf_op jit(solution)/shard_map/ppermute | solution.py:307
  10.7 13.3 %collective-permute-start.6 = (f32[11,48,128]{2,1,0:T(8,128)S(1)}, f32[11,48,128]{2,1,0:T(8,128)S(1)}, u32[]{:S(2)}, u32[]{:S(2)}) collective-permute-start(f32[11,48,128]{2,1,0:T(8,128)S(1)} %get-tuple-element.27), channel_id=1, source_target_pairs={{0,9},{1,10},{2,11},{3,12},{4,13},{5,14},{6,15},{7,8},{8,1},{9,2},... | collective-permute-start | bytes 811016 | tf_op jit(solution)/shard_map/ppermute | solution.py:307
  10.7 13.4 %collective-permute-start.5 = (f32[11,48,128]{2,1,0:T(8,128)S(1)}, f32[11,48,128]{2,1,0:T(8,128)S(1)}, u32[]{:S(2)}, u32[]{:S(2)}) collective-permute-start(f32[11,48,128]{2,1,0:T(8,128)S(1)} %get-tuple-element.26), channel_id=1, source_target_pairs={{0,7},{1,0},{2,1},{3,2},{4,3},{5,4},{6,5},{7,6},{8,15},{9,8},{10,9... | collective-permute-start | bytes 811016 | tf_op jit(solution)/shard_map/ppermute | solution.py:297
  17.3 11.6 %collective-permute-start.8 = (f32[11,48,128]{2,1,0:T(8,128)S(1)}, f32[11,48,128]{2,1,0:T(8,128)S(1)}, u32[]{:S(2)}, u32[]{:S(2)}) collective-permute-start(f32[11,48,128]{2,1,0:T(8,128)S(1)} %slice.40), channel_id=1, source_target_pairs={{0,1},{1,2},{2,3},{3,4},{4,5},{5,6},{6,7},{7,0},{8,9},{9,10},{10,1... | collective-permute-start | bytes 811016 | tf_op jit(solution)/shard_map/ppermute | solution.py:297
  18.2 16.5 %copy-start = (f32[4,64,1024]{2,1,0:T(8,128)S(1)}, f32[4,64,1024]{2,1,0:T(8,128)}, u32[]{:S(2)}) copy-start(f32[4,64,1024]{2,1,0:T(8,128)} %b_hbm.3) | copy-start | bytes 3145732
  18.3 11.6 %collective-permute-start.11 = (f32[11,48,128]{2,1,0:T(8,128)S(1)}, f32[11,48,128]{2,1,0:T(8,128)S(1)}, u32[]{:S(2)}, u32[]{:S(2)}) collective-permute-start(f32[11,48,128]{2,1,0:T(8,128)S(1)} %slice.43), channel_id=1, source_target_pairs={{0,7},{1,0},{2,1},{3,2},{4,3},{5,4},{6,5},{7,6},{8,15},{9,8},{10,9... | collective-permute-start | bytes 811016 | tf_op jit(solution)/shard_map/ppermute | solution.py:297
  24.0 11.4 %collective-permute-start.10 = (f32[10,48,128]{2,1,0:T(8,128)S(1)}, f32[10,48,128]{2,1,0:T(8,128)S(1)}, u32[]{:S(2)}, u32[]{:S(2)}) collective-permute-start(f32[10,48,128]{2,1,0:T(8,128)S(1)} %slice.42), channel_id=1, source_target_pairs={{0,1},{1,2},{2,3},{3,4},{4,5},{5,6},{6,7},{7,0},{8,9},{9,10},{10,1... | collective-permute-start | bytes 737288 | tf_op jit(solution)/shard_map/ppermute | solution.py:297
  24.1 11.4 %collective-permute-start.9 = (f32[10,48,128]{2,1,0:T(8,128)S(1)}, f32[10,48,128]{2,1,0:T(8,128)S(1)}, u32[]{:S(2)}, u32[]{:S(2)}) collective-permute-start(f32[10,48,128]{2,1,0:T(8,128)S(1)} %slice.41), channel_id=1, source_target_pairs={{0,7},{1,0},{2,1},{3,2},{4,3},{5,4},{6,5},{7,6},{8,15},{9,8},{10,9... | collective-permute-start | bytes 737288 | tf_op jit(solution)/shard_map/ppermute | solution.py:297
  28.9 10.0 %collective-permute-start.12 = (f32[10,48,128]{2,1,0:T(8,128)S(1)}, f32[10,48,128]{2,1,0:T(8,128)S(1)}, u32[]{:S(2)}, u32[]{:S(2)}) collective-permute-start(f32[10,48,128]{2,1,0:T(8,128)S(1)} %slice.44), channel_id=1, source_target_pairs={{0,1},{1,2},{2,3},{3,4},{4,5},{5,6},{6,7},{7,0},{8,9},{9,10},{10,1... | collective-permute-start | bytes 737288 | tf_op jit(solution)/shard_map/ppermute | solution.py:297
  29.8 4.9 %copy-start.1 = (s32[64]{0:T(128)S(1)}, s32[64]{0:T(128)}, u32[]{:S(2)}) copy-start(s32[64]{0:T(128)} %plan_hbm.3) | copy-start | bytes 772
  29.8 14.1 %collective-permute-start.15 = (f32[10,48,128]{2,1,0:T(8,128)S(1)}, f32[10,48,128]{2,1,0:T(8,128)S(1)}, u32[]{:S(2)}, u32[]{:S(2)}) collective-permute-start(f32[10,48,128]{2,1,0:T(8,128)S(1)} %slice.47), channel_id=1, source_target_pairs={{0,7},{1,0},{2,1},{3,2},{4,3},{5,4},{6,5},{7,6},{8,15},{9,8},{10,9... | collective-permute-start | bytes 737288 | tf_op jit(solution)/shard_map/ppermute | solution.py:297
  33.6 10.4 %collective-permute-start.3 = (f32[9,48,128]{2,1,0:T(8,128)S(1)}, f32[9,48,128]{2,1,0:T(8,128)S(1)}, u32[]{:S(2)}, u32[]{:S(2)}) collective-permute-start(f32[9,48,128]{2,1,0:T(8,128)S(1)} %get-tuple-element.25), channel_id=1, source_target_pairs={{0,8},{1,9},{2,10},{3,11},{4,12},{5,13},{6,14},{7,15},{8,0},{9,1},... | collective-permute-start | bytes 663560 | tf_op jit(solution)/shard_map/ppermute | solution.py:307
  35.4 17.7 %collective-permute-start = (f32[2,64,1024]{2,1,0:T(8,128)S(1)}, f32[2,64,1024]{2,1,0:T(8,128)S(1)}, u32[]{:S(2)}, u32[]{:S(2)}) collective-permute-start(f32[2,64,1024]{2,1,0:T(8,128)S(1)} %stiff_out.1), channel_id=1, source_target_pairs={{0,16},{16,0},{32,48},{48,32},{64,80},{80,64},{96,112},{112,96},{1... | collective-permute-start | bytes 1572872 | tf_op jit(solution)/shard_map/ppermute | solution.py:301
  35.6 13.1 %collective-permute-start.14 = (f32[9,48,128]{2,1,0:T(8,128)S(1)}, f32[9,48,128]{2,1,0:T(8,128)S(1)}, u32[]{:S(2)}, u32[]{:S(2)}) collective-permute-start(f32[9,48,128]{2,1,0:T(8,128)S(1)} %slice.46), channel_id=1, source_target_pairs={{0,1},{1,2},{2,3},{3,4},{4,5},{5,6},{6,7},{7,0},{8,9},{9,10},{10,1... | collective-permute-start | bytes 663560 | tf_op jit(solution)/shard_map/ppermute | solution.py:297
  38.9 10.5 %collective-permute-start.13 = (f32[9,48,128]{2,1,0:T(8,128)S(1)}, f32[9,48,128]{2,1,0:T(8,128)S(1)}, u32[]{:S(2)}, u32[]{:S(2)}) collective-permute-start(f32[9,48,128]{2,1,0:T(8,128)S(1)} %slice.45), channel_id=1, source_target_pairs={{0,7},{1,0},{2,1},{3,2},{4,3},{5,4},{6,5},{7,6},{8,15},{9,8},{10,9... | collective-permute-start | bytes 663560 | tf_op jit(solution)/shard_map/ppermute | solution.py:297
  43.9 7.2 %collective-permute-start.16 = (f32[9,48,128]{2,1,0:T(8,128)S(1)}, f32[9,48,128]{2,1,0:T(8,128)S(1)}, u32[]{:S(2)}, u32[]{:S(2)}) collective-permute-start(f32[9,48,128]{2,1,0:T(8,128)S(1)} %slice.48), channel_id=1, source_target_pairs={{0,1},{1,2},{2,3},{3,4},{4,5},{5,6},{6,7},{7,0},{8,9},{9,10},{10,1... | collective-permute-start | bytes 663560 | tf_op jit(solution)/shard_map/ppermute | solution.py:297
  44.0 8.0 %collective-permute-start.17 = (f32[9,48,128]{2,1,0:T(8,128)S(1)}, f32[9,48,128]{2,1,0:T(8,128)S(1)}, u32[]{:S(2)}, u32[]{:S(2)}) collective-permute-start(f32[9,48,128]{2,1,0:T(8,128)S(1)} %slice.49), channel_id=1, source_target_pairs={{0,7},{1,0},{2,1},{3,2},{4,3},{5,4},{6,5},{7,6},{8,15},{9,8},{10,9... | collective-permute-start | bytes 663560 | tf_op jit(solution)/shard_map/ppermute | solution.py:297
  52.5 6.5 %collective-permute-start.18 = (f32[64,1024]{1,0:T(8,128)S(1)}, f32[64,1024]{1,0:T(8,128)S(1)}, u32[]{:S(2)}, u32[]{:S(2)}) collective-permute-start(f32[64,1024]{1,0:T(8,128)S(1)} %get-tuple-element.30), channel_id=1, source_target_pairs={{0,8},{8,0},{1,9},{9,1},{2,10},{10,2},{3,11},{11,3},{4,12},{12,4},... | collective-permute-start | bytes 786440 | tf_op jit(solution)/shard_map/ppermute | solution.py:301

commit v11 on v10

--- a/solution.py
+++ b/solution.py
@@ -16,7 +16,7 @@
 
 
 def hops(chain):
-    return (4, 3) if chain == 0 else (3, 4)
+    return (3, 4) if chain == 0 else (4, 3)
 
 
 def slot_of(chain):
@@ -341,9 +341,9 @@
             left_up, left_down = hops(chain)[0] - step, hops(chain)[1] - step
             sources.append((ups[chain], run(left_up + 1), ups[chain], 0))
             sources.append((downs[chain], run(0), downs[chain], blocks + left_down))
-    far0, far1 = shifted(ups[0][1:], "tile_1", 1), shifted(downs[1][:-1], "tile_1", -1)
+    far0, far1 = shifted(downs[0][:-1], "tile_1", -1), shifted(ups[1][1:], "tile_1", 1)
     total = accumulate(total, sources, width, "chunks_4")
-    send, keep = last_chunks(total, [(far0, run(1), far0, 0), (far1, run(0), far1, blocks)])
+    send, keep = last_chunks(total, [(far0, run(0), far0, blocks), (far1, run(1), far1, 0)])
     other = swapped(send, "tile_0")
     return finish(finish(None, stiff, keep, 0), stiff, other, 1)
 

time: 60.4 us -> 59.1 us (0.978)
  starting transfers between devices: 34.3 us -> 30 us
  waiting for transfers between devices: 17 us -> 20.2 us
    ppermute x12, starting transfers between devices: 26.7 us -> 20.3 us  [shifted(): lax.ppermute(array, axis, [(i, (i + distance) % size) for i in range(size)])]
    ppermute x3, waiting for transfers between devices: 2.05 us -> 6.85 us  [crossed(): return lax.ppermute(array, TILE, pairs)]
    ppermute x3, starting transfers between devices: 6.3 us -> 7.32 us  [crossed(): return lax.ppermute(array, TILE, pairs)]
    ppermute x4, starting transfers between devices: 1.3 us -> 2.3 us  [swapped(): lax.ppermute(array, axis, [(i, i ^ 1) for i in range(lax.axis_size(axis))])]
    ppermute x12, waiting for transfers between devices: 10.5 us -> 9.61 us  [shifted(): lax.ppermute(array, axis, [(i, (i + distance) % size) for i in range(size)])]
    ppermute x4, waiting for transfers between devices: 4.45 us -> 3.76 us  [swapped(): lax.ppermute(array, axis, [(i, i ^ 1) for i in range(lax.axis_size(axis))])]
  transfers between devices with their start and end apart: 19 -> 19, of which waited for: 10 -> 9; matrix products, arithmetic and copies ran while one was open for 0% -> 0% of each run, Pallas kernels for 10% -> 10%
where the time goes in v11:
time: 59.1 us; the launch traced here: 58.7 us
  starting transfers between devices  30 us (51%)
  waiting for transfers between devices  20.2 us (34%)
  Pallas kernels  7.92 us (13%)
    ppermute x12, starting transfers between devices, shifted(): lax.ppermute(array, axis, [(i, (i + distance) % size) for i in range(size)])  20.3 us
    ppermute x12, waiting for transfers between devices, shifted(): lax.ppermute(array, axis, [(i, (i + distance) % size) for i in range(size)])  9.61 us
    ppermute x3, starting transfers between devices, crossed(): return lax.ppermute(array, TILE, pairs)  7.32 us
    ppermute x3, waiting for transfers between devices, crossed(): return lax.ppermute(array, TILE, pairs)  6.85 us
    ppermute x4, waiting for transfers between devices, swapped(): lax.ppermute(array, axis, [(i, i ^ 1) for i in range(lax.axis_size(axis))])  3.76 us
    pallas_call x2, Pallas kernels, pack(): pl.pallas_call(kernel, out_shape=(packet, packet) + ((jax.ShapeDtypeStruc...  2.85 us
    ppermute x4, starting transfers between devices, swapped(): lax.ppermute(array, axis, [(i, i ^ 1) for i in range(lax.axis_size(axis))])  2.3 us
    pallas_call x4, Pallas kernels, accumulate(): pl.pallas_call(kernel, out_shape=jax.ShapeDtypeStruct((LANES, width), jnp...  1.83 us
  transfers between devices with their start and end apart: 19, of which 9 were waited for; matrix products, arithmetic and copies ran while one was open for 0% of the time, Pallas kernels for 10%

profile of v11, /device:TPU:24, one launch (start us, length us, event | category | flops | bytes accessed | tf_op | source)
XLA Modules:
  0.0 58.7 jit_solution(9388254723585645273)
XLA Ops:
  0.0 1.4 %pack_partner.1 = (f32[16,48,128]{2,1,0:T(8,128)S(1)}, f32[16,48,128]{2,1,0:T(8,128)S(1)}, s32[2,8,128]{2,1,0:T(8,128)S(1)}) custom-call(s32[64]{0:T(128)} %plan_hbm.3, f32[4,48,1024]{2,1,0:T(8,128)} %bitcast.1, f32[4,48,1024]{2,1,0:T(8,128)} %x_hbm.3), custom_call_target="tpu_custom_call" | custom-call | tf_op jit(solution)/shard_map/pack_partner/pallas_call | solution.py:79
  1.4 0.1 collective-permute-start.2
  1.5 0.5 collective-permute-start.1
  2.0 1.4 %pack_own.1 = (f32[16,48,128]{2,1,0:T(8,128)S(1)}, f32[16,48,128]{2,1,0:T(8,128)S(1)}) custom-call(s32[64]{0:T(128)} %plan_hbm.3, f32[4,48,1024]{2,1,0:T(8,128)} %bitcast.2, f32[4,48,1024]{2,1,0:T(8,128)} %x_hbm.3), custom_call_target="tpu_custom_call" | custom-call | tf_op jit(solution)/shard_map/pack_own/pallas_call | solution.py:79
  3.5 0.0 collective-permute-done.2.arrived_ref
  3.5 0.1 merge_1.1
  3.5 2.9 %collective-permute-start.6 = (f32[12,48,128]{2,1,0:T(8,128)S(1)}, f32[12,48,128]{2,1,0:T(8,128)S(1)}, u32[]{:S(2)}, u32[]{:S(2)}) collective-permute-start(f32[12,48,128]{2,1,0:T(8,128)S(1)} %get-tuple-element.27), channel_id=1, source_target_pairs={{0,9},{1,10},{2,11},{3,12},{4,13},{5,14},{6,15},{7,8},{8,1},{9,2},... | collective-permute-start | bytes 884744 | tf_op jit(solution)/shard_map/ppermute | solution.py:307
  6.5 0.0 collective-permute-done.1.arrived_ref
  6.5 3.3 %collective-permute-start.5 = (f32[12,48,128]{2,1,0:T(8,128)S(1)}, f32[12,48,128]{2,1,0:T(8,128)S(1)}, u32[]{:S(2)}, u32[]{:S(2)}) collective-permute-start(f32[12,48,128]{2,1,0:T(8,128)S(1)} %get-tuple-element.26), channel_id=1, source_target_pairs={{0,7},{1,0},{2,1},{3,2},{4,3},{5,4},{6,5},{7,6},{8,15},{9,8},{10,9... | collective-permute-start | bytes 884744 | tf_op jit(solution)/shard_map/ppermute | solution.py:297
  9.8 0.0 collective-permute-start.4
  9.8 4.2 %collective-permute-start.7 = (f32[11,48,128]{2,1,0:T(8,128)S(1)}, f32[11,48,128]{2,1,0:T(8,128)S(1)}, u32[]{:S(2)}, u32[]{:S(2)}) collective-permute-start(f32[11,48,128]{2,1,0:T(8,128)S(1)} %get-tuple-element.28), channel_id=1, source_target_pairs={{0,15},{1,8},{2,9},{3,10},{4,11},{5,12},{6,13},{7,14},{8,7},{9,0},... | collective-permute-start | bytes 811016 | tf_op jit(solution)/shard_map/ppermute | solution.py:307
  14.0 5.7 %collective-permute-done.6.refs_4_ = f32[12,48,128]{2,1,0:T(8,128)S(1)} collective-permute-done((f32[12,48,128]{2,1,0:T(8,128)S(1)}, f32[12,48,128]{2,1,0:T(8,128)S(1)}, u32[]{:S(2)}, u32[]{:S(2)}) %collective-permute-start.6) | collective-permute-done | bytes 294944 | tf_op jit(solution)/shard_map/ppermute | solution.py:307
  19.6 0.1 collective-permute-start.10
  19.7 0.0 collective-permute-done.5.refs_3_
  19.8 0.0 copy-start
  19.8 3.3 %collective-permute-start.9 = (f32[11,48,128]{2,1,0:T(8,128)S(1)}, f32[11,48,128]{2,1,0:T(8,128)S(1)}, u32[]{:S(2)}, u32[]{:S(2)}) collective-permute-start(f32[11,48,128]{2,1,0:T(8,128)S(1)} %slice.41), channel_id=1, source_target_pairs={{0,7},{1,0},{2,1},{3,2},{4,3},{5,4},{6,5},{7,6},{8,15},{9,8},{10,9... | collective-permute-start | bytes 811016 | tf_op jit(solution)/shard_map/ppermute | solution.py:297
  23.1 0.0 collective-permute-done.4.refs_2_
  23.1 0.1 collective-permute-start.8
  23.2 1.2 %collective-permute-done.7.refs_5_ = f32[11,48,128]{2,1,0:T(8,128)S(1)} collective-permute-done((f32[11,48,128]{2,1,0:T(8,128)S(1)}, f32[11,48,128]{2,1,0:T(8,128)S(1)}, u32[]{:S(2)}, u32[]{:S(2)}) %collective-permute-start.7) | collective-permute-done | bytes 270368 | tf_op jit(solution)/shard_map/ppermute | solution.py:307
  24.4 3.3 %collective-permute-start.11 = (f32[10,48,128]{2,1,0:T(8,128)S(1)}, f32[10,48,128]{2,1,0:T(8,128)S(1)}, u32[]{:S(2)}, u32[]{:S(2)}) collective-permute-start(f32[10,48,128]{2,1,0:T(8,128)S(1)} %slice.43), channel_id=1, source_target_pairs={{0,7},{1,0},{2,1},{3,2},{4,3},{5,4},{6,5},{7,6},{8,15},{9,8},{10,9... | collective-permute-start | bytes 737288 | tf_op jit(solution)/shard_map/ppermute | solution.py:297
  27.7 2.7 %collective-permute-done.10.refs_3_ = f32[11,48,128]{2,1,0:T(8,128)S(1)} collective-permute-done((f32[11,48,128]{2,1,0:T(8,128)S(1)}, f32[11,48,128]{2,1,0:T(8,128)S(1)}, u32[]{:S(2)}, u32[]{:S(2)}) %collective-permute-start.10) | collective-permute-done | bytes 270368 | tf_op jit(solution)/shard_map/ppermute | solution.py:297
  30.4 0.1 collective-permute-start.14
  30.5 0.0 collective-permute-done.9.refs_2_
  30.5 0.0 copy-start.1
  30.5 3.3 %collective-permute-start.13 = (f32[10,48,128]{2,1,0:T(8,128)S(1)}, f32[10,48,128]{2,1,0:T(8,128)S(1)}, u32[]{:S(2)}, u32[]{:S(2)}) collective-permute-start(f32[10,48,128]{2,1,0:T(8,128)S(1)} %slice.45), channel_id=1, source_target_pairs={{0,7},{1,0},{2,1},{3,2},{4,3},{5,4},{6,5},{7,6},{8,15},{9,8},{10,9... | collective-permute-start | bytes 737288 | tf_op jit(solution)/shard_map/ppermute | solution.py:297
  33.8 0.2 collective-permute-start.3
  34.0 0.0 copy-done
  34.0 0.0 copy-done.1
  34.0 0.6 %stiff_out.1 = f32[2,64,1024]{2,1,0:T(8,128)S(1)} custom-call(s32[64]{0:T(128)S(1)} %copy-done.1, f32[4,64,1024]{2,1,0:T(8,128)S(1)} %copy-done), custom_call_target="tpu_custom_call" | custom-call | tf_op jit(solution)/shard_map/stiff_out/pallas_call | solution.py:143
  34.7 0.9 %collective-permute-done.8.refs_1_ = f32[10,48,128]{2,1,0:T(8,128)S(1)} collective-permute-done((f32[10,48,128]{2,1,0:T(8,128)S(1)}, f32[10,48,128]{2,1,0:T(8,128)S(1)}, u32[]{:S(2)}, u32[]{:S(2)}) %collective-permute-start.8) | collective-permute-done | bytes 245792 | tf_op jit(solution)/shard_map/ppermute | solution.py:297
  35.6 0.0 collective-permute-start
  35.6 0.0 collective-permute-done.11.refs_4_
  35.7 0.1 collective-permute-start.12
  35.8 3.1 %collective-permute-done.14.refs_3_ = f32[10,48,128]{2,1,0:T(8,128)S(1)} collective-permute-done((f32[10,48,128]{2,1,0:T(8,128)S(1)}, f32[10,48,128]{2,1,0:T(8,128)S(1)}, u32[]{:S(2)}, u32[]{:S(2)}) %collective-permute-start.14) | collective-permute-done | bytes 245792 | tf_op jit(solution)/shard_map/ppermute | solution.py:297
  38.9 3.5 %collective-permute-start.15 = (f32[9,48,128]{2,1,0:T(8,128)S(1)}, f32[9,48,128]{2,1,0:T(8,128)S(1)}, u32[]{:S(2)}, u32[]{:S(2)}) collective-permute-start(f32[9,48,128]{2,1,0:T(8,128)S(1)} %slice.47), channel_id=1, source_target_pairs={{0,7},{1,0},{2,1},{3,2},{4,3},{5,4},{6,5},{7,6},{8,15},{9,8},{10,9... | collective-permute-start | bytes 663560 | tf_op jit(solution)/shard_map/ppermute | solution.py:297
  42.4 0.0 collective-permute-done.13.refs_2_
  42.4 0.1 collective-permute-start.17
  42.5 0.0 collective-permute-done.3.refs_1_
  42.5 3.3 %collective-permute-start.16 = (f32[9,48,128]{2,1,0:T(8,128)S(1)}, f32[9,48,128]{2,1,0:T(8,128)S(1)}, u32[]{:S(2)}, u32[]{:S(2)}) collective-permute-start(f32[9,48,128]{2,1,0:T(8,128)S(1)} %slice.48), channel_id=1, source_target_pairs={{0,7},{1,0},{2,1},{3,2},{4,3},{5,4},{6,5},{7,6},{8,15},{9,8},{10,9... | collective-permute-start | bytes 663560 | tf_op jit(solution)/shard_map/ppermute | solution.py:297
  45.8 0.3 chunks_1.1.refs_0_
  46.1 0.6 chunks_2.1.refs_0_
  46.7 0.5 chunks_3.1.refs_0_
  47.2 0.0 collective-permute-done.12.refs_1_
  47.2 0.7 %collective-permute-done.15.refs_4_ = f32[9,48,128]{2,1,0:T(8,128)S(1)} collective-permute-done((f32[9,48,128]{2,1,0:T(8,128)S(1)}, f32[9,48,128]{2,1,0:T(8,128)S(1)}, u32[]{:S(2)}, u32[]{:S(2)}) %collective-permute-start.15) | collective-permute-done | bytes 221216 | tf_op jit(solution)/shard_map/ppermute | solution.py:297
  47.9 0.5 chunks_4.1.total_ref
  48.4 1.3 %collective-permute-done.17.refs_1_ = f32[9,48,128]{2,1,0:T(8,128)S(1)} collective-permute-done((f32[9,48,128]{2,1,0:T(8,128)S(1)}, f32[9,48,128]{2,1,0:T(8,128)S(1)}, u32[]{:S(2)}, u32[]{:S(2)}) %collective-permute-start.17) | collective-permute-done | bytes 221216 | tf_op jit(solution)/shard_map/ppermute | solution.py:297
  49.6 0.9 %collective-permute-done.16.refs_0_ = f32[9,48,128]{2,1,0:T(8,128)S(1)} collective-permute-done((f32[9,48,128]{2,1,0:T(8,128)S(1)}, f32[9,48,128]{2,1,0:T(8,128)S(1)}, u32[]{:S(2)}, u32[]{:S(2)}) %collective-permute-start.16) | collective-permute-done | bytes 221216 | tf_op jit(solution)/shard_map/ppermute | solution.py:297
  50.6 0.4 last_chunks.1
  51.0 1.7 %collective-permute-start.18 = (f32[64,1024]{1,0:T(8,128)S(1)}, f32[64,1024]{1,0:T(8,128)S(1)}, u32[]{:S(2)}, u32[]{:S(2)}) collective-permute-start(f32[64,1024]{1,0:T(8,128)S(1)} %get-tuple-element.30), channel_id=1, source_target_pairs={{0,8},{8,0},{1,9},{9,1},{2,10},{10,2},{3,11},{11,3},{4,12},{12,4},... | collective-permute-start | bytes 786440 | tf_op jit(solution)/shard_map/ppermute | solution.py:301
  52.7 0.0 collective-permute-done.arrived_ref
  52.7 0.6 %stiff_merge.1.refs_0_.refs_1_ = f32[2,64,1024]{2,1,0:T(8,128)S(1)} custom-call(s32[64]{0:T(128)S(1)} %copy-done.1, f32[4,64,1024]{2,1,0:T(8,128)S(1)} %copy-done, f32[2,64,1024]{2,1,0:T(8,128)S(1)} %collective-permute-done.arrived_ref), custom_call_target="tpu_custom_call" | custom-call | tf_op jit(solution)/shard_map/stiff_merge/pallas_call | solution.py:172
  53.3 0.7 %finish_0.1.refs_0_ = f32[2,64,1024]{2,1,0:T(8,128)} custom-call(f32[2,64,1024]{2,1,0:T(8,128)S(1)} %stiff_merge.1.refs_0_.refs_1_, f32[64,1024]{1,0:T(8,128)S(1)} %get-tuple-element.29.refs_1_), custom_call_target="tpu_custom_call" | custom-call | tf_op jit(solution)/shard_map/finish_0/pallas_call | solution.py:283
  54.1 3.8 %collective-permute-done.18.refs_2_ = f32[64,1024]{1,0:T(8,128)S(1)} collective-permute-done((f32[64,1024]{1,0:T(8,128)S(1)}, f32[64,1024]{1,0:T(8,128)S(1)}, u32[]{:S(2)}, u32[]{:S(2)}) %collective-permute-start.18) | collective-permute-done | bytes 262176 | tf_op jit(solution)/shard_map/ppermute | solution.py:301
  57.8 0.7 %finish_1.1 = f32[2,64,1024]{2,1,0:T(8,128)} custom-call(f32[2,64,1024]{2,1,0:T(8,128)} %finish_0.1.refs_0_, f32[2,64,1024]{2,1,0:T(8,128)S(1)} %stiff_merge.1.refs_0_.refs_1_, f32[64,1024]{1,0:T(8,128)S(1)} %collective-permute-done.18.refs_2_), custom_call_target="tpu_custom_call", output_to_operand_aliasing={{}: (0, {})} | custom-call | tf_op jit(solution)/shard_map/finish_1/pallas_call | solution.py:283
  (11 shorter events, 0.2 us)
Async XLA Ops:
  1.4 2.0 %collective-permute-start.2 = (f32[16,48,128]{2,1,0:T(8,128)S(1)}, f32[16,48,128]{2,1,0:T(8,128)S(1)}, u32[]{:S(2)}, u32[]{:S(2)}) collective-permute-start(f32[16,48,128]{2,1,0:T(8,128)S(1)} %get-tuple-element.23), channel_id=1, source_target_pairs={{0,16},{16,0},{32,48},{48,32},{64,80},{80,64},{96,112},{112,96},{1... | collective-permute-start | bytes 1179656 | tf_op jit(solution)/shard_map/ppermute | solution.py:301
  1.5 4.9 %collective-permute-start.1 = (f32[16,48,128]{2,1,0:T(8,128)S(1)}, f32[16,48,128]{2,1,0:T(8,128)S(1)}, u32[]{:S(2)}, u32[]{:S(2)}) collective-permute-start(f32[16,48,128]{2,1,0:T(8,128)S(1)} %get-tuple-element.19), channel_id=1, source_target_pairs={{0,16},{16,0},{32,48},{48,32},{64,80},{80,64},{96,112},{112,96},{1... | collective-permute-start | bytes 1179656 | tf_op jit(solution)/shard_map/ppermute | solution.py:301
  3.5 16.1 %collective-permute-start.6 = (f32[12,48,128]{2,1,0:T(8,128)S(1)}, f32[12,48,128]{2,1,0:T(8,128)S(1)}, u32[]{:S(2)}, u32[]{:S(2)}) collective-permute-start(f32[12,48,128]{2,1,0:T(8,128)S(1)} %get-tuple-element.27), channel_id=1, source_target_pairs={{0,9},{1,10},{2,11},{3,12},{4,13},{5,14},{6,15},{7,8},{8,1},{9,2},... | collective-permute-start | bytes 884744 | tf_op jit(solution)/shard_map/ppermute | solution.py:307
  6.5 13.2 %collective-permute-start.5 = (f32[12,48,128]{2,1,0:T(8,128)S(1)}, f32[12,48,128]{2,1,0:T(8,128)S(1)}, u32[]{:S(2)}, u32[]{:S(2)}) collective-permute-start(f32[12,48,128]{2,1,0:T(8,128)S(1)} %get-tuple-element.26), channel_id=1, source_target_pairs={{0,7},{1,0},{2,1},{3,2},{4,3},{5,4},{6,5},{7,6},{8,15},{9,8},{10,9... | collective-permute-start | bytes 884744 | tf_op jit(solution)/shard_map/ppermute | solution.py:297
  9.8 13.3 %collective-permute-start.4 = (f32[11,48,128]{2,1,0:T(8,128)S(1)}, f32[11,48,128]{2,1,0:T(8,128)S(1)}, u32[]{:S(2)}, u32[]{:S(2)}) collective-permute-start(f32[11,48,128]{2,1,0:T(8,128)S(1)} %get-tuple-element.21.refs_0_), channel_id=1, source_target_pairs={{0,1},{1,2},{2,3},{3,4},{4,5},{5,6},{6,7},{7,0},{8,9},{9,10},{10,1... | collective-permute-start | bytes 811016 | tf_op jit(solution)/shard_map/ppermute | solution.py:297
  9.8 14.6 %collective-permute-start.7 = (f32[11,48,128]{2,1,0:T(8,128)S(1)}, f32[11,48,128]{2,1,0:T(8,128)S(1)}, u32[]{:S(2)}, u32[]{:S(2)}) collective-permute-start(f32[11,48,128]{2,1,0:T(8,128)S(1)} %get-tuple-element.28), channel_id=1, source_target_pairs={{0,15},{1,8},{2,9},{3,10},{4,11},{5,12},{6,13},{7,14},{8,7},{9,0},... | collective-permute-start | bytes 811016 | tf_op jit(solution)/shard_map/ppermute | solution.py:307
  19.6 10.7 %collective-permute-start.10 = (f32[11,48,128]{2,1,0:T(8,128)S(1)}, f32[11,48,128]{2,1,0:T(8,128)S(1)}, u32[]{:S(2)}, u32[]{:S(2)}) collective-permute-start(f32[11,48,128]{2,1,0:T(8,128)S(1)} %slice.42), channel_id=1, source_target_pairs={{0,1},{1,2},{2,3},{3,4},{4,5},{5,6},{6,7},{7,0},{8,9},{9,10},{10,1... | collective-permute-start | bytes 811016 | tf_op jit(solution)/shard_map/ppermute | solution.py:297
  19.8 14.3 %copy-start = (f32[4,64,1024]{2,1,0:T(8,128)S(1)}, f32[4,64,1024]{2,1,0:T(8,128)}, u32[]{:S(2)}) copy-start(f32[4,64,1024]{2,1,0:T(8,128)} %b_hbm.3) | copy-start | bytes 3145732
  19.8 10.7 %collective-permute-start.9 = (f32[11,48,128]{2,1,0:T(8,128)S(1)}, f32[11,48,128]{2,1,0:T(8,128)S(1)}, u32[]{:S(2)}, u32[]{:S(2)}) collective-permute-start(f32[11,48,128]{2,1,0:T(8,128)S(1)} %slice.41), channel_id=1, source_target_pairs={{0,7},{1,0},{2,1},{3,2},{4,3},{5,4},{6,5},{7,6},{8,15},{9,8},{10,9... | collective-permute-start | bytes 811016 | tf_op jit(solution)/shard_map/ppermute | solution.py:297
  23.1 12.5 %collective-permute-start.8 = (f32[10,48,128]{2,1,0:T(8,128)S(1)}, f32[10,48,128]{2,1,0:T(8,128)S(1)}, u32[]{:S(2)}, u32[]{:S(2)}) collective-permute-start(f32[10,48,128]{2,1,0:T(8,128)S(1)} %slice.40), channel_id=1, source_target_pairs={{0,1},{1,2},{2,3},{3,4},{4,5},{5,6},{6,7},{7,0},{8,9},{9,10},{10,1... | collective-permute-start | bytes 737288 | tf_op jit(solution)/shard_map/ppermute | solution.py:297
  24.4 11.3 %collective-permute-start.11 = (f32[10,48,128]{2,1,0:T(8,128)S(1)}, f32[10,48,128]{2,1,0:T(8,128)S(1)}, u32[]{:S(2)}, u32[]{:S(2)}) collective-permute-start(f32[10,48,128]{2,1,0:T(8,128)S(1)} %slice.43), channel_id=1, source_target_pairs={{0,7},{1,0},{2,1},{3,2},{4,3},{5,4},{6,5},{7,6},{8,15},{9,8},{10,9... | collective-permute-start | bytes 737288 | tf_op jit(solution)/shard_map/ppermute | solution.py:297
  30.4 8.5 %collective-permute-start.14 = (f32[10,48,128]{2,1,0:T(8,128)S(1)}, f32[10,48,128]{2,1,0:T(8,128)S(1)}, u32[]{:S(2)}, u32[]{:S(2)}) collective-permute-start(f32[10,48,128]{2,1,0:T(8,128)S(1)} %slice.46), channel_id=1, source_target_pairs={{0,1},{1,2},{2,3},{3,4},{4,5},{5,6},{6,7},{7,0},{8,9},{9,10},{10,1... | collective-permute-start | bytes 737288 | tf_op jit(solution)/shard_map/ppermute | solution.py:297
  30.5 3.5 %copy-start.1 = (s32[64]{0:T(128)S(1)}, s32[64]{0:T(128)}, u32[]{:S(2)}) copy-start(s32[64]{0:T(128)} %plan_hbm.3) | copy-start | bytes 772
  30.5 11.9 %collective-permute-start.13 = (f32[10,48,128]{2,1,0:T(8,128)S(1)}, f32[10,48,128]{2,1,0:T(8,128)S(1)}, u32[]{:S(2)}, u32[]{:S(2)}) collective-permute-start(f32[10,48,128]{2,1,0:T(8,128)S(1)} %slice.45), channel_id=1, source_target_pairs={{0,7},{1,0},{2,1},{3,2},{4,3},{5,4},{6,5},{7,6},{8,15},{9,8},{10,9... | collective-permute-start | bytes 737288 | tf_op jit(solution)/shard_map/ppermute | solution.py:297
  33.8 8.7 %collective-permute-start.3 = (f32[9,48,128]{2,1,0:T(8,128)S(1)}, f32[9,48,128]{2,1,0:T(8,128)S(1)}, u32[]{:S(2)}, u32[]{:S(2)}) collective-permute-start(f32[9,48,128]{2,1,0:T(8,128)S(1)} %get-tuple-element.25), channel_id=1, source_target_pairs={{0,8},{1,9},{2,10},{3,11},{4,12},{5,13},{6,14},{7,15},{8,0},{9,1},... | collective-permute-start | bytes 663560 | tf_op jit(solution)/shard_map/ppermute | solution.py:307
  35.6 17.1 %collective-permute-start = (f32[2,64,1024]{2,1,0:T(8,128)S(1)}, f32[2,64,1024]{2,1,0:T(8,128)S(1)}, u32[]{:S(2)}, u32[]{:S(2)}) collective-permute-start(f32[2,64,1024]{2,1,0:T(8,128)S(1)} %stiff_out.1), channel_id=1, source_target_pairs={{0,16},{16,0},{32,48},{48,32},{64,80},{80,64},{96,112},{112,96},{1... | collective-permute-start | bytes 1572872 | tf_op jit(solution)/shard_map/ppermute | solution.py:301
  35.7 11.5 %collective-permute-start.12 = (f32[9,48,128]{2,1,0:T(8,128)S(1)}, f32[9,48,128]{2,1,0:T(8,128)S(1)}, u32[]{:S(2)}, u32[]{:S(2)}) collective-permute-start(f32[9,48,128]{2,1,0:T(8,128)S(1)} %slice.44), channel_id=1, source_target_pairs={{0,1},{1,2},{2,3},{3,4},{4,5},{5,6},{6,7},{7,0},{8,9},{9,10},{10,1... | collective-permute-start | bytes 663560 | tf_op jit(solution)/shard_map/ppermute | solution.py:297
  38.9 9.0 %collective-permute-start.15 = (f32[9,48,128]{2,1,0:T(8,128)S(1)}, f32[9,48,128]{2,1,0:T(8,128)S(1)}, u32[]{:S(2)}, u32[]{:S(2)}) collective-permute-start(f32[9,48,128]{2,1,0:T(8,128)S(1)} %slice.47), channel_id=1, source_target_pairs={{0,7},{1,0},{2,1},{3,2},{4,3},{5,4},{6,5},{7,6},{8,15},{9,8},{10,9... | collective-permute-start | bytes 663560 | tf_op jit(solution)/shard_map/ppermute | solution.py:297
  42.4 7.2 %collective-permute-start.17 = (f32[9,48,128]{2,1,0:T(8,128)S(1)}, f32[9,48,128]{2,1,0:T(8,128)S(1)}, u32[]{:S(2)}, u32[]{:S(2)}) collective-permute-start(f32[9,48,128]{2,1,0:T(8,128)S(1)} %slice.49), channel_id=1, source_target_pairs={{0,1},{1,2},{2,3},{3,4},{4,5},{5,6},{6,7},{7,0},{8,9},{9,10},{10,1... | collective-permute-start | bytes 663560 | tf_op jit(solution)/shard_map/ppermute | solution.py:297
  42.5 8.0 %collective-permute-start.16 = (f32[9,48,128]{2,1,0:T(8,128)S(1)}, f32[9,48,128]{2,1,0:T(8,128)S(1)}, u32[]{:S(2)}, u32[]{:S(2)}) collective-permute-start(f32[9,48,128]{2,1,0:T(8,128)S(1)} %slice.48), channel_id=1, source_target_pairs={{0,7},{1,0},{2,1},{3,2},{4,3},{5,4},{6,5},{7,6},{8,15},{9,8},{10,9... | collective-permute-start | bytes 663560 | tf_op jit(solution)/shard_map/ppermute | solution.py:297
  51.0 6.9 %collective-permute-start.18 = (f32[64,1024]{1,0:T(8,128)S(1)}, f32[64,1024]{1,0:T(8,128)S(1)}, u32[]{:S(2)}, u32[]{:S(2)}) collective-permute-start(f32[64,1024]{1,0:T(8,128)S(1)} %get-tuple-element.30), channel_id=1, source_target_pairs={{0,8},{8,0},{1,9},{9,1},{2,10},{10,2},{3,11},{11,3},{4,12},{12,4},... | collective-permute-start | bytes 786440 | tf_op jit(solution)/shard_map/ppermute | solution.py:301

commit v12 on v11

--- a/solution.py
+++ b/solution.py
@@ -126,58 +126,38 @@
     )(at_home, arrived, local)
 
 
-def stiff_out(plan, stiff):
+def pack_stiff(plan, stiff):
     home, rows, width = stiff.shape
 
-    def kernel(plan_ref, b_hbm, out_ref, sem):
+    def kernel(plan_hbm, b_hbm, leaving_ref, own_ref, plan_ref, plan_sem, sem):
         group = lax.axis_index("group")
+        plan_copy = pltpu.make_async_copy(plan_hbm, plan_ref, plan_sem)
+        plan_copy.start()
+        plan_copy.wait()
         copies = []
-        for slot in range(OWN):
-            position, _ = locate(plan_ref, group, jnp.bitwise_xor(group, 1) * OWN + slot, home)
-            copy = pltpu.make_async_copy(b_hbm.at[position], out_ref.at[slot], sem.at[slot])
+        for k, (owner, out_ref) in enumerate(((jnp.bitwise_xor(group, 1), leaving_ref), (group, own_ref))):
+            for slot in range(OWN):
+                position, _ = locate(plan_ref, group, owner * OWN + slot, home)
+                copies.append(pltpu.make_async_copy(b_hbm.at[position], out_ref.at[slot], sem.at[k, slot]))
+        for copy in copies:
             copy.start()
-            copies.append(copy)
         for copy in copies:
             copy.wait()
 
-    return pl.pallas_call(
-        kernel,
-        out_shape=jax.ShapeDtypeStruct((OWN, rows, width), jnp.float32),
-        in_specs=[SMEM, HBM],
-        out_specs=VMEM,
-        scratch_shapes=[pltpu.SemaphoreType.DMA((OWN,))],
-        compiler_params=PARAMS,
-        name="stiff_out",
+    half = jax.ShapeDtypeStruct((OWN, rows, width), jnp.float32)
+    return pl.pallas_call(
+        kernel,
+        out_shape=(half, half),
+        in_specs=[HBM, HBM],
+        out_specs=(VMEM, VMEM),
+        scratch_shapes=[
+            pltpu.SMEM(plan.shape, jnp.int32),
+            pltpu.SemaphoreType.DMA,
+            pltpu.SemaphoreType.DMA((2, OWN)),
+        ],
+        compiler_params=PARAMS,
+        name="pack_stiff",
     )(plan, stiff)
-
-
-def stiff_merge(plan, stiff, arrived):
-    home, rows, width = stiff.shape
-
-    def kernel(plan_ref, b_hbm, arrived_ref, out_ref, sem):
-        group = lax.axis_index("group")
-        for slot in range(OWN):
-            position, here = locate(plan_ref, group, group * OWN + slot, home)
-
-            @pl.when(here)
-            def _():
-                copy = pltpu.make_async_copy(b_hbm.at[position], out_ref.at[slot], sem.at[slot])
-                copy.start()
-                copy.wait()
-
-            @pl.when(jnp.logical_not(here))
-            def _():
-                out_ref[slot] = arrived_ref[slot]
-
-    return pl.pallas_call(
-        kernel,
-        out_shape=jax.ShapeDtypeStruct((OWN, rows, width), jnp.float32),
-        in_specs=[SMEM, HBM, VMEM],
-        out_specs=VMEM,
-        scratch_shapes=[pltpu.SemaphoreType.DMA((OWN,))],
-        compiler_params=PARAMS,
-        name="stiff_merge",
-    )(plan, stiff, arrived)
 
 
 def split(value):
@@ -268,14 +248,18 @@
     )(total, *arrays)
 
 
-def finish(result, stiff, product, chain):
+def finish(result, at_home, stiff_own, stiff_arrived, product, chain):
     rows, width = product.shape
     given = [] if result is None else [result]
 
     def kernel(*refs):
-        stiff_ref, product_ref, out_hbm, buf, sem = refs[len(given) :]
+        home_ref, own_ref, arrived_ref, product_ref, out_hbm, buf, sem = refs[len(given) :]
         slot = slot_of(chain)
-        buf[...] = stiff_ref[slot] - product_ref[...]
+        for n in range(0, width, LANES):
+            columns = pl.ds(n, LANES)
+            here = jnp.broadcast_to(home_ref[chain, 0:1, :], (rows, LANES)) != 0
+            stiff = jnp.where(here, own_ref[slot, :, columns], arrived_ref[slot, :, columns])
+            buf[:, columns] = stiff - product_ref[:, columns]
         copy = pltpu.make_async_copy(buf, out_hbm.at[slot], sem)
         copy.start()
         copy.wait()
@@ -283,13 +267,17 @@
     return pl.pallas_call(
         kernel,
         out_shape=jax.ShapeDtypeStruct((OWN, rows, width), jnp.float32),
-        in_specs=[HBM] * len(given) + [VMEM, VMEM],
+        in_specs=[HBM] * len(given) + [VMEM] * 4,
         out_specs=HBM,
         scratch_shapes=[pltpu.VMEM((rows, width), jnp.float32), pltpu.SemaphoreType.DMA],
         input_output_aliases={0: 0} if given else {},
         compiler_params=PARAMS,
         name=f"finish_{chain}",
-    )(*given, stiff, product)
+    )(*given, at_home, stiff_own, stiff_arrived, product)
+
+
+def after(array, *earlier):
+    return lax.optimization_barrier((array, *earlier))[0]
 
 
 def shifted(array, axis, distance):
@@ -318,8 +306,10 @@
     ups, downs, owns = [None, None], [None, None], [None, None]
     for chain in range(2):
         ups[chain], downs[chain], owns[chain] = merge(outgoing[2], arrived[chain], local[chain], chain)
-    stiff_arrived = swapped(stiff_out(migration, boundary_stiffness), "group")
-    stiff = stiff_merge(migration, boundary_stiffness, stiff_arrived)
+    stiff_leaving, stiff_own = pack_stiff(
+        after(in_hbm[0], ups[1]), pltpu.with_memory_space_constraint(boundary_stiffness, pltpu.HBM)
+    )
+    stiff_arrived = swapped(stiff_leaving, "group")
 
     def run(first):
         return list(range(first, first + blocks))
@@ -333,6 +323,8 @@
                 ups[chain], downs[chain] = crossed(ups[chain], 1), crossed(downs[chain], -1)
             else:
                 sent_up = ups[chain] if step == 1 else ups[chain][1:]
+                if step == 2 and chain == 0:
+                    sent_up = after(sent_up, stiff_leaving)
                 sent_down = downs[chain] if step == 1 else downs[chain][:-1]
                 ups[chain], downs[chain] = shifted(sent_up, "tile_1", 1), shifted(sent_down, "tile_1", -1)
         total = accumulate(total, sources, width, f"chunks_{step}")
@@ -345,7 +337,8 @@
     total = accumulate(total, sources, width, "chunks_4")
     send, keep = last_chunks(total, [(far0, run(0), far0, blocks), (far1, run(1), far1, 0)])
     other = swapped(send, "tile_0")
-    return finish(finish(None, stiff, keep, 0), stiff, other, 1)
+    result = finish(None, outgoing[2], stiff_own, stiff_arrived, keep, 0)
+    return finish(result, outgoing[2], stiff_own, stiff_arrived, other, 1)
 
 
 def solution(mesh):

time: 59.1 us -> 58.9 us (level)
  waiting for transfers between devices: 20.2 us -> 18.1 us
  starting transfers between devices: 30 us -> 31.2 us
  Pallas kernels: 7.92 us -> 8.59 us
    ppermute x12, waiting for transfers between devices: 9.61 us -> 8.25 us  [shifted(): lax.ppermute(array, axis, [(i, (i + distance) % size) for i in range(size)])]
    ppermute x3, waiting for transfers between devices: 6.85 us -> 5.67 us  [crossed(): return lax.ppermute(array, TILE, pairs)]
    ppermute x3, starting transfers between devices: 7.32 us -> 8.18 us  [crossed(): return lax.ppermute(array, TILE, pairs)]
    pallas_call x2 -> x1, Pallas kernels: 1.26 us -> 1.9 us  [pack_stiff(): pl.pallas_call(kernel, out_shape=(half, half), in_specs=[HBM, HBM], out_s...]
  transfers between devices with their start and end apart: 19 -> 19, of which waited for: 9 -> 8; matrix products, arithmetic and copies ran while one was open for 0% -> 0% of each run, Pallas kernels for 10% -> 11%
where the time goes in v12:
time: 58.9 us; the launch traced here: 58.5 us
  starting transfers between devices  31.2 us (53%)
  waiting for transfers between devices  18.1 us (31%)
  Pallas kernels  8.59 us (15%)
    ppermute x12, starting transfers between devices, shifted(): lax.ppermute(array, axis, [(i, (i + distance) % size) for i in range(size)])  20.8 us
    ppermute x12, waiting for transfers between devices, shifted(): lax.ppermute(array, axis, [(i, (i + distance) % size) for i in range(size)])  8.25 us
    ppermute x3, starting transfers between devices, crossed(): return lax.ppermute(array, TILE, pairs)  8.18 us
    ppermute x3, waiting for transfers between devices, crossed(): return lax.ppermute(array, TILE, pairs)  5.67 us
    ppermute x4, waiting for transfers between devices, swapped(): lax.ppermute(array, axis, [(i, i ^ 1) for i in range(lax.axis_size(axis))])  4.14 us
    pallas_call x2, Pallas kernels, pack(): pl.pallas_call(kernel, out_shape=(packet, packet) + ((jax.ShapeDtypeStruc...  2.85 us
    ppermute x4, starting transfers between devices, swapped(): lax.ppermute(array, axis, [(i, i ^ 1) for i in range(lax.axis_size(axis))])  2.3 us
    pallas_call x1, Pallas kernels, pack_stiff(): pl.pallas_call(kernel, out_shape=(half, half), in_specs=[HBM, HBM], out_s...  1.9 us
  transfers between devices with their start and end apart: 19, of which 8 were waited for; matrix products, arithmetic and copies ran while one was open for 0% of the time, Pallas kernels for 11%

profile of v12, /device:TPU:24, one launch (start us, length us, event | category | flops | bytes accessed | tf_op | source)
XLA Modules:
  0.0 58.5 jit_solution(13770087701471708498)
XLA Ops:
  0.0 1.4 %pack_partner.1 = (f32[16,48,128]{2,1,0:T(8,128)S(1)}, f32[16,48,128]{2,1,0:T(8,128)S(1)}, s32[2,8,128]{2,1,0:T(8,128)S(1)}) custom-call(s32[64]{0:T(128)} %plan_hbm.4, f32[4,48,1024]{2,1,0:T(8,128)} %bitcast.1, f32[4,48,1024]{2,1,0:T(8,128)} %x_hbm.3), custom_call_target="tpu_custom_call" | custom-call | tf_op jit(solution)/shard_map/pack_partner/pallas_call | solution.py:79
  1.4 0.1 collective-permute-start
  1.5 0.5 collective-permute-start.2
  2.0 1.4 %pack_own.1 = (f32[16,48,128]{2,1,0:T(8,128)S(1)}, f32[16,48,128]{2,1,0:T(8,128)S(1)}) custom-call(s32[64]{0:T(128)} %plan_hbm.4, f32[4,48,1024]{2,1,0:T(8,128)} %bitcast.2, f32[4,48,1024]{2,1,0:T(8,128)} %x_hbm.3), custom_call_target="tpu_custom_call" | custom-call | tf_op jit(solution)/shard_map/pack_own/pallas_call | solution.py:79
  3.5 0.0 collective-permute-done.arrived_ref
  3.5 0.1 merge_1.1
  3.5 2.9 %collective-permute-start.6 = (f32[12,48,128]{2,1,0:T(8,128)S(1)}, f32[12,48,128]{2,1,0:T(8,128)S(1)}, u32[]{:S(2)}, u32[]{:S(2)}) collective-permute-start(f32[12,48,128]{2,1,0:T(8,128)S(1)} %get-tuple-element.25), channel_id=1, source_target_pairs={{0,9},{1,10},{2,11},{3,12},{4,13},{5,14},{6,15},{7,8},{8,1},{9,2},... | collective-permute-start | bytes 884744 | tf_op jit(solution)/shard_map/ppermute | solution.py:295
  6.5 0.0 collective-permute-done.2.arrived_ref
  6.5 3.3 %collective-permute-start.5 = (f32[12,48,128]{2,1,0:T(8,128)S(1)}, f32[12,48,128]{2,1,0:T(8,128)S(1)}, u32[]{:S(2)}, u32[]{:S(2)}) collective-permute-start(f32[12,48,128]{2,1,0:T(8,128)S(1)} %get-tuple-element.34), channel_id=1, source_target_pairs={{0,7},{1,0},{2,1},{3,2},{4,3},{5,4},{6,5},{7,6},{8,15},{9,8},{10,9... | collective-permute-start | bytes 884744 | tf_op jit(solution)/shard_map/ppermute | solution.py:285
  9.8 0.0 collective-permute-start.4
  9.8 4.2 %collective-permute-start.7 = (f32[11,48,128]{2,1,0:T(8,128)S(1)}, f32[11,48,128]{2,1,0:T(8,128)S(1)}, u32[]{:S(2)}, u32[]{:S(2)}) collective-permute-start(f32[11,48,128]{2,1,0:T(8,128)S(1)} %get-tuple-element.35), channel_id=1, source_target_pairs={{0,15},{1,8},{2,9},{3,10},{4,11},{5,12},{6,13},{7,14},{8,7},{9,0},... | collective-permute-start | bytes 811016 | tf_op jit(solution)/shard_map/ppermute | solution.py:295
  14.0 5.7 %collective-permute-done.6.refs_4_ = f32[12,48,128]{2,1,0:T(8,128)S(1)} collective-permute-done((f32[12,48,128]{2,1,0:T(8,128)S(1)}, f32[12,48,128]{2,1,0:T(8,128)S(1)}, u32[]{:S(2)}, u32[]{:S(2)}) %collective-permute-start.6) | collective-permute-done | bytes 294944 | tf_op jit(solution)/shard_map/ppermute | solution.py:295
  19.6 0.1 collective-permute-start.10
  19.7 0.0 collective-permute-done.5.refs_3_
  19.8 3.3 %collective-permute-start.9 = (f32[11,48,128]{2,1,0:T(8,128)S(1)}, f32[11,48,128]{2,1,0:T(8,128)S(1)}, u32[]{:S(2)}, u32[]{:S(2)}) collective-permute-start(f32[11,48,128]{2,1,0:T(8,128)S(1)} %slice.41), channel_id=1, source_target_pairs={{0,7},{1,0},{2,1},{3,2},{4,3},{5,4},{6,5},{7,6},{8,15},{9,8},{10,9... | collective-permute-start | bytes 811016 | tf_op jit(solution)/shard_map/ppermute | solution.py:285
  23.1 1.9 %pack_stiff.1 = (f32[2,64,1024]{2,1,0:T(8,128)S(1)}, f32[2,64,1024]{2,1,0:T(8,128)S(1)}) custom-call(s32[64]{0:T(128)} %plan_hbm.4, f32[4,64,1024]{2,1,0:T(8,128)} %b_hbm.1), custom_call_target="tpu_custom_call" | custom-call | tf_op jit(solution)/shard_map/pack_stiff/pallas_call | solution.py:148
  25.0 0.0 collective-permute-done.4.refs_2_
  25.0 0.1 collective-permute-start.8
  25.1 0.0 collective-permute-done.7.refs_5_
  25.1 3.3 %collective-permute-start.11 = (f32[10,48,128]{2,1,0:T(8,128)S(1)}, f32[10,48,128]{2,1,0:T(8,128)S(1)}, u32[]{:S(2)}, u32[]{:S(2)}) collective-permute-start(f32[10,48,128]{2,1,0:T(8,128)S(1)} %slice.43), channel_id=1, source_target_pairs={{0,7},{1,0},{2,1},{3,2},{4,3},{5,4},{6,5},{7,6},{8,15},{9,8},{10,9... | collective-permute-start | bytes 737288 | tf_op jit(solution)/shard_map/ppermute | solution.py:285
  28.4 0.9 %collective-permute-done.10.refs_3_ = f32[11,48,128]{2,1,0:T(8,128)S(1)} collective-permute-done((f32[11,48,128]{2,1,0:T(8,128)S(1)}, f32[11,48,128]{2,1,0:T(8,128)S(1)}, u32[]{:S(2)}, u32[]{:S(2)}) %collective-permute-start.10) | collective-permute-done | bytes 270368 | tf_op jit(solution)/shard_map/ppermute | solution.py:285
  29.3 0.1 collective-permute-start.14
  29.4 0.0 collective-permute-done.9.refs_2_
  29.4 3.5 %collective-permute-start.13 = (f32[10,48,128]{2,1,0:T(8,128)S(1)}, f32[10,48,128]{2,1,0:T(8,128)S(1)}, u32[]{:S(2)}, u32[]{:S(2)}) collective-permute-start(f32[10,48,128]{2,1,0:T(8,128)S(1)} %slice.45), channel_id=1, source_target_pairs={{0,7},{1,0},{2,1},{3,2},{4,3},{5,4},{6,5},{7,6},{8,15},{9,8},{10,9... | collective-permute-start | bytes 737288 | tf_op jit(solution)/shard_map/ppermute | solution.py:285
  32.9 1.1 %collective-permute-start.3 = (f32[9,48,128]{2,1,0:T(8,128)S(1)}, f32[9,48,128]{2,1,0:T(8,128)S(1)}, u32[]{:S(2)}, u32[]{:S(2)}) collective-permute-start(f32[9,48,128]{2,1,0:T(8,128)S(1)} %get-tuple-element.33), channel_id=1, source_target_pairs={{0,8},{1,9},{2,10},{3,11},{4,12},{5,13},{6,14},{7,15},{8,0},{9,1},... | collective-permute-start | bytes 663560 | tf_op jit(solution)/shard_map/ppermute | solution.py:295
  34.0 1.2 %collective-permute-done.8.refs_1_ = f32[10,48,128]{2,1,0:T(8,128)S(1)} collective-permute-done((f32[10,48,128]{2,1,0:T(8,128)S(1)}, f32[10,48,128]{2,1,0:T(8,128)S(1)}, u32[]{:S(2)}, u32[]{:S(2)}) %collective-permute-start.8) | collective-permute-done | bytes 245792 | tf_op jit(solution)/shard_map/ppermute | solution.py:285
  35.2 0.0 collective-permute-start.1
  35.2 0.0 collective-permute-done.11.refs_4_
  35.2 0.1 collective-permute-start.12
  35.3 3.5 %collective-permute-done.14.refs_3_ = f32[10,48,128]{2,1,0:T(8,128)S(1)} collective-permute-done((f32[10,48,128]{2,1,0:T(8,128)S(1)}, f32[10,48,128]{2,1,0:T(8,128)S(1)}, u32[]{:S(2)}, u32[]{:S(2)}) %collective-permute-start.14) | collective-permute-done | bytes 245792 | tf_op jit(solution)/shard_map/ppermute | solution.py:285
  38.9 3.5 %collective-permute-start.15 = (f32[9,48,128]{2,1,0:T(8,128)S(1)}, f32[9,48,128]{2,1,0:T(8,128)S(1)}, u32[]{:S(2)}, u32[]{:S(2)}) collective-permute-start(f32[9,48,128]{2,1,0:T(8,128)S(1)} %slice.47), channel_id=1, source_target_pairs={{0,7},{1,0},{2,1},{3,2},{4,3},{5,4},{6,5},{7,6},{8,15},{9,8},{10,9... | collective-permute-start | bytes 663560 | tf_op jit(solution)/shard_map/ppermute | solution.py:285
  42.4 0.0 collective-permute-done.13.refs_2_
  42.4 0.3 collective-permute-start.17
  42.7 0.0 collective-permute-done.3.refs_1_
  42.7 3.3 %collective-permute-start.16 = (f32[9,48,128]{2,1,0:T(8,128)S(1)}, f32[9,48,128]{2,1,0:T(8,128)S(1)}, u32[]{:S(2)}, u32[]{:S(2)}) collective-permute-start(f32[9,48,128]{2,1,0:T(8,128)S(1)} %slice.48), channel_id=1, source_target_pairs={{0,7},{1,0},{2,1},{3,2},{4,3},{5,4},{6,5},{7,6},{8,15},{9,8},{10,9... | collective-permute-start | bytes 663560 | tf_op jit(solution)/shard_map/ppermute | solution.py:285
  46.0 0.3 chunks_1.1.refs_0_
  46.3 0.6 chunks_2.1.refs_0_
  46.8 0.5 chunks_3.1.refs_0_
  47.4 0.0 collective-permute-done.12.refs_1_
  47.4 0.4 collective-permute-done.15.refs_4_
  47.7 0.5 chunks_4.1.total_ref
  48.3 1.6 %collective-permute-done.17.refs_1_ = f32[9,48,128]{2,1,0:T(8,128)S(1)} collective-permute-done((f32[9,48,128]{2,1,0:T(8,128)S(1)}, f32[9,48,128]{2,1,0:T(8,128)S(1)}, u32[]{:S(2)}, u32[]{:S(2)}) %collective-permute-start.17) | collective-permute-done | bytes 221216 | tf_op jit(solution)/shard_map/ppermute | solution.py:285
  49.8 0.8 %collective-permute-done.16.refs_0_ = f32[9,48,128]{2,1,0:T(8,128)S(1)} collective-permute-done((f32[9,48,128]{2,1,0:T(8,128)S(1)}, f32[9,48,128]{2,1,0:T(8,128)S(1)}, u32[]{:S(2)}, u32[]{:S(2)}) %collective-permute-start.16) | collective-permute-done | bytes 221216 | tf_op jit(solution)/shard_map/ppermute | solution.py:285
  50.6 0.4 last_chunks.1
  51.0 1.7 %collective-permute-start.18 = (f32[64,1024]{1,0:T(8,128)S(1)}, f32[64,1024]{1,0:T(8,128)S(1)}, u32[]{:S(2)}, u32[]{:S(2)}) collective-permute-start(f32[64,1024]{1,0:T(8,128)S(1)} %get-tuple-element.38), channel_id=1, source_target_pairs={{0,8},{8,0},{1,9},{9,1},{2,10},{10,2},{3,11},{11,3},{4,12},{12,4},... | collective-permute-start | bytes 786440 | tf_op jit(solution)/shard_map/ppermute | solution.py:289
  52.7 0.0 collective-permute-done.1.refs_2_.refs_3_
  52.7 0.8 %finish_0.1.refs_0_ = f32[2,64,1024]{2,1,0:T(8,128)} custom-call(s32[2,8,128]{2,1,0:T(8,128)S(1)} %get-tuple-element.22.home_ref.refs_0_.refs_1_, f32[2,64,1024]{2,1,0:T(8,128)S(1)} %get-tuple-element.27.refs_1_.refs_2_, f32[2,64,1024]{2,1,0:T(8,128)S(1)} %collective-permute-done.1.refs_2_.refs_3_, f32[64,1024]{1,0:T(8,128)S(1)} %get-tuple-element.37.refs_3_), custom_call_target="tpu_custom_call" | custom-call | tf_op jit(solution)/shard_map/finish_0/pallas_call | solution.py:267
  53.4 4.1 %collective-permute-done.18.refs_4_ = f32[64,1024]{1,0:T(8,128)S(1)} collective-permute-done((f32[64,1024]{1,0:T(8,128)S(1)}, f32[64,1024]{1,0:T(8,128)S(1)}, u32[]{:S(2)}, u32[]{:S(2)}) %collective-permute-start.18) | collective-permute-done | bytes 262176 | tf_op jit(solution)/shard_map/ppermute | solution.py:289
  57.6 0.8 %finish_1.1 = f32[2,64,1024]{2,1,0:T(8,128)} custom-call(f32[2,64,1024]{2,1,0:T(8,128)} %finish_0.1.refs_0_, s32[2,8,128]{2,1,0:T(8,128)S(1)} %get-tuple-element.22.home_ref.refs_0_.refs_1_, f32[2,64,1024]{2,1,0:T(8,128)S(1)} %get-tuple-element.27.refs_1_.refs_2_, ...), custom_call_target="tpu_custom_call", output_to_operand_aliasing={{}: (0, {})} | custom-call | tf_op jit(solution)/shard_map/finish_1/pallas_call | solution.py:267
  (11 shorter events, 0.2 us)
Async XLA Ops:
  1.4 2.0 %collective-permute-start = (f32[16,48,128]{2,1,0:T(8,128)S(1)}, f32[16,48,128]{2,1,0:T(8,128)S(1)}, u32[]{:S(2)}, u32[]{:S(2)}) collective-permute-start(f32[16,48,128]{2,1,0:T(8,128)S(1)} %get-tuple-element.23), channel_id=1, source_target_pairs={{0,16},{16,0},{32,48},{48,32},{64,80},{80,64},{96,112},{112,96},{1... | collective-permute-start | bytes 1179656 | tf_op jit(solution)/shard_map/ppermute | solution.py:289
  1.5 4.9 %collective-permute-start.2 = (f32[16,48,128]{2,1,0:T(8,128)S(1)}, f32[16,48,128]{2,1,0:T(8,128)S(1)}, u32[]{:S(2)}, u32[]{:S(2)}) collective-permute-start(f32[16,48,128]{2,1,0:T(8,128)S(1)} %get-tuple-element.29), channel_id=1, source_target_pairs={{0,16},{16,0},{32,48},{48,32},{64,80},{80,64},{96,112},{112,96},{1... | collective-permute-start | bytes 1179656 | tf_op jit(solution)/shard_map/ppermute | solution.py:289
  3.5 16.1 %collective-permute-start.6 = (f32[12,48,128]{2,1,0:T(8,128)S(1)}, f32[12,48,128]{2,1,0:T(8,128)S(1)}, u32[]{:S(2)}, u32[]{:S(2)}) collective-permute-start(f32[12,48,128]{2,1,0:T(8,128)S(1)} %get-tuple-element.25), channel_id=1, source_target_pairs={{0,9},{1,10},{2,11},{3,12},{4,13},{5,14},{6,15},{7,8},{8,1},{9,2},... | collective-permute-start | bytes 884744 | tf_op jit(solution)/shard_map/ppermute | solution.py:295
  6.5 13.2 %collective-permute-start.5 = (f32[12,48,128]{2,1,0:T(8,128)S(1)}, f32[12,48,128]{2,1,0:T(8,128)S(1)}, u32[]{:S(2)}, u32[]{:S(2)}) collective-permute-start(f32[12,48,128]{2,1,0:T(8,128)S(1)} %get-tuple-element.34), channel_id=1, source_target_pairs={{0,7},{1,0},{2,1},{3,2},{4,3},{5,4},{6,5},{7,6},{8,15},{9,8},{10,9... | collective-permute-start | bytes 884744 | tf_op jit(solution)/shard_map/ppermute | solution.py:285
  9.8 15.2 %collective-permute-start.4 = (f32[11,48,128]{2,1,0:T(8,128)S(1)}, f32[11,48,128]{2,1,0:T(8,128)S(1)}, u32[]{:S(2)}, u32[]{:S(2)}) collective-permute-start(f32[11,48,128]{2,1,0:T(8,128)S(1)} %get-tuple-element.31.refs_0_), channel_id=1, source_target_pairs={{0,1},{1,2},{2,3},{3,4},{4,5},{5,6},{6,7},{7,0},{8,9},{9,10},{10,1... | collective-permute-start | bytes 811016 | tf_op jit(solution)/shard_map/ppermute | solution.py:285
  9.8 15.3 %collective-permute-start.7 = (f32[11,48,128]{2,1,0:T(8,128)S(1)}, f32[11,48,128]{2,1,0:T(8,128)S(1)}, u32[]{:S(2)}, u32[]{:S(2)}) collective-permute-start(f32[11,48,128]{2,1,0:T(8,128)S(1)} %get-tuple-element.35), channel_id=1, source_target_pairs={{0,15},{1,8},{2,9},{3,10},{4,11},{5,12},{6,13},{7,14},{8,7},{9,0},... | collective-permute-start | bytes 811016 | tf_op jit(solution)/shard_map/ppermute | solution.py:295
  19.6 9.6 %collective-permute-start.10 = (f32[11,48,128]{2,1,0:T(8,128)S(1)}, f32[11,48,128]{2,1,0:T(8,128)S(1)}, u32[]{:S(2)}, u32[]{:S(2)}) collective-permute-start(f32[11,48,128]{2,1,0:T(8,128)S(1)} %slice.42), channel_id=1, source_target_pairs={{0,1},{1,2},{2,3},{3,4},{4,5},{5,6},{6,7},{7,0},{8,9},{9,10},{10,1... | collective-permute-start | bytes 811016 | tf_op jit(solution)/shard_map/ppermute | solution.py:285
  19.8 9.6 %collective-permute-start.9 = (f32[11,48,128]{2,1,0:T(8,128)S(1)}, f32[11,48,128]{2,1,0:T(8,128)S(1)}, u32[]{:S(2)}, u32[]{:S(2)}) collective-permute-start(f32[11,48,128]{2,1,0:T(8,128)S(1)} %slice.41), channel_id=1, source_target_pairs={{0,7},{1,0},{2,1},{3,2},{4,3},{5,4},{6,5},{7,6},{8,15},{9,8},{10,9... | collective-permute-start | bytes 811016 | tf_op jit(solution)/shard_map/ppermute | solution.py:285
  25.0 10.2 %collective-permute-start.8 = (f32[10,48,128]{2,1,0:T(8,128)S(1)}, f32[10,48,128]{2,1,0:T(8,128)S(1)}, u32[]{:S(2)}, u32[]{:S(2)}) collective-permute-start(f32[10,48,128]{2,1,0:T(8,128)S(1)} %slice.40), channel_id=1, source_target_pairs={{0,1},{1,2},{2,3},{3,4},{4,5},{5,6},{6,7},{7,0},{8,9},{9,10},{10,1... | collective-permute-start | bytes 737288 | tf_op jit(solution)/shard_map/ppermute | solution.py:285
  25.1 10.1 %collective-permute-start.11 = (f32[10,48,128]{2,1,0:T(8,128)S(1)}, f32[10,48,128]{2,1,0:T(8,128)S(1)}, u32[]{:S(2)}, u32[]{:S(2)}) collective-permute-start(f32[10,48,128]{2,1,0:T(8,128)S(1)} %slice.43), channel_id=1, source_target_pairs={{0,7},{1,0},{2,1},{3,2},{4,3},{5,4},{6,5},{7,6},{8,15},{9,8},{10,9... | collective-permute-start | bytes 737288 | tf_op jit(solution)/shard_map/ppermute | solution.py:285
  29.3 9.6 %collective-permute-start.14 = (f32[10,48,128]{2,1,0:T(8,128)S(1)}, f32[10,48,128]{2,1,0:T(8,128)S(1)}, u32[]{:S(2)}, u32[]{:S(2)}) collective-permute-start(f32[10,48,128]{2,1,0:T(8,128)S(1)} %slice.46), channel_id=1, source_target_pairs={{0,1},{1,2},{2,3},{3,4},{4,5},{5,6},{6,7},{7,0},{8,9},{9,10},{10,1... | collective-permute-start | bytes 737288 | tf_op jit(solution)/shard_map/ppermute | solution.py:285
  29.4 13.0 %collective-permute-start.13 = (f32[10,48,128]{2,1,0:T(8,128)S(1)}, f32[10,48,128]{2,1,0:T(8,128)S(1)}, u32[]{:S(2)}, u32[]{:S(2)}) collective-permute-start(f32[10,48,128]{2,1,0:T(8,128)S(1)} %slice.45), channel_id=1, source_target_pairs={{0,7},{1,0},{2,1},{3,2},{4,3},{5,4},{6,5},{7,6},{8,15},{9,8},{10,9... | collective-permute-start | bytes 737288 | tf_op jit(solution)/shard_map/ppermute | solution.py:285
  32.9 9.8 %collective-permute-start.3 = (f32[9,48,128]{2,1,0:T(8,128)S(1)}, f32[9,48,128]{2,1,0:T(8,128)S(1)}, u32[]{:S(2)}, u32[]{:S(2)}) collective-permute-start(f32[9,48,128]{2,1,0:T(8,128)S(1)} %get-tuple-element.33), channel_id=1, source_target_pairs={{0,8},{1,9},{2,10},{3,11},{4,12},{5,13},{6,14},{7,15},{8,0},{9,1},... | collective-permute-start | bytes 663560 | tf_op jit(solution)/shard_map/ppermute | solution.py:295
  35.2 17.5 %collective-permute-start.1 = (f32[2,64,1024]{2,1,0:T(8,128)S(1)}, f32[2,64,1024]{2,1,0:T(8,128)S(1)}, u32[]{:S(2)}, u32[]{:S(2)}) collective-permute-start(f32[2,64,1024]{2,1,0:T(8,128)S(1)} %get-tuple-element.28), channel_id=1, source_target_pairs={{0,16},{16,0},{32,48},{48,32},{64,80},{80,64},{96,112},{112,96},{1... | collective-permute-start | bytes 1572872 | tf_op jit(solution)/shard_map/ppermute | solution.py:289
  35.2 12.1 %collective-permute-start.12 = (f32[9,48,128]{2,1,0:T(8,128)S(1)}, f32[9,48,128]{2,1,0:T(8,128)S(1)}, u32[]{:S(2)}, u32[]{:S(2)}) collective-permute-start(f32[9,48,128]{2,1,0:T(8,128)S(1)} %slice.44), channel_id=1, source_target_pairs={{0,1},{1,2},{2,3},{3,4},{4,5},{5,6},{6,7},{7,0},{8,9},{9,10},{10,1... | collective-permute-start | bytes 663560 | tf_op jit(solution)/shard_map/ppermute | solution.py:285
  38.9 8.9 %collective-permute-start.15 = (f32[9,48,128]{2,1,0:T(8,128)S(1)}, f32[9,48,128]{2,1,0:T(8,128)S(1)}, u32[]{:S(2)}, u32[]{:S(2)}) collective-permute-start(f32[9,48,128]{2,1,0:T(8,128)S(1)} %slice.47), channel_id=1, source_target_pairs={{0,7},{1,0},{2,1},{3,2},{4,3},{5,4},{6,5},{7,6},{8,15},{9,8},{10,9... | collective-permute-start | bytes 663560 | tf_op jit(solution)/shard_map/ppermute | solution.py:285
  42.4 7.4 %collective-permute-start.17 = (f32[9,48,128]{2,1,0:T(8,128)S(1)}, f32[9,48,128]{2,1,0:T(8,128)S(1)}, u32[]{:S(2)}, u32[]{:S(2)}) collective-permute-start(f32[9,48,128]{2,1,0:T(8,128)S(1)} %slice.49), channel_id=1, source_target_pairs={{0,1},{1,2},{2,3},{3,4},{4,5},{5,6},{6,7},{7,0},{8,9},{9,10},{10,1... | collective-permute-start | bytes 663560 | tf_op jit(solution)/shard_map/ppermute | solution.py:285
  42.7 7.9 %collective-permute-start.16 = (f32[9,48,128]{2,1,0:T(8,128)S(1)}, f32[9,48,128]{2,1,0:T(8,128)S(1)}, u32[]{:S(2)}, u32[]{:S(2)}) collective-permute-start(f32[9,48,128]{2,1,0:T(8,128)S(1)} %slice.48), channel_id=1, source_target_pairs={{0,7},{1,0},{2,1},{3,2},{4,3},{5,4},{6,5},{7,6},{8,15},{9,8},{10,9... | collective-permute-start | bytes 663560 | tf_op jit(solution)/shard_map/ppermute | solution.py:285
  51.0 6.6 %collective-permute-start.18 = (f32[64,1024]{1,0:T(8,128)S(1)}, f32[64,1024]{1,0:T(8,128)S(1)}, u32[]{:S(2)}, u32[]{:S(2)}) collective-permute-start(f32[64,1024]{1,0:T(8,128)S(1)} %get-tuple-element.38), channel_id=1, source_target_pairs={{0,8},{8,0},{1,9},{9,1},{2,10},{10,2},{3,11},{11,3},{4,12},{12,4},... | collective-permute-start | bytes 786440 | tf_op jit(solution)/shard_map/ppermute | solution.py:289
